TPU v7x, 32 devices: a whole 2x2x4 slice. The times are simulated.
32 devices in a mesh: exp: 4 (over y, x), seq: 8 (over z, core).
Axes of the slice: x: 2, y: 2, z: 4, core: 2. Of those that a mesh axis runs over, the one named last changes fastest.
Arguments:
- tokens: bfloat16 [4096, 2048], P(('exp', 'seq')), may hold values from -6 to 6
- routes: int32 [4096, 6], P(('exp', 'seq')), may hold values from 0 to 63, all different within a row; in each aligned block of 128 rows (0 to 127, 128 to 255, ...) at most 16 rows name the same one
- route_weights: float32 [4096, 6], P(('exp', 'seq')), may hold values from 0.2 to 1
- norm_gain: bfloat16 [2048], P(('exp', 'seq')), may hold values from 0.099609375 to 1.8984375
- w_query: bfloat16 [2048, 3072], P('exp', 'seq'), may hold values from -0.125 to 0.125
- w_kv_down: bfloat16 [2048, 576], P(('exp', 'seq')), may hold values from -0.125 to 0.125
- latent_gain: bfloat16 [512], P(('exp', 'seq')), may hold values from 0.099609375 to 1.8984375
- w_kv_up: bfloat16 [512, 4096], P('exp', 'seq'), may hold values from -0.25 to 0.25
- w_output: bfloat16 [2048, 2048], P('seq', 'exp'), may hold values from -2 to 2
- ffn_gain: bfloat16 [2048], P(('exp', 'seq')), may hold values from 0.099609375 to 1.8984375
- shared_gate: bfloat16 [2048, 2816], P('exp', 'seq'), may hold values from -0.125 to 0.125
- shared_up: bfloat16 [2048, 2816], P('exp', 'seq'), may hold values from -0.125 to 0.125
- shared_down: bfloat16 [2816, 2048], P('seq', 'exp'), may hold values from -0.109375 to 0.109375
- expert_gate: bfloat16 [64, 2048, 1408], P(('exp', 'seq')), may hold values from -0.125 to 0.125
- expert_up: bfloat16 [64, 2048, 1408], P(('exp', 'seq')), may hold values from -0.125 to 0.125
- expert_down: bfloat16 [64, 1408, 2048], P(('exp', 'seq')), may hold values from -0.15625 to 0.15625
- out_grad: bfloat16 [4096, 2048], P(('exp', 'seq')), may hold values from -6 to 6
Outputs:
- output: bfloat16 [4096, 2048], P(('exp', 'seq'))
- tokens_grad: bfloat16 [4096, 2048], P(('exp', 'seq'))
- norm_gain_grad: float32 [2048], P(('exp', 'seq'))
- w_query_grad: float32 [2048, 3072], P('exp', 'seq')
- w_kv_down_grad: float32 [2048, 576], P(('exp', 'seq'))
- latent_gain_grad: float32 [512], P(('exp', 'seq'))
- w_kv_up_grad: float32 [512, 4096], P('exp', 'seq')
- w_output_grad: float32 [2048, 2048], P('seq', 'exp')
- ffn_gain_grad: float32 [2048], P(('exp', 'seq'))
- shared_gate_grad: float32 [2048, 2816], P('exp', 'seq')
- shared_up_grad: float32 [2048, 2816], P('exp', 'seq')
- shared_down_grad: float32 [2816, 2048], P('seq', 'exp')
- expert_gate_grad: float32 [64, 2048, 1408], P(('exp', 'seq'))
- expert_up_grad: float32 [64, 2048, 1408], P(('exp', 'seq'))
- expert_down_grad: float32 [64, 1408, 2048], P(('exp', 'seq'))
Inputs may be any that keep to these rules, and one draw needn't show every extreme that they name: `routes`: each token names 6 different experts. Among the 128 tokens of one device (aligned blocks of rows) no expert is named more than 16 times, a bound that some block reaches.
All inputs are finite; a program needn't handle non-finite values.
Results may differ from a plain program's by a relative error of at most 0.023.
Values may be sent and summed in bfloat16 or wider, within the bound.
No kernel may reach another device: no remote copies, remote signals or barrier semaphores. Data moves between devices by JAX's collectives and lax.ppermute only.
A program may use at most 448 MiB of HBM per device.

v0:
```python
import math

import jax
import jax.numpy as jnp
from jax import lax
from jax.sharding import PartitionSpec as P

H = 16
DN = 128
DR = 64
DV = 128
R = 512
EXPERTS = 64
TOP = 6
CAP = 16


eps_norm = 1e-06
rope_base = 50000.0


def rms_scale(values, scales):
    inverse = lax.rsqrt(jnp.mean(values * values, axis=-1, keepdims=True) + eps_norm)
    return values * inverse * scales


def rope_tables(positions, width):
    middle = width // 2
    frequency = rope_base ** (-(jnp.arange(middle, dtype=jnp.float32) * 2.0 / width))
    angles = positions.astype(jnp.float32)[:, None] * frequency[None, :]
    return (jnp.cos(angles), jnp.sin(angles))


def rotate(values, cosine_table, sine_table):
    middle = values.shape[-1] // 2
    leading = values[..., :middle]
    trailing = values[..., middle:]
    return jnp.concatenate(
        [
            leading * cosine_table - trailing * sine_table,
            trailing * cosine_table + leading * sine_table,
        ],
        axis=-1,
    )


def unrotate(values, cosine_table, sine_table):
    middle = values.shape[-1] // 2
    leading = values[..., :middle]
    trailing = values[..., middle:]
    return jnp.concatenate(
        [
            leading * cosine_table + trailing * sine_table,
            trailing * cosine_table - leading * sine_table,
        ],
        axis=-1,
    )


def silu_slope(gate_values):
    sigmoid = jax.nn.sigmoid(gate_values)
    return sigmoid * (1.0 + gate_values * (1.0 - sigmoid))


def causal_scores(query_head, key_head, factor):
    scores = jnp.dot(query_head, key_head.T, preferred_element_type=jnp.float32) * factor
    length = scores.shape[0]
    allowed = jnp.arange(length)[:, None] >= jnp.arange(length)[None, :]
    return jnp.where(allowed, scores, -1e30)


def attend_head(query_head, key_head, value_head, factor):
    scores = causal_scores(query_head, key_head, factor)
    exponent = jnp.exp(scores)
    row_sum = jnp.sum(exponent, axis=1, keepdims=True)
    weights_half = (exponent / row_sum).astype(jnp.bfloat16)
    result = jnp.dot(weights_half, value_head, preferred_element_type=jnp.float32).astype(
        jnp.bfloat16
    )
    return (result, jnp.log(row_sum)[:, 0])


def attend_back(query_head, key_head, value_head, result_head, result_grad, logsum, factor):
    scores = causal_scores(query_head, key_head, factor)
    probs_wide = jnp.exp(scores - logsum[:, None])
    probs_half = probs_wide.astype(jnp.bfloat16)
    value_grad = jnp.dot(probs_half.T, result_grad, preferred_element_type=jnp.float32)
    row_dot = jnp.sum(
        result_grad.astype(jnp.float32) * result_head.astype(jnp.float32), axis=1, keepdims=True
    )
    probs_grad = jnp.dot(result_grad, value_head.T, preferred_element_type=jnp.float32)
    score_grad = (probs_wide * (probs_grad - row_dot) * factor).astype(jnp.bfloat16)
    query_grad = jnp.dot(score_grad, key_head, preferred_element_type=jnp.float32)
    key_grad = jnp.dot(score_grad.T, query_head, preferred_element_type=jnp.float32)
    return (
        query_grad.astype(jnp.bfloat16),
        key_grad.astype(jnp.bfloat16),
        value_grad.astype(jnp.bfloat16),
    )


def shards(
    tokens,
    routes,
    route_weights,
    norm_gain,
    w_query,
    w_kv_down,
    latent_gain,
    w_kv_up,
    w_output,
    ffn_gain,
    shared_gate,
    shared_up,
    shared_down,
    expert_gate,
    expert_up,
    expert_down,
    out_grad,
):
    local_count = tokens.shape[0]
    seq_count = lax.axis_size("seq")
    seq_index = lax.axis_index("seq")
    device_count = lax.axis_size("exp") * seq_count
    head_local = H // seq_count
    full_length = local_count * seq_count
    pieces = expert_gate.shape[0]
    parts_per = pieces * device_count // EXPERTS
    factor = 1.0 / math.sqrt(DN + DR)
    model_width = tokens.shape[1]
    gain_first_half, down_full, latent_scale, gain_second_half = (
        lax.all_gather(norm_gain, ("exp", "seq"), axis=0, tiled=True),
        lax.all_gather(w_kv_down, ("exp", "seq"), axis=0, tiled=True),
        lax.all_gather(latent_gain, ("exp", "seq"), axis=0, tiled=True),
        lax.all_gather(ffn_gain, ("exp", "seq"), axis=0, tiled=True),
    )
    query_cols, up_columns, output_rows, gate_cols, lift_cols, drop_rows = (
        lax.all_gather(w_query, "exp", axis=0, tiled=True),
        lax.all_gather(w_kv_up, "exp", axis=0, tiled=True),
        lax.all_gather(w_output, "exp", axis=1, tiled=True),
        lax.all_gather(shared_gate, "exp", axis=0, tiled=True),
        lax.all_gather(shared_up, "exp", axis=0, tiled=True),
        lax.all_gather(shared_down, "exp", axis=1, tiled=True),
    )
    token_wide = tokens.astype(jnp.float32)
    gain_first = gain_first_half.astype(jnp.float32)
    normed_one = rms_scale(token_wide, gain_first).astype(jnp.bfloat16)
    positions = seq_index * local_count + jnp.arange(local_count, dtype=jnp.int32)
    cosine_table, sine_table = rope_tables(positions, DR)
    down_raw = jnp.dot(normed_one, down_full, preferred_element_type=jnp.float32)
    latent_raw = down_raw[:, :R]
    rope_key = rotate(down_raw[:, R:], cosine_table, sine_table).astype(jnp.bfloat16)
    latent_wide = latent_scale.astype(jnp.float32)
    latent_rows = rms_scale(latent_raw, latent_wide).astype(jnp.bfloat16)
    column_width = head_local * (DN + DV)
    latent_all, rope_all = (
        lax.all_gather(latent_rows, "seq", axis=0, tiled=True),
        lax.all_gather(rope_key, "seq", axis=0, tiled=True),
    )
    head_up_raw = jnp.dot(latent_all, up_columns, preferred_element_type=jnp.float32).reshape(
        full_length, head_local, DN + DV
    )
    key_heads = jnp.concatenate(
        [
            head_up_raw[..., :DN].astype(jnp.bfloat16),
            jnp.broadcast_to(rope_all[:, None, :], (full_length, head_local, DR)),
        ],
        axis=-1,
    )
    value_heads = head_up_raw[..., DN:].astype(jnp.bfloat16)
    query_full, output_full, gate_full, lift_full, drop_full = (
        lax.all_gather(query_cols, "seq", axis=1, tiled=True),
        lax.all_gather(output_rows, "seq", axis=0, tiled=True),
        lax.all_gather(gate_cols, "seq", axis=1, tiled=True),
        lax.all_gather(lift_cols, "seq", axis=1, tiled=True),
        lax.all_gather(drop_rows, "seq", axis=0, tiled=True),
    )
    query_raw = jnp.dot(normed_one, query_full, preferred_element_type=jnp.float32).reshape(
        local_count, H, DN + DR
    )
    query_rows = jnp.concatenate(
        [
            query_raw[..., :DN],
            rotate(query_raw[..., DN:], cosine_table[:, None, :], sine_table[:, None, :]),
        ],
        axis=-1,
    ).astype(jnp.bfloat16)
    query_heads = lax.all_to_all(query_rows, "seq", split_axis=1, concat_axis=0, tiled=True)
    result_list = []
    logsum_list = []
    for head_number in range(head_local):
        result, logsum = attend_head(
            query_heads[:, head_number],
            key_heads[:, head_number],
            value_heads[:, head_number],
            factor,
        )
        result_list.append(result)
        logsum_list.append(logsum)
    result_heads = jnp.stack(result_list, axis=1)
    attention_rows = lax.all_to_all(
        result_heads, "seq", split_axis=0, concat_axis=1, tiled=True
    ).reshape(local_count, H * DV)
    residual = token_wide + jnp.dot(attention_rows, output_full, preferred_element_type=jnp.float32)
    gain_second = gain_second_half.astype(jnp.float32)
    normed_two = rms_scale(residual, gain_second).astype(jnp.bfloat16)
    shared_gate_raw = jnp.dot(normed_two, gate_full, preferred_element_type=jnp.float32)
    shared_up_raw = jnp.dot(normed_two, lift_full, preferred_element_type=jnp.float32)
    shared_hidden = (jax.nn.silu(shared_gate_raw) * shared_up_raw).astype(jnp.bfloat16)
    shared_out = jnp.dot(shared_hidden, drop_full, preferred_element_type=jnp.float32)
    route_count = local_count * TOP
    slot_count = EXPERTS * CAP
    flat_expert = routes.reshape(route_count)
    onehot = (flat_expert[:, None] == jnp.arange(EXPERTS, dtype=jnp.int32)[None, :]).astype(
        jnp.int32
    )
    earlier = jnp.cumsum(onehot, axis=0) - onehot
    slot_within = jnp.sum(earlier * onehot, axis=1)
    target = flat_expert * CAP + slot_within
    placed = (
        (target[:, None] == jnp.arange(slot_count, dtype=jnp.int32)[None, :])
        .astype(jnp.float32)
        .reshape(local_count, TOP, slot_count)
    )
    select = jnp.sum(placed, axis=1)
    weighted = jnp.sum(placed * route_weights[:, :, None], axis=1)

    def spread_parts(slot_rows):
        shaped = slot_rows.reshape(EXPERTS, 1, CAP, model_width)
        return jnp.broadcast_to(shaped, (EXPERTS, parts_per, CAP, model_width)).reshape(
            EXPERTS * parts_per, CAP, model_width
        )

    def join_parts(slot_rows):
        return jnp.sum(
            slot_rows.astype(jnp.float32).reshape(EXPERTS, parts_per, CAP, model_width), axis=1
        ).reshape(slot_count, model_width)

    grad_wide = out_grad.astype(jnp.float32)
    send_rows = jnp.dot(
        select.astype(jnp.bfloat16).T, normed_two, preferred_element_type=jnp.float32
    ).astype(jnp.bfloat16)
    route_cot = jnp.dot(weighted.T, grad_wide, precision=lax.Precision.HIGHEST).astype(jnp.bfloat16)
    received, received_grad = (
        lax.all_to_all(
            spread_parts(send_rows), ("exp", "seq"), split_axis=0, concat_axis=1, tiled=True
        ),
        lax.all_to_all(
            spread_parts(route_cot), ("exp", "seq"), split_axis=0, concat_axis=1, tiled=True
        ),
    )
    expert_gate_raw = jnp.einsum(
        "pnd,pdf->pnf", received, expert_gate, preferred_element_type=jnp.float32
    )
    expert_up_raw = jnp.einsum(
        "pnd,pdf->pnf", received, expert_up, preferred_element_type=jnp.float32
    )
    expert_hidden = (jax.nn.silu(expert_gate_raw) * expert_up_raw).astype(jnp.bfloat16)
    expert_result = jnp.einsum(
        "pnf,pfd->pnd", expert_hidden, expert_down, preferred_element_type=jnp.float32
    ).astype(jnp.bfloat16)
    expert_down_grad = jnp.einsum(
        "pnf,pnd->pfd", expert_hidden, received_grad, preferred_element_type=jnp.float32
    )
    hidden_grad = jnp.einsum(
        "pnd,pfd->pnf", received_grad, expert_down, preferred_element_type=jnp.float32
    )
    gate_rows_grad = (hidden_grad * expert_up_raw * silu_slope(expert_gate_raw)).astype(
        jnp.bfloat16
    )
    up_rows_grad = (hidden_grad * jax.nn.silu(expert_gate_raw)).astype(jnp.bfloat16)
    expert_gate_grad = jnp.einsum(
        "pnd,pnf->pdf", received, gate_rows_grad, preferred_element_type=jnp.float32
    )
    expert_up_grad = jnp.einsum(
        "pnd,pnf->pdf", received, up_rows_grad, preferred_element_type=jnp.float32
    )
    input_grad_rows = (
        jnp.einsum("pnf,pdf->pnd", gate_rows_grad, expert_gate, preferred_element_type=jnp.float32)
        + jnp.einsum("pnf,pdf->pnd", up_rows_grad, expert_up, preferred_element_type=jnp.float32)
    ).astype(jnp.bfloat16)
    returned, returned_grad = (
        lax.all_to_all(expert_result, ("exp", "seq"), split_axis=1, concat_axis=0, tiled=True),
        lax.all_to_all(input_grad_rows, ("exp", "seq"), split_axis=1, concat_axis=0, tiled=True),
    )
    routed = jnp.dot(weighted, join_parts(returned), precision=lax.Precision.HIGHEST)
    routed_grad = jnp.dot(select, join_parts(returned_grad), precision=lax.Precision.HIGHEST)
    output = (residual + shared_out + routed).astype(jnp.bfloat16)
    shared_hidden_grad = jnp.dot(out_grad, drop_full.T, preferred_element_type=jnp.float32)
    drop_grad = jnp.dot(shared_hidden.T, out_grad, preferred_element_type=jnp.float32)
    sgate_grad = (shared_hidden_grad * shared_up_raw * silu_slope(shared_gate_raw)).astype(
        jnp.bfloat16
    )
    sup_grad = (shared_hidden_grad * jax.nn.silu(shared_gate_raw)).astype(jnp.bfloat16)
    gate_grad = jnp.dot(normed_two.T, sgate_grad, preferred_element_type=jnp.float32)
    lift_grad = jnp.dot(normed_two.T, sup_grad, preferred_element_type=jnp.float32)
    normed_two_grad = (
        jnp.dot(sgate_grad, gate_full.T, preferred_element_type=jnp.float32)
        + jnp.dot(sup_grad, lift_full.T, preferred_element_type=jnp.float32)
        + routed_grad
    )
    _, pullback_two = jax.vjp(rms_scale, residual, gain_second)
    residual_norm_grad, gain_second_grad = pullback_two(normed_two_grad)
    residual_grad = grad_wide + residual_norm_grad
    residual_half = residual_grad.astype(jnp.bfloat16)
    output_weight_grad = jnp.dot(
        attention_rows.T, residual_half, preferred_element_type=jnp.float32
    )
    attention_grad = (
        jnp.dot(residual_half, output_full.T, preferred_element_type=jnp.float32)
        .astype(jnp.bfloat16)
        .reshape(local_count, H, DV)
    )
    attention_grad_heads = lax.all_to_all(
        attention_grad, "seq", split_axis=1, concat_axis=0, tiled=True
    )
    query_grad_list = []
    key_grad_list = []
    value_grad_list = []
    for head_number in range(head_local):
        query_grad, key_grad, value_grad = attend_back(
            query_heads[:, head_number],
            key_heads[:, head_number],
            value_heads[:, head_number],
            result_heads[:, head_number],
            attention_grad_heads[:, head_number],
            logsum_list[head_number],
            factor,
        )
        query_grad_list.append(query_grad)
        key_grad_list.append(key_grad)
        value_grad_list.append(value_grad)
    query_grad_heads = jnp.stack(query_grad_list, axis=1)
    key_grad_heads = jnp.stack(key_grad_list, axis=1)
    value_grad_heads = jnp.stack(value_grad_list, axis=1)
    head_kv_grad = jnp.concatenate([key_grad_heads[..., :DN], value_grad_heads], axis=-1).reshape(
        full_length, column_width
    )
    up_grad = jnp.dot(latent_all.T, head_kv_grad, preferred_element_type=jnp.float32)
    latent_part = jnp.dot(head_kv_grad, up_columns.T, preferred_element_type=jnp.float32)
    rope_part = jnp.sum(key_grad_heads[..., DN:].astype(jnp.float32), axis=1)
    query_grad_rows = lax.all_to_all(
        query_grad_heads, "seq", split_axis=0, concat_axis=1, tiled=True
    )
    latent_grad, rope_key_grad = (
        lax.psum_scatter(
            latent_part.astype(jnp.bfloat16), "seq", scatter_dimension=0, tiled=True
        ).astype(jnp.float32),
        lax.psum_scatter(
            rope_part.astype(jnp.bfloat16), "seq", scatter_dimension=0, tiled=True
        ).astype(jnp.float32),
    )
    query_in_grad = (
        jnp.concatenate(
            [
                query_grad_rows[..., :DN].astype(jnp.float32),
                unrotate(
                    query_grad_rows[..., DN:].astype(jnp.float32),
                    cosine_table[:, None, :],
                    sine_table[:, None, :],
                ),
            ],
            axis=-1,
        )
        .reshape(local_count, H * (DN + DR))
        .astype(jnp.bfloat16)
    )
    query_weight_grad = jnp.dot(normed_one.T, query_in_grad, preferred_element_type=jnp.float32)
    query_contribution = jnp.dot(query_in_grad, query_full.T, preferred_element_type=jnp.float32)
    _, pullback_latent = jax.vjp(rms_scale, latent_raw, latent_wide)
    latent_raw_grad, latent_scale_grad = pullback_latent(latent_grad)
    down_grad_rows = jnp.concatenate(
        [latent_raw_grad, unrotate(rope_key_grad, cosine_table, sine_table)], axis=-1
    ).astype(jnp.bfloat16)
    down_grad = jnp.dot(normed_one.T, down_grad_rows, preferred_element_type=jnp.float32)
    normed_one_grad = query_contribution + jnp.dot(
        down_grad_rows, down_full.T, preferred_element_type=jnp.float32
    )
    _, pullback_one = jax.vjp(rms_scale, token_wide, gain_first)
    token_norm_grad, gain_first_grad = pullback_one(normed_one_grad)
    tokens_grad = (residual_grad + token_norm_grad).astype(jnp.bfloat16)
    query_weight_grad, output_weight_grad, gate_grad, lift_grad, drop_grad = (
        lax.psum_scatter(
            query_weight_grad.astype(jnp.bfloat16), "seq", scatter_dimension=1, tiled=True
        ).astype(jnp.float32),
        lax.psum_scatter(
            output_weight_grad.astype(jnp.bfloat16), "seq", scatter_dimension=0, tiled=True
        ).astype(jnp.float32),
        lax.psum_scatter(
            gate_grad.astype(jnp.bfloat16), "seq", scatter_dimension=1, tiled=True
        ).astype(jnp.float32),
        lax.psum_scatter(
            lift_grad.astype(jnp.bfloat16), "seq", scatter_dimension=1, tiled=True
        ).astype(jnp.float32),
        lax.psum_scatter(
            drop_grad.astype(jnp.bfloat16), "seq", scatter_dimension=0, tiled=True
        ).astype(jnp.float32),
    )
    query_weight_out, up_out, output_out, gate_out, lift_out, drop_out = (
        lax.psum_scatter(
            query_weight_grad.astype(jnp.bfloat16), "exp", scatter_dimension=0, tiled=True
        ).astype(jnp.float32),
        lax.psum_scatter(
            up_grad.astype(jnp.bfloat16), "exp", scatter_dimension=0, tiled=True
        ).astype(jnp.float32),
        lax.psum_scatter(
            output_weight_grad.astype(jnp.bfloat16), "exp", scatter_dimension=1, tiled=True
        ).astype(jnp.float32),
        lax.psum_scatter(
            gate_grad.astype(jnp.bfloat16), "exp", scatter_dimension=0, tiled=True
        ).astype(jnp.float32),
        lax.psum_scatter(
            lift_grad.astype(jnp.bfloat16), "exp", scatter_dimension=0, tiled=True
        ).astype(jnp.float32),
        lax.psum_scatter(
            drop_grad.astype(jnp.bfloat16), "exp", scatter_dimension=1, tiled=True
        ).astype(jnp.float32),
    )
    gain_first_out, down_out, latent_out, gain_second_out = (
        lax.psum_scatter(gain_first_grad, ("exp", "seq"), scatter_dimension=0, tiled=True),
        lax.psum_scatter(down_grad, ("exp", "seq"), scatter_dimension=0, tiled=True),
        lax.psum_scatter(latent_scale_grad, ("exp", "seq"), scatter_dimension=0, tiled=True),
        lax.psum_scatter(gain_second_grad, ("exp", "seq"), scatter_dimension=0, tiled=True),
    )
    return (
        output,
        tokens_grad,
        gain_first_out,
        query_weight_out,
        down_out,
        latent_out,
        up_out,
        output_out,
        gain_second_out,
        gate_out,
        lift_out,
        drop_out,
        expert_gate_grad,
        expert_up_grad,
        expert_down_grad,
    )


def solution(mesh):
    return jax.shard_map(
        shards,
        mesh=mesh,
        in_specs=(
            P(("exp", "seq"), None),
            P(("exp", "seq"), None),
            P(("exp", "seq"), None),
            P(("exp", "seq")),
            P("exp", "seq"),
            P(("exp", "seq"), None),
            P(("exp", "seq")),
            P("exp", "seq"),
            P("seq", "exp"),
            P(("exp", "seq")),
            P("exp", "seq"),
            P("exp", "seq"),
            P("seq", "exp"),
            P(("exp", "seq"), None, None),
            P(("exp", "seq"), None, None),
            P(("exp", "seq"), None, None),
            P(("exp", "seq"), None),
        ),
        out_specs=(
            P(("exp", "seq"), None),
            P(("exp", "seq"), None),
            P(("exp", "seq")),
            P("exp", "seq"),
            P(("exp", "seq"), None),
            P(("exp", "seq")),
            P("exp", "seq"),
            P("seq", "exp"),
            P(("exp", "seq")),
            P("exp", "seq"),
            P("exp", "seq"),
            P("seq", "exp"),
            P(("exp", "seq"), None, None),
            P(("exp", "seq"), None, None),
            P(("exp", "seq"), None, None),
        ),
        check_vma=False,
    )
```

profile of v0, /device:TPU:0, one launch (start us, length us, event | category | flops | bytes accessed | tf_op | source)
XLA Modules:
  0.0 2117.0 jit_solution(7864792267633562565)
XLA Ops:
  11.2 32.4 %all-gather.13.cloned.1.call-done = bf16[2048,384]{1,0:T(8,128)(2,1)} async-done(((bf16[512,384]{1,0:T(8,128)(2,1)}), bf16[2048,384]{1,0:T(8,128)(2,1)}) %all-gather.13.cloned.1.call-update) | async-done | bytes 1572880 | tf_op jit(solution)/shard_map/all_gather | solution.py:138
  46.2 39.6 %all-reduce.7 = (bf16[2048]{0:T(1024)(128)(2,1)S(1)}, bf16[512]{0:T(512)(128)(2,1)S(1)}, bf16[2048]{0:T(1024)(128)(2,1)S(1)}) all-reduce(bf16[2048]{0:T(1024)(128)(2,1)S(1)} %dynamic-update-slice, bf16[512]{0:T(512)(128)(2,1)S(1)} %dynamic-update-slice.1, ...), channel_id=1, replica_groups=mesh['exp'=4,'seq'=8] {'exp','seq'}, use_global_device_ids=true, to_apply=%add | all-reduce | flops 4608 | bytes 18432
  108.6 23.4 %all-gather.21.cloned.1.call-done = bf16[256,2048]{1,0:T(8,128)(2,1)} async-done(((bf16[256,512]{1,0:T(8,128)(2,1)}), bf16[256,2048]{1,0:T(8,128)(2,1)}) %all-gather.21.cloned.1.call-update) | async-done | bytes 1048592 | tf_op jit(solution)/shard_map/all_gather | solution.py:140
  132.0 31.4 %all-gather.29.cloned.1.call-done = bf16[2048,352]{0,1:T(8,128)(2,1)} async-done(((bf16[512,352]{0,1:T(8,128)(2,1)}), bf16[2048,352]{0,1:T(8,128)(2,1)}) %all-gather.29.cloned.1.call-update) | async-done | bytes 1441808 | tf_op jit(solution)/shard_map/all_gather | solution.py:142
  163.5 31.4 %all-gather.25.cloned.1.call-done = bf16[2048,352]{0,1:T(8,128)(2,1)} async-done(((bf16[512,352]{0,1:T(8,128)(2,1)}), bf16[2048,352]{0,1:T(8,128)(2,1)}) %all-gather.25.cloned.1.call-update) | async-done | bytes 1441808 | tf_op jit(solution)/shard_map/all_gather | solution.py:141
  194.9 31.4 %all-gather.33.cloned.1.call-done = bf16[352,2048]{1,0:T(8,128)(2,1)} async-done(((bf16[352,512]{1,0:T(8,128)(2,1)}), bf16[352,2048]{1,0:T(8,128)(2,1)}) %all-gather.33.cloned.1.call-update) | async-done | bytes 1441808 | tf_op jit(solution)/shard_map/all_gather | solution.py:143
  226.6 118.0 %all-gather.15.cloned.1.call-done = bf16[2048,3072]{1,0:T(8,128)(2,1)} async-done(((bf16[2048,384]{1,0:T(8,128)(2,1)}), bf16[2048,3072]{1,0:T(8,128)(2,1)}) %all-gather.15.cloned.1.call-update) | async-done | bytes 12582928 | tf_op jit(solution)/shard_map/all_gather | solution.py:172
  368.0 21.8 %all_gather.58 = bf16[1024,64]{0,1:T(8,128)(2,1)S(1)} all-gather(bf16[128,64]{0,1:T(8,128)(2,1)S(1)} %pad_maximum_fusion.9), channel_id=1, replica_groups=mesh['exp'=4,'seq'=8] {'seq'}, dimensions={0}, use_global_device_ids=true | all-gather | bytes 147456 | tf_op jit(solution)/shard_map/all_gather | solution.py:158
  403.0 29.0 %all-to-all-done.1 = bf16[1024,2,128]{2,1,0:T(2,128)(2,1)S(1)} async-done(((bf16[1024,2,128]{2,1,0:T(2,128)(2,1)}), bf16[1024,2,128]{2,1,0:T(2,128)(2,1)S(1)}, u32[]{:S(2)}, u32[]{:S(2)}) %all-to-all-start.1) | async-done | bytes 524320 | tf_op jit(solution)/shard_map/all_to_all | solution.py:201
  432.4 37.4 %all-gather.23.cloned.1.call-done = bf16[2048,2048]{1,0:T(8,128)(2,1)} async-done(((bf16[256,2048]{1,0:T(8,128)(2,1)}), bf16[2048,2048]{1,0:T(8,128)(2,1)}) %all-gather.23.cloned.1.call-update) | async-done | bytes 8388624 | tf_op jit(solution)/shard_map/all_gather | solution.py:173
  474.7 103.1 %all-gather.31.cloned.1.call-done = bf16[2048,2816]{0,1:T(8,128)(2,1)} async-done(((bf16[2048,352]{0,1:T(8,128)(2,1)}), bf16[2048,2816]{0,1:T(8,128)(2,1)}) %all-gather.31.cloned.1.call-update) | async-done | bytes 11534352 | tf_op jit(solution)/shard_map/all_gather | solution.py:175
  587.1 98.8 %all-gather.27.cloned.1.call-done = bf16[2048,2816]{0,1:T(8,128)(2,1)} async-done(((bf16[2048,352]{0,1:T(8,128)(2,1)}), bf16[2048,2816]{0,1:T(8,128)(2,1)}) %all-gather.27.cloned.1.call-update) | async-done | bytes 11534352 | tf_op jit(solution)/shard_map/all_gather | solution.py:174
  695.1 98.6 %all-gather.35.cloned.1.call-done = bf16[2816,2048]{1,0:T(8,128)(2,1)} async-done(((bf16[352,2048]{1,0:T(8,128)(2,1)}), bf16[2816,2048]{1,0:T(8,128)(2,1)}) %all-gather.35.cloned.1.call-update) | async-done | bytes 11534352 | tf_op jit(solution)/shard_map/all_gather | solution.py:176
  845.3 154.9 %all-to-all-done.4 = bf16[64,16,2048]{2,1,0:T(8,128)(2,1)} async-done(((bf16[64,16,2048]{2,1,0:T(8,128)(2,1)}), bf16[64,16,2048]{2,1,0:T(8,128)(2,1)}, u32[]{:S(2)}, u32[]{:S(2)}) %all-to-all-start.4) | async-done | bytes 4194336 | tf_op jit(solution)/shard_map/all_to_all | solution.py:248
  1014.8 132.0 %all-to-all-done.2 = bf16[64,16,2048]{2,1,0:T(8,128)(2,1)} async-done(((bf16[64,16,2048]{2,1,0:T(8,128)(2,1)}), bf16[64,16,2048]{2,1,0:T(8,128)(2,1)}, u32[]{:S(2)}, u32[]{:S(2)}) %all-to-all-start.2) | async-done | bytes 4194336 | tf_op jit(solution)/shard_map/all_to_all | solution.py:245
  1236.2 153.9 %all-to-all-done.5 = bf16[2,512,2048]{2,0,1:T(2,128)(2,1)} async-done(((bf16[2,512,2048]{2,0,1:T(2,128)(2,1)}), bf16[2,512,2048]{2,0,1:T(2,128)(2,1)}, u32[]{:S(2)}, u32[]{:S(2)}) %all-to-all-start.5) | async-done | bytes 4194336 | tf_op jit(solution)/shard_map/all_to_all | solution.py:284
  1415.0 18.3 all-to-all-done.6
  1448.2 48.2 %all_to_all.135 = bf16[1024,2,192]{2,1,0:T(2,128)(2,1)} all-to-all(bf16[1024,2,192]{2,1,0:T(2,128)(2,1)} %copy.170), channel_id=1, replica_groups=mesh['exp'=4,'seq'=8] {'seq'}, dimensions={0} | all-to-all | bytes 1572864 | tf_op jit(solution)/shard_map/all_to_all | solution.py:342
  1551.8 125.0 %reduce-scatter.47.cloned.1.call-done = bf16[384,2048]{1,0:T(8,128)(2,1)} async-done(((bf16[3072,2048]{1,0:T(8,128)(2,1)}), bf16[384,2048]{1,0:T(8,128)(2,1)}) %reduce-scatter.47.cloned.1.call-update) | async-done | bytes 1572880
  1709.3 39.5 %reduce-scatter.43.cloned.1.call-done = bf16[128,512]{1,0:T(8,128)(2,1)} async-done(((bf16[1024,512]{1,0:T(8,128)(2,1)}), bf16[128,512]{1,0:T(8,128)(2,1)}) %reduce-scatter.43.cloned.1.call-update) | async-done | bytes 131088
  1828.6 47.9 %all-reduce.6 = (f32[2048]{0:T(1024)S(1)}, f32[512]{0:T(512)S(1)}, f32[2048]{0:T(1024)S(1)}) all-reduce(f32[2048]{0:T(1024)S(1)} %get-tuple-element.17, f32[512]{0:T(512)S(1)} %get-tuple-element.21, f32[2048]{0:T(1024)S(1)} %get-tuple-element.15), channel_id=4, replica_groups=mesh['exp'=4,'seq'=8] {'exp','seq'}, use_global_device_ids=true, to_apply=%region_19.20.clone | all-reduce | flops 4608 | bytes 36864
  1900.1 28.8 %reduce-scatter.29.cloned.1.call-done = bf16[256,512]{1,0:T(8,128)(2,1)} async-done(((bf16[256,2048]{1,0:T(8,128)(2,1)}), bf16[256,512]{1,0:T(8,128)(2,1)}) %reduce-scatter.29.cloned.1.call-update) | async-done | bytes 262160 | tf_op jit(solution)/shard_map/reduce_scatter | solution.py:406
  1930.7 32.1 %reduce-scatter.21.cloned.1.call-done = bf16[512,384]{1,0:T(8,128)(2,1)} async-done(((bf16[2048,384]{1,0:T(8,128)(2,1)}), bf16[512,384]{1,0:T(8,128)(2,1)}) %reduce-scatter.21.cloned.1.call-update) | async-done | bytes 393232 | tf_op jit(solution)/shard_map/reduce_scatter | solution.py:400
  1964.7 145.6 %reduce-scatter.23.cloned.1.call-done = f32[64,576]{1,0:T(8,128)} async-done(((f32[2048,576]{1,0:T(8,128)}), f32[64,576]{1,0:T(8,128)}) %reduce-scatter.23.cloned.1.call-update) | async-done | bytes 147472 | tf_op jit(solution)/shard_map/reduce_scatter | solution.py:421
  (363 shorter events, 479.1 us)
Async XLA Ops:
  10.0 184.9 %all-gather.25.cloned.1.call-start = ((), (), s32[]{:S(2)}) async-start(), calls=%async_computation.28 | async-start | bytes 1802240 | tf_op jit(solution)/shard_map/all_gather | solution.py:141
  10.6 215.7 %all-gather.33.cloned.1.call-start = ((), (), s32[]{:S(2)}) async-start(), calls=%async_computation.32 | async-start | bytes 1802240 | tf_op jit(solution)/shard_map/all_gather | solution.py:143
  11.1 333.5 %all-gather.15.cloned.1.call-start = ((), (), s32[]{:S(2)}) async-start(), calls=%async_computation.23 | async-start | bytes 14155776 | tf_op jit(solution)/shard_map/all_gather | solution.py:172
  43.6 346.2 %all-gather.19.cloned.1.call-start = ((), (), s32[]{:S(2)}) async-start(), calls=%async_computation.25 | async-start | bytes 1179648 | tf_op jit(solution)/shard_map/all_gather | solution.py:157
  108.5 361.3 %all-gather.23.cloned.1.call-start = ((), (), s32[]{:S(2)}) async-start(), calls=%async_computation.27 | async-start | bytes 9437184 | tf_op jit(solution)/shard_map/all_gather | solution.py:173
  132.0 445.8 %all-gather.31.cloned.1.call-start = ((), (), s32[]{:S(2)}) async-start(), calls=%async_computation.31 | async-start | bytes 12976128 | tf_op jit(solution)/shard_map/all_gather | solution.py:175
  163.4 522.4 %all-gather.27.cloned.1.call-start = ((), (), s32[]{:S(2)}) async-start(), calls=%async_computation.29 | async-start | bytes 12976128 | tf_op jit(solution)/shard_map/all_gather | solution.py:174
  194.9 598.9 %all-gather.35.cloned.1.call-start = ((), (), s32[]{:S(2)}) async-start(), calls=%async_computation.33 | async-start | bytes 12976128 | tf_op jit(solution)/shard_map/all_gather | solution.py:176
  402.7 1146.0 %reduce-scatter.39.cloned.1.call-start = ((), (), s32[]{:S(2)}) async-start(), calls=%async_computation.43 | async-start | bytes 12976128 | tf_op jit(solution)/shard_map/reduce_scatter | solution.py:395
  810.0 739.4 %reduce-scatter.31.cloned.1.call-start = ((), (), s32[]{:S(2)}) async-start(), calls=%async_computation.39 | async-start | bytes 12976128 | tf_op jit(solution)/shard_map/reduce_scatter | solution.py:389
  838.4 161.7 %all-to-all-start.4 = ((bf16[64,16,2048]{2,1,0:T(8,128)(2,1)}), bf16[64,16,2048]{2,1,0:T(8,128)(2,1)}, u32[]{:S(2)}, u32[]{:S(2)}) async-start(bf16[64,16,2048]{2,1,0:T(8,128)(2,1)} %bitcast.199), calls=%async_computation.4 | async-start | bytes 8388608 | tf_op jit(solution)/shard_map/all_to_all | solution.py:248
  1003.9 546.2 %reduce-scatter.35.cloned.1.call-start = ((), (), s32[]{:S(2)}) async-start(), calls=%async_computation.41 | async-start | bytes 12976128 | tf_op jit(solution)/shard_map/reduce_scatter | solution.py:392
  1219.3 170.8 %all-to-all-start.5 = ((bf16[2,512,2048]{2,0,1:T(2,128)(2,1)}), bf16[2,512,2048]{2,0,1:T(2,128)(2,1)}, u32[]{:S(2)}, u32[]{:S(2)}) async-start(bf16[2,512,2048]{2,0,1:T(2,128)(2,1)} %copy.163), calls=%async_computation.5 | async-start | bytes 8388608 | tf_op jit(solution)/shard_map/all_to_all | solution.py:284
  1223.0 327.9 %reduce-scatter.27.cloned.1.call-start = ((), (), s32[]{:S(2)}) async-start(), calls=%async_computation.37 | async-start | bytes 9437184 | tf_op jit(solution)/shard_map/reduce_scatter | solution.py:386
  1414.9 261.9 %reduce-scatter.47.cloned.1.call-start = ((), (), s32[]{:S(2)}) async-start(), calls=%async_computation.47 | async-start | bytes 14155776
  1526.5 181.7 %reduce-scatter.45.cloned.1.call-start = ((), (), s32[]{:S(2)}) async-start(), calls=%async_computation.46 | async-start | bytes 294912
  1540.5 208.3 %reduce-scatter.43.cloned.1.call-start = ((), (), s32[]{:S(2)}) async-start(), calls=%async_computation.45 | async-start | bytes 1179648
  1545.4 271.3 %reduce-scatter.25.cloned.1.call-start = ((), (), s32[]{:S(2)}) async-start(), calls=%async_computation.36 | async-start | bytes 655360 | tf_op jit(solution)/shard_map/reduce_scatter | solution.py:403
  1548.6 330.8 %reduce-scatter.41.cloned.1.call-start = ((), (), s32[]{:S(2)}) async-start(), calls=%async_computation.44 | async-start | bytes 1802240 | tf_op jit(solution)/shard_map/reduce_scatter | solution.py:415
  1549.3 332.0 %reduce-scatter.33.cloned.1.call-start = ((), (), s32[]{:S(2)}) async-start(), calls=%async_computation.40 | async-start | bytes 1802240 | tf_op jit(solution)/shard_map/reduce_scatter | solution.py:409
  1550.1 348.1 %reduce-scatter.37.cloned.1.call-start = ((), (), s32[]{:S(2)}) async-start(), calls=%async_computation.42 | async-start | bytes 1802240 | tf_op jit(solution)/shard_map/reduce_scatter | solution.py:412
  1550.8 378.0 %reduce-scatter.29.cloned.1.call-start = ((), (), s32[]{:S(2)}) async-start(), calls=%async_computation.38 | async-start | bytes 1310720 | tf_op jit(solution)/shard_map/reduce_scatter | solution.py:406
  1551.4 411.4 %reduce-scatter.21.cloned.1.call-start = ((), (), s32[]{:S(2)}) async-start(), calls=%async_computation.34 | async-start | bytes 1966080 | tf_op jit(solution)/shard_map/reduce_scatter | solution.py:400
  1703.5 406.8 %reduce-scatter.23.cloned.1.call-start = ((), (), s32[]{:S(2)}) async-start(), calls=%async_computation.35 | async-start | bytes 5406720 | tf_op jit(solution)/shard_map/reduce_scatter | solution.py:421
  (86 other events, 3616.6 us)
Sparse Core Ops, SparseCore 0:
  9.9 33.6 all-gather.12
  46.4 58.1 all-gather.16
  133.6 29.7 all-gather.28
  165.1 29.7 all-gather.24
  196.5 29.7 all-gather.32
  227.9 116.6 all-gather.14
  346.8 28.4 all-gather.18
  376.9 92.8 all-gather.22
  471.3 106.4 all-gather.30
  579.5 106.3 all-gather.26
  687.4 106.3 all-gather.34
  810.1 180.1 reduce-scatter.38
  993.0 208.0 reduce-scatter.30
  1203.2 204.4 reduce-scatter.34
  1409.8 131.9 reduce-scatter.26
  1544.6 132.1 reduce-scatter.46
  1679.5 28.7 reduce-scatter.44
  1710.6 38.0 reduce-scatter.42
  1752.2 44.7 reduce-scatter.24
  1800.0 31.2 reduce-scatter.40
  1834.5 30.3 reduce-scatter.32
  1867.9 30.2 reduce-scatter.36
  1931.8 30.8 reduce-scatter.20
  1965.5 144.7 reduce-scatter.22
  (2 shorter events, 53.0 us)
where the time goes:
time: 2120 us
  waiting for transfers between devices  1520 us (72%)
  matrix products  267 us (13%)
  blocking collectives  168 us (8%)
  local copies, waits for them, and re-layouts  82.5 us (4%)
  starting transfers between devices  38.7 us (2%)
  other arithmetic  24.4 us (1%)
    unnamed x29, waiting for transfers between devices  176 us
    all_to_all x1, waiting for transfers between devices, shards(): lax.all_to_all(spread_parts(route_cot), ('exp', 'seq'), split_axis=0, con...  155 us
    all_to_all x1, waiting for transfers between devices, shards(): lax.all_to_all(input_grad_rows, ('exp', 'seq'), split_axis=1, concat_axis...  154 us
    reduce_scatter x1, waiting for transfers between devices, shards(): lax.psum_scatter(down_grad, ('exp', 'seq'), scatter_dimension=0, tiled=True)  146 us
    all_to_all x1, waiting for transfers between devices, shards(): lax.all_to_all(spread_parts(send_rows), ('exp', 'seq'), split_axis=0, con...  132 us
    all_gather x1, waiting for transfers between devices, shards(): lax.all_gather(query_cols, 'seq', axis=1, tiled=True)  118 us
    all_gather x1, waiting for transfers between devices, shards(): lax.all_gather(lift_cols, 'seq', axis=1, tiled=True)  103 us
    all_gather x1, waiting for transfers between devices, shards(): lax.all_gather(gate_cols, 'seq', axis=1, tiled=True)  98.8 us
  transfers between devices with their start and end apart: 33, of which 24 were waited for; matrix products, arithmetic and copies ran while one was open for 17% of the time, Pallas kernels for 0%

commit v1 on v0

v1 whole, which is shorter than its diff:
```python
import math

import jax
import jax.numpy as jnp
from jax import lax
from jax.sharding import PartitionSpec as P

H = 16
DN = 128
DR = 64
DV = 128
R = 512
EXPERTS = 64
TOP = 6
CAP = 16


eps_norm = 1e-06
rope_base = 50000.0
BF = jnp.bfloat16
F32 = jnp.float32


def dot(a, b):
    return jnp.dot(a, b, preferred_element_type=F32)


def dot_t(a, b):
    return lax.dot_general(a, b, (((1,), (1,)), ((), ())), preferred_element_type=F32)


def t_dot(a, b):
    return lax.dot_general(a, b, (((0,), (0,)), ((), ())), preferred_element_type=F32)


def rope_tables(positions, width):
    middle = width // 2
    frequency = rope_base ** (-(jnp.arange(middle, dtype=F32) * 2.0 / width))
    angles = positions.astype(F32)[:, None] * frequency[None, :]
    return (jnp.cos(angles), jnp.sin(angles))


def rotate(values, cosine_table, sine_table):
    middle = values.shape[-1] // 2
    leading = values[..., :middle]
    trailing = values[..., middle:]
    return jnp.concatenate(
        [
            leading * cosine_table - trailing * sine_table,
            trailing * cosine_table + leading * sine_table,
        ],
        axis=-1,
    )


def silu_slope(gate_values):
    sigmoid = jax.nn.sigmoid(gate_values)
    return sigmoid * (1.0 + gate_values * (1.0 - sigmoid))


def norm_back(dy, v, inverse, gain):
    hat = v * inverse
    scaled = dy * gain
    dv = inverse * (scaled - hat * jnp.mean(scaled * hat, axis=-1, keepdims=True))
    return dv, dy * hat


def inverse_rms(v):
    return lax.rsqrt(jnp.mean(v * v, axis=-1, keepdims=True) + eps_norm)


def swap(x, axis, mask):
    n = lax.axis_size(axis)
    return lax.ppermute(x, axis, [(i, i ^ mask) for i in range(n)])


def after(x, *earlier):
    return lax.optimization_barrier((x, *earlier))[0]


class Lane:
    def __init__(self, axis, depth):
        self.axis = axis
        self.depth = depth
        self.sent = []

    def send(self, x, mask):
        if len(self.sent) >= self.depth:
            x = after(x, self.sent[-self.depth])
        got = swap(x, self.axis, mask)
        self.sent.append(got)
        return got

    def chips(self, x):
        chips = lax.axis_size("seq") // 2
        return [x] + [self.send(x, 2 * k) for k in range(1, chips)]

    def group(self, x):
        evens = self.chips(x)
        return evens + [swap(b, "seq", 1) for b in evens]

    def scatter(self, even, odd):
        chips = lax.axis_size("seq") // 2
        rows = even.shape[0] // chips
        got = swap(odd.astype(BF), "seq", 1)
        blocks = [
            even[k * rows : (k + 1) * rows] + got[k * rows : (k + 1) * rows].astype(F32)
            for k in range(chips)
        ]
        total = blocks[0]
        for k in range(1, chips):
            total = total + self.send(blocks[k].astype(BF), 2 * k).astype(F32)
        return total

    def stack(self, x):
        n = lax.axis_size("exp")
        me = lax.axis_index("exp")
        out = jnp.zeros((n, *x.shape), x.dtype)
        for j in range(n):
            block = x if j == 0 else self.send(x, j)
            out = lax.dynamic_update_slice_in_dim(out, block[None], me ^ j, 0)
        return out

    def sum_stack(self, x):
        n = lax.axis_size("exp")
        me = lax.axis_index("exp")
        total = lax.dynamic_index_in_dim(x, me, 0, keepdims=False)
        for j in range(1, n):
            piece = lax.dynamic_index_in_dim(x, me ^ j, 0, keepdims=False).astype(BF)
            total = total + self.send(piece, j).astype(F32)
        return total


def relative_order(count):
    chips = count // 2
    return [2 * k for k in range(chips)] + [2 * k + 1 for k in range(chips)]


def scatter_small(x):
    for axis in ("exp", "seq"):
        n = lax.axis_size(axis)
        me = lax.axis_index(axis)
        total = lax.dynamic_index_in_dim(x, me, 0, keepdims=False)
        for j in range(1, n):
            piece = lax.dynamic_index_in_dim(x, me ^ j, 0, keepdims=False)
            total = total + swap(piece, axis, j)
        x = total
    return x


def columns_first(x, blocks):
    rows, columns = x.shape
    return x.reshape(rows, blocks, columns // blocks).transpose(1, 0, 2)


def columns_last(x):
    blocks, rows, w = x.shape
    return x.transpose(1, 0, 2).reshape(rows, blocks * w)


def shards(
    tokens,
    routes,
    route_weights,
    norm_gain,
    w_query,
    w_kv_down,
    latent_gain,
    w_kv_up,
    w_output,
    ffn_gain,
    shared_gate,
    shared_up,
    shared_down,
    expert_gate,
    expert_up,
    expert_down,
    out_grad,
):
    count, width = tokens.shape
    n_seq = lax.axis_size("seq")
    n_exp = lax.axis_size("exp")
    seq = lax.axis_index("seq")
    order = relative_order(n_seq)
    place = {r: p for p, r in enumerate(order)}
    chips = n_seq // 2
    heads = H // n_seq
    length = count * n_seq
    half = length // 2
    pieces = expert_gate.shape[0]
    parts_per = pieces * n_seq * n_exp // EXPERTS
    factor = 1.0 / math.sqrt(DN + DR)
    gain_rows = norm_gain.shape[0]
    latent_rows_local = latent_gain.shape[0]
    along = Lane("seq", 3)
    across = Lane("exp", 2)

    packed = jnp.concatenate(
        [
            w_kv_down,
            norm_gain[:, None],
            ffn_gain[:, None],
            jnp.pad(latent_gain, (0, gain_rows - latent_rows_local))[:, None],
            jnp.zeros((gain_rows, 61), BF),
        ],
        axis=1,
    )
    packed_even = jnp.stack(along.chips(packed))
    query_stack = across.stack(w_query)
    token_blocks = along.group(tokens)
    packed_even = across.stack(packed_even)
    packed_odd = swap(packed_even, "seq", 1)
    up_stack = across.stack(w_kv_up)
    route_pack = jnp.concatenate([routes.astype(F32).T, route_weights.T], axis=0)
    route_blocks = along.group(route_pack)
    output_even = jnp.concatenate(along.chips(w_output), axis=0)
    output_even = across.stack(output_even)
    output_odd = swap(output_even, "seq", 1)
    shared_stack = across.stack(jnp.stack([shared_gate, shared_up]))
    grad_blocks = along.group(out_grad)
    drop_stack = across.stack(shared_down)

    packed_all = jnp.zeros((n_exp, n_seq, gain_rows, packed.shape[1]), BF)
    for p in range(n_seq):
        block = packed_even[:, p] if p < chips else packed_odd[:, p - chips]
        packed_all = lax.dynamic_update_slice_in_dim(
            packed_all, block[:, None], seq ^ order[p], 1
        )
    packed_all = packed_all.reshape(width, packed.shape[1])
    query_cols = query_stack.reshape(width, w_query.shape[1])
    up_cols = up_stack.reshape(R, w_kv_up.shape[1])
    output_full = jnp.concatenate([columns_last(output_even), columns_last(output_odd)], axis=0)
    gate_cols = shared_stack[:, 0].reshape(width, shared_gate.shape[1])
    lift_cols = shared_stack[:, 1].reshape(width, shared_up.shape[1])
    drop_rows = columns_last(drop_stack)
    down_full = packed_all[:, : R + DR]
    gain_first = packed_all[:, R + DR].astype(F32)
    gain_second = packed_all[:, R + DR + 1].astype(F32)
    latent_wide = (
        packed_all[:, R + DR + 2]
        .reshape(n_exp * n_seq, gain_rows)[:, :latent_rows_local]
        .reshape(R)
        .astype(F32)
    )

    token_all = lax.optimization_barrier(jnp.concatenate(token_blocks, axis=0))
    token_wide = token_all.astype(F32)
    inverse_one = inverse_rms(token_wide)
    normed_one = (token_wide * inverse_one * gain_first).astype(BF)
    positions = jnp.concatenate(
        [(seq ^ r) * count + jnp.arange(count, dtype=jnp.int32) for r in order]
    )
    cosine_table, sine_table = rope_tables(positions, DR)
    allowed = positions[:, None] >= positions[None, :]
    query_raw = dot(normed_one, query_cols)
    down_raw = dot(normed_one, down_full)
    latent_raw = down_raw[:, :R]
    rope_key = rotate(down_raw[:, R:], cosine_table, sine_table).astype(BF)
    inverse_latent = inverse_rms(latent_raw)
    latent_all = (latent_raw * inverse_latent * latent_wide).astype(BF)
    up_raw = dot(latent_all, up_cols).astype(BF)
    query_heads, key_heads, value_heads = [], [], []
    for n in range(heads):
        own = query_raw[:, n * (DN + DR) : (n + 1) * (DN + DR)]
        query_heads.append(
            jnp.concatenate(
                [own[:, :DN], rotate(own[:, DN:], cosine_table, sine_table)], axis=1
            ).astype(BF)
        )
        own = up_raw[:, n * (DN + DV) : (n + 1) * (DN + DV)]
        key_heads.append(jnp.concatenate([own[:, :DN], rope_key], axis=1))
        value_heads.append(own[:, DN:])
    results, logsums = [], []
    for n in range(heads):
        scores = jnp.where(allowed, dot_t(query_heads[n], key_heads[n]) * factor, -1e30)
        exponent = jnp.exp(scores)
        row_sum = jnp.sum(exponent, axis=1, keepdims=True)
        results.append(dot((exponent / row_sum).astype(BF), value_heads[n]).astype(BF))
        logsums.append(jnp.log(row_sum))
    result = jnp.concatenate(results, axis=1)

    result_blocks = along.group(result)
    aligned = []
    for q, block in enumerate(result_blocks):
        aligned.append(
            jnp.concatenate(
                [
                    block[place[order[q] ^ r] * count : (place[order[q] ^ r] + 1) * count]
                    for r in order
                ],
                axis=0,
            )
        )
    attention = jnp.concatenate(aligned, axis=1)
    residual = token_wide + dot(attention, output_full)
    inverse_two = inverse_rms(residual)
    normed_two = (residual * inverse_two * gain_second).astype(BF)

    column = jnp.stack(
        [
            ((other * n_seq + seq) * pieces + i) // parts_per
            for i in range(pieces)
            for other in range(n_exp)
        ]
    )
    kinds = n_exp * pieces
    route_all = jnp.stack(route_blocks)
    named = route_all[:, None, :TOP, :].astype(jnp.int32) == column[None, :, None, None]
    matched = jnp.any(named, axis=2)
    match_weight = jnp.sum(jnp.where(named, route_all[:, None, TOP:, :], 0.0), axis=2)
    earlier = (jnp.arange(count)[:, None] < jnp.arange(count)[None, :]).astype(BF)
    rank = jnp.dot(matched.astype(BF), earlier, preferred_element_type=F32).astype(jnp.int32)
    chosen = (rank[:, :, None, :] == jnp.arange(CAP, dtype=jnp.int32)[None, None, :, None]) & (
        matched[:, :, None, :]
    )
    select = chosen.astype(BF).reshape(n_seq, kinds * CAP, count)
    weighted = jnp.where(chosen, match_weight[:, :, None, :], 0.0).reshape(
        n_seq, kinds * CAP, count
    )
    slot_weight = jnp.sum(weighted, axis=2, keepdims=True)
    weighted_high = weighted.astype(BF)
    weighted_low = (weighted - weighted_high.astype(F32)).astype(BF)

    def spread(rows):
        shaped = rows.reshape(n_seq, pieces, n_exp, CAP, width).transpose(1, 2, 0, 3, 4)
        return [give(shaped[i].reshape(n_exp, n_seq * CAP, width)) for i in range(pieces)]

    def give(rows):
        return lax.all_to_all(rows, "exp", split_axis=0, concat_axis=0, tiled=True)

    def join(parts):
        shaped = jnp.stack(parts).reshape(pieces, n_exp, n_seq, CAP, width)
        return shaped.transpose(2, 0, 1, 3, 4).reshape(n_seq, kinds * CAP, width)

    grad_all = jnp.stack(grad_blocks)
    cot_rows = (
        jnp.einsum("bst,btd->bsd", select, grad_all, preferred_element_type=F32) * slot_weight
    ).astype(BF)
    received_grad = spread(cot_rows)
    send_rows = jnp.einsum(
        "bst,btd->bsd",
        select,
        normed_two.reshape(n_seq, count, width),
        preferred_element_type=F32,
    ).astype(BF)
    received = spread(send_rows)

    results_back, grads_back, gate_grads, up_grads, down_grads = [], [], [], [], []
    for i in range(pieces):
        rows = received[i].reshape(n_exp * n_seq * CAP, width)
        cots = received_grad[i].reshape(n_exp * n_seq * CAP, width)
        hidden_grad = dot_t(cots, expert_down[i])
        gate_raw = dot(rows, expert_gate[i])
        lift_raw = dot(rows, expert_up[i])
        expert_hidden = (jax.nn.silu(gate_raw) * lift_raw).astype(BF)
        gate_rows_grad = (hidden_grad * lift_raw * silu_slope(gate_raw)).astype(BF)
        up_rows_grad = (hidden_grad * jax.nn.silu(gate_raw)).astype(BF)
        input_grad = (
            dot_t(gate_rows_grad, expert_gate[i]) + dot_t(up_rows_grad, expert_up[i])
        ).astype(BF)
        grads_back.append(give(input_grad.reshape(n_exp, n_seq * CAP, width)))
        expert_result = dot(expert_hidden, expert_down[i]).astype(BF)
        results_back.append(give(expert_result.reshape(n_exp, n_seq * CAP, width)))
        down_grads.append(t_dot(expert_hidden, cots))
        gate_grads.append(t_dot(rows, gate_rows_grad))
        up_grads.append(t_dot(rows, up_rows_grad))
    expert_gate_grad = jnp.stack(gate_grads)
    expert_up_grad = jnp.stack(up_grads)
    expert_down_grad = jnp.stack(down_grads)
    returned_grad = join(grads_back)
    routed_grad = jnp.einsum(
        "bst,bsd->btd", select, returned_grad, preferred_element_type=F32
    ).reshape(length, width)

    grad_rows = grad_all.reshape(length, width)
    shared_gate_raw = dot(normed_two, gate_cols)
    shared_up_raw = dot(normed_two, lift_cols)
    shared_hidden = (jax.nn.silu(shared_gate_raw) * shared_up_raw).astype(BF)
    shared_hidden_grad = dot_t(grad_rows, drop_rows)
    sgate_grad = (shared_hidden_grad * shared_up_raw * silu_slope(shared_gate_raw)).astype(BF)
    sup_grad = (shared_hidden_grad * jax.nn.silu(shared_gate_raw)).astype(BF)
    two_part = dot_t(sgate_grad, gate_cols) + dot_t(sup_grad, lift_cols) + routed_grad
    two_grad = along.scatter(two_part[:half], two_part[half:])
    shared_grad_stack = jnp.stack(
        [
            t_dot(normed_two, sgate_grad).reshape(n_exp, width // n_exp, -1),
            t_dot(normed_two, sup_grad).reshape(n_exp, width // n_exp, -1),
        ],
        axis=1,
    )

    residual_norm_grad, second_terms = norm_back(
        two_grad, residual[:count], inverse_two[:count], gain_second
    )
    residual_grad = out_grad.astype(F32) + residual_norm_grad
    residual_half = residual_grad.astype(BF)
    all_heads = dot_t(residual_half, output_full).astype(BF)
    wide = heads * DV
    pairs = [
        jnp.stack(
            [
                all_heads[:, k * wide : (k + 1) * wide],
                all_heads[:, (chips + k) * wide : (chips + k + 1) * wide],
            ]
        )
        for k in range(chips)
    ]
    pairs = [pairs[0]] + [along.send(pairs[k], 2 * k) for k in range(1, chips)]
    other_half = swap(jnp.stack([pair[1] for pair in pairs]), "seq", 1)
    attention_grad = jnp.concatenate(
        [jnp.stack([pair[0] for pair in pairs]), other_half], axis=0
    ).reshape(length, wide)
    half_all = along.group(residual_half)

    returned = join(results_back)
    routed = (
        jnp.einsum("bst,bsd->btd", weighted_high, returned, preferred_element_type=F32)
        + jnp.einsum("bst,bsd->btd", weighted_low, returned, preferred_element_type=F32)
    ).reshape(length, width)
    out_part = dot(shared_hidden, drop_rows) + routed

    query_grads, kv_grads, rope_part = [], [], 0.0
    for n in range(heads):
        own = attention_grad[:, n * DV : (n + 1) * DV]
        scores = jnp.where(allowed, dot_t(query_heads[n], key_heads[n]) * factor, -1e30)
        probs_wide = jnp.exp(scores - logsums[n])
        value_grad = t_dot(probs_wide.astype(BF), own).astype(BF)
        row_dot = jnp.sum(own.astype(F32) * results[n].astype(F32), axis=1, keepdims=True)
        probs_grad = dot_t(own, value_heads[n])
        score_grad = (probs_wide * (probs_grad - row_dot) * factor).astype(BF)
        query_grad = dot(score_grad, key_heads[n]).astype(BF).astype(F32)
        key_grad = t_dot(score_grad, query_heads[n]).astype(BF)
        query_grads += [query_grad[:, :DN], rotate(query_grad[:, DN:], cosine_table, -sine_table)]
        kv_grads += [key_grad[:, :DN], value_grad]
        rope_part = rope_part + key_grad[:, DN:].astype(F32)
    query_in_grad = jnp.concatenate(query_grads, axis=1).astype(BF)
    kv_grad = jnp.concatenate(kv_grads, axis=1)
    latent_part = jnp.concatenate([dot_t(kv_grad, up_cols), rope_part], axis=1)
    latent_grad = along.scatter(latent_part[:half], latent_part[half:])
    one_part = dot_t(query_in_grad, query_cols)
    one_grad = along.scatter(one_part[:half], one_part[half:])
    latent_raw_grad, latent_terms = norm_back(
        latent_grad[:, :R], latent_raw[:count], inverse_latent[:count], latent_wide
    )
    down_rows = jnp.concatenate(
        [
            latent_raw_grad,
            rotate(latent_grad[:, R:], cosine_table[:count], -sine_table[:count]),
        ],
        axis=1,
    ).astype(BF)
    down_rows_all = jnp.concatenate(along.group(down_rows), axis=0)
    output = (residual[:count] + along.scatter(out_part[:half], out_part[half:])).astype(BF)

    shared_out = across.sum_stack(shared_grad_stack)
    drop_out = across.sum_stack(columns_first(t_dot(shared_hidden, grad_rows), n_exp))
    output_out = across.sum_stack(
        columns_first(t_dot(result, jnp.concatenate(half_all, axis=0)), n_exp)
    )
    up_out = across.sum_stack(t_dot(latent_all, kv_grad).reshape(n_exp, R // n_exp, -1))
    query_out = across.sum_stack(
        t_dot(normed_one, query_in_grad).reshape(n_exp, width // n_exp, -1)
    )
    mine = lax.dynamic_slice_in_dim(
        normed_one.reshape(length, n_exp, n_seq * gain_rows), seq * gain_rows, gain_rows, 2
    ).reshape(length, n_exp * gain_rows)
    down_out = across.sum_stack(t_dot(mine, down_rows_all).reshape(n_exp, gain_rows, -1))

    down_back = dot_t(down_rows, down_full)
    one_hat = token_wide * inverse_one
    first_sum = jnp.sum(one_part * one_hat, axis=0) + jnp.sum(down_back * one_hat[:count], axis=0)
    token_norm_grad, _ = norm_back(
        one_grad + down_back, token_wide[:count], inverse_one[:count], gain_first
    )
    tokens_grad = (residual_grad + token_norm_grad).astype(BF)
    small = scatter_small(
        jnp.concatenate(
            [
                first_sum.reshape(n_exp, n_seq, gain_rows),
                jnp.sum(second_terms, axis=0).reshape(n_exp, n_seq, gain_rows),
                jnp.sum(latent_terms, axis=0).reshape(n_exp, n_seq, latent_rows_local),
            ],
            axis=2,
        )
    )
    return (
        output,
        tokens_grad,
        small[:gain_rows],
        query_out,
        down_out,
        small[2 * gain_rows :],
        up_out,
        output_out,
        small[gain_rows : 2 * gain_rows],
        shared_out[0],
        shared_out[1],
        drop_out,
        expert_gate_grad,
        expert_up_grad,
        expert_down_grad,
    )


def solution(mesh):
    rows = P(("exp", "seq"), None)
    line = P(("exp", "seq"))
    grid = P("exp", "seq")
    turned = P("seq", "exp")
    part = P(("exp", "seq"), None, None)
    return jax.shard_map(
        shards,
        mesh=mesh,
        in_specs=(
            rows,
            rows,
            rows,
            line,
            grid,
            rows,
            line,
            grid,
            turned,
            line,
            grid,
            grid,
            turned,
            part,
            part,
            part,
            rows,
        ),
        out_specs=(
            rows,
            rows,
            line,
            grid,
            rows,
            line,
            grid,
            turned,
            line,
            grid,
            grid,
            turned,
            part,
            part,
            part,
        ),
        check_vma=False,
    )
```

time: 2120 us -> 1200 us (0.57)
  waiting for transfers between devices: 1520 us -> 293 us
  local copies, waits for them, and re-layouts: 82.5 us -> 357 us
  blocking collectives: 168 us -> 0 us
  starting transfers between devices: 38.7 us -> 182 us
  other arithmetic: 24.4 us -> 108 us
  matrix products: 267 us -> 236 us
    all_gather x12 -> x0, waiting for transfers between devices: 623 us -> none  [the longest x1 118 us: shards(): lax.all_gather(query_cols, 'seq', axis=1, tiled=True)]
    all_to_all x7 -> x8, waiting for transfers between devices: 500 us -> 10.8 us  [give(): return lax.all_to_all(rows, 'exp', split_axis=0, concat_axis=0, tiled=True)]
    ppermute x0 -> x116, waiting for transfers between devices: none -> 282 us  [swap(): return lax.ppermute(x, axis, [(i, i ^ mask) for i in range(n)])]
    reduce_scatter x11 -> x0, waiting for transfers between devices: 221 us -> none  [the longest x1 146 us: shards(): lax.psum_scatter(down_grad, ('exp', 'seq'), scatter_dimension=0, tiled=True)]
    unnamed x29 -> x0, waiting for transfers between devices: 176 us -> none
    dynamic_update_slice x0 -> x30, local copies, waits for them, and re-layouts: none -> 164 us  [the longest x22 156 us: stack(): out = lax.dynamic_update_slice_in_dim(out, block[None], me ^ j, 0)]
    ppermute x0 -> x116, starting transfers between devices: none -> 146 us  [swap(): return lax.ppermute(x, axis, [(i, i ^ mask) for i in range(n)])]
    unnamed x2 -> x0, blocking collectives: 87.5 us -> none
  transfers between devices with their start and end apart: 33 -> 124, of which waited for: 24 -> 39; matrix products, arithmetic and copies ran while one was open for 17% -> 54% of each run, Pallas kernels for 0% -> 0%
where the time goes in v1:
time: 1200 us; the launch traced here: 1180 us
  local copies, waits for them, and re-layouts  357 us (30%)
  waiting for transfers between devices  293 us (24%)
  matrix products  236 us (20%)
  starting transfers between devices  182 us (15%)
  other arithmetic  108 us (9%)
    ppermute x116, waiting for transfers between devices, swap(): return lax.ppermute(x, axis, [(i, i ^ mask) for i in range(n)])  282 us
    dynamic_update_slice x22, local copies, waits for them, and re-layouts, stack(): out = lax.dynamic_update_slice_in_dim(out, block[None], me ^ j, 0)  156 us
    ppermute x116, starting transfers between devices, swap(): return lax.ppermute(x, axis, [(i, i ^ mask) for i in range(n)])  146 us
    unnamed x415, local copies, waits for them, and re-layouts  91 us
    dot_general x17, matrix products, dot(): return jnp.dot(a, b, preferred_element_type=F32)  79.9 us
    dot_general x17, matrix products, dot_t(): lax.dot_general(a, b, (((1,), (1,)), ((), ())), preferred_element_type=F32)  77.3 us
    dot_general x17, matrix products, t_dot(): lax.dot_general(a, b, (((0,), (0,)), ((), ())), preferred_element_type=F32)  69.3 us
    all_to_all x8, starting transfers between devices, give(): return lax.all_to_all(rows, 'exp', split_axis=0, concat_axis=0, tiled=True)  35.2 us
  transfers between devices with their start and end apart: 124, of which 39 were waited for; matrix products, arithmetic and copies ran while one was open for 54% of the time, Pallas kernels for 0%

profile of v1, /device:TPU:0, one launch (start us, length us, event | category | flops | bytes accessed | tf_op | source)
XLA Modules:
  0.0 1179.9 jit_solution(17533846658013368635)
XLA Ops:
  28.9 23.2 %dynamic_update_slice.120 = bf16[4,2,512,352]{2,0,3,1:T(4,128)(2,1)S(1)} dynamic-update-slice(bf16[4,2,512,352]{2,0,3,1:T(4,128)(2,1)S(1)} %broadcast_in_dim.196, bf16[1,2,512,352]{2,0,3,1:T(2,128)(2,1)} %copy.129, s32[]{:T(128)S(6)} %select_n.134, s32[]{:T(128)} %constant.220.clone.1, s32[]{:T(128)} %constant.220.clone.1, s32[]{:T(128)} %constant.220.clone.1) | dynamic-update-slice | bytes 1441796 | tf_op jit(solution)/shard_map/dynamic_update_slice | solution.py:121
  53.8 13.7 %dynamic_update_slice.124 = bf16[4,352,512]{2,0,1:T(4,128)(2,1)} dynamic-update-slice(bf16[4,352,512]{2,0,1:T(4,128)(2,1)} %broadcast_in_dim.201, bf16[1,352,512]{2,0,1:T(2,128)(2,1)} %copy.133, s32[]{:T(128)S(6)} %select_n.134, s32[]{:T(128)} %constant.220.clone.1, s32[]{:T(128)} %constant.220.clone.1) | dynamic-update-slice | bytes 720900 | tf_op jit(solution)/shard_map/dynamic_update_slice | solution.py:121
  93.2 20.8 %collective-permute-done.3 = bf16[128,2048]{1,0:T(8,128)(2,1)} collective-permute-done((bf16[128,2048]{1,0:T(8,128)(2,1)}, bf16[128,2048]{1,0:T(8,128)(2,1)}, u32[]{:S(2)}, u32[]{:S(2)}) %collective-permute-start.3) | collective-permute-done | bytes 524320 | tf_op jit(solution)/shard_map/ppermute | solution.py:74
  198.5 12.5 %collective-permute-done.26 = bf16[128,2048]{1,0:T(8,128)(2,1)S(1)} collective-permute-done((bf16[128,2048]{1,0:T(8,128)(2,1)S(1)}, bf16[128,2048]{1,0:T(8,128)(2,1)S(1)}, u32[]{:S(2)}, u32[]{:S(2)}) %collective-permute-start.26) | collective-permute-done | bytes 524320 | tf_op jit(solution)/shard_map/ppermute | solution.py:74
  267.8 10.2 collective-permute-start.23
  305.0 21.2 %collective-permute-done.27 = bf16[1024,256]{0,1:T(8,128)(2,1)} collective-permute-done((bf16[1024,256]{0,1:T(8,128)(2,1)}, bf16[1024,256]{0,1:T(8,128)(2,1)}, u32[]{:S(2)}, u32[]{:S(2)}) %collective-permute-start.27) | collective-permute-done | bytes 524320 | tf_op jit(solution)/shard_map/ppermute | solution.py:74
  344.7 23.0 %dynamic_update_slice.121 = bf16[4,2,512,352]{2,0,3,1:T(4,128)(2,1)S(1)} dynamic-update-slice(bf16[4,2,512,352]{2,0,3,1:T(4,128)(2,1)S(1)} %copy-done.19, bf16[1,2,512,352]{2,0,3,1:T(2,128)(2,1)} %copy.130, s32[]{:T(128)S(6)} %select_n.135, s32[]{:T(128)} %constant.220.clone.1, s32[]{:T(128)} %constant.220.clone.1, s32[]{:T(128)} %constant.220.clone.1) | dynamic-update-slice | bytes 1441796 | tf_op jit(solution)/shard_map/dynamic_update_slice | solution.py:121
  414.0 15.5 %collective-permute-done.43 = bf16[352,512]{1,0:T(8,128)(2,1)} collective-permute-done((bf16[352,512]{1,0:T(8,128)(2,1)}, bf16[352,512]{1,0:T(8,128)(2,1)}, u32[]{:S(2)}, u32[]{:S(2)}) %collective-permute-start.43) | collective-permute-done | bytes 360480 | tf_op jit(solution)/shard_map/ppermute | solution.py:74
  445.9 23.0 %dynamic_update_slice.122 = bf16[4,2,512,352]{2,0,3,1:T(4,128)(2,1)S(1)} dynamic-update-slice(bf16[4,2,512,352]{2,0,3,1:T(4,128)(2,1)S(1)} %dynamic_update_slice.121, bf16[1,2,512,352]{2,0,3,1:T(2,128)(2,1)} %copy.131, s32[]{:T(128)S(6)} %select_n.136, s32[]{:T(128)} %constant.220.clone.1, s32[]{:T(128)} %constant.220.clone.1, s32[]{:T(128)} %constant.220.clone.1) | dynamic-update-slice | bytes 1441796 | tf_op jit(solution)/shard_map/dynamic_update_slice | solution.py:121
  468.9 23.0 %dynamic_update_slice.123 = bf16[4,2,512,352]{2,0,3,1:T(4,128)(2,1)S(1)} dynamic-update-slice(bf16[4,2,512,352]{2,0,3,1:T(4,128)(2,1)S(1)} %dynamic_update_slice.122, bf16[1,2,512,352]{2,0,3,1:T(2,128)(2,1)} %copy.132, s32[]{:T(128)S(6)} %select_n.137, s32[]{:T(128)} %constant.220.clone.1, s32[]{:T(128)} %constant.220.clone.1, s32[]{:T(128)} %constant.220.clone.1) | dynamic-update-slice | bytes 1441796 | tf_op jit(solution)/shard_map/dynamic_update_slice | solution.py:121
  499.8 11.5 dynamic_update_slice.125
  511.3 11.9 %dynamic_update_slice.126 = bf16[4,352,512]{2,0,1:T(4,128)(2,1)S(1)} dynamic-update-slice(bf16[4,352,512]{2,0,1:T(4,128)(2,1)S(1)} %dynamic_update_slice.125, bf16[1,352,512]{2,0,1:T(2,128)(2,1)} %copy.135, s32[]{:T(128)S(6)} %select_n.136, s32[]{:T(128)} %constant.220.clone.1, s32[]{:T(128)} %constant.220.clone.1) | dynamic-update-slice | bytes 720900 | tf_op jit(solution)/shard_map/dynamic_update_slice | solution.py:121
  525.6 11.5 dynamic_update_slice.127
  537.5 14.0 %multiply_reduce_fusion.1 = (f32[1024]{0:T(1024)S(1)}, f32[1024,2048]{1,0:T(8,128)S(1)}) fusion(bf16[1024,2048]{0,1:T(8,128)(2,1)} %slice_dynamic-update-slice_fusion.10, bf16[1024,2048]{0,1:T(8,128)(2,1)} %bitcast.31, bf16[1024,2048]{0,1:T(8,128)(2,1)} %bitcast.29, bf16[1024,2048]{1,0:T(8,128)(2,1)} %constant_dynamic-update-slice_fusion), kind=kOutput, calls=%fused_computation.15 | convolution fusion | flops 8615099392 | bytes 25169920 | tf_op jit(solution)/shard_map/dot_general | solution.py:25
  597.1 9.4 collective-permute-done.94
  626.7 23.3 %collective-permute-done.102 = bf16[352,512]{1,0:T(8,128)(2,1)S(1)} collective-permute-done((bf16[352,512]{1,0:T(8,128)(2,1)S(1)}, bf16[352,512]{1,0:T(8,128)(2,1)S(1)}, u32[]{:S(2)}, u32[]{:S(2)}) %collective-permute-start.102) | collective-permute-done | bytes 360480 | tf_op jit(solution)/shard_map/ppermute | solution.py:74
  776.7 10.8 all-to-all-done.5
  791.3 9.3 convolution_bitcast_fusion
  823.2 9.3 bitcast_add_fusion
  834.5 15.4 %pad_maximum_fusion.2 = f32[2,1408,2048]{2,1,0:T(8,128)} fusion(f32[1,1408,2048]{2,1,0:T(8,128)S(1)} %bitcast.461, f32[1,1408,2048]{2,1,0:T(8,128)} %convolution_bitcast_fusion.1), kind=kLoop, calls=%fused_computation.2 | loop fusion | flops 5767168 | bytes 46137344 | tf_op jit(solution)/shard_map/stack | solution.py:369
  862.9 9.6 collective-permute-start.57
  877.1 32.0 %collective-permute-done.57 = bf16[128,2048]{1,0:T(8,128)(2,1)S(1)} collective-permute-done((bf16[128,2048]{1,0:T(8,128)(2,1)S(1)}, bf16[128,2048]{1,0:T(8,128)(2,1)S(1)}, u32[]{:S(2)}, u32[]{:S(2)}) %collective-permute-start.57) | collective-permute-done | bytes 524320 | tf_op jit(solution)/shard_map/ppermute | solution.py:74
  1066.4 29.4 %collective-permute-done.74 = bf16[128,2048]{1,0:T(8,128)(2,1)S(1)} collective-permute-done((bf16[128,2048]{1,0:T(8,128)(2,1)S(1)}, bf16[128,2048]{1,0:T(8,128)(2,1)S(1)}, u32[]{:S(2)}, u32[]{:S(2)}) %collective-permute-start.74) | collective-permute-done | bytes 524320 | tf_op jit(solution)/shard_map/ppermute | solution.py:74
  1144.6 30.9 %collective-permute-done.76 = bf16[128,2048]{1,0:T(8,128)(2,1)S(1)} collective-permute-done((bf16[128,2048]{1,0:T(8,128)(2,1)S(1)}, bf16[128,2048]{1,0:T(8,128)(2,1)S(1)}, u32[]{:S(2)}, u32[]{:S(2)}) %collective-permute-start.76) | collective-permute-done | bytes 524320 | tf_op jit(solution)/shard_map/ppermute | solution.py:74
  (901 shorter events, 761.6 us)
Async XLA Ops:
  4.1 64.0 %collective-permute-start = (bf16[64,640]{1,0:T(8,128)(2,1)S(1)}, bf16[64,640]{1,0:T(8,128)(2,1)S(1)}, u32[]{:S(2)}, u32[]{:S(2)}) collective-permute-start(bf16[64,640]{1,0:T(8,128)(2,1)S(1)} %concatenate.101), channel_id=1, source_target_pairs={{0,2},{1,3},{2,0},{3,1},{4,6},{5,7},{6,4},{7,5},{8,10},{9,11},{10,... | collective-permute-start | bytes 245768 | tf_op jit(solution)/shard_map/ppermute | solution.py:74
  7.2 62.5 %collective-permute-start.2 = (bf16[64,640]{1,0:T(8,128)(2,1)S(1)}, bf16[64,640]{1,0:T(8,128)(2,1)S(1)}, u32[]{:S(2)}, u32[]{:S(2)}) collective-permute-start(bf16[64,640]{1,0:T(8,128)(2,1)S(1)} %concatenate.101), channel_id=1, source_target_pairs={{0,4},{1,5},{2,6},{3,7},{4,0},{5,1},{6,2},{7,3},{8,12},{9,13},{10,... | collective-permute-start | bytes 245768 | tf_op jit(solution)/shard_map/ppermute | solution.py:74
  9.8 59.9 %collective-permute-start.4 = (bf16[64,640]{1,0:T(8,128)(2,1)S(1)}, bf16[64,640]{1,0:T(8,128)(2,1)}, u32[]{:S(2)}, u32[]{:S(2)}) collective-permute-start(bf16[64,640]{1,0:T(8,128)(2,1)S(1)} %concatenate.101), channel_id=1, source_target_pairs={{0,6},{1,7},{2,4},{3,5},{4,2},{5,3},{6,0},{7,1},{8,14},{9,15},{10,... | collective-permute-start | bytes 245768 | tf_op jit(solution)/shard_map/ppermute | solution.py:74
  9.8 116.4 %collective-permute-start.6 = (bf16[128,2048]{1,0:T(8,128)(2,1)}, bf16[128,2048]{1,0:T(8,128)(2,1)}, u32[]{:S(2)}, u32[]{:S(2)}) collective-permute-start(bf16[128,2048]{1,0:T(8,128)(2,1)} %param.17), channel_id=1, source_target_pairs={{0,1},{1,0},{2,3},{3,2},{4,5},{5,4},{6,7},{7,6},{8,9},{9,8},{10,11... | collective-permute-start | bytes 1572872 | tf_op jit(solution)/shard_map/ppermute | solution.py:74
  9.8 65.2 %collective-permute-start.12 = (bf16[512,384]{1,0:T(8,128)(2,1)}, bf16[512,384]{1,0:T(8,128)(2,1)S(1)}, u32[]{:S(2)}, u32[]{:S(2)}) collective-permute-start(bf16[512,384]{1,0:T(8,128)(2,1)} %param.21), channel_id=1, source_target_pairs={{0,8},{8,0},{16,24},{24,16},{1,9},{9,1},{17,25},{25,17},{2,10},{10... | collective-permute-start | bytes 1179656 | tf_op jit(solution)/shard_map/ppermute | solution.py:74
  69.7 68.6 %collective-permute-start.46 = (f32[12,128]{1,0:T(8,128)S(1)}, f32[12,128]{1,0:T(8,128)}, u32[]{:S(2)}, u32[]{:S(2)}) collective-permute-start(f32[12,128]{1,0:T(8,128)S(1)} %pad_maximum_fusion.40), channel_id=1, source_target_pairs={{0,1},{1,0},{2,3},{3,2},{4,5},{5,4},{6,7},{7,6},{8,9},{9,8},{10,11... | collective-permute-start | bytes 18440 | tf_op jit(solution)/shard_map/ppermute | solution.py:74
  90.8 58.1 %collective-permute-start.11 = (bf16[4,64,640]{2,1,0:T(8,128)(2,1)}, bf16[4,64,640]{2,1,0:T(8,128)(2,1)}, u32[]{:S(2)}, u32[]{:S(2)}) collective-permute-start(bf16[4,64,640]{2,1,0:T(8,128)(2,1)} %pad_maximum_fusion.22), channel_id=1, source_target_pairs={{0,8},{8,0},{16,24},{24,16},{1,9},{9,1},{17,25},{25,17},{2,10},{10... | collective-permute-start | bytes 983048 | tf_op jit(solution)/shard_map/ppermute | solution.py:74
  154.3 57.3 %collective-permute-start.51 = (bf16[128,2048]{1,0:T(8,128)(2,1)S(1)}, bf16[128,2048]{1,0:T(8,128)(2,1)S(1)}, u32[]{:S(2)}, u32[]{:S(2)}) collective-permute-start(bf16[128,2048]{1,0:T(8,128)(2,1)S(1)} %copy-done.31), channel_id=1, source_target_pairs={{0,1},{1,0},{2,3},{3,2},{4,5},{5,4},{6,7},{7,6},{8,9},{9,8},{10,11... | collective-permute-start | bytes 1572872 | tf_op jit(solution)/shard_map/ppermute | solution.py:74
  211.0 78.3 %collective-permute-start.37 = (bf16[1024,512]{0,1:T(8,128)(2,1)}, bf16[1024,512]{0,1:T(8,128)(2,1)}, u32[]{:S(2)}, u32[]{:S(2)}) collective-permute-start(bf16[1024,512]{0,1:T(8,128)(2,1)} %pad_maximum_fusion.12), channel_id=1, source_target_pairs={{0,16},{8,24},{16,0},{24,8},{1,17},{9,25},{17,1},{25,9},{2,18},{10... | collective-permute-start | bytes 3145736 | tf_op jit(solution)/shard_map/ppermute | solution.py:74
  220.4 171.5 %all-to-all-start.6 = ((bf16[4,128,2048]{2,1,0:T(8,128)(2,1)}), bf16[4,128,2048]{2,1,0:T(8,128)(2,1)}, u32[]{:S(2)}, u32[]{:S(2)}) async-start(bf16[4,128,2048]{2,1,0:T(8,128)(2,1)} %bitcast.467), calls=%async_computation.6 | async-start | bytes 4194304 | tf_op jit(solution)/shard_map/all_to_all | solution.py:329
  231.7 136.0 %collective-permute-start.38 = (bf16[1024,512]{0,1:T(8,128)(2,1)}, bf16[1024,512]{0,1:T(8,128)(2,1)}, u32[]{:S(2)}, u32[]{:S(2)}) collective-permute-start(bf16[1024,512]{0,1:T(8,128)(2,1)} %pad_maximum_fusion.12), channel_id=1, source_target_pairs={{0,24},{8,16},{16,8},{24,0},{1,25},{9,17},{17,9},{25,1},{2,26},{10... | collective-permute-start | bytes 3145736 | tf_op jit(solution)/shard_map/ppermute | solution.py:74
  280.3 58.7 %collective-permute-start.32 = (bf16[1024,256]{0,1:T(8,128)(2,1)}, bf16[1024,256]{0,1:T(8,128)(2,1)}, u32[]{:S(2)}, u32[]{:S(2)}) collective-permute-start(bf16[1024,256]{0,1:T(8,128)(2,1)} %pad_maximum_fusion.15), channel_id=1, source_target_pairs={{0,1},{1,0},{2,3},{3,2},{4,5},{5,4},{6,7},{7,6},{8,9},{9,8},{10,11... | collective-permute-start | bytes 1572872 | tf_op jit(solution)/shard_map/ppermute | solution.py:74
  328.2 55.7 %collective-permute-start.34 = (bf16[1024,256]{0,1:T(8,128)(2,1)}, bf16[1024,256]{0,1:T(8,128)(2,1)}, u32[]{:S(2)}, u32[]{:S(2)}) collective-permute-start(bf16[1024,256]{0,1:T(8,128)(2,1)} %collective-permute-done.27), channel_id=1, source_target_pairs={{0,1},{1,0},{2,3},{3,2},{4,5},{5,4},{6,7},{7,6},{8,9},{9,8},{10,11... | collective-permute-start | bytes 1572872 | tf_op jit(solution)/shard_map/ppermute | solution.py:74
  344.7 67.8 %collective-permute-start.42 = (bf16[2,512,352]{1,2,0:T(8,128)(2,1)}, bf16[2,512,352]{1,2,0:T(8,128)(2,1)}, u32[]{:S(2)}, u32[]{:S(2)}) collective-permute-start(bf16[2,512,352]{1,2,0:T(8,128)(2,1)} %get-tuple-element.112), channel_id=1, source_target_pairs={{0,24},{8,16},{16,8},{24,0},{1,25},{9,17},{17,9},{25,1},{2,26},{10... | collective-permute-start | bytes 2162696 | tf_op jit(solution)/shard_map/ppermute | solution.py:74
  370.0 167.5 %collective-permute-start.39 = (bf16[4,1024,512]{1,2,0:T(8,128)(2,1)}, bf16[4,1024,512]{1,2,0:T(8,128)(2,1)}, u32[]{:S(2)}, u32[]{:S(2)}) collective-permute-start(bf16[4,1024,512]{1,2,0:T(8,128)(2,1)} %bitcast_dynamic-update-slice_fusion), channel_id=1, source_target_pairs={{0,1},{1,0},{2,3},{3,2},{4,5},{5,4},{6,7},{7,6},{8,9},{9,8},{10,11... | collective-permute-start | bytes 12582920 | tf_op jit(solution)/shard_map/ppermute | solution.py:74
  412.5 82.4 %collective-permute-start.44 = (bf16[352,512]{1,0:T(8,128)(2,1)S(1)}, bf16[352,512]{1,0:T(8,128)(2,1)}, u32[]{:S(2)}, u32[]{:S(2)}) collective-permute-start(bf16[352,512]{1,0:T(8,128)(2,1)S(1)} %copy-done.79), channel_id=1, source_target_pairs={{0,16},{8,24},{16,0},{24,8},{1,17},{9,25},{17,1},{25,9},{2,18},{10... | collective-permute-start | bytes 1081352 | tf_op jit(solution)/shard_map/ppermute | solution.py:74
  429.5 93.7 %collective-permute-start.45 = (bf16[352,512]{1,0:T(8,128)(2,1)S(1)}, bf16[352,512]{1,0:T(8,128)(2,1)}, u32[]{:S(2)}, u32[]{:S(2)}) collective-permute-start(bf16[352,512]{1,0:T(8,128)(2,1)S(1)} %copy-done.79), channel_id=1, source_target_pairs={{0,24},{8,16},{16,8},{24,0},{1,25},{9,17},{17,9},{25,1},{2,26},{10... | collective-permute-start | bytes 1081352 | tf_op jit(solution)/shard_map/ppermute | solution.py:74
  593.4 62.9 %all-to-all-start.2 = ((bf16[4,128,2048]{2,1,0:T(8,128)(2,1)}), bf16[4,128,2048]{2,1,0:T(8,128)(2,1)S(1)}, u32[]{:S(2)}, u32[]{:S(2)}) async-start(bf16[4,128,2048]{2,1,0:T(8,128)(2,1)} %bitcast.73), calls=%async_computation.2 | async-start | bytes 4194304 | tf_op jit(solution)/shard_map/all_to_all | solution.py:329
  650.0 199.8 %collective-permute-start.103 = (bf16[352,512]{1,0:T(8,128)(2,1)}, bf16[352,512]{1,0:T(8,128)(2,1)}, u32[]{:S(2)}, u32[]{:S(2)}) collective-permute-start(bf16[352,512]{1,0:T(8,128)(2,1)} %get-tuple-element.146), channel_id=1, source_target_pairs={{0,24},{8,16},{16,8},{24,0},{1,25},{9,17},{17,9},{25,1},{2,26},{10... | collective-permute-start | bytes 1081352 | tf_op jit(solution)/shard_map/ppermute | solution.py:74
  651.4 198.4 %collective-permute-start.96 = (bf16[352,512]{1,0:T(8,128)(2,1)}, bf16[352,512]{1,0:T(8,128)(2,1)}, u32[]{:S(2)}, u32[]{:S(2)}) collective-permute-start(bf16[352,512]{1,0:T(8,128)(2,1)} %get-tuple-element.139), channel_id=1, source_target_pairs={{0,16},{8,24},{16,0},{24,8},{1,17},{9,25},{17,1},{25,9},{2,18},{10... | collective-permute-start | bytes 1081352 | tf_op jit(solution)/shard_map/ppermute | solution.py:74
  689.9 66.9 %all-to-all-start.7 = ((bf16[4,128,2048]{2,1,0:T(8,128)(2,1)}), bf16[4,128,2048]{2,1,0:T(8,128)(2,1)S(1)}, u32[]{:S(2)}, u32[]{:S(2)}) async-start(bf16[4,128,2048]{2,1,0:T(8,128)(2,1)} %bitcast.492), calls=%async_computation.7 | async-start | bytes 4194304 | tf_op jit(solution)/shard_map/all_to_all | solution.py:329
  875.3 57.4 %collective-permute-start.50 = (bf16[512,2048]{1,0:T(8,128)(2,1)S(1)}, bf16[512,2048]{1,0:T(8,128)(2,1)S(1)}, u32[]{:S(2)}, u32[]{:S(2)}) collective-permute-start(bf16[512,2048]{1,0:T(8,128)(2,1)S(1)} %slice.1241), channel_id=1, source_target_pairs={{0,1},{1,0},{2,3},{3,2},{4,5},{5,4},{6,7},{7,6},{8,9},{9,8},{10,11... | collective-permute-start | bytes 6291464 | tf_op jit(solution)/shard_map/ppermute | solution.py:74
  971.3 75.4 %collective-permute-start.70 = (bf16[512,2048]{1,0:T(8,128)(2,1)}, bf16[512,2048]{1,0:T(8,128)(2,1)}, u32[]{:S(2)}, u32[]{:S(2)}) collective-permute-start(bf16[512,2048]{1,0:T(8,128)(2,1)} %slice.1239), channel_id=1, source_target_pairs={{0,1},{1,0},{2,3},{3,2},{4,5},{5,4},{6,7},{7,6},{8,9},{9,8},{10,11... | collective-permute-start | bytes 6291464 | tf_op jit(solution)/shard_map/ppermute | solution.py:74
  1062.6 55.5 %collective-permute-start.109 = (bf16[128,576]{0,1:T(8,128)(2,1)}, bf16[128,576]{0,1:T(8,128)(2,1)S(1)}, u32[]{:S(2)}, u32[]{:S(2)}) collective-permute-start(bf16[128,576]{0,1:T(8,128)(2,1)} %get-tuple-element.129), channel_id=1, source_target_pairs={{0,1},{1,0},{2,3},{3,2},{4,5},{5,4},{6,7},{7,6},{8,9},{9,8},{10,11... | collective-permute-start | bytes 442376 | tf_op jit(solution)/shard_map/ppermute | solution.py:74
  (269 other events, 5226.2 us)

commit v2 on v1

v2 whole, which is shorter than its diff:
```python
import math

import jax
import jax.numpy as jnp
from jax import lax
from jax.experimental import pallas as pl
from jax.experimental.pallas import tpu as pltpu
from jax.sharding import PartitionSpec as P

H = 16
DN = 128
DR = 64
DV = 128
R = 512
EXPERTS = 64
TOP = 6
CAP = 16


eps_norm = 1e-06
rope_base = 50000.0
BF = jnp.bfloat16
F32 = jnp.float32


def dot(a, b):
    return jnp.dot(a, b, preferred_element_type=F32)


def dot_t(a, b):
    return lax.dot_general(a, b, (((1,), (1,)), ((), ())), preferred_element_type=F32)


def t_dot(a, b):
    return lax.dot_general(a, b, (((0,), (0,)), ((), ())), preferred_element_type=F32)


def rope_tables(positions, width):
    middle = width // 2
    frequency = rope_base ** (-(jnp.arange(middle, dtype=F32) * 2.0 / width))
    angles = positions.astype(F32)[:, None] * frequency[None, :]
    return (jnp.cos(angles), jnp.sin(angles))


def rotate(values, cosine_table, sine_table):
    middle = values.shape[-1] // 2
    leading = values[..., :middle]
    trailing = values[..., middle:]
    return jnp.concatenate(
        [
            leading * cosine_table - trailing * sine_table,
            trailing * cosine_table + leading * sine_table,
        ],
        axis=-1,
    )


def silu_slope(gate_values):
    sigmoid = jax.nn.sigmoid(gate_values)
    return sigmoid * (1.0 + gate_values * (1.0 - sigmoid))


def norm_back(dy, v, inverse, gain):
    hat = v * inverse
    scaled = dy * gain
    dv = inverse * (scaled - hat * jnp.mean(scaled * hat, axis=-1, keepdims=True))
    return dv, dy * hat


def inverse_rms(v):
    return lax.rsqrt(jnp.mean(v * v, axis=-1, keepdims=True) + eps_norm)


LIMIT = 56 * 1024 * 1024
ANY = pl.BlockSpec(memory_space=pl.ANY)
SCALARS = pl.BlockSpec(memory_space=pltpu.SMEM)


def whole(shape):
    return pl.BlockSpec(shape, lambda *grid: (0,) * len(shape))


def arrange(index, blocks, outs, plan):
    def kernel(index_ref, *refs):
        sources = refs[: len(blocks)]
        targets = refs[len(blocks) :]
        for block, source, out, target in plan:
            targets[out][target(index_ref)] = sources[block][source]

    size = sum(math.prod(s) * 2 for s in outs)
    return pl.pallas_call(
        kernel,
        out_shape=[jax.ShapeDtypeStruct(s, BF) for s in outs],
        in_specs=[SCALARS] + [pl.BlockSpec(memory_space=pltpu.VMEM)] * len(blocks),
        out_specs=[pl.BlockSpec(memory_space=pltpu.VMEM)] * len(outs),
        compiler_params=pltpu.CompilerParams(vmem_limit_bytes=LIMIT),
        cost_estimate=pl.CostEstimate(flops=0, transcendentals=0, bytes_accessed=2 * size),
        name="arrange",
    )(index, *blocks)


def span(start, size):
    return pl.ds(pl.multiple_of(start * size, size), size)


def turned(v, cosine, sine):
    middle = v.shape[1] // 2
    return v * cosine + jnp.concatenate([v[:, middle:], v[:, :middle]], axis=1) * sine


def project(index, chip, pair, gain, w_query, w_down, latent_gain, w_up, cosine, sine, heads, length, earlier):
    count, width = pair[0].shape
    wide = DN + DR
    many = len(w_query)
    kept = list(earlier or ())
    query_rows = w_query[0].shape[0]

    def kernel(index_ref, a_ref, b_ref, g_ref, wd_ref, lg_ref, *refs):
        wq_refs = refs[:many]
        wu_ref, c_ref, s_ref = refs[many : many + 3]
        n_ref, l_ref, r_ref, q_ref, k_ref, v_ref = refs[many + 3 + len(kept) :]
        me = index_ref[0]
        x = jnp.where(pl.program_id(0) == 0, a_ref[...], b_ref[...]).astype(F32)
        inverse = lax.rsqrt(jnp.mean(x * x, axis=1, keepdims=True) + eps_norm)
        n_ref[...] = (x * inverse * g_ref[...]).astype(BF)
        down = dot(n_ref[...], wd_ref[...])
        raw = down[:, :R]
        r_ref[...] = raw
        inverse = lax.rsqrt(jnp.mean(raw * raw, axis=1, keepdims=True) + eps_norm)
        l_ref[...] = (raw * inverse * lg_ref[...]).astype(BF)
        query = 0.0
        for j in range(many):
            query = query + dot(n_ref[:, span(me ^ j, query_rows)], wq_refs[j][...])
        up = dot(l_ref[...], wu_ref[...]).astype(BF)
        cosine, sine = c_ref[...], s_ref[...]
        zeros = jnp.zeros((count, 256 - wide), BF)
        rope = jnp.concatenate([turned(down[:, R : R + DR], cosine, sine).astype(BF), zeros], axis=1)
        for n in range(heads):
            own = query[:, n * wide : (n + 1) * wide]
            q_ref[n, :, :DN] = own[:, :DN].astype(BF)
            q_ref[n, :, DN:] = jnp.concatenate(
                [turned(own[:, DN:], cosine, sine).astype(BF), zeros], axis=1
            )
            k_ref[n, :, :DN] = up[:, n * (DN + DV) : n * (DN + DV) + DN]
            k_ref[n, :, DN:] = rope
            v_ref[n] = up[:, n * (DN + DV) + DN : (n + 1) * (DN + DV)]

    chips = length // count // 2

    def rows(w):
        return pl.BlockSpec((count, w), lambda i: (chip + i * chips, 0))

    def head_rows(w):
        return pl.BlockSpec((heads, count, w), lambda i: (0, chip + i * chips, 0))

    columns = w_query[0].shape[1] + w_down.shape[1]
    first = 6 + many + 3
    return pl.pallas_call(
        kernel,
        grid=(2,),
        in_specs=[
            SCALARS,
            whole((count, width)),
            whole((count, width)),
            whole((1, width)),
            whole(w_down.shape),
            whole((1, R)),
        ]
        + [whole(w.shape) for w in w_query]
        + [whole(w_up.shape), rows(DR), rows(DR)]
        + [ANY] * len(kept),
        out_specs=[rows(width), rows(R), rows(R), head_rows(256), head_rows(256), head_rows(DV)],
        out_shape=[
            jax.ShapeDtypeStruct((length, width), BF),
            jax.ShapeDtypeStruct((length, R), BF),
            jax.ShapeDtypeStruct((length, R), F32),
            jax.ShapeDtypeStruct((heads, length, 256), BF),
            jax.ShapeDtypeStruct((heads, length, 256), BF),
            jax.ShapeDtypeStruct((heads, length, DV), BF),
        ],
        input_output_aliases={first + n: n for n in range(len(kept))},
        compiler_params=pltpu.CompilerParams(vmem_limit_bytes=LIMIT),
        cost_estimate=pl.CostEstimate(
            flops=4 * count * (width * columns + R * w_up.shape[1]),
            transcendentals=0,
            bytes_accessed=8 * count * width + 2 * width * columns,
        ),
        name="project",
    )(index, *pair, gain, w_down, latent_gain, *w_query, w_up, cosine, sine, *kept)


def attend(query, key, value, row_position, column_position, factor):
    heads, length, _ = query.shape
    tile = 256

    def kernel(q_ref, k_ref, v_ref, row_ref, column_ref, o_ref, s_ref):
        allowed = column_ref[...] <= row_ref[...]
        for n in range(heads):
            scores = dot_t(k_ref[n], q_ref[n]) * factor
            exponent = jnp.where(allowed, jnp.exp(jnp.where(allowed, scores, -1e30)), 0.0)
            total = jnp.sum(exponent, axis=0, keepdims=True)
            probs = (exponent / total).astype(BF)
            o_ref[:, n * DV : (n + 1) * DV] = t_dot(v_ref[n], probs).T.astype(BF)
            s_ref[n : n + 1, :] = jnp.log(total)

    return pl.pallas_call(
        kernel,
        grid=(length // tile,),
        in_specs=[
            pl.BlockSpec((heads, tile, 256), lambda i: (0, i, 0)),
            whole(key.shape),
            whole(value.shape),
            pl.BlockSpec((1, tile), lambda i: (0, i)),
            whole((length, 1)),
        ],
        out_specs=[
            pl.BlockSpec((tile, heads * DV), lambda i: (i, 0)),
            pl.BlockSpec((heads, tile), lambda i: (0, i)),
        ],
        out_shape=[
            jax.ShapeDtypeStruct((length, heads * DV), BF),
            jax.ShapeDtypeStruct((heads, length), F32),
        ],
        compiler_params=pltpu.CompilerParams(vmem_limit_bytes=LIMIT),
        cost_estimate=pl.CostEstimate(
            flops=2 * heads * length * length * (256 + DV),
            transcendentals=heads * length * length,
            bytes_accessed=4 * heads * length * 640,
        ),
        name="attend",
    )(query, key, value, row_position, column_position)


def attend_back(query, key, value, result, result_grad, logsum, row_position, column_position, cosine, sine, w_up, factor):
    heads, length, _ = query.shape
    tile = 256
    steps = length // tile
    wide = DN + DR

    def kernel(q_ref, k_ref, v_ref, o_ref, do_ref, ls_ref, row_ref, column_ref, c_ref, s_ref, wu_ref, dq_ref, kv_ref, lp_ref, rope_ref, dk_acc, dv_acc, kt):
        step = pl.program_id(0)

        @pl.when(step == 0)
        def _():
            dk_acc[...] = jnp.zeros_like(dk_acc)
            dv_acc[...] = jnp.zeros_like(dv_acc)
            for n in range(heads):
                kt[n] = k_ref[n].T

        allowed = column_ref[...] <= row_ref[...]
        cosine, sine = c_ref[...], s_ref[...]
        parts = []
        for n in range(heads):
            q = q_ref[n]
            grad = do_ref[:, n * DV : (n + 1) * DV]
            scores = jnp.where(allowed, dot_t(k_ref[n], q) * factor, -1e30)
            probs = jnp.exp(scores - ls_ref[n : n + 1, :])
            dv_acc[n] += dot(probs.astype(BF), grad)
            product = grad.astype(F32) * o_ref[:, n * DV : (n + 1) * DV].astype(F32)
            row_dot = jnp.sum(product.T, axis=0, keepdims=True)
            probs_grad = dot_t(v_ref[n], grad)
            score_grad = (probs * (probs_grad - row_dot) * factor).astype(BF)
            dk_acc[n] += dot(score_grad, q)
            query_grad = dot(kt[n], score_grad).T.astype(BF)
            parts.append(query_grad[:, :DN])
            parts.append(turned(query_grad[:, DN:wide].astype(F32), cosine, sine).astype(BF))
        dq_ref[...] = jnp.concatenate(parts, axis=1)

        @pl.when(step == steps - 1)
        def _():
            rope = jnp.zeros((length, DR), F32)
            for n in range(heads):
                key_grad = dk_acc[n].astype(BF)
                value_grad = dv_acc[n].astype(BF)
                base = n * (DN + DV)
                kv_ref[:, base : base + DN] = key_grad[:, :DN]
                kv_ref[:, base + DN : base + DN + DV] = value_grad
                rope = rope + key_grad[:, DN:wide].astype(F32)
            lp_ref[...] = dot_t(kv_ref[...], wu_ref[...])
            rope_ref[...] = rope

    return pl.pallas_call(
        kernel,
        grid=(steps,),
        in_specs=[
            pl.BlockSpec((heads, tile, 256), lambda i: (0, i, 0)),
            whole(key.shape),
            whole(value.shape),
            pl.BlockSpec((tile, heads * DV), lambda i: (i, 0)),
            pl.BlockSpec((tile, heads * DV), lambda i: (i, 0)),
            pl.BlockSpec((heads, tile), lambda i: (0, i)),
            pl.BlockSpec((1, tile), lambda i: (0, i)),
            whole((length, 1)),
            pl.BlockSpec((tile, DR), lambda i: (i, 0)),
            pl.BlockSpec((tile, DR), lambda i: (i, 0)),
            whole(w_up.shape),
        ],
        out_specs=[
            pl.BlockSpec((tile, heads * wide), lambda i: (i, 0)),
            whole((length, heads * (DN + DV))),
            whole((length, R)),
            whole((length, DR)),
        ],
        out_shape=[
            jax.ShapeDtypeStruct((length, heads * wide), BF),
            jax.ShapeDtypeStruct((length, heads * (DN + DV)), BF),
            jax.ShapeDtypeStruct((length, R), F32),
            jax.ShapeDtypeStruct((length, DR), F32),
        ],
        scratch_shapes=[
            pltpu.VMEM((heads, length, 256), F32),
            pltpu.VMEM((heads, length, DV), F32),
            pltpu.VMEM((heads, 256, length), BF),
        ],
        compiler_params=pltpu.CompilerParams(vmem_limit_bytes=LIMIT),
        cost_estimate=pl.CostEstimate(
            flops=2 * heads * length * length * (3 * 256 + 2 * DV),
            transcendentals=heads * length * length,
            bytes_accessed=8 * heads * length * 640,
        ),
        name="attend_back",
    )(query, key, value, result, result_grad, logsum, row_position, column_position, cosine, sine, w_up)


def add_norm(token_blocks, blocks, w_output, gain):
    count, width = token_blocks[0].shape
    many = len(blocks)
    length = count * many
    tile = 2 * count
    depth = blocks[0].shape[1]

    def kernel(w_ref, g_ref, *refs):
        parts, tokens = refs[:many], refs[many : 2 * many]
        n_ref, r_ref, x_ref = refs[2 * many :]
        rows = []
        for q in range(many):
            block = parts[q][...]
            if q % 2:
                block = jnp.concatenate([block[count:], block[:count]], axis=0)
            rows.append(block)
        total = dot(jnp.concatenate(rows, axis=1), w_ref[...])
        for i in range(many // 2):

            @pl.when(pl.program_id(0) == i)
            def _():
                x_ref[:count] = tokens[2 * i][...]
                x_ref[count:] = tokens[2 * i + 1][...]

        total = total + x_ref[...].astype(F32)
        inverse = lax.rsqrt(jnp.mean(total * total, axis=1, keepdims=True) + eps_norm)
        n_ref[...] = (total * inverse * g_ref[...]).astype(BF)

        @pl.when(pl.program_id(0) == 0)
        def _():
            r_ref[...] = total[:count]

    def source(q):
        return pl.BlockSpec((tile, depth), lambda i: (i ^ (q >> 1), 0))

    return pl.pallas_call(
        kernel,
        grid=(length // tile,),
        in_specs=[whole(w_output.shape), whole((1, width))]
        + [source(q) for q in range(many)]
        + [whole((count, width))] * many,
        out_specs=[pl.BlockSpec((tile, width), lambda i: (i, 0)), whole((count, width))],
        out_shape=[
            jax.ShapeDtypeStruct((length, width), BF),
            jax.ShapeDtypeStruct((count, width), F32),
        ],
        scratch_shapes=[pltpu.VMEM((tile, width), BF)],
        compiler_params=pltpu.CompilerParams(vmem_limit_bytes=LIMIT),
        cost_estimate=pl.CostEstimate(
            flops=2 * length * width * w_output.shape[0],
            transcendentals=0,
            bytes_accessed=6 * length * width + 2 * width * w_output.shape[0],
        ),
        name="add_norm",
    )(w_output, gain, *blocks, *token_blocks)


def expert(rows, cots, gate, up, down, piece):
    count, width = rows.shape
    units = gate.shape[2]
    tile = min(512, count)
    step = 256
    full = units // step
    rest = units % step
    spans = [(n * step, step) for n in range(full)] + ([(full * step, rest)] if rest else [])

    def kernel(x_ref, c_ref, gate_hbm, up_hbm, down_hbm, res_ref, in_ref, h_ref, gg_ref, ug_ref, wg, wu, wd, acc_r, acc_i, sems):
        first = pl.program_id(0) == 0

        def copies(n, start, size):
            span = pl.ds(start, size)
            return [
                pltpu.make_async_copy(gate_hbm.at[piece, :, span], wg.at[:, span], sems.at[0, n]),
                pltpu.make_async_copy(up_hbm.at[piece, :, span], wu.at[:, span], sems.at[1, n]),
                pltpu.make_async_copy(down_hbm.at[piece, span, :], wd.at[span, :], sems.at[2, n]),
            ]

        @pl.when(first)
        def _():
            for n, (start, size) in enumerate(spans):
                for copy in copies(n, start, size):
                    copy.start()

        acc_r[...] = jnp.zeros_like(acc_r)
        acc_i[...] = jnp.zeros_like(acc_i)

        def chunk(n, start, size):
            @pl.when(first)
            def _():
                for copy in copies(n, start, size):
                    copy.wait()

            span = pl.ds(start, size)
            x, c = x_ref[...], c_ref[...]
            w_gate, w_up, w_down = wg[:, span], wu[:, span], wd[span, :]
            g = dot(x, w_gate)
            u = dot(x, w_up)
            hidden_grad = dot_t(c, w_down)
            s = jax.nn.sigmoid(g)
            silu = g * s
            hidden = (silu * u).astype(BF)
            gate_grad = (hidden_grad * u * (s * (1.0 + g * (1.0 - s)))).astype(BF)
            up_grad = (hidden_grad * silu).astype(BF)
            h_ref[:, span] = hidden
            gg_ref[:, span] = gate_grad
            ug_ref[:, span] = up_grad
            acc_r[...] += dot(hidden, w_down)
            acc_i[...] += dot_t(gate_grad, w_gate) + dot_t(up_grad, w_up)

        if full:

            @pl.loop(0, full)
            def _(n):
                chunk(n, pl.multiple_of(n * step, step), step)

        if rest:
            chunk(full, full * step, rest)
        res_ref[...] = acc_r[...].astype(BF)
        in_ref[...] = acc_i[...].astype(BF)

    def block(w):
        return pl.BlockSpec((tile, w), lambda i: (i, 0))

    def array(w):
        return jax.ShapeDtypeStruct((count, w), BF)

    return pl.pallas_call(
        kernel,
        grid=(count // tile,),
        in_specs=[block(width), block(width), ANY, ANY, ANY],
        out_specs=[block(width), block(width), block(units), block(units), block(units)],
        out_shape=[array(width), array(width), array(units), array(units), array(units)],
        scratch_shapes=[
            pltpu.VMEM((width, units), BF),
            pltpu.VMEM((width, units), BF),
            pltpu.VMEM((units, width), BF),
            pltpu.VMEM((tile, width), F32),
            pltpu.VMEM((tile, width), F32),
            pltpu.SemaphoreType.DMA((3, len(spans))),
        ],
        compiler_params=pltpu.CompilerParams(vmem_limit_bytes=LIMIT),
        cost_estimate=pl.CostEstimate(
            flops=12 * count * width * units,
            transcendentals=count * units,
            bytes_accessed=6 * width * units + 8 * count * width + 6 * count * units,
        ),
        name="expert",
    )(rows, cots, gate, up, down)


def expert_weights(rows, cots, hidden, gate_grad, up_grad, piece, pieces, earlier):
    count, width = rows.shape
    units = hidden.shape[1]
    tile = 256

    def kernel(x_ref, c_ref, h_ref, gg_ref, ug_ref, *refs):
        g_ref, u_ref, d_ref = refs[-3:]
        g_ref[0] = t_dot(x_ref[...], gg_ref[...])
        u_ref[0] = t_dot(x_ref[...], ug_ref[...])
        d_ref[0] = t_dot(h_ref[...], c_ref[...])

    tall = pl.BlockSpec((1, tile, units), lambda i: (piece, i, 0))
    flat = pl.BlockSpec((1, units, tile), lambda i: (piece, 0, i))
    column = pl.BlockSpec((count, tile), lambda i: (0, i))
    kept = list(earlier or ())
    return pl.pallas_call(
        kernel,
        grid=(width // tile,),
        in_specs=[column, column] + [whole((count, units))] * 3 + [ANY] * len(kept),
        out_specs=[tall, tall, flat],
        out_shape=[
            jax.ShapeDtypeStruct((pieces, width, units), F32),
            jax.ShapeDtypeStruct((pieces, width, units), F32),
            jax.ShapeDtypeStruct((pieces, units, width), F32),
        ],
        input_output_aliases={5 + n: n for n in range(len(kept))},
        compiler_params=pltpu.CompilerParams(vmem_limit_bytes=LIMIT),
        cost_estimate=pl.CostEstimate(
            flops=6 * count * width * units,
            transcendentals=0,
            bytes_accessed=12 * width * units + 4 * count * width,
        ),
        name="expert_weights",
    )(rows, cots, hidden, gate_grad, up_grad, *kept)


def dispatch(select, rows, slot_weight, pieces):
    blocks, slots, count = select.shape
    width = rows.shape[1]
    others = slots // pieces // CAP

    def kernel(m_ref, x_ref, *refs):
        got = dot(m_ref[0], x_ref[...])
        if slot_weight is not None:
            got = got * refs[0][0]
        got = got.astype(BF)
        for i in range(pieces):
            for j in range(others):
                start = (i * others + j) * CAP
                refs[-pieces + i][j] = got[start : start + CAP]

    weights = [] if slot_weight is None else [slot_weight]
    out = pl.BlockSpec((others, CAP, width), lambda b: (0, b, 0))
    return pl.pallas_call(
        kernel,
        grid=(blocks,),
        in_specs=[
            pl.BlockSpec((1, slots, count), lambda b: (b, 0, 0)),
            pl.BlockSpec((count, width), lambda b: (b, 0)),
        ]
        + [pl.BlockSpec((1, slots, 1), lambda b: (b, 0, 0))] * len(weights),
        out_specs=[out] * pieces,
        out_shape=[jax.ShapeDtypeStruct((others, blocks * CAP, width), BF)] * pieces,
        compiler_params=pltpu.CompilerParams(vmem_limit_bytes=LIMIT),
        cost_estimate=pl.CostEstimate(
            flops=2 * blocks * slots * count * width,
            transcendentals=0,
            bytes_accessed=2 * blocks * (slots + count) * width,
        ),
        name="dispatch",
    )(select, rows, *weights)


def combine(base, masks, returned, products, dtype):
    half = masks[0].shape[0] // 2
    slots, count = masks[0].shape[1:]
    pieces = len(returned)
    others, _, width = returned[0].shape
    many = len(masks)

    def kernel(*refs):
        mask_refs, row_refs = refs[:many], refs[many : many + pieces]
        rest, out_ref = refs[many + pieces : -1], refs[-1]
        rows = jnp.concatenate([row_refs[i][j] for i in range(pieces) for j in range(others)], axis=0)
        total = 0.0
        for n, (_, _, flipped) in enumerate(products):
            total = total + (dot_t if flipped else dot)(rest[2 * n][...], rest[2 * n + 1][...])
        for mask_ref in mask_refs:
            total = total + t_dot(mask_ref[0], rows)
        out_ref[...] = total.astype(dtype)

    factors = []
    specs = []
    for left, right, _ in products:
        factors += [left, right]
        specs += [
            pl.BlockSpec((count, left.shape[1]), lambda b: (base + b, 0)),
            whole(right.shape),
        ]
    return pl.pallas_call(
        kernel,
        grid=(half,),
        in_specs=[pl.BlockSpec((1, slots, count), lambda b: (base + b, 0, 0))] * many
        + [pl.BlockSpec((others, CAP, width), lambda b: (0, base + b, 0))] * pieces
        + specs,
        out_specs=pl.BlockSpec((count, width), lambda b: (b, 0)),
        out_shape=jax.ShapeDtypeStruct((half * count, width), dtype),
        compiler_params=pltpu.CompilerParams(vmem_limit_bytes=LIMIT),
        cost_estimate=pl.CostEstimate(
            flops=2 * half * count * width * (many * slots + sum(p[0].shape[1] for p in products)),
            transcendentals=0,
            bytes_accessed=half * count * width * 6,
        ),
        name="combine",
    )(*masks, *returned, *factors)


def swap(x, axis, mask):
    n = lax.axis_size(axis)
    return lax.ppermute(x, axis, [(i, i ^ mask) for i in range(n)])


def after(x, *earlier):
    return lax.optimization_barrier((x, *earlier))[0]


class Lane:
    def __init__(self, axis, depth):
        self.axis = axis
        self.depth = depth
        self.sent = []

    def send(self, x, mask):
        if len(self.sent) >= self.depth:
            x = after(x, self.sent[-self.depth])
        got = swap(x, self.axis, mask)
        self.sent.append(got)
        return got

    def chips(self, x):
        chips = lax.axis_size("seq") // 2
        return [x] + [self.send(x, 2 * k) for k in range(1, chips)]

    def group(self, x):
        evens = self.chips(x)
        return evens + [swap(b, "seq", 1) for b in evens]

    def scatter(self, even, odd):
        chips = lax.axis_size("seq") // 2
        rows = even.shape[0] // chips
        got = swap(odd.astype(BF), "seq", 1)
        blocks = [
            even[k * rows : (k + 1) * rows] + got[k * rows : (k + 1) * rows].astype(F32)
            for k in range(chips)
        ]
        total = blocks[0]
        for k in range(1, chips):
            total = total + self.send(blocks[k].astype(BF), 2 * k).astype(F32)
        return total

    def others(self, x):
        return [x] + [self.send(x, j) for j in range(1, lax.axis_size("exp"))]

    def sum_stack(self, x):
        n = lax.axis_size("exp")
        me = lax.axis_index("exp")
        total = lax.dynamic_index_in_dim(x, me, 0, keepdims=False)
        for j in range(1, n):
            piece = lax.dynamic_index_in_dim(x, me ^ j, 0, keepdims=False).astype(BF)
            total = total + self.send(piece, j).astype(F32)
        return total


def relative_order(count):
    chips = count // 2
    return [2 * k for k in range(chips)] + [2 * k + 1 for k in range(chips)]


def scatter_small(x):
    for axis in ("exp", "seq"):
        n = lax.axis_size(axis)
        me = lax.axis_index(axis)
        total = lax.dynamic_index_in_dim(x, me, 0, keepdims=False)
        for j in range(1, n):
            piece = lax.dynamic_index_in_dim(x, me ^ j, 0, keepdims=False)
            total = total + swap(piece, axis, j)
        x = total
    return x


def columns_first(x, blocks):
    rows, columns = x.shape
    return x.reshape(rows, blocks, columns // blocks).transpose(1, 0, 2)


def columns_last(x):
    blocks, rows, w = x.shape
    return x.transpose(1, 0, 2).reshape(rows, blocks * w)


def shards(
    tokens,
    routes,
    route_weights,
    norm_gain,
    w_query,
    w_kv_down,
    latent_gain,
    w_kv_up,
    w_output,
    ffn_gain,
    shared_gate,
    shared_up,
    shared_down,
    expert_gate,
    expert_up,
    expert_down,
    out_grad,
):
    count, width = tokens.shape
    n_seq = lax.axis_size("seq")
    n_exp = lax.axis_size("exp")
    seq = lax.axis_index("seq")
    order = relative_order(n_seq)
    chips = n_seq // 2
    heads = H // n_seq
    length = count * n_seq
    half = length // 2
    pieces = expert_gate.shape[0]
    parts_per = pieces * n_seq * n_exp // EXPERTS
    factor = 1.0 / math.sqrt(DN + DR)
    gain_rows = norm_gain.shape[0]
    latent_rows_local = latent_gain.shape[0]
    along = Lane("seq", 3)
    across = Lane("exp", 2)

    index = jnp.stack([lax.axis_index("exp"), seq]).astype(jnp.int32)
    extra = jnp.stack(
        [norm_gain, ffn_gain, jnp.pad(latent_gain, (0, gain_rows - latent_rows_local))]
    )
    packed = jnp.concatenate(
        [w_kv_down, jnp.pad(extra, ((0, 13), (0, w_kv_down.shape[1] - gain_rows)))], axis=0
    )
    packed_even = jnp.stack(along.chips(packed))
    query_parts = across.others(w_query)
    token_blocks = along.group(tokens)
    packed_parts = across.others(packed_even)
    packed_parts = packed_parts + [swap(x, "seq", 1) for x in packed_parts]
    up_parts = across.others(w_kv_up)
    route_pack = jnp.concatenate([routes.astype(F32).T, route_weights.T], axis=0)
    route_blocks = along.group(route_pack)
    output_even = jnp.concatenate(along.chips(w_output), axis=0)
    shared_parts = across.others(jnp.stack([shared_gate, shared_up]))
    drop_parts = across.others(shared_down)
    output_parts = across.others(output_even)
    output_parts = output_parts + [swap(x, "seq", 1) for x in output_parts]
    grad_blocks = along.group(out_grad)

    plan = []
    for n in range(2 * n_exp):
        for k in range(chips):

            def where(ref, n=n, k=k):
                return (ref[0] ^ (n % n_exp)) * n_seq + (ref[1] ^ (2 * k + n // n_exp))

            plan.append(
                (
                    n,
                    (k, slice(0, gain_rows)),
                    0,
                    lambda ref, where=where: (span(where(ref), gain_rows), slice(None)),
                )
            )
            plan.append(
                (
                    n,
                    (k, slice(gain_rows, gain_rows + 16)),
                    1,
                    lambda ref, where=where: (where(ref),),
                )
            )
    down_full, extra_all = arrange(
        index,
        packed_parts,
        [(width, R + DR), (n_exp * n_seq, 16, R + DR)],
        plan,
    )
    gain_first = extra_all[:, 0, :gain_rows].reshape(1, width).astype(F32)
    gain_second = extra_all[:, 1, :gain_rows].reshape(1, width).astype(F32)
    latent_wide = extra_all[:, 2, :latent_rows_local].reshape(1, R).astype(F32)
    block_rows = width // n_exp
    everything = slice(None)
    (up_cols,) = arrange(
        index,
        up_parts,
        [(R, w_kv_up.shape[1])],
        [
            (j, (everything,), 0, lambda ref, j=j: (span(ref[0] ^ j, R // n_exp), everything))
            for j in range(n_exp)
        ],
    )
    gate_cols, lift_cols = arrange(
        index,
        shared_parts,
        [(width, shared_gate.shape[1])] * 2,
        [
            (j, (n,), n, lambda ref, j=j: (span(ref[0] ^ j, block_rows), everything))
            for j in range(n_exp)
            for n in range(2)
        ],
    )
    (drop_rows,) = arrange(
        index,
        drop_parts,
        [(shared_down.shape[0], width)],
        [
            (j, (everything,), 0, lambda ref, j=j: (everything, span(ref[0] ^ j, block_rows)))
            for j in range(n_exp)
        ],
    )
    output_half = H * DV // 2
    (output_full,) = arrange(
        index,
        output_parts,
        [(H * DV, width)],
        [
            (
                n,
                (everything,),
                0,
                lambda ref, n=n: (
                    slice(n // n_exp * output_half, (n // n_exp + 1) * output_half),
                    span(ref[0] ^ (n % n_exp), block_rows),
                ),
            )
            for n in range(2 * n_exp)
        ],
    )

    positions = jnp.concatenate(
        [(seq ^ r) * count + jnp.arange(count, dtype=jnp.int32) for r in order]
    )
    row_position, column_position = positions[None, :], positions[:, None]
    cosine_table, sine_table = rope_tables(positions, DR)
    cosine_wide = jnp.concatenate([cosine_table, cosine_table], axis=1)
    sine_wide = jnp.concatenate([-sine_table, sine_table], axis=1)
    projected = None
    for k in range(chips):
        projected = project(
            index,
            k,
            (token_blocks[k], token_blocks[chips + k]),
            gain_first,
            query_parts,
            down_full,
            latent_wide,
            up_cols,
            cosine_wide,
            sine_wide,
            heads,
            length,
            projected,
        )
    normed_one, latent_all, latent_raw, query_heads, key_heads, value_heads = projected
    result, logsum = attend(
        query_heads, key_heads, value_heads, row_position, column_position, factor
    )

    result_blocks = along.group(result)
    normed_two, residual = add_norm(token_blocks, result_blocks, output_full, gain_second)
    inverse_two = inverse_rms(residual)

    column = jnp.stack(
        [
            ((other * n_seq + seq) * pieces + i) // parts_per
            for i in range(pieces)
            for other in range(n_exp)
        ]
    )
    kinds = n_exp * pieces
    route_all = jnp.stack(route_blocks)
    named = route_all[:, None, :TOP, :].astype(jnp.int32) == column[None, :, None, None]
    matched = jnp.any(named, axis=2)
    match_weight = jnp.sum(jnp.where(named, route_all[:, None, TOP:, :], 0.0), axis=2)
    earlier = (jnp.arange(count)[:, None] < jnp.arange(count)[None, :]).astype(BF)
    rank = jnp.dot(matched.astype(BF), earlier, preferred_element_type=F32).astype(jnp.int32)
    chosen = (rank[:, :, None, :] == jnp.arange(CAP, dtype=jnp.int32)[None, None, :, None]) & (
        matched[:, :, None, :]
    )
    select = chosen.astype(BF).reshape(n_seq, kinds * CAP, count)
    weighted = jnp.where(chosen, match_weight[:, :, None, :], 0.0).reshape(
        n_seq, kinds * CAP, count
    )
    slot_weight = jnp.sum(weighted, axis=2, keepdims=True)
    weighted_high = weighted.astype(BF)
    weighted_low = (weighted - weighted_high.astype(F32)).astype(BF)

    def give(rows):
        return lax.all_to_all(rows, "exp", split_axis=0, concat_axis=0, tiled=True)

    grad_rows = jnp.concatenate(grad_blocks, axis=0)
    send_cots = dispatch(select, grad_rows, slot_weight, pieces)
    received_grad = [give(rows) for rows in send_cots]
    send_rows = dispatch(select, normed_two, None, pieces)
    received = [give(rows) for rows in send_rows]

    slot_rows = n_exp * n_seq * CAP
    pairs = []
    results_back, grads_back, kept = [], [], []
    for i in range(pieces):
        rows = received[i].reshape(slot_rows, width)
        cots = received_grad[i].reshape(slot_rows, width)
        expert_result, input_grad, *saved = expert(
            rows, cots, expert_gate, expert_up, expert_down, i
        )
        grads_back.append(give(input_grad.reshape(n_exp, n_seq * CAP, width)))
        results_back.append(expert_result.reshape(n_exp, n_seq * CAP, width))
        kept.append((rows, cots, *saved))
    last = input_grad
    results_back = [give(after(rows, grads_back[-1])) for rows in results_back]
    expert_grads = None
    for i in range(pieces):
        expert_grads = expert_weights(after(kept[i][0], last), *kept[i][1:], i, pieces, expert_grads)
    expert_gate_grad, expert_up_grad, expert_down_grad = expert_grads

    shared_rows = after(normed_two, *send_rows)
    shared_gate_raw = dot(shared_rows, gate_cols)
    shared_up_raw = dot(shared_rows, lift_cols)
    shared_hidden = (jax.nn.silu(shared_gate_raw) * shared_up_raw).astype(BF)
    shared_hidden_grad = dot_t(grad_rows, drop_rows)
    sgate_grad = (shared_hidden_grad * shared_up_raw * silu_slope(shared_gate_raw)).astype(BF)
    sup_grad = (shared_hidden_grad * jax.nn.silu(shared_gate_raw)).astype(BF)
    two_products = [(sgate_grad, gate_cols, True), (sup_grad, lift_cols, True)]
    two_odd = combine(chips, [select], grads_back, two_products, BF)
    two_even = combine(0, [select], grads_back, two_products, F32)
    two_grad = along.scatter(two_even, two_odd)
    shared_grad_stack = jnp.stack(
        [
            t_dot(shared_rows, sgate_grad).reshape(n_exp, width // n_exp, -1),
            t_dot(shared_rows, sup_grad).reshape(n_exp, width // n_exp, -1),
        ],
        axis=1,
    )

    residual_norm_grad, second_terms = norm_back(
        two_grad, residual, inverse_two, gain_second
    )
    residual_grad = out_grad.astype(F32) + residual_norm_grad
    residual_half = residual_grad.astype(BF)
    all_heads = dot_t(residual_half, output_full).astype(BF)
    wide = heads * DV
    pairs = [
        jnp.stack(
            [
                all_heads[:, k * wide : (k + 1) * wide],
                all_heads[:, (chips + k) * wide : (chips + k + 1) * wide],
            ]
        )
        for k in range(chips)
    ]
    pairs = [pairs[0]] + [along.send(pairs[k], 2 * k) for k in range(1, chips)]
    other_half = swap(jnp.stack([pair[1] for pair in pairs]), "seq", 1)
    attention_grad = jnp.concatenate(
        [jnp.stack([pair[0] for pair in pairs]), other_half], axis=0
    ).reshape(length, wide)
    half_all = along.group(residual_half)

    out_products = [(shared_hidden, drop_rows, False)]
    out_masks = [weighted_high, weighted_low]
    out_odd = combine(chips, out_masks, results_back, out_products, BF)
    out_even = combine(0, out_masks, results_back, out_products, F32)

    query_in_grad, kv_grad, latent_part, rope_part = attend_back(
        query_heads,
        key_heads,
        value_heads,
        result,
        attention_grad,
        logsum,
        row_position,
        column_position,
        cosine_wide,
        -sine_wide,
        up_cols,
        factor,
    )
    latent_part = jnp.concatenate([latent_part, rope_part], axis=1)
    latent_grad = along.scatter(latent_part[:half], latent_part[half:])
    (query_cols,) = arrange(
        index,
        query_parts,
        [(width, w_query.shape[1])],
        [
            (j, (everything,), 0, lambda ref, j=j: (span(ref[0] ^ j, block_rows), everything))
            for j in range(n_exp)
        ],
    )
    one_part = dot_t(query_in_grad, query_cols)
    one_grad = along.scatter(one_part[:half], one_part[half:])
    latent_raw_grad, latent_terms = norm_back(
        latent_grad[:, :R], latent_raw[:count], inverse_rms(latent_raw[:count]), latent_wide
    )
    down_rows = jnp.concatenate(
        [
            latent_raw_grad,
            rotate(latent_grad[:, R:], cosine_table[:count], -sine_table[:count]),
        ],
        axis=1,
    ).astype(BF)
    down_rows_all = jnp.concatenate(along.group(down_rows), axis=0)
    output = (residual + along.scatter(out_even, out_odd)).astype(BF)

    shared_out = across.sum_stack(shared_grad_stack)
    drop_out = across.sum_stack(columns_first(t_dot(shared_hidden, grad_rows), n_exp))
    output_out = across.sum_stack(
        columns_first(t_dot(result, jnp.concatenate(half_all, axis=0)), n_exp)
    )
    up_out = across.sum_stack(t_dot(latent_all, kv_grad).reshape(n_exp, R // n_exp, -1))
    query_out = across.sum_stack(
        t_dot(normed_one, query_in_grad).reshape(n_exp, width // n_exp, -1)
    )
    mine = lax.dynamic_slice_in_dim(
        normed_one.reshape(length, n_exp, n_seq * gain_rows), seq * gain_rows, gain_rows, 2
    ).reshape(length, n_exp * gain_rows)
    down_out = across.sum_stack(t_dot(mine, down_rows_all).reshape(n_exp, gain_rows, -1))

    down_back = dot_t(down_rows, down_full)
    token_wide = jnp.concatenate(token_blocks, axis=0).astype(F32)
    inverse_one = inverse_rms(token_wide)
    one_hat = token_wide * inverse_one
    first_sum = jnp.sum(one_part * one_hat, axis=0) + jnp.sum(down_back * one_hat[:count], axis=0)
    token_norm_grad, _ = norm_back(
        one_grad + down_back, token_wide[:count], inverse_one[:count], gain_first
    )
    tokens_grad = (residual_grad + token_norm_grad).astype(BF)
    small = scatter_small(
        jnp.concatenate(
            [
                first_sum.reshape(n_exp, n_seq, gain_rows),
                jnp.sum(second_terms, axis=0).reshape(n_exp, n_seq, gain_rows),
                jnp.sum(latent_terms, axis=0).reshape(n_exp, n_seq, latent_rows_local),
            ],
            axis=2,
        )
    )
    return (
        output,
        tokens_grad,
        small[:gain_rows],
        query_out,
        down_out,
        small[2 * gain_rows :],
        up_out,
        output_out,
        small[gain_rows : 2 * gain_rows],
        shared_out[0],
        shared_out[1],
        drop_out,
        expert_gate_grad,
        expert_up_grad,
        expert_down_grad,
    )


def solution(mesh):
    rows = P(("exp", "seq"), None)
    line = P(("exp", "seq"))
    grid = P("exp", "seq")
    turned = P("seq", "exp")
    part = P(("exp", "seq"), None, None)
    return jax.shard_map(
        shards,
        mesh=mesh,
        in_specs=(
            rows,
            rows,
            rows,
            line,
            grid,
            rows,
            line,
            grid,
            turned,
            line,
            grid,
            grid,
            turned,
            part,
            part,
            part,
            rows,
        ),
        out_specs=(
            rows,
            rows,
            line,
            grid,
            rows,
            line,
            grid,
            turned,
            line,
            grid,
            grid,
            turned,
            part,
            part,
            part,
        ),
        check_vma=False,
    )
```

time: 1200 us -> 966 us (0.81)
  local copies, waits for them, and re-layouts: 357 us -> 130 us
  Pallas kernels: 0 us -> 220 us
  matrix products: 236 us -> 60.6 us
  other arithmetic: 108 us -> 65.8 us
  waiting for transfers between devices: 293 us -> 257 us
  starting transfers between devices: 182 us -> 212 us
    pallas_call x0 -> x23, Pallas kernels: none -> 220 us  [the longest x2 55.3 us: expert(): pl.pallas_call(kernel, grid=(count // tile,), in_specs=[block(width), blo...]
    dynamic_update_slice x30 -> x0, local copies, waits for them, and re-layouts: 164 us -> none  [the longest x22 156 us: stack(): out = lax.dynamic_update_slice_in_dim(out, block[None], me ^ j, 0)]
    dot_general x17 -> x2, matrix products: 79.9 us -> 9.33 us  [dot(): return jnp.dot(a, b, preferred_element_type=F32)]
    dot_general x17 -> x4, matrix products: 77.3 us -> 26.8 us  [dot_t(): lax.dot_general(a, b, (((1,), (1,)), ((), ())), preferred_element_type=F32)]
    dot_general x17 -> x7, matrix products: 69.3 us -> 24.3 us  [t_dot(): lax.dot_general(a, b, (((0,), (0,)), ((), ())), preferred_element_type=F32)]
    another operation x10 -> x5, other arithmetic: 42.1 us -> 3.44 us  [the longest x1 15.4 us: shards(): expert_down_grad = jnp.stack(down_grads)]
    unnamed x415 -> x256, local copies, waits for them, and re-layouts: 91 us -> 59.7 us
    ppermute x116 -> x122, starting transfers between devices: 146 us -> 177 us  [swap(): return lax.ppermute(x, axis, [(i, i ^ mask) for i in range(n)])]
  transfers between devices with their start and end apart: 124 -> 130, of which waited for: 39 -> 33; matrix products, arithmetic and copies ran while one was open for 54% -> 25% of each run, Pallas kernels for 0% -> 23%
where the time goes in v2:
time: 966 us; the launch traced here: 947 us
  waiting for transfers between devices  257 us (27%)
  Pallas kernels  220 us (23%)
  starting transfers between devices  212 us (22%)
  local copies, waits for them, and re-layouts  130 us (13%)
  other arithmetic  65.8 us (7%)
  matrix products  60.6 us (6%)
    ppermute x122, waiting for transfers between devices, swap(): return lax.ppermute(x, axis, [(i, i ^ mask) for i in range(n)])  257 us
    ppermute x122, starting transfers between devices, swap(): return lax.ppermute(x, axis, [(i, i ^ mask) for i in range(n)])  177 us
    unnamed x256, local copies, waits for them, and re-layouts  59.7 us
    pallas_call x2, Pallas kernels, expert(): pl.pallas_call(kernel, grid=(count // tile,), in_specs=[block(width), blo...  55.3 us
    all_to_all x8, starting transfers between devices, give(): return lax.all_to_all(rows, 'exp', split_axis=0, concat_axis=0, tiled=True)  35.4 us
    pallas_call x2, Pallas kernels, expert_weights(): pl.pallas_call(kernel, grid=(width // tile,), in_specs=[column, column] +...  29.8 us
    pallas_call x4, Pallas kernels, combine(): pl.pallas_call(kernel, grid=(half,), in_specs=[pl.BlockSpec((1, slots, co...  29.2 us
    dot_general x4, matrix products, dot_t(): lax.dot_general(a, b, (((1,), (1,)), ((), ())), preferred_element_type=F32)  26.8 us
  transfers between devices with their start and end apart: 130, of which 33 were waited for; matrix products, arithmetic and copies ran while one was open for 25% of the time, Pallas kernels for 23%

profile of v2, /device:TPU:0, one launch (start us, length us, event | category | flops | bytes accessed | tf_op | source)
XLA Modules:
  0.0 946.9 jit_solution(984419109154556175)
XLA Ops:
  33.9 10.6 %collective-permute-done.1.a_ref.refs_9_ = bf16[128,2048]{1,0:T(8,128)(2,1)} collective-permute-done((bf16[128,2048]{1,0:T(8,128)(2,1)S(1)}, bf16[128,2048]{1,0:T(8,128)(2,1)}, u32[]{:S(2)}, u32[]{:S(2)}) %collective-permute-start.1) | collective-permute-done | bytes 524320 | tf_op jit(solution)/shard_map/ppermute | solution.py:594
  46.9 16.9 %collective-permute-done.5.a_ref.refs_10_ = bf16[128,2048]{1,0:T(8,128)(2,1)} collective-permute-done((bf16[128,2048]{1,0:T(8,128)(2,1)S(1)}, bf16[128,2048]{1,0:T(8,128)(2,1)}, u32[]{:S(2)}, u32[]{:S(2)}) %collective-permute-start.5) | collective-permute-done | bytes 524320 | tf_op jit(solution)/shard_map/ppermute | solution.py:594
  120.3 17.3 %collective-permute-done.24.refs_3_ = bf16[128,512]{1,0:T(8,128)(2,1)S(1)} collective-permute-done((bf16[128,512]{1,0:T(8,128)(2,1)}, bf16[128,512]{1,0:T(8,128)(2,1)S(1)}, u32[]{:S(2)}, u32[]{:S(2)}) %collective-permute-start.24) | collective-permute-done | bytes 131104 | tf_op jit(solution)/shard_map/ppermute | solution.py:594
  159.2 27.0 %collective-permute-done.44 = bf16[128,2048]{1,0:T(8,128)(2,1)S(1)} collective-permute-done((bf16[128,2048]{1,0:T(8,128)(2,1)S(1)}, bf16[128,2048]{1,0:T(8,128)(2,1)S(1)}, u32[]{:S(2)}, u32[]{:S(2)}) %collective-permute-start.44) | collective-permute-done | bytes 524320 | tf_op jit(solution)/shard_map/ppermute | solution.py:594
  217.2 12.6 %collective-permute-done.27.refs_3_ = bf16[352,512]{1,0:T(8,128)(2,1)S(1)} collective-permute-done((bf16[352,512]{1,0:T(8,128)(2,1)}, bf16[352,512]{1,0:T(8,128)(2,1)S(1)}, u32[]{:S(2)}, u32[]{:S(2)}) %collective-permute-start.27) | collective-permute-done | bytes 360480 | tf_op jit(solution)/shard_map/ppermute | solution.py:594
  244.2 8.4 attend.1
  254.9 9.9 %collective-permute-start.43 = (bf16[1024,256]{1,0:T(8,128)(2,1)}, bf16[1024,256]{1,0:T(8,128)(2,1)}, u32[]{:S(2)}, u32[]{:S(2)}) collective-permute-start(bf16[1024,256]{1,0:T(8,128)(2,1)} %get-tuple-element.200.refs_0_.o_ref), channel_id=1, source_target_pairs={{0,2},{1,3},{2,0},{3,1},{4,6},{5,7},{6,4},{7,5},{8,10},{9,11},{10,... | collective-permute-start | bytes 1572872 | tf_op jit(solution)/shard_map/ppermute | solution.py:594
  287.3 30.7 %collective-permute-done.45.refs_2_ = bf16[1024,256]{1,0:T(8,128)(2,1)} collective-permute-done((bf16[1024,256]{1,0:T(8,128)(2,1)}, bf16[1024,256]{1,0:T(8,128)(2,1)}, u32[]{:S(2)}, u32[]{:S(2)}) %collective-permute-start.45) | collective-permute-done | bytes 524320 | tf_op jit(solution)/shard_map/ppermute | solution.py:594
  352.8 20.1 %add_norm.1 = (bf16[1024,2048]{1,0:T(8,128)(2,1)}, f32[128,2048]{1,0:T(8,128)}) custom-call(bf16[2048,2048]{1,0:T(8,128)(2,1)} %arrange.6.w_ref, f32[1,2048]{1,0:T(1,128)} %reshape.315.g_ref, bf16[1024,256]{1,0:T(8,128)(2,1)} %get-tuple-element.200.refs_0_.o_ref, bf16[1024,256]{1,0:T(8,128)(2,1)} %collective-permute-done.43.refs_1_, ...), custom_call_target="tpu_custom_call" | custom-call | flops 8589934592 | bytes 20971520 | tf_op jit(solution)/shard_map/add_norm/pallas_call | solution.py:360
  426.2 27.6 %expert.3 = (bf16[512,2048]{1,0:T(8,128)(2,1)}, bf16[512,2048]{1,0:T(8,128)(2,1)}, bf16[512,1408]{1,0:T(8,128)(2,1)}, bf16[512,1408]{1,0:T(8,128)(2,1)}, bf16[512,1408]{1,0:T(8,128)(2,1)}) custom-call(bf16[512,2048]{1,0:T(8,128)(2,1)} %bitcast.38.x_ref, bf16[512,2048]{1,0:T(8,128)(2,1)} %bitcast.253, bf16[2,2048,1408]{2,1,0:T(8,128)(2,1)} %gate_hbm.3, ...), custom_call_target="tpu_custom_call" | custom-call | flops 17716740096 | bytes 30015488 | tf_op jit(solution)/shard_map/expert/pallas_call | solution.py:451
  459.3 27.7 %expert.2 = (bf16[512,2048]{1,0:T(8,128)(2,1)}, bf16[512,2048]{1,0:T(8,128)(2,1)}, bf16[512,1408]{1,0:T(8,128)(2,1)}, bf16[512,1408]{1,0:T(8,128)(2,1)}, bf16[512,1408]{1,0:T(8,128)(2,1)}) custom-call(bf16[512,2048]{1,0:T(8,128)(2,1)} %bitcast.258, bf16[512,2048]{1,0:T(8,128)(2,1)} %bitcast.36.c_ref, bf16[2,2048,1408]{2,1,0:T(8,128)(2,1)} %gate_hbm.3, ...), custom_call_target="tpu_custom_call" | custom-call | flops 17716740096 | bytes 30015488 | tf_op jit(solution)/shard_map/expert/pallas_call | solution.py:451
  518.6 12.8 %collective-permute-done.100 = bf16[2,512,352]{1,2,0:T(8,128)(2,1)} collective-permute-done((bf16[2,512,352]{1,2,0:T(8,128)(2,1)}, bf16[2,512,352]{1,2,0:T(8,128)(2,1)}, u32[]{:S(2)}, u32[]{:S(2)}) %collective-permute-start.100) | collective-permute-done | bytes 720928 | tf_op jit(solution)/shard_map/ppermute | solution.py:594
  563.8 14.9 %expert_weights.2 = (f32[2,2048,1408]{2,1,0:T(8,128)}, f32[2,2048,1408]{2,1,0:T(8,128)}, f32[2,1408,2048]{2,1,0:T(8,128)}) custom-call(bf16[512,2048]{1,0:T(8,128)(2,1)} %bitcast.259, bf16[512,2048]{1,0:T(8,128)(2,1)} %bitcast.36.c_ref, bf16[512,1408]{1,0:T(8,128)(2,1)} %get-tuple-element.268.h_ref, bf16[512,1408]{1,0:T(8,128)(2,1)} %get-tuple-element.269.gg_ref, ...), custom_call_target="tpu_custom_call" | custom-call | flops 8858370048 | bytes 38797312 | tf_op jit(solution)/shard_map/expert_weights/pallas_call | solution.py:490
  578.7 8.7 combine.6
  591.4 11.9 %collective-permute-start.63 = (bf16[128,2048]{1,0:T(8,128)(2,1)}, bf16[128,2048]{1,0:T(8,128)(2,1)}, u32[]{:S(2)}, u32[]{:S(2)}) collective-permute-start(bf16[128,2048]{1,0:T(8,128)(2,1)} %get-tuple-element.218), channel_id=1, source_target_pairs={{0,4},{1,5},{2,6},{3,7},{4,0},{5,1},{6,2},{7,3},{8,12},{9,13},{10,... | collective-permute-start | bytes 1572872 | tf_op jit(solution)/shard_map/ppermute | solution.py:594
  605.4 14.9 %expert_weights.3 = (f32[2,2048,1408]{2,1,0:T(8,128)}, f32[2,2048,1408]{2,1,0:T(8,128)}, f32[2,1408,2048]{2,1,0:T(8,128)}) custom-call(bf16[512,2048]{1,0:T(8,128)(2,1)} %bitcast.38.x_ref, bf16[512,2048]{1,0:T(8,128)(2,1)} %bitcast.254, bf16[512,1408]{1,0:T(8,128)(2,1)} %get-tuple-element.264.h_ref, ...), custom_call_target="tpu_custom_call", output_to_operand_aliasing={{0}: (5, {}), {1}: (6, {}), {2}: (7, {})} | custom-call | flops 8858370048 | bytes 38797312 | tf_op jit(solution)/shard_map/expert_weights/pallas_call | solution.py:490
  623.9 15.1 %collective-permute-done.63 = bf16[128,2048]{1,0:T(8,128)(2,1)} collective-permute-done((bf16[128,2048]{1,0:T(8,128)(2,1)}, bf16[128,2048]{1,0:T(8,128)(2,1)}, u32[]{:S(2)}, u32[]{:S(2)}) %collective-permute-start.63) | collective-permute-done | bytes 524320 | tf_op jit(solution)/shard_map/ppermute | solution.py:594
  659.2 9.7 %collective-permute-start.66 = (bf16[2,128,256]{2,1,0:T(8,128)(2,1)S(1)}, bf16[2,128,256]{2,1,0:T(8,128)(2,1)S(1)}, u32[]{:S(2)}, u32[]{:S(2)}) collective-permute-start(bf16[2,128,256]{2,1,0:T(8,128)(2,1)S(1)} %get-tuple-element.221), channel_id=1, source_target_pairs={{0,4},{1,5},{2,6},{3,7},{4,0},{5,1},{6,2},{7,3},{8,12},{9,13},{10,... | collective-permute-start | bytes 393224 | tf_op jit(solution)/shard_map/ppermute | solution.py:594
  692.3 10.6 %collective-permute-start.70 = (bf16[128,2048]{1,0:T(8,128)(2,1)S(1)}, bf16[128,2048]{1,0:T(8,128)(2,1)}, u32[]{:S(2)}, u32[]{:S(2)}) collective-permute-start(bf16[128,2048]{1,0:T(8,128)(2,1)S(1)} %copy-done.48), channel_id=1, source_target_pairs={{0,2},{1,3},{2,0},{3,1},{4,6},{5,7},{6,4},{7,5},{8,10},{9,11},{10,... | collective-permute-start | bytes 1572872 | tf_op jit(solution)/shard_map/ppermute | solution.py:594
  706.1 13.9 %attend_back.1 = (bf16[1024,384]{1,0:T(8,128)(2,1)}, bf16[1024,512]{1,0:T(8,128)(2,1)}, f32[1024,512]{1,0:T(8,128)}, f32[1024,64]{1,0:T(8,128)}) custom-call(bf16[2,1024,256]{2,1,0:T(8,128)(2,1)} %get-tuple-element.191.q_ref, bf16[2,1024,256]{2,1,0:T(8,128)(2,1)} %get-tuple-element.192.k_ref, bf16[2,1024,128]{2,1,0:T(8,128)(2,1)} %get-tuple-element.193.v_ref, ...), custom_call_target="tpu_custom_call" | custom-call | flops 4294967296 | bytes 10485760 | tf_op jit(solution)/shard_map/attend_back/pallas_call | solution.py:282
  804.5 9.7 %collective-permute-done.112 = bf16[128,512]{1,0:T(8,128)(2,1)} collective-permute-done((bf16[128,512]{1,0:T(8,128)(2,1)}, bf16[128,512]{1,0:T(8,128)(2,1)}, u32[]{:S(2)}, u32[]{:S(2)}) %collective-permute-start.112) | collective-permute-done | bytes 131104 | tf_op jit(solution)/shard_map/ppermute | solution.py:594
  835.4 20.7 %collective-permute-done.80 = bf16[128,2048]{1,0:T(8,128)(2,1)S(1)} collective-permute-done((bf16[128,2048]{1,0:T(8,128)(2,1)S(1)}, bf16[128,2048]{1,0:T(8,128)(2,1)S(1)}, u32[]{:S(2)}, u32[]{:S(2)}) %collective-permute-start.80) | collective-permute-done | bytes 524320 | tf_op jit(solution)/shard_map/ppermute | solution.py:594
  866.8 18.5 %collective-permute-start.78 = (bf16[128,576]{1,0:T(8,128)(2,1)S(1)}, bf16[128,576]{1,0:T(8,128)(2,1)S(1)}, u32[]{:S(2)}, u32[]{:S(2)}) collective-permute-start(bf16[128,576]{1,0:T(8,128)(2,1)S(1)} %get-tuple-element.234), channel_id=1, source_target_pairs={{0,2},{1,3},{2,0},{3,1},{4,6},{5,7},{6,4},{7,5},{8,10},{9,11},{10,... | collective-permute-start | bytes 442376 | tf_op jit(solution)/shard_map/ppermute | solution.py:594
  917.9 24.1 %collective-permute-done.82 = bf16[128,2048]{1,0:T(8,128)(2,1)S(1)} collective-permute-done((bf16[128,2048]{1,0:T(8,128)(2,1)S(1)}, bf16[128,2048]{1,0:T(8,128)(2,1)S(1)}, u32[]{:S(2)}, u32[]{:S(2)}) %collective-permute-start.82) | collective-permute-done | bytes 524320 | tf_op jit(solution)/shard_map/ppermute | solution.py:594
  (654 shorter events, 550.1 us)
Async XLA Ops:
  33.4 56.0 %collective-permute-start.52 = (f32[12,128]{1,0:T(8,128)}, f32[12,128]{1,0:T(8,128)S(1)}, u32[]{:S(2)}, u32[]{:S(2)}) collective-permute-start(f32[12,128]{1,0:T(8,128)} %pad_maximum_fusion.11), channel_id=1, source_target_pairs={{0,1},{1,0},{2,3},{3,2},{4,5},{5,4},{6,7},{7,6},{8,9},{9,8},{10,11... | collective-permute-start | bytes 18440 | tf_op jit(solution)/shard_map/ppermute | solution.py:594
  44.5 53.3 %collective-permute-start.21 = (bf16[512,384]{1,0:T(8,128)(2,1)S(1)}, bf16[512,384]{1,0:T(8,128)(2,1)S(1)}, u32[]{:S(2)}, u32[]{:S(2)}) collective-permute-start(bf16[512,384]{1,0:T(8,128)(2,1)S(1)} %copy-done.10), channel_id=1, source_target_pairs={{0,24},{8,16},{16,8},{24,0},{1,25},{9,17},{17,9},{25,1},{2,26},{10... | collective-permute-start | bytes 1179656 | tf_op jit(solution)/shard_map/ppermute | solution.py:594
  79.2 41.1 %collective-permute-start.3 = (bf16[256,512]{1,0:T(8,128)(2,1)}, bf16[256,512]{1,0:T(8,128)(2,1)S(1)}, u32[]{:S(2)}, u32[]{:S(2)}) collective-permute-start(bf16[256,512]{1,0:T(8,128)(2,1)} %param.25), channel_id=1, source_target_pairs={{0,2},{1,3},{2,0},{3,1},{4,6},{5,7},{6,4},{7,5},{8,10},{9,11},{10,... | collective-permute-start | bytes 786440 | tf_op jit(solution)/shard_map/ppermute | solution.py:594
  81.6 64.3 %collective-permute-start.7 = (bf16[256,512]{1,0:T(8,128)(2,1)}, bf16[256,512]{1,0:T(8,128)(2,1)}, u32[]{:S(2)}, u32[]{:S(2)}) collective-permute-start(bf16[256,512]{1,0:T(8,128)(2,1)} %param.25), channel_id=1, source_target_pairs={{0,4},{1,5},{2,6},{3,7},{4,0},{5,1},{6,2},{7,3},{8,12},{9,13},{10,... | collective-permute-start | bytes 786440 | tf_op jit(solution)/shard_map/ppermute | solution.py:594
  99.9 50.7 %collective-permute-start.11 = (bf16[256,512]{1,0:T(8,128)(2,1)}, bf16[256,512]{1,0:T(8,128)(2,1)}, u32[]{:S(2)}, u32[]{:S(2)}) collective-permute-start(bf16[256,512]{1,0:T(8,128)(2,1)} %param.25), channel_id=1, source_target_pairs={{0,6},{1,7},{2,4},{3,5},{4,2},{5,3},{6,0},{7,1},{8,14},{9,15},{10,... | collective-permute-start | bytes 786440 | tf_op jit(solution)/shard_map/ppermute | solution.py:594
  189.6 63.0 %collective-permute-start.19 = (bf16[1024,512]{1,0:T(8,128)(2,1)}, bf16[1024,512]{1,0:T(8,128)(2,1)}, u32[]{:S(2)}, u32[]{:S(2)}) collective-permute-start(bf16[1024,512]{1,0:T(8,128)(2,1)} %copy-done.50), channel_id=1, source_target_pairs={{0,8},{8,0},{16,24},{24,16},{1,9},{9,1},{17,25},{25,17},{2,10},{10... | collective-permute-start | bytes 3145736 | tf_op jit(solution)/shard_map/ppermute | solution.py:594
  193.9 43.2 %collective-permute-start.38 = (bf16[128,2048]{1,0:T(8,128)(2,1)S(1)}, bf16[128,2048]{1,0:T(8,128)(2,1)S(1)}, u32[]{:S(2)}, u32[]{:S(2)}) collective-permute-start(bf16[128,2048]{1,0:T(8,128)(2,1)S(1)} %copy-done.36), channel_id=1, source_target_pairs={{0,1},{1,0},{2,3},{3,2},{4,5},{5,4},{6,7},{7,6},{8,9},{9,8},{10,11... | collective-permute-start | bytes 1572872 | tf_op jit(solution)/shard_map/ppermute | solution.py:594
  204.3 48.8 %collective-permute-start.57 = (bf16[128,2048]{1,0:T(8,128)(2,1)}, bf16[128,2048]{1,0:T(8,128)(2,1)S(1)}, u32[]{:S(2)}, u32[]{:S(2)}) collective-permute-start(bf16[128,2048]{1,0:T(8,128)(2,1)} %collective-permute-done.42), channel_id=1, source_target_pairs={{0,1},{1,0},{2,3},{3,2},{4,5},{5,4},{6,7},{7,6},{8,9},{9,8},{10,11... | collective-permute-start | bytes 1572872 | tf_op jit(solution)/shard_map/ppermute | solution.py:594
  229.9 48.7 %collective-permute-start.28 = (bf16[1024,512]{1,0:T(8,128)(2,1)S(1)}, bf16[1024,512]{1,0:T(8,128)(2,1)}, u32[]{:S(2)}, u32[]{:S(2)}) collective-permute-start(bf16[1024,512]{1,0:T(8,128)(2,1)S(1)} %copy-done.51), channel_id=1, source_target_pairs={{0,16},{8,24},{16,0},{24,8},{1,17},{9,25},{17,1},{25,9},{2,18},{10... | collective-permute-start | bytes 3145736 | tf_op jit(solution)/shard_map/ppermute | solution.py:594
  274.0 74.4 %all-to-all-start.1 = ((bf16[4,128,2048]{2,1,0:T(8,128)(2,1)}), bf16[4,128,2048]{2,1,0:T(8,128)(2,1)}, u32[]{:S(2)}, u32[]{:S(2)}) async-start(bf16[4,128,2048]{2,1,0:T(8,128)(2,1)} %get-tuple-element.204), calls=%async_computation.1 | async-start | bytes 4194304 | tf_op jit(solution)/shard_map/all_to_all | solution.py:873
  283.2 56.8 %collective-permute-start.33 = (bf16[1024,512]{1,0:T(8,128)(2,1)}, bf16[1024,512]{1,0:T(8,128)(2,1)S(1)}, u32[]{:S(2)}, u32[]{:S(2)}) collective-permute-start(bf16[1024,512]{1,0:T(8,128)(2,1)} %collective-permute-done.29.refs_3_), channel_id=1, source_target_pairs={{0,1},{1,0},{2,3},{3,2},{4,5},{5,4},{6,7},{7,6},{8,9},{9,8},{10,11... | collective-permute-start | bytes 3145736 | tf_op jit(solution)/shard_map/ppermute | solution.py:594
  348.4 41.6 %all-to-all-start.3 = ((bf16[4,128,2048]{2,1,0:T(8,128)(2,1)}), bf16[4,128,2048]{2,1,0:T(8,128)(2,1)S(1)}, u32[]{:S(2)}, u32[]{:S(2)}) async-start(bf16[4,128,2048]{2,1,0:T(8,128)(2,1)} %get-tuple-element.207), calls=%async_computation.3 | async-start | bytes 4194304 | tf_op jit(solution)/shard_map/all_to_all | solution.py:873
  487.0 45.8 %all-to-all-start.7 = ((bf16[4,128,2048]{2,1,0:T(8,128)(2,1)}), bf16[4,128,2048]{2,1,0:T(8,128)(2,1)}, u32[]{:S(2)}, u32[]{:S(2)}) async-start(bf16[4,128,2048]{2,1,0:T(8,128)(2,1)} %bitcast.260), calls=%async_computation.7 | async-start | bytes 4194304 | tf_op jit(solution)/shard_map/all_to_all | solution.py:873
  540.8 46.5 %collective-permute-start.61 = (bf16[512,2048]{1,0:T(8,128)(2,1)}, bf16[512,2048]{1,0:T(8,128)(2,1)S(1)}, u32[]{:S(2)}, u32[]{:S(2)}) collective-permute-start(bf16[512,2048]{1,0:T(8,128)(2,1)} %combine.7), channel_id=1, source_target_pairs={{0,1},{1,0},{2,3},{3,2},{4,5},{5,4},{6,7},{7,6},{8,9},{9,8},{10,11... | collective-permute-start | bytes 6291464 | tf_op jit(solution)/shard_map/ppermute | solution.py:594
  557.5 119.6 %collective-permute-start.109 = (bf16[352,512]{1,0:T(8,128)(2,1)}, bf16[352,512]{1,0:T(8,128)(2,1)}, u32[]{:S(2)}, u32[]{:S(2)}) collective-permute-start(bf16[352,512]{1,0:T(8,128)(2,1)} %bitcast.248), channel_id=1, source_target_pairs={{0,24},{8,16},{16,8},{24,0},{1,25},{9,17},{17,9},{25,1},{2,26},{10... | collective-permute-start | bytes 1081352 | tf_op jit(solution)/shard_map/ppermute | solution.py:594
  559.0 118.1 %collective-permute-start.102 = (bf16[352,512]{1,0:T(8,128)(2,1)}, bf16[352,512]{1,0:T(8,128)(2,1)}, u32[]{:S(2)}, u32[]{:S(2)}) collective-permute-start(bf16[352,512]{1,0:T(8,128)(2,1)} %bitcast.247), channel_id=1, source_target_pairs={{0,16},{8,24},{16,0},{24,8},{1,17},{9,25},{17,1},{25,9},{2,18},{10... | collective-permute-start | bytes 1081352 | tf_op jit(solution)/shard_map/ppermute | solution.py:594
  591.4 47.6 %collective-permute-start.63 = (bf16[128,2048]{1,0:T(8,128)(2,1)}, bf16[128,2048]{1,0:T(8,128)(2,1)}, u32[]{:S(2)}, u32[]{:S(2)}) collective-permute-start(bf16[128,2048]{1,0:T(8,128)(2,1)} %get-tuple-element.218), channel_id=1, source_target_pairs={{0,4},{1,5},{2,6},{3,7},{4,0},{5,1},{6,2},{7,3},{8,12},{9,13},{10,... | collective-permute-start | bytes 1572872 | tf_op jit(solution)/shard_map/ppermute | solution.py:594
  685.3 89.0 %collective-permute-start.60 = (bf16[512,2048]{1,0:T(8,128)(2,1)}, bf16[512,2048]{1,0:T(8,128)(2,1)}, u32[]{:S(2)}, u32[]{:S(2)}) collective-permute-start(bf16[512,2048]{1,0:T(8,128)(2,1)} %combine.5), channel_id=1, source_target_pairs={{0,1},{1,0},{2,3},{3,2},{4,5},{5,4},{6,7},{7,6},{8,9},{9,8},{10,11... | collective-permute-start | bytes 6291464 | tf_op jit(solution)/shard_map/ppermute | solution.py:594
  691.9 54.9 %collective-permute-start.96 = (bf16[128,2048]{1,0:T(8,128)(2,1)S(1)}, bf16[128,2048]{1,0:T(8,128)(2,1)}, u32[]{:S(2)}, u32[]{:S(2)}) collective-permute-start(bf16[128,2048]{1,0:T(8,128)(2,1)S(1)} %copy-done.48), channel_id=1, source_target_pairs={{0,1},{1,0},{2,3},{3,2},{4,5},{5,4},{6,7},{7,6},{8,9},{9,8},{10,11... | collective-permute-start | bytes 1572872 | tf_op jit(solution)/shard_map/ppermute | solution.py:594
  692.3 49.3 %collective-permute-start.70 = (bf16[128,2048]{1,0:T(8,128)(2,1)S(1)}, bf16[128,2048]{1,0:T(8,128)(2,1)}, u32[]{:S(2)}, u32[]{:S(2)}) collective-permute-start(bf16[128,2048]{1,0:T(8,128)(2,1)S(1)} %copy-done.48), channel_id=1, source_target_pairs={{0,2},{1,3},{2,0},{3,1},{4,6},{5,7},{6,4},{7,5},{8,10},{9,11},{10,... | collective-permute-start | bytes 1572872 | tf_op jit(solution)/shard_map/ppermute | solution.py:594
  702.9 40.6 %collective-permute-start.72 = (bf16[128,2048]{1,0:T(8,128)(2,1)S(1)}, bf16[128,2048]{1,0:T(8,128)(2,1)}, u32[]{:S(2)}, u32[]{:S(2)}) collective-permute-start(bf16[128,2048]{1,0:T(8,128)(2,1)S(1)} %copy-done.48), channel_id=1, source_target_pairs={{0,4},{1,5},{2,6},{3,7},{4,0},{5,1},{6,2},{7,3},{8,12},{9,13},{10,... | collective-permute-start | bytes 1572872 | tf_op jit(solution)/shard_map/ppermute | solution.py:594
  703.5 42.4 %collective-permute-start.74 = (bf16[128,2048]{1,0:T(8,128)(2,1)S(1)}, bf16[128,2048]{1,0:T(8,128)(2,1)S(1)}, u32[]{:S(2)}, u32[]{:S(2)}) collective-permute-start(bf16[128,2048]{1,0:T(8,128)(2,1)S(1)} %copy-done.48), channel_id=1, source_target_pairs={{0,6},{1,7},{2,4},{3,5},{4,2},{5,3},{6,0},{7,1},{8,14},{9,15},{10,... | collective-permute-start | bytes 1572872 | tf_op jit(solution)/shard_map/ppermute | solution.py:594
  743.6 72.7 %collective-permute-start.76 = (bf16[512,2048]{1,0:T(8,128)(2,1)}, bf16[512,2048]{1,0:T(8,128)(2,1)}, u32[]{:S(2)}, u32[]{:S(2)}) collective-permute-start(bf16[512,2048]{1,0:T(8,128)(2,1)} %slice.488), channel_id=1, source_target_pairs={{0,1},{1,0},{2,3},{3,2},{4,5},{5,4},{6,7},{7,6},{8,9},{9,8},{10,11... | collective-permute-start | bytes 6291464 | tf_op jit(solution)/shard_map/ppermute | solution.py:594
  833.0 60.9 %collective-permute-start.115 = (bf16[128,576]{1,0:T(8,128)(2,1)S(1)}, bf16[128,576]{1,0:T(8,128)(2,1)S(1)}, u32[]{:S(2)}, u32[]{:S(2)}) collective-permute-start(bf16[128,576]{1,0:T(8,128)(2,1)S(1)} %get-tuple-element.234), channel_id=1, source_target_pairs={{0,1},{1,0},{2,3},{3,2},{4,5},{5,4},{6,7},{7,6},{8,9},{9,8},{10,11... | collective-permute-start | bytes 442376 | tf_op jit(solution)/shard_map/ppermute | solution.py:594
  (209 other events, 3915.5 us)

commit v3 on v2

--- a/solution.py
+++ b/solution.py
@@ -108,19 +108,27 @@
     return v * cosine + jnp.concatenate([v[:, middle:], v[:, :middle]], axis=1) * sine
 
 
-def project(index, chip, pair, gain, w_query, w_down, latent_gain, w_up, cosine, sine, heads, length, earlier):
-    count, width = pair[0].shape
+def project(index, token_blocks, gain, w_first, w_down, latent_gain, w_up, cosine, sine, heads):
+    count, width = token_blocks[0].shape
+    chips = len(token_blocks) // 2
+    half = chips * count
     wide = DN + DR
-    many = len(w_query)
-    kept = list(earlier or ())
-    query_rows = w_query[0].shape[0]
-
-    def kernel(index_ref, a_ref, b_ref, g_ref, wd_ref, lg_ref, *refs):
-        wq_refs = refs[:many]
-        wu_ref, c_ref, s_ref = refs[many : many + 3]
-        n_ref, l_ref, r_ref, q_ref, k_ref, v_ref = refs[many + 3 + len(kept) :]
+    many = len(w_first)
+    query_rows = w_first[0].shape[0]
+    columns = heads * wide
+
+    def kernel(index_ref, g_ref, wd_ref, lg_ref, wu_ref, c_ref, s_ref, *refs):
+        tokens, weights = refs[: 2 * chips], refs[2 * chips : 2 * chips + many]
+        n_ref, l_ref, r_ref, q_ref, k_ref, v_ref, x_ref = refs[2 * chips + many :]
         me = index_ref[0]
-        x = jnp.where(pl.program_id(0) == 0, a_ref[...], b_ref[...]).astype(F32)
+        for h in range(2):
+
+            @pl.when(pl.program_id(0) == h)
+            def _():
+                for k in range(chips):
+                    x_ref[k * count : (k + 1) * count] = tokens[h * chips + k][...]
+
+        x = x_ref[...].astype(F32)
         inverse = lax.rsqrt(jnp.mean(x * x, axis=1, keepdims=True) + eps_norm)
         n_ref[...] = (x * inverse * g_ref[...]).astype(BF)
         down = dot(n_ref[...], wd_ref[...])
@@ -130,10 +138,10 @@
         l_ref[...] = (raw * inverse * lg_ref[...]).astype(BF)
         query = 0.0
         for j in range(many):
-            query = query + dot(n_ref[:, span(me ^ j, query_rows)], wq_refs[j][...])
+            query = query + dot(n_ref[:, span(me ^ j, query_rows)], weights[j][:, :columns])
         up = dot(l_ref[...], wu_ref[...]).astype(BF)
         cosine, sine = c_ref[...], s_ref[...]
-        zeros = jnp.zeros((count, 256 - wide), BF)
+        zeros = jnp.zeros((half, 256 - wide), BF)
         rope = jnp.concatenate([turned(down[:, R : R + DR], cosine, sine).astype(BF), zeros], axis=1)
         for n in range(heads):
             own = query[:, n * wide : (n + 1) * wide]
@@ -145,30 +153,27 @@
             k_ref[n, :, DN:] = rope
             v_ref[n] = up[:, n * (DN + DV) + DN : (n + 1) * (DN + DV)]
 
-    chips = length // count // 2
-
     def rows(w):
-        return pl.BlockSpec((count, w), lambda i: (chip + i * chips, 0))
+        return pl.BlockSpec((half, w), lambda i: (i, 0))
 
     def head_rows(w):
-        return pl.BlockSpec((heads, count, w), lambda i: (0, chip + i * chips, 0))
-
-    columns = w_query[0].shape[1] + w_down.shape[1]
-    first = 6 + many + 3
+        return pl.BlockSpec((heads, half, w), lambda i: (0, i, 0))
+
+    length = 2 * half
     return pl.pallas_call(
         kernel,
         grid=(2,),
         in_specs=[
             SCALARS,
-            whole((count, width)),
-            whole((count, width)),
             whole((1, width)),
             whole(w_down.shape),
             whole((1, R)),
+            whole(w_up.shape),
+            rows(DR),
+            rows(DR),
         ]
-        + [whole(w.shape) for w in w_query]
-        + [whole(w_up.shape), rows(DR), rows(DR)]
-        + [ANY] * len(kept),
+        + [whole((count, width))] * (2 * chips)
+        + [whole(w.shape) for w in w_first],
         out_specs=[rows(width), rows(R), rows(R), head_rows(256), head_rows(256), head_rows(DV)],
         out_shape=[
             jax.ShapeDtypeStruct((length, width), BF),
@@ -178,15 +183,56 @@
             jax.ShapeDtypeStruct((heads, length, 256), BF),
             jax.ShapeDtypeStruct((heads, length, DV), BF),
         ],
-        input_output_aliases={first + n: n for n in range(len(kept))},
+        scratch_shapes=[pltpu.VMEM((half, width), BF)],
         compiler_params=pltpu.CompilerParams(vmem_limit_bytes=LIMIT),
         cost_estimate=pl.CostEstimate(
-            flops=4 * count * (width * columns + R * w_up.shape[1]),
+            flops=2 * length * (width * (columns + w_down.shape[1]) + R * w_up.shape[1]),
             transcendentals=0,
-            bytes_accessed=8 * count * width + 2 * width * columns,
+            bytes_accessed=4 * length * width + 2 * width * (columns + w_down.shape[1]),
         ),
         name="project",
-    )(index, *pair, gain, w_down, latent_gain, *w_query, w_up, cosine, sine, *kept)
+    )(index, gain, w_down, latent_gain, w_up, cosine, sine, *token_blocks, *w_first)
+
+
+def query_back(index, base, query_grad, w_first, normed, gain, dtype):
+    length, columns = query_grad.shape
+    half = length // 2
+    width = normed.shape[1]
+    many = len(w_first)
+    query_rows = w_first[0].shape[0]
+
+    def kernel(index_ref, q_ref, n_ref, g_ref, *refs):
+        weights, (o_ref, t_ref) = refs[:many], refs[many:]
+        me = index_ref[0]
+        for j in range(many):
+            where = span(me ^ j, query_rows)
+            part = dot_t(q_ref[...], weights[j][:, :columns])
+            o_ref[:, where] = part.astype(dtype)
+            t_ref[:, where] = jnp.sum(
+                part * n_ref[:, where].astype(F32), axis=0, keepdims=True
+            ) / g_ref[:, where]
+
+    return pl.pallas_call(
+        kernel,
+        grid=(1,),
+        in_specs=[
+            SCALARS,
+            pl.BlockSpec((half, columns), lambda i: (base, 0)),
+            pl.BlockSpec((half, width), lambda i: (base, 0)),
+            whole((1, width)),
+        ]
+        + [whole(w.shape) for w in w_first],
+        out_specs=[whole((half, width)), whole((1, width))],
+        out_shape=[
+            jax.ShapeDtypeStruct((half, width), dtype),
+            jax.ShapeDtypeStruct((1, width), F32),
+        ],
+        compiler_params=pltpu.CompilerParams(vmem_limit_bytes=LIMIT),
+        cost_estimate=pl.CostEstimate(
+            flops=2 * half * columns * width, transcendentals=0, bytes_accessed=8 * half * width
+        ),
+        name="query_back",
+    )(index, query_grad, normed, gain, *w_first)
 
 
 def attend(query, key, value, row_position, column_position, factor):
@@ -231,13 +277,13 @@
     )(query, key, value, row_position, column_position)
 
 
-def attend_back(query, key, value, result, result_grad, logsum, row_position, column_position, cosine, sine, w_up, factor):
+def attend_back(query, key, value, result, result_grad, logsum, row_position, column_position, cosine, sine, w_up, latent_all, latent_gain, factor):
     heads, length, _ = query.shape
     tile = 256
     steps = length // tile
     wide = DN + DR
 
-    def kernel(q_ref, k_ref, v_ref, o_ref, do_ref, ls_ref, row_ref, column_ref, c_ref, s_ref, wu_ref, dq_ref, kv_ref, lp_ref, rope_ref, dk_acc, dv_acc, kt):
+    def kernel(q_ref, k_ref, v_ref, o_ref, do_ref, ls_ref, row_ref, column_ref, c_ref, s_ref, wu_ref, l_ref, lg_ref, dq_ref, kv_ref, lp_ref, t_ref, dk_acc, dv_acc, kt):
         step = pl.program_id(0)
 
         @pl.when(step == 0)
@@ -276,8 +322,12 @@
                 kv_ref[:, base : base + DN] = key_grad[:, :DN]
                 kv_ref[:, base + DN : base + DN + DV] = value_grad
                 rope = rope + key_grad[:, DN:wide].astype(F32)
-            lp_ref[...] = dot_t(kv_ref[...], wu_ref[...])
-            rope_ref[...] = rope
+            latent = dot_t(kv_ref[...], wu_ref[...])
+            lp_ref[:, :R] = latent
+            lp_ref[:, R:] = rope
+            t_ref[...] = jnp.sum(
+                latent * l_ref[...].astype(F32), axis=0, keepdims=True
+            ) / lg_ref[...]
 
     return pl.pallas_call(
         kernel,
@@ -294,18 +344,20 @@
             pl.BlockSpec((tile, DR), lambda i: (i, 0)),
             pl.BlockSpec((tile, DR), lambda i: (i, 0)),
             whole(w_up.shape),
+            whole((length, R)),
+            whole((1, R)),
         ],
         out_specs=[
             pl.BlockSpec((tile, heads * wide), lambda i: (i, 0)),
             whole((length, heads * (DN + DV))),
-            whole((length, R)),
-            whole((length, DR)),
+            whole((length, R + DR)),
+            whole((1, R)),
         ],
         out_shape=[
             jax.ShapeDtypeStruct((length, heads * wide), BF),
             jax.ShapeDtypeStruct((length, heads * (DN + DV)), BF),
-            jax.ShapeDtypeStruct((length, R), F32),
-            jax.ShapeDtypeStruct((length, DR), F32),
+            jax.ShapeDtypeStruct((length, R + DR), F32),
+            jax.ShapeDtypeStruct((1, R), F32),
         ],
         scratch_shapes=[
             pltpu.VMEM((heads, length, 256), F32),
@@ -319,33 +371,35 @@
             bytes_accessed=8 * heads * length * 640,
         ),
         name="attend_back",
-    )(query, key, value, result, result_grad, logsum, row_position, column_position, cosine, sine, w_up)
-
-
-def add_norm(token_blocks, blocks, w_output, gain):
+    )(query, key, value, result, result_grad, logsum, row_position, column_position, cosine, sine, w_up, latent_all, latent_gain)
+
+
+def add_norm(token_blocks, blocks, w_even, w_odd, gain):
     count, width = token_blocks[0].shape
     many = len(blocks)
+    chips = many // 2
+    half = chips * count
     length = count * many
-    tile = 2 * count
     depth = blocks[0].shape[1]
 
-    def kernel(w_ref, g_ref, *refs):
+    def kernel(we_ref, wo_ref, g_ref, *refs):
         parts, tokens = refs[:many], refs[many : 2 * many]
-        n_ref, r_ref, x_ref = refs[2 * many :]
-        rows = []
+        n_ref, r_ref, x_ref, a_ref = refs[2 * many :]
         for q in range(many):
-            block = parts[q][...]
-            if q % 2:
-                block = jnp.concatenate([block[count:], block[:count]], axis=0)
-            rows.append(block)
-        total = dot(jnp.concatenate(rows, axis=1), w_ref[...])
-        for i in range(many // 2):
-
-            @pl.when(pl.program_id(0) == i)
+            for p in range(chips):
+                other = p ^ (q % chips)
+                a_ref[p * count : (p + 1) * count, q * depth : (q + 1) * depth] = parts[q][
+                    other * count : (other + 1) * count
+                ]
+        for h in range(2):
+
+            @pl.when(pl.program_id(0) == h)
             def _():
-                x_ref[:count] = tokens[2 * i][...]
-                x_ref[count:] = tokens[2 * i + 1][...]
-
+                for k in range(chips):
+                    x_ref[k * count : (k + 1) * count] = tokens[h * chips + k][...]
+
+        middle = chips * depth
+        total = dot(a_ref[:, :middle], we_ref[...]) + dot(a_ref[:, middle:], wo_ref[...])
         total = total + x_ref[...].astype(F32)
         inverse = lax.rsqrt(jnp.mean(total * total, axis=1, keepdims=True) + eps_norm)
         n_ref[...] = (total * inverse * g_ref[...]).astype(BF)
@@ -355,28 +409,28 @@
             r_ref[...] = total[:count]
 
     def source(q):
-        return pl.BlockSpec((tile, depth), lambda i: (i ^ (q >> 1), 0))
+        return pl.BlockSpec((half, depth), lambda i: (i ^ (q // chips), 0))
 
     return pl.pallas_call(
         kernel,
-        grid=(length // tile,),
-        in_specs=[whole(w_output.shape), whole((1, width))]
+        grid=(2,),
+        in_specs=[whole(w_even.shape), whole(w_odd.shape), whole((1, width))]
         + [source(q) for q in range(many)]
         + [whole((count, width))] * many,
-        out_specs=[pl.BlockSpec((tile, width), lambda i: (i, 0)), whole((count, width))],
+        out_specs=[pl.BlockSpec((half, width), lambda i: (i, 0)), whole((count, width))],
         out_shape=[
             jax.ShapeDtypeStruct((length, width), BF),
             jax.ShapeDtypeStruct((count, width), F32),
         ],
-        scratch_shapes=[pltpu.VMEM((tile, width), BF)],
+        scratch_shapes=[pltpu.VMEM((half, width), BF), pltpu.VMEM((half, many * depth), BF)],
         compiler_params=pltpu.CompilerParams(vmem_limit_bytes=LIMIT),
         cost_estimate=pl.CostEstimate(
-            flops=2 * length * width * w_output.shape[0],
+            flops=4 * length * width * w_even.shape[0],
             transcendentals=0,
-            bytes_accessed=6 * length * width + 2 * width * w_output.shape[0],
+            bytes_accessed=6 * length * width + 4 * width * w_even.shape[0],
         ),
         name="add_norm",
-    )(w_output, gain, *blocks, *token_blocks)
+    )(w_even, w_odd, gain, *blocks, *token_blocks)
 
 
 def expert(rows, cots, gate, up, down, piece):
@@ -545,6 +599,36 @@
     )(select, rows, *weights)
 
 
+def down_weights(normed, down_rows, sums, gain_rows):
+    count, columns = down_rows.shape
+    devices, extra, _ = sums.shape
+    per = 128 // gain_rows
+
+    def kernel(n_ref, d_ref, s_ref, o_ref):
+        part = t_dot(n_ref[...], d_ref[...]).astype(BF)
+        for i in range(per):
+            o_ref[i, :gain_rows] = part[i * gain_rows : (i + 1) * gain_rows]
+            o_ref[i, gain_rows:] = s_ref[i]
+
+    return pl.pallas_call(
+        kernel,
+        grid=(devices // per,),
+        in_specs=[
+            pl.BlockSpec((count, 128), lambda i: (0, i)),
+            whole((count, columns)),
+            pl.BlockSpec((per, extra, columns), lambda i: (i, 0, 0)),
+        ],
+        out_specs=pl.BlockSpec((per, gain_rows + extra, columns), lambda i: (i, 0, 0)),
+        out_shape=jax.ShapeDtypeStruct((devices, gain_rows + extra, columns), BF),
+        cost_estimate=pl.CostEstimate(
+            flops=2 * devices * gain_rows * count * columns,
+            transcendentals=0,
+            bytes_accessed=4 * devices * (gain_rows + extra) * columns,
+        ),
+        name="down_weights",
+    )(normed, down_rows, sums)
+
+
 def combine(base, masks, returned, products, dtype):
     half = masks[0].shape[0] // 2
     slots, count = masks[0].shape[1:]
@@ -552,32 +636,44 @@
     others, _, width = returned[0].shape
     many = len(masks)
 
+    tile = 512
+
     def kernel(*refs):
         mask_refs, row_refs = refs[:many], refs[many : many + pieces]
         rest, out_ref = refs[many + pieces : -1], refs[-1]
-        rows = jnp.concatenate([row_refs[i][j] for i in range(pieces) for j in range(others)], axis=0)
         total = 0.0
         for n, (_, _, flipped) in enumerate(products):
             total = total + (dot_t if flipped else dot)(rest[2 * n][...], rest[2 * n + 1][...])
-        for mask_ref in mask_refs:
-            total = total + t_dot(mask_ref[0], rows)
-        out_ref[...] = total.astype(dtype)
+        for b in range(half):
+            rows = jnp.concatenate(
+                [
+                    row_refs[i][j, b * CAP : (b + 1) * CAP]
+                    for i in range(pieces)
+                    for j in range(others)
+                ],
+                axis=0,
+            )
+            block = total[b * count : (b + 1) * count]
+            for mask_ref in mask_refs:
+                block = block + t_dot(mask_ref[b], rows)
+            out_ref[b * count : (b + 1) * count] = block.astype(dtype)
 
     factors = []
     specs = []
-    for left, right, _ in products:
+    for left, right, flipped in products:
         factors += [left, right]
-        specs += [
-            pl.BlockSpec((count, left.shape[1]), lambda b: (base + b, 0)),
-            whole(right.shape),
-        ]
+        specs.append(pl.BlockSpec((half * count, left.shape[1]), lambda t: (base, 0)))
+        if flipped:
+            specs.append(pl.BlockSpec((tile, right.shape[1]), lambda t: (t, 0)))
+        else:
+            specs.append(pl.BlockSpec((right.shape[0], tile), lambda t: (0, t)))
     return pl.pallas_call(
         kernel,
-        grid=(half,),
-        in_specs=[pl.BlockSpec((1, slots, count), lambda b: (base + b, 0, 0))] * many
-        + [pl.BlockSpec((others, CAP, width), lambda b: (0, base + b, 0))] * pieces
+        grid=(width // tile,),
+        in_specs=[pl.BlockSpec((half, slots, count), lambda t: (base, 0, 0))] * many
+        + [pl.BlockSpec((others, half * CAP, tile), lambda t: (0, base, t))] * pieces
         + specs,
-        out_specs=pl.BlockSpec((count, width), lambda b: (b, 0)),
+        out_specs=pl.BlockSpec((half * count, tile), lambda t: (0, t)),
         out_shape=jax.ShapeDtypeStruct((half * count, width), dtype),
         compiler_params=pltpu.CompilerParams(vmem_limit_bytes=LIMIT),
         cost_estimate=pl.CostEstimate(
@@ -617,7 +713,18 @@
 
     def group(self, x):
         evens = self.chips(x)
-        return evens + [swap(b, "seq", 1) for b in evens]
+        rows = x.shape[0]
+        everything = slice(None)
+        (even,) = arrange(
+            jnp.zeros((1,), jnp.int32),
+            evens,
+            [(rows * len(evens), x.shape[1])],
+            [
+                (k, everything, 0, lambda ref, k=k: (slice(k * rows, (k + 1) * rows), everything))
+                for k in range(len(evens))
+            ],
+        )
+        return even, swap(even, "seq", 1)
 
     def scatter(self, even, odd):
         chips = lax.axis_size("seq") // 2
@@ -635,41 +742,13 @@
     def others(self, x):
         return [x] + [self.send(x, j) for j in range(1, lax.axis_size("exp"))]
 
-    def sum_stack(self, x):
-        n = lax.axis_size("exp")
-        me = lax.axis_index("exp")
-        total = lax.dynamic_index_in_dim(x, me, 0, keepdims=False)
-        for j in range(1, n):
-            piece = lax.dynamic_index_in_dim(x, me ^ j, 0, keepdims=False).astype(BF)
-            total = total + self.send(piece, j).astype(F32)
-        return total
-
-
 def relative_order(count):
     chips = count // 2
     return [2 * k for k in range(chips)] + [2 * k + 1 for k in range(chips)]
 
 
-def scatter_small(x):
-    for axis in ("exp", "seq"):
-        n = lax.axis_size(axis)
-        me = lax.axis_index(axis)
-        total = lax.dynamic_index_in_dim(x, me, 0, keepdims=False)
-        for j in range(1, n):
-            piece = lax.dynamic_index_in_dim(x, me ^ j, 0, keepdims=False)
-            total = total + swap(piece, axis, j)
-        x = total
-    return x
-
-
-def columns_first(x, blocks):
-    rows, columns = x.shape
-    return x.reshape(rows, blocks, columns // blocks).transpose(1, 0, 2)
-
-
-def columns_last(x):
-    blocks, rows, w = x.shape
-    return x.transpose(1, 0, 2).reshape(rows, blocks * w)
+def sum_exp(x, axis):
+    return lax.psum_scatter(x.astype(BF), "exp", scatter_dimension=axis, tiled=True).astype(F32)
 
 
 def shards(
@@ -709,107 +788,82 @@
     across = Lane("exp", 2)
 
     index = jnp.stack([lax.axis_index("exp"), seq]).astype(jnp.int32)
-    extra = jnp.stack(
-        [norm_gain, ffn_gain, jnp.pad(latent_gain, (0, gain_rows - latent_rows_local))]
-    )
     packed = jnp.concatenate(
-        [w_kv_down, jnp.pad(extra, ((0, 13), (0, w_kv_down.shape[1] - gain_rows)))], axis=0
-    )
-    packed_even = jnp.stack(along.chips(packed))
-    query_parts = across.others(w_query)
-    token_blocks = along.group(tokens)
-    packed_parts = across.others(packed_even)
-    packed_parts = packed_parts + [swap(x, "seq", 1) for x in packed_parts]
-    up_parts = across.others(w_kv_up)
+        [
+            w_kv_down,
+            norm_gain[:, None],
+            ffn_gain[:, None],
+            jnp.pad(latent_gain, (0, gain_rows - latent_rows_local))[:, None],
+            jnp.zeros((gain_rows, 61), BF),
+        ],
+        axis=1,
+    )
+    down_full = lax.all_gather(packed, ("exp", "seq"), axis=0, tiled=True)
+    gate_cols = lax.all_gather(shared_gate, "exp", axis=0, tiled=True)
+    lift_cols = lax.all_gather(shared_up, "exp", axis=0, tiled=True)
+    drop_rows = lax.all_gather(shared_down, "exp", axis=1, tiled=True)
+    token_even = along.chips(tokens)
+    token_odd = [swap(x, "seq", 1) for x in token_even]
+    token_blocks = token_even + token_odd
+    ratio = w_query.shape[0] // w_kv_up.shape[0]
+    slim = w_kv_up.shape[1] // ratio
+    first_parts = across.others(
+        jnp.concatenate(
+            [
+                w_query,
+                jnp.concatenate(
+                    [w_kv_up[:, g * slim : (g + 1) * slim] for g in range(ratio)], axis=0
+                ),
+            ],
+            axis=1,
+        )
+    )
+    output_even = jnp.concatenate(along.chips(after(w_output, *token_odd)), axis=0)
     route_pack = jnp.concatenate([routes.astype(F32).T, route_weights.T], axis=0)
-    route_blocks = along.group(route_pack)
-    output_even = jnp.concatenate(along.chips(w_output), axis=0)
-    shared_parts = across.others(jnp.stack([shared_gate, shared_up]))
-    drop_parts = across.others(shared_down)
+    route_even = jnp.stack(along.chips(after(route_pack, *token_odd)))
+    route_all = jnp.concatenate([route_even, swap(route_even, "seq", 1)], axis=0)
     output_parts = across.others(output_even)
-    output_parts = output_parts + [swap(x, "seq", 1) for x in output_parts]
-    grad_blocks = along.group(out_grad)
-
-    plan = []
-    for n in range(2 * n_exp):
-        for k in range(chips):
-
-            def where(ref, n=n, k=k):
-                return (ref[0] ^ (n % n_exp)) * n_seq + (ref[1] ^ (2 * k + n // n_exp))
-
-            plan.append(
-                (
-                    n,
-                    (k, slice(0, gain_rows)),
-                    0,
-                    lambda ref, where=where: (span(where(ref), gain_rows), slice(None)),
-                )
-            )
-            plan.append(
-                (
-                    n,
-                    (k, slice(gain_rows, gain_rows + 16)),
-                    1,
-                    lambda ref, where=where: (where(ref),),
-                )
-            )
-    down_full, extra_all = arrange(
-        index,
-        packed_parts,
-        [(width, R + DR), (n_exp * n_seq, 16, R + DR)],
-        plan,
-    )
-    gain_first = extra_all[:, 0, :gain_rows].reshape(1, width).astype(F32)
-    gain_second = extra_all[:, 1, :gain_rows].reshape(1, width).astype(F32)
-    latent_wide = extra_all[:, 2, :latent_rows_local].reshape(1, R).astype(F32)
+
+    everything = slice(None)
     block_rows = width // n_exp
-    everything = slice(None)
+    gain_first = down_full[:, R + DR].astype(F32).reshape(1, width)
+    gain_second = down_full[:, R + DR + 1].astype(F32).reshape(1, width)
+    latent_wide = (
+        down_full[:, R + DR + 2]
+        .reshape(n_exp * n_seq, gain_rows)[:, :latent_rows_local]
+        .reshape(1, R)
+        .astype(F32)
+    )
+    up_rows = w_kv_up.shape[0]
+    query_width = w_query.shape[1]
     (up_cols,) = arrange(
         index,
-        up_parts,
+        first_parts,
         [(R, w_kv_up.shape[1])],
         [
-            (j, (everything,), 0, lambda ref, j=j: (span(ref[0] ^ j, R // n_exp), everything))
+            (
+                j,
+                (slice(g * up_rows, (g + 1) * up_rows), slice(query_width, query_width + slim)),
+                0,
+                lambda ref, j=j, g=g: (
+                    span(ref[0] ^ j, up_rows),
+                    slice(g * slim, (g + 1) * slim),
+                ),
+            )
             for j in range(n_exp)
-        ],
-    )
-    gate_cols, lift_cols = arrange(
-        index,
-        shared_parts,
-        [(width, shared_gate.shape[1])] * 2,
-        [
-            (j, (n,), n, lambda ref, j=j: (span(ref[0] ^ j, block_rows), everything))
-            for j in range(n_exp)
-            for n in range(2)
-        ],
-    )
-    (drop_rows,) = arrange(
-        index,
-        drop_parts,
-        [(shared_down.shape[0], width)],
-        [
-            (j, (everything,), 0, lambda ref, j=j: (everything, span(ref[0] ^ j, block_rows)))
-            for j in range(n_exp)
-        ],
-    )
-    output_half = H * DV // 2
-    (output_full,) = arrange(
+            for g in range(ratio)
+        ],
+    )
+    (output_even,) = arrange(
         index,
         output_parts,
-        [(H * DV, width)],
+        [(H * DV // 2, width)],
         [
-            (
-                n,
-                (everything,),
-                0,
-                lambda ref, n=n: (
-                    slice(n // n_exp * output_half, (n // n_exp + 1) * output_half),
-                    span(ref[0] ^ (n % n_exp), block_rows),
-                ),
-            )
-            for n in range(2 * n_exp)
-        ],
-    )
+            (j, everything, 0, lambda ref, j=j: (everything, span(ref[0] ^ j, block_rows)))
+            for j in range(n_exp)
+        ],
+    )
+    output_odd = swap(output_even, "seq", 1)
 
     positions = jnp.concatenate(
         [(seq ^ r) * count + jnp.arange(count, dtype=jnp.int32) for r in order]
@@ -818,31 +872,38 @@
     cosine_table, sine_table = rope_tables(positions, DR)
     cosine_wide = jnp.concatenate([cosine_table, cosine_table], axis=1)
     sine_wide = jnp.concatenate([-sine_table, sine_table], axis=1)
-    projected = None
-    for k in range(chips):
-        projected = project(
-            index,
-            k,
-            (token_blocks[k], token_blocks[chips + k]),
-            gain_first,
-            query_parts,
-            down_full,
-            latent_wide,
-            up_cols,
-            cosine_wide,
-            sine_wide,
-            heads,
-            length,
-            projected,
-        )
-    normed_one, latent_all, latent_raw, query_heads, key_heads, value_heads = projected
+    normed_one, latent_all, latent_raw, query_heads, key_heads, value_heads = project(
+        index,
+        token_blocks,
+        gain_first,
+        first_parts,
+        down_full,
+        latent_wide,
+        up_cols,
+        cosine_wide,
+        sine_wide,
+        heads,
+    )
     result, logsum = attend(
         query_heads, key_heads, value_heads, row_position, column_position, factor
     )
 
-    result_blocks = along.group(result)
-    normed_two, residual = add_norm(token_blocks, result_blocks, output_full, gain_second)
+    result_even = along.chips(result)
+    result_blocks = result_even + [swap(x, "seq", 1) for x in result_even]
+    normed_two, residual = add_norm(
+        token_blocks, result_blocks, output_even, output_odd, gain_second
+    )
     inverse_two = inverse_rms(residual)
+    grad_even, grad_odd = along.group(out_grad)
+    (grad_rows,) = arrange(
+        index,
+        [grad_even, grad_odd],
+        [(length, width)],
+        [
+            (h, everything, 0, lambda ref, h=h: (slice(h * half, (h + 1) * half), everything))
+            for h in range(2)
+        ],
+    )
 
     column = jnp.stack(
         [
@@ -852,7 +913,6 @@
         ]
     )
     kinds = n_exp * pieces
-    route_all = jnp.stack(route_blocks)
     named = route_all[:, None, :TOP, :].astype(jnp.int32) == column[None, :, None, None]
     matched = jnp.any(named, axis=2)
     match_weight = jnp.sum(jnp.where(named, route_all[:, None, TOP:, :], 0.0), axis=2)
@@ -872,11 +932,15 @@
     def give(rows):
         return lax.all_to_all(rows, "exp", split_axis=0, concat_axis=0, tiled=True)
 
-    grad_rows = jnp.concatenate(grad_blocks, axis=0)
     send_cots = dispatch(select, grad_rows, slot_weight, pieces)
     received_grad = [give(rows) for rows in send_cots]
     send_rows = dispatch(select, normed_two, None, pieces)
     received = [give(rows) for rows in send_rows]
+
+    own_heads = jnp.concatenate(
+        [block[p * count : (p + 1) * count] for p, block in enumerate(result_blocks)], axis=1
+    )
+    attention_parts = across.others(after(own_heads, received_grad[-1]))
 
     slot_rows = n_exp * n_seq * CAP
     pairs = []
@@ -905,31 +969,24 @@
     sgate_grad = (shared_hidden_grad * shared_up_raw * silu_slope(shared_gate_raw)).astype(BF)
     sup_grad = (shared_hidden_grad * jax.nn.silu(shared_gate_raw)).astype(BF)
     two_products = [(sgate_grad, gate_cols, True), (sup_grad, lift_cols, True)]
-    two_odd = combine(chips, [select], grads_back, two_products, BF)
+    two_odd = combine(1, [select], grads_back, two_products, BF)
     two_even = combine(0, [select], grads_back, two_products, F32)
     two_grad = along.scatter(two_even, two_odd)
-    shared_grad_stack = jnp.stack(
-        [
-            t_dot(shared_rows, sgate_grad).reshape(n_exp, width // n_exp, -1),
-            t_dot(shared_rows, sup_grad).reshape(n_exp, width // n_exp, -1),
-        ],
-        axis=1,
-    )
-
+    gate_out = sum_exp(t_dot(shared_rows, sgate_grad), 0)
+    lift_out = sum_exp(t_dot(shared_rows, sup_grad), 0)
+    drop_out = sum_exp(t_dot(shared_hidden, grad_rows), 1)
+
+    two_grad = after(two_grad, *expert_grads, results_back[0])
     residual_norm_grad, second_terms = norm_back(
         two_grad, residual, inverse_two, gain_second
     )
     residual_grad = out_grad.astype(F32) + residual_norm_grad
     residual_half = residual_grad.astype(BF)
-    all_heads = dot_t(residual_half, output_full).astype(BF)
+    even_heads = dot_t(residual_half, output_even).astype(BF)
+    odd_heads = dot_t(residual_half, output_odd).astype(BF)
     wide = heads * DV
     pairs = [
-        jnp.stack(
-            [
-                all_heads[:, k * wide : (k + 1) * wide],
-                all_heads[:, (chips + k) * wide : (chips + k + 1) * wide],
-            ]
-        )
+        jnp.stack([even_heads[:, k * wide : (k + 1) * wide], odd_heads[:, k * wide : (k + 1) * wide]])
         for k in range(chips)
     ]
     pairs = [pairs[0]] + [along.send(pairs[k], 2 * k) for k in range(1, chips)]
@@ -937,41 +994,51 @@
     attention_grad = jnp.concatenate(
         [jnp.stack([pair[0] for pair in pairs]), other_half], axis=0
     ).reshape(length, wide)
-    half_all = along.group(residual_half)
+    mine = lax.axis_index("exp")
+    column_blocks = [
+        lax.dynamic_slice_in_dim(residual_half, (mine ^ j) * block_rows, block_rows, 1)
+        for j in range(n_exp)
+    ]
+    column_blocks = [column_blocks[0]] + [
+        across.send(column_blocks[j], j) for j in range(1, n_exp)
+    ]
+    output_part = t_dot(
+        jnp.concatenate(attention_parts, axis=0), jnp.concatenate(column_blocks, axis=0)
+    )
+    output_out = along.scatter(output_part[: H * DV // 2], output_part[H * DV // 2 :])
 
     out_products = [(shared_hidden, drop_rows, False)]
     out_masks = [weighted_high, weighted_low]
-    out_odd = combine(chips, out_masks, results_back, out_products, BF)
+    out_odd = combine(1, out_masks, results_back, out_products, BF)
     out_even = combine(0, out_masks, results_back, out_products, F32)
 
-    query_in_grad, kv_grad, latent_part, rope_part = attend_back(
+    query_in_grad, kv_grad, latent_part, latent_sum = attend_back(
         query_heads,
         key_heads,
         value_heads,
         result,
-        attention_grad,
+        after(attention_grad, out_odd, out_even),
         logsum,
         row_position,
         column_position,
         cosine_wide,
         -sine_wide,
         up_cols,
+        latent_all,
+        latent_wide,
         factor,
     )
-    latent_part = jnp.concatenate([latent_part, rope_part], axis=1)
     latent_grad = along.scatter(latent_part[:half], latent_part[half:])
-    (query_cols,) = arrange(
-        index,
-        query_parts,
-        [(width, w_query.shape[1])],
-        [
-            (j, (everything,), 0, lambda ref, j=j: (span(ref[0] ^ j, block_rows), everything))
-            for j in range(n_exp)
-        ],
-    )
-    one_part = dot_t(query_in_grad, query_cols)
-    one_grad = along.scatter(one_part[:half], one_part[half:])
-    latent_raw_grad, latent_terms = norm_back(
+    one_odd, odd_sum = query_back(
+        index, 1, query_in_grad, first_parts, normed_one, gain_first, BF
+    )
+    one_even, even_sum = query_back(
+        index, 0, query_in_grad, first_parts, normed_one, gain_first, F32
+    )
+    one_grad = along.scatter(one_even, one_odd)
+    up_out = sum_exp(t_dot(latent_all, kv_grad), 0)
+    query_out = sum_exp(t_dot(normed_one, query_in_grad), 0)
+    latent_raw_grad, _ = norm_back(
         latent_grad[:, :R], latent_raw[:count], inverse_rms(latent_raw[:count]), latent_wide
     )
     down_rows = jnp.concatenate(
@@ -981,54 +1048,49 @@
         ],
         axis=1,
     ).astype(BF)
-    down_rows_all = jnp.concatenate(along.group(down_rows), axis=0)
+    devices = n_exp * n_seq
+    sums = jnp.concatenate(
+        [
+            (odd_sum + even_sum).reshape(devices, gain_rows),
+            jnp.sum(second_terms, axis=0).reshape(devices, gain_rows),
+            latent_sum.reshape(devices, latent_rows_local),
+        ],
+        axis=1,
+    )
+    many = sums.shape[1]
+    sums = jnp.pad(sums[:, None, :], ((0, 0), (0, 15), (0, R + DR - many))).astype(BF)
+    down_part = down_weights(normed_one, down_rows, sums, gain_rows)
+    down_sum = lax.psum_scatter(
+        down_part.reshape(devices * (gain_rows + 16), R + DR),
+        ("exp", "seq"),
+        scatter_dimension=0,
+        tiled=True,
+    ).astype(F32)
+    down_out = down_sum[:gain_rows]
+    small = down_sum[gain_rows, :many]
+    first_out = small[:gain_rows] + jnp.sum(
+        w_kv_down.astype(F32) * down_out, axis=1
+    ) / norm_gain.astype(F32)
     output = (residual + along.scatter(out_even, out_odd)).astype(BF)
 
-    shared_out = across.sum_stack(shared_grad_stack)
-    drop_out = across.sum_stack(columns_first(t_dot(shared_hidden, grad_rows), n_exp))
-    output_out = across.sum_stack(
-        columns_first(t_dot(result, jnp.concatenate(half_all, axis=0)), n_exp)
-    )
-    up_out = across.sum_stack(t_dot(latent_all, kv_grad).reshape(n_exp, R // n_exp, -1))
-    query_out = across.sum_stack(
-        t_dot(normed_one, query_in_grad).reshape(n_exp, width // n_exp, -1)
-    )
-    mine = lax.dynamic_slice_in_dim(
-        normed_one.reshape(length, n_exp, n_seq * gain_rows), seq * gain_rows, gain_rows, 2
-    ).reshape(length, n_exp * gain_rows)
-    down_out = across.sum_stack(t_dot(mine, down_rows_all).reshape(n_exp, gain_rows, -1))
-
-    down_back = dot_t(down_rows, down_full)
-    token_wide = jnp.concatenate(token_blocks, axis=0).astype(F32)
-    inverse_one = inverse_rms(token_wide)
-    one_hat = token_wide * inverse_one
-    first_sum = jnp.sum(one_part * one_hat, axis=0) + jnp.sum(down_back * one_hat[:count], axis=0)
+    down_back = dot_t(down_rows, down_full[:, : R + DR])
+    token_wide = tokens.astype(F32)
     token_norm_grad, _ = norm_back(
-        one_grad + down_back, token_wide[:count], inverse_one[:count], gain_first
+        one_grad + down_back, token_wide, inverse_rms(token_wide), gain_first
     )
     tokens_grad = (residual_grad + token_norm_grad).astype(BF)
-    small = scatter_small(
-        jnp.concatenate(
-            [
-                first_sum.reshape(n_exp, n_seq, gain_rows),
-                jnp.sum(second_terms, axis=0).reshape(n_exp, n_seq, gain_rows),
-                jnp.sum(latent_terms, axis=0).reshape(n_exp, n_seq, latent_rows_local),
-            ],
-            axis=2,
-        )
-    )
     return (
         output,
         tokens_grad,
-        small[:gain_rows],
+        first_out,
         query_out,
         down_out,
-        small[2 * gain_rows :],
+        small[2 * gain_rows : many],
         up_out,
         output_out,
         small[gain_rows : 2 * gain_rows],
-        shared_out[0],
-        shared_out[1],
+        gate_out,
+        lift_out,
         drop_out,
         expert_gate_grad,
         expert_up_grad,

time: 966 us -> 1010 us (1.046)
  waiting for transfers between devices: 257 us -> 433 us
  local copies, waits for them, and re-layouts: 130 us -> 48.3 us
  starting transfers between devices: 212 us -> 175 us
  between operations: 2.61 us -> 15.5 us
  matrix products: 60.6 us -> 49.4 us
    ppermute x122 -> x62, waiting for transfers between devices: 257 us -> 347 us  [swap(): return lax.ppermute(x, axis, [(i, i ^ mask) for i in range(n)])]
    ppermute x122 -> x62, starting transfers between devices: 177 us -> 141 us  [swap(): return lax.ppermute(x, axis, [(i, i ^ mask) for i in range(n)])]
    reduce_scatter x0 -> x6, waiting for transfers between devices: none -> 34.2 us  [the longest x1 34.2 us: shards(): lax.psum_scatter(down_part.reshape(devices * (gain_rows + 16), R + DR), (...]
    all_to_all x8, waiting for transfers between devices: 0.02 us -> 30.9 us  [give(): return lax.all_to_all(rows, 'exp', split_axis=0, concat_axis=0, tiled=True)]
    unnamed x256 -> x153, local copies, waits for them, and re-layouts: 59.7 us -> 30.7 us
    another operation x10 -> x3, local copies, waits for them, and re-layouts: 24.1 us -> 0.12 us  [the longest x1 0.08 us: shards(): latent_wide = down_full[:, R + DR + 2].reshape(n_exp * n_seq, gain_rows)[...]
    all_gather x0 -> x4, waiting for transfers between devices: none -> 20.7 us  [the longest x1 20.7 us: shards(): drop_rows = lax.all_gather(shared_down, 'exp', axis=1, tiled=True)]
    reshape x5 -> x3, local copies, waits for them, and re-layouts: 12.6 us -> 0.25 us  [the longest x1 0.09 us: shards(): latent_sum.reshape(devices, latent_rows_local)]
  transfers between devices with their start and end apart: 130 -> 80, of which waited for: 33 -> 32; matrix products, arithmetic and copies ran while one was open for 25% -> 13% of each run, Pallas kernels for 23% -> 22%
where the time goes in v3:
time: 1010 us; the launch traced here: 996 us
  waiting for transfers between devices  433 us (43%)
  Pallas kernels  218 us (22%)
  starting transfers between devices  175 us (17%)
  other arithmetic  56.5 us (6%)
  matrix products  49.4 us (5%)
  local copies, waits for them, and re-layouts  48.3 us (5%)
  between operations  15.5 us (2%)
    ppermute x62, waiting for transfers between devices, swap(): return lax.ppermute(x, axis, [(i, i ^ mask) for i in range(n)])  347 us
    ppermute x62, starting transfers between devices, swap(): return lax.ppermute(x, axis, [(i, i ^ mask) for i in range(n)])  141 us
    pallas_call x2, Pallas kernels, expert(): pl.pallas_call(kernel, grid=(count // tile,), in_specs=[block(width), blo...  55.5 us
    reduce_scatter x1, waiting for transfers between devices, shards(): lax.psum_scatter(down_part.reshape(devices * (gain_rows + 16), R + DR), (...  34.2 us
    all_to_all x8, starting transfers between devices, give(): return lax.all_to_all(rows, 'exp', split_axis=0, concat_axis=0, tiled=True)  32.9 us
    all_to_all x8, waiting for transfers between devices, give(): return lax.all_to_all(rows, 'exp', split_axis=0, concat_axis=0, tiled=True)  30.9 us
    unnamed x153, local copies, waits for them, and re-layouts  30.7 us
    pallas_call x2, Pallas kernels, expert_weights(): pl.pallas_call(kernel, grid=(width // tile,), in_specs=[column, column] +...  29.9 us
  transfers between devices with their start and end apart: 80, of which 32 were waited for; matrix products, arithmetic and copies ran while one was open for 13% of the time, Pallas kernels for 22%

profile of v3, /device:TPU:0, one launch (start us, length us, event | category | flops | bytes accessed | tf_op | source)
XLA Modules:
  0.0 995.7 jit_solution(6567297562510437827)
XLA Ops:
  17.0 13.0 %collective-permute-done.5.refs_3_.refs_11_ = bf16[128,2048]{1,0:T(8,128)(2,1)S(1)} collective-permute-done((bf16[128,2048]{1,0:T(8,128)(2,1)}, bf16[128,2048]{1,0:T(8,128)(2,1)S(1)}, u32[]{:S(2)}, u32[]{:S(2)}) %collective-permute-start.5) | collective-permute-done | bytes 524320 | tf_op jit(solution)/shard_map/ppermute | solution.py:690
  30.0 36.0 %collective-permute-done.3.refs_2_.refs_10_ = bf16[128,2048]{1,0:T(8,128)(2,1)S(1)} collective-permute-done((bf16[128,2048]{1,0:T(8,128)(2,1)}, bf16[128,2048]{1,0:T(8,128)(2,1)S(1)}, u32[]{:S(2)}, u32[]{:S(2)}) %collective-permute-start.3) | collective-permute-done | bytes 524320 | tf_op jit(solution)/shard_map/ppermute | solution.py:690
  81.8 19.4 %collective-permute-done.8 = bf16[256,512]{1,0:T(8,128)(2,1)S(1)} collective-permute-done((bf16[256,512]{1,0:T(8,128)(2,1)S(1)}, bf16[256,512]{1,0:T(8,128)(2,1)S(1)}, u32[]{:S(2)}, u32[]{:S(2)}) %collective-permute-start.8) | collective-permute-done | bytes 262176 | tf_op jit(solution)/shard_map/ppermute | solution.py:690
  103.5 45.7 %collective-permute-done.13.refs_3_.refs_11_ = bf16[512,512]{1,0:T(8,128)(2,1)S(1)} collective-permute-done((bf16[512,512]{1,0:T(8,128)(2,1)S(1)}, bf16[512,512]{1,0:T(8,128)(2,1)S(1)}, u32[]{:S(2)}, u32[]{:S(2)}) %collective-permute-start.13) | collective-permute-done | bytes 524320 | tf_op jit(solution)/shard_map/ppermute | solution.py:690
  154.5 50.8 %collective-permute-done.14.refs_2_ = bf16[1024,512]{1,0:T(8,128)(2,1)} collective-permute-done((bf16[1024,512]{1,0:T(8,128)(2,1)S(1)}, bf16[1024,512]{1,0:T(8,128)(2,1)}, u32[]{:S(2)}, u32[]{:S(2)}) %collective-permute-start.14) | collective-permute-done | bytes 1048608 | tf_op jit(solution)/shard_map/ppermute | solution.py:690
  235.6 14.6 %project.1 = (bf16[1024,2048]{1,0:T(8,128)(2,1)}, bf16[1024,512]{1,0:T(8,128)(2,1)}, f32[1024,512]{1,0:T(8,128)}, bf16[2,1024,256]{2,1,0:T(8,128)(2,1)}, bf16[2,...) custom-call(s32[2]{0:T(128)} %pad_add_fusion.index_ref, f32[1,2048]{1,0:T(1,128)} %bitcast.137, ...), custom_call_target="tpu_custom_call" | custom-call | flops 4831838208 | bytes 12582912 | tf_op jit(solution)/shard_map/project/pallas_call | solution.py:163
  263.1 20.3 %collective-permute-done.18.refs_1_ = bf16[1024,256]{1,0:T(8,128)(2,1)S(1)} collective-permute-done((bf16[1024,256]{1,0:T(8,128)(2,1)}, bf16[1024,256]{1,0:T(8,128)(2,1)S(1)}, u32[]{:S(2)}, u32[]{:S(2)}) %collective-permute-start.18) | collective-permute-done | bytes 524320 | tf_op jit(solution)/shard_map/ppermute | solution.py:690
  283.4 13.8 %collective-permute-done.20.refs_2_ = bf16[1024,256]{1,0:T(8,128)(2,1)S(1)} collective-permute-done((bf16[1024,256]{1,0:T(8,128)(2,1)}, bf16[1024,256]{1,0:T(8,128)(2,1)S(1)}, u32[]{:S(2)}, u32[]{:S(2)}) %collective-permute-start.20) | collective-permute-done | bytes 524320 | tf_op jit(solution)/shard_map/ppermute | solution.py:690
  300.6 18.3 %add_norm.1 = (bf16[1024,2048]{1,0:T(8,128)(2,1)}, f32[128,2048]{1,0:T(8,128)}) custom-call(bf16[1024,2048]{1,0:T(8,128)(2,1)} %arrange.4.we_ref, bf16[1024,2048]{1,0:T(8,128)(2,1)} %collective-permute-done.16.wo_ref, f32[1,2048]{1,0:T(1,128)} %bitcast.135, bf16[1024,256]{1,0:T(8,128)(2,1)} %get-tuple-element.121.refs_0_.o_ref, ...), custom_call_target="tpu_custom_call" | custom-call | flops 8589934592 | bytes 20971520 | tf_op jit(solution)/shard_map/add_norm/pallas_call | solution.py:414
  343.3 20.1 %collective-permute-done.28.refs_1_ = bf16[128,2048]{1,0:T(8,128)(2,1)S(1)} collective-permute-done((bf16[128,2048]{1,0:T(8,128)(2,1)S(1)}, bf16[128,2048]{1,0:T(8,128)(2,1)S(1)}, u32[]{:S(2)}, u32[]{:S(2)}) %collective-permute-start.28) | collective-permute-done | bytes 524320 | tf_op jit(solution)/shard_map/ppermute | solution.py:690
  363.4 15.6 %collective-permute-done.29.refs_2_ = bf16[128,2048]{1,0:T(8,128)(2,1)S(1)} collective-permute-done((bf16[128,2048]{1,0:T(8,128)(2,1)S(1)}, bf16[128,2048]{1,0:T(8,128)(2,1)S(1)}, u32[]{:S(2)}, u32[]{:S(2)}) %collective-permute-start.29) | collective-permute-done | bytes 524320 | tf_op jit(solution)/shard_map/ppermute | solution.py:690
  431.1 20.7 %all-gather.11.cloned.1.call-done.refs_5_ = bf16[352,2048]{1,0:T(8,128)(2,1)} async-done(((bf16[352,512]{1,0:T(8,128)(2,1)}), bf16[352,2048]{1,0:T(8,128)(2,1)}) %all-gather.11.cloned.1.call-update) | async-done | bytes 1441808 | tf_op jit(solution)/shard_map/all_gather | solution.py:804
  466.3 27.8 %expert.3 = (bf16[512,2048]{1,0:T(8,128)(2,1)}, bf16[512,2048]{1,0:T(8,128)(2,1)}, bf16[512,1408]{1,0:T(8,128)(2,1)}, bf16[512,1408]{1,0:T(8,128)(2,1)}, bf16[512,1408]{1,0:T(8,128)(2,1)}) custom-call(bf16[512,2048]{1,0:T(8,128)(2,1)} %bitcast.125, bf16[512,2048]{1,0:T(8,128)(2,1)} %bitcast.29.c_ref, bf16[2,2048,1408]{2,1,0:T(8,128)(2,1)} %gate_hbm.3, ...), custom_call_target="tpu_custom_call" | custom-call | flops 17716740096 | bytes 30015488 | tf_op jit(solution)/shard_map/expert/pallas_call | solution.py:505
  503.8 27.7 %expert.2 = (bf16[512,2048]{1,0:T(8,128)(2,1)}, bf16[512,2048]{1,0:T(8,128)(2,1)}, bf16[512,1408]{1,0:T(8,128)(2,1)}, bf16[512,1408]{1,0:T(8,128)(2,1)}, bf16[512,1408]{1,0:T(8,128)(2,1)}) custom-call(bf16[512,2048]{1,0:T(8,128)(2,1)} %bitcast.128, bf16[512,2048]{1,0:T(8,128)(2,1)} %bitcast.131, bf16[2,2048,1408]{2,1,0:T(8,128)(2,1)} %gate_hbm.3, ...), custom_call_target="tpu_custom_call" | custom-call | flops 17716740096 | bytes 30015488 | tf_op jit(solution)/shard_map/expert/pallas_call | solution.py:505
  553.3 16.8 %all-to-all-done.7.refs_1_ = bf16[4,128,2048]{2,1,0:T(8,128)(2,1)} async-done(((bf16[4,128,2048]{2,1,0:T(8,128)(2,1)}), bf16[4,128,2048]{2,1,0:T(8,128)(2,1)}, u32[]{:S(2)}, u32[]{:S(2)}) %all-to-all-start.7) | async-done | bytes 2097184 | tf_op jit(solution)/shard_map/all_to_all | solution.py:933
  585.0 14.9 %expert_weights.2 = (f32[2,2048,1408]{2,1,0:T(8,128)}, f32[2,2048,1408]{2,1,0:T(8,128)}, f32[2,1408,2048]{2,1,0:T(8,128)}) custom-call(bf16[512,2048]{1,0:T(8,128)(2,1)} %bitcast.129, bf16[512,2048]{1,0:T(8,128)(2,1)} %bitcast.132, bf16[512,1408]{1,0:T(8,128)(2,1)} %get-tuple-element.146.h_ref, bf16[512,1408]{1,0:T(8,128)(2,1)} %get-tuple-element.147.gg_ref, ...), custom_call_target="tpu_custom_call" | custom-call | flops 8858370048 | bytes 38797312 | tf_op jit(solution)/shard_map/expert_weights/pallas_call | solution.py:544
  618.8 14.9 %expert_weights.3 = (f32[2,2048,1408]{2,1,0:T(8,128)}, f32[2,2048,1408]{2,1,0:T(8,128)}, f32[2,1408,2048]{2,1,0:T(8,128)}) custom-call(bf16[512,2048]{1,0:T(8,128)(2,1)} %bitcast.126, bf16[512,2048]{1,0:T(8,128)(2,1)} %bitcast.29.c_ref, bf16[512,1408]{1,0:T(8,128)(2,1)} %get-tuple-element.142.h_ref, ...), custom_call_target="tpu_custom_call", output_to_operand_aliasing={{0}: (5, {}), {1}: (6, {}), {2}: (7, {})} | custom-call | flops 8858370048 | bytes 38797312 | tf_op jit(solution)/shard_map/expert_weights/pallas_call | solution.py:544
  636.7 15.2 %collective-permute-done.35 = bf16[128,2048]{1,0:T(8,128)(2,1)S(1)} collective-permute-done((bf16[128,2048]{1,0:T(8,128)(2,1)S(1)}, bf16[128,2048]{1,0:T(8,128)(2,1)S(1)}, u32[]{:S(2)}, u32[]{:S(2)}) %collective-permute-start.35) | collective-permute-done | bytes 524320 | tf_op jit(solution)/shard_map/ppermute | solution.py:690
  708.8 14.0 %attend_back.1 = (bf16[1024,384]{1,0:T(8,128)(2,1)}, bf16[1024,512]{1,0:T(8,128)(2,1)}, f32[1024,576]{1,0:T(8,128)}, f32[1,512]{1,0:T(1,128)}) custom-call(bf16[2,1024,256]{2,1,0:T(8,128)(2,1)} %get-tuple-element.111.q_ref, bf16[2,1024,256]{2,1,0:T(8,128)(2,1)} %get-tuple-element.112.k_ref, bf16[2,1024,128]{2,1,0:T(8,128)(2,1)} %get-tuple-element.113.v_ref, ...), custom_call_target="tpu_custom_call" | custom-call | flops 4294967296 | bytes 10485760 | tf_op jit(solution)/shard_map/attend_back/pallas_call | solution.py:332
  769.5 14.8 %collective-permute-done.54 = bf16[256,512]{1,0:T(8,128)(2,1)} collective-permute-done((bf16[256,512]{1,0:T(8,128)(2,1)}, bf16[256,512]{1,0:T(8,128)(2,1)}, u32[]{:S(2)}, u32[]{:S(2)}) %collective-permute-start.54) | collective-permute-done | bytes 262176 | tf_op jit(solution)/shard_map/ppermute | solution.py:690
  839.9 34.7 %collective-permute-done.56 = bf16[128,2048]{1,0:T(8,128)(2,1)} collective-permute-done((bf16[128,2048]{1,0:T(8,128)(2,1)}, bf16[128,2048]{1,0:T(8,128)(2,1)}, u32[]{:S(2)}, u32[]{:S(2)}) %collective-permute-start.56) | collective-permute-done | bytes 524320 | tf_op jit(solution)/shard_map/ppermute | solution.py:690
  877.2 40.8 %collective-permute-start.53 = (bf16[128,2048]{1,0:T(8,128)(2,1)}, bf16[128,2048]{1,0:T(8,128)(2,1)}, u32[]{:S(2)}, u32[]{:S(2)}) collective-permute-start(bf16[128,2048]{1,0:T(8,128)(2,1)} %get-tuple-element.177), channel_id=1, source_target_pairs={{0,2},{1,3},{2,0},{3,1},{4,6},{5,7},{6,4},{7,5},{8,10},{9,11},{10,... | collective-permute-start | bytes 1572872 | tf_op jit(solution)/shard_map/ppermute | solution.py:690
  931.5 14.5 %collective-permute-done.53 = bf16[128,2048]{1,0:T(8,128)(2,1)} collective-permute-done((bf16[128,2048]{1,0:T(8,128)(2,1)}, bf16[128,2048]{1,0:T(8,128)(2,1)}, u32[]{:S(2)}, u32[]{:S(2)}) %collective-permute-start.53) | collective-permute-done | bytes 524320 | tf_op jit(solution)/shard_map/ppermute | solution.py:690
  950.2 34.2 %reduce-scatter.7.cloned.1.call-done = bf16[80,576]{1,0:T(8,128)(2,1)} async-done(((bf16[2560,576]{1,0:T(8,128)(2,1)}), bf16[80,576]{1,0:T(8,128)(2,1)}) %reduce-scatter.7.cloned.1.call-update) | async-done | bytes 92176 | tf_op jit(solution)/shard_map/reduce_scatter | solution.py:1063
  (436 shorter events, 421.5 us)
Async XLA Ops:
  7.2 223.6 %all-gather.5.cloned.1.call-start = ((), (), s32[]{:S(2)}) async-start(), calls=%async_computation.14 | async-start | bytes 2703360 | tf_op jit(solution)/shard_map/all_gather | solution.py:801
  11.2 379.7 %all-gather.9.cloned.1.call-start = ((), (), s32[]{:S(2)}) async-start(), calls=%async_computation.16 | async-start | bytes 1966080 | tf_op jit(solution)/shard_map/all_gather | solution.py:803
  16.4 49.6 %collective-permute-start.3 = (bf16[128,2048]{1,0:T(8,128)(2,1)}, bf16[128,2048]{1,0:T(8,128)(2,1)S(1)}, u32[]{:S(2)}, u32[]{:S(2)}) collective-permute-start(bf16[128,2048]{1,0:T(8,128)(2,1)} %refs_8_.1), channel_id=1, source_target_pairs={{0,4},{1,5},{2,6},{3,7},{4,0},{5,1},{6,2},{7,3},{8,12},{9,13},{10,... | collective-permute-start | bytes 1572872 | tf_op jit(solution)/shard_map/ppermute | solution.py:690
  16.4 49.7 %collective-permute-start.1 = (bf16[128,2048]{1,0:T(8,128)(2,1)}, bf16[128,2048]{1,0:T(8,128)(2,1)S(1)}, u32[]{:S(2)}, u32[]{:S(2)}) collective-permute-start(bf16[128,2048]{1,0:T(8,128)(2,1)} %refs_8_.1), channel_id=1, source_target_pairs={{0,2},{1,3},{2,0},{3,1},{4,6},{5,7},{6,4},{7,5},{8,10},{9,11},{10,... | collective-permute-start | bytes 1572872 | tf_op jit(solution)/shard_map/ppermute | solution.py:690
  17.0 50.3 %collective-permute-start = (bf16[128,2048]{1,0:T(8,128)(2,1)}, bf16[128,2048]{1,0:T(8,128)(2,1)S(1)}, u32[]{:S(2)}, u32[]{:S(2)}) collective-permute-start(bf16[128,2048]{1,0:T(8,128)(2,1)} %refs_8_.1), channel_id=1, source_target_pairs={{0,1},{1,0},{2,3},{3,2},{4,5},{5,4},{6,7},{7,6},{8,9},{9,8},{10,11... | collective-permute-start | bytes 1572872 | tf_op jit(solution)/shard_map/ppermute | solution.py:690
  74.7 350.2 %all-gather.7.cloned.1.call-start = ((), (), s32[]{:S(2)}) async-start(), calls=%async_computation.15 | async-start | bytes 1966080 | tf_op jit(solution)/shard_map/all_gather | solution.py:802
  149.2 56.2 %collective-permute-start.14 = (bf16[1024,512]{1,0:T(8,128)(2,1)S(1)}, bf16[1024,512]{1,0:T(8,128)(2,1)}, u32[]{:S(2)}, u32[]{:S(2)}) collective-permute-start(bf16[1024,512]{1,0:T(8,128)(2,1)S(1)} %constant_dynamic-update-slice_fusion.refs_0_), channel_id=1, source_target_pairs={{0,16},{8,24},{16,0},{24,8},{1,17},{9,25},{17,1},{25,9},{2,18},{10... | collective-permute-start | bytes 3145736 | tf_op jit(solution)/shard_map/ppermute | solution.py:690
  151.5 53.8 %collective-permute-start.15 = (bf16[1024,512]{1,0:T(8,128)(2,1)S(1)}, bf16[1024,512]{1,0:T(8,128)(2,1)}, u32[]{:S(2)}, u32[]{:S(2)}) collective-permute-start(bf16[1024,512]{1,0:T(8,128)(2,1)S(1)} %constant_dynamic-update-slice_fusion.refs_0_), channel_id=1, source_target_pairs={{0,24},{8,16},{16,8},{24,0},{1,25},{9,17},{17,9},{25,1},{2,26},{10... | collective-permute-start | bytes 3145736 | tf_op jit(solution)/shard_map/ppermute | solution.py:690
  209.9 89.9 %collective-permute-start.16 = (bf16[1024,2048]{1,0:T(8,128)(2,1)}, bf16[1024,2048]{1,0:T(8,128)(2,1)}, u32[]{:S(2)}, u32[]{:S(2)}) collective-permute-start(bf16[1024,2048]{1,0:T(8,128)(2,1)} %arrange.4.we_ref), channel_id=1, source_target_pairs={{0,1},{1,0},{2,3},{3,2},{4,5},{5,4},{6,7},{7,6},{8,9},{9,8},{10,11... | collective-permute-start | bytes 12582920 | tf_op jit(solution)/shard_map/ppermute | solution.py:690
  326.5 57.2 %all-to-all-start = ((bf16[4,128,2048]{2,1,0:T(8,128)(2,1)}), bf16[4,128,2048]{2,1,0:T(8,128)(2,1)S(1)}, u32[]{:S(2)}, u32[]{:S(2)}) async-start(bf16[4,128,2048]{2,1,0:T(8,128)(2,1)} %get-tuple-element.124), calls=%async_computation | async-start | bytes 4194304 | tf_op jit(solution)/shard_map/all_to_all | solution.py:933
  330.2 121.6 %all-gather.11.cloned.1.call-start = ((), (), s32[]{:S(2)}) async-start(), calls=%async_computation.17 | async-start | bytes 1802240 | tf_op jit(solution)/shard_map/all_gather | solution.py:804
  424.8 395.1 %reduce-scatter.17.cloned.1.call-start = ((), (), s32[]{:S(2)}) async-start(), calls=%async_computation.23 | async-start | bytes 1802240 | tf_op jit(solution)/shard_map/reduce_scatter | solution.py:751
  537.4 284.4 %reduce-scatter.15.cloned.1.call-start = ((), (), s32[]{:S(2)}) async-start(), calls=%async_computation.22 | async-start | bytes 1802240 | tf_op jit(solution)/shard_map/reduce_scatter | solution.py:751
  542.5 281.2 %reduce-scatter.13.cloned.1.call-start = ((), (), s32[]{:S(2)}) async-start(), calls=%async_computation.21 | async-start | bytes 1802240 | tf_op jit(solution)/shard_map/reduce_scatter | solution.py:751
  583.1 50.7 %collective-permute-start.43 = (bf16[128,2048]{1,0:T(8,128)(2,1)}, bf16[128,2048]{1,0:T(8,128)(2,1)}, u32[]{:S(2)}, u32[]{:S(2)}) collective-permute-start(bf16[128,2048]{1,0:T(8,128)(2,1)} %slice_dynamic-update-slice_fusion), channel_id=1, source_target_pairs={{0,8},{8,0},{16,24},{24,16},{1,9},{9,1},{17,25},{25,17},{2,10},{10... | collective-permute-start | bytes 1572872 | tf_op jit(solution)/shard_map/ppermute | solution.py:690
  584.6 121.6 %collective-permute-start.44 = (bf16[128,2048]{1,0:T(8,128)(2,1)}, bf16[128,2048]{1,0:T(8,128)(2,1)}, u32[]{:S(2)}, u32[]{:S(2)}) collective-permute-start(bf16[128,2048]{1,0:T(8,128)(2,1)} %slice_dynamic-update-slice_fusion), channel_id=1, source_target_pairs={{0,16},{8,24},{16,0},{24,8},{1,17},{9,25},{17,1},{25,9},{2,18},{10... | collective-permute-start | bytes 1572872 | tf_op jit(solution)/shard_map/ppermute | solution.py:690
  600.0 55.0 %all-to-all-start.5 = ((bf16[4,128,2048]{2,1,0:T(8,128)(2,1)}), bf16[4,128,2048]{2,1,0:T(8,128)(2,1)S(1)}, u32[]{:S(2)}, u32[]{:S(2)}) async-start(bf16[4,128,2048]{2,1,0:T(8,128)(2,1)} %bitcast.130), calls=%async_computation.5 | async-start | bytes 4194304 | tf_op jit(solution)/shard_map/all_to_all | solution.py:933
  633.8 91.9 %collective-permute-start.45 = (bf16[128,2048]{1,0:T(8,128)(2,1)}, bf16[128,2048]{1,0:T(8,128)(2,1)}, u32[]{:S(2)}, u32[]{:S(2)}) collective-permute-start(bf16[128,2048]{1,0:T(8,128)(2,1)} %slice_dynamic-update-slice_fusion), channel_id=1, source_target_pairs={{0,24},{8,16},{16,8},{24,0},{1,25},{9,17},{17,9},{25,1},{2,26},{10... | collective-permute-start | bytes 1572872 | tf_op jit(solution)/shard_map/ppermute | solution.py:690
  660.8 175.2 %reduce-scatter.11.cloned.1.call-start = ((), (), s32[]{:S(2)}) async-start(), calls=%async_computation.20 | async-start | bytes 655360 | tf_op jit(solution)/shard_map/reduce_scatter | solution.py:751
  725.6 197.1 %reduce-scatter.9.cloned.1.call-start = ((), (), s32[]{:S(2)}) async-start(), calls=%async_computation.19 | async-start | bytes 1966080 | tf_op jit(solution)/shard_map/reduce_scatter | solution.py:751
  744.5 240.0 %reduce-scatter.7.cloned.1.call-start = ((), (), s32[]{:S(2)}) async-start(), calls=%async_computation.18 | async-start | bytes 3379200 | tf_op jit(solution)/shard_map/reduce_scatter | solution.py:1063
  874.6 56.8 %collective-permute-start.57 = (bf16[128,2048]{1,0:T(8,128)(2,1)}, bf16[128,2048]{1,0:T(8,128)(2,1)}, u32[]{:S(2)}, u32[]{:S(2)}) collective-permute-start(bf16[128,2048]{1,0:T(8,128)(2,1)} %get-tuple-element.181), channel_id=1, source_target_pairs={{0,4},{1,5},{2,6},{3,7},{4,0},{5,1},{6,2},{7,3},{8,12},{9,13},{10,... | collective-permute-start | bytes 1572872 | tf_op jit(solution)/shard_map/ppermute | solution.py:690
  874.6 56.8 %collective-permute-start.61 = (bf16[128,2048]{1,0:T(8,128)(2,1)}, bf16[128,2048]{1,0:T(8,128)(2,1)}, u32[]{:S(2)}, u32[]{:S(2)}) collective-permute-start(bf16[128,2048]{1,0:T(8,128)(2,1)} %get-tuple-element.185), channel_id=1, source_target_pairs={{0,6},{1,7},{2,4},{3,5},{4,2},{5,3},{6,0},{7,1},{8,14},{9,15},{10,... | collective-permute-start | bytes 1572872 | tf_op jit(solution)/shard_map/ppermute | solution.py:690
  877.2 68.8 %collective-permute-start.53 = (bf16[128,2048]{1,0:T(8,128)(2,1)}, bf16[128,2048]{1,0:T(8,128)(2,1)}, u32[]{:S(2)}, u32[]{:S(2)}) collective-permute-start(bf16[128,2048]{1,0:T(8,128)(2,1)} %get-tuple-element.177), channel_id=1, source_target_pairs={{0,2},{1,3},{2,0},{3,1},{4,6},{5,7},{6,4},{7,5},{8,10},{9,11},{10,... | collective-permute-start | bytes 1572872 | tf_op jit(solution)/shard_map/ppermute | solution.py:690
  (122 other events, 2852.9 us)
Sparse Core Ops, SparseCore 0:
  11.5 88.4 all-gather.4
  101.8 43.1 all-gather.8
  154.0 53.5 all-gather.6
  383.8 67.9 all-gather.10
  462.6 62.0 reduce-scatter.16
  542.6 41.9 reduce-scatter.14
  587.5 48.7 reduce-scatter.12
  725.7 24.4 reduce-scatter.10
  753.2 30.8 reduce-scatter.8
  818.7 165.6 reduce-scatter.6

commit v4 on v3

--- a/solution.py
+++ b/solution.py
@@ -72,6 +72,7 @@
 
 
 LIMIT = 56 * 1024 * 1024
+LIGHT = pl.CostEstimate(flops=0, transcendentals=0, bytes_accessed=0)
 ANY = pl.BlockSpec(memory_space=pl.ANY)
 SCALARS = pl.BlockSpec(memory_space=pltpu.SMEM)
 
@@ -87,14 +88,13 @@
         for block, source, out, target in plan:
             targets[out][target(index_ref)] = sources[block][source]
 
-    size = sum(math.prod(s) * 2 for s in outs)
     return pl.pallas_call(
         kernel,
         out_shape=[jax.ShapeDtypeStruct(s, BF) for s in outs],
         in_specs=[SCALARS] + [pl.BlockSpec(memory_space=pltpu.VMEM)] * len(blocks),
         out_specs=[pl.BlockSpec(memory_space=pltpu.VMEM)] * len(outs),
         compiler_params=pltpu.CompilerParams(vmem_limit_bytes=LIMIT),
-        cost_estimate=pl.CostEstimate(flops=0, transcendentals=0, bytes_accessed=2 * size),
+        cost_estimate=LIGHT,
         name="arrange",
     )(index, *blocks)
 
@@ -108,19 +108,16 @@
     return v * cosine + jnp.concatenate([v[:, middle:], v[:, :middle]], axis=1) * sine
 
 
-def project(index, token_blocks, gain, w_first, w_down, latent_gain, w_up, cosine, sine, heads):
+def project(token_blocks, gain, w_first, w_down, latent_gain, w_up, cosine, sine, heads):
     count, width = token_blocks[0].shape
     chips = len(token_blocks) // 2
     half = chips * count
     wide = DN + DR
-    many = len(w_first)
-    query_rows = w_first[0].shape[0]
     columns = heads * wide
 
-    def kernel(index_ref, g_ref, wd_ref, lg_ref, wu_ref, c_ref, s_ref, *refs):
-        tokens, weights = refs[: 2 * chips], refs[2 * chips : 2 * chips + many]
-        n_ref, l_ref, r_ref, q_ref, k_ref, v_ref, x_ref = refs[2 * chips + many :]
-        me = index_ref[0]
+    def kernel(g_ref, wd_ref, lg_ref, wu_ref, c_ref, s_ref, *refs):
+        tokens, w_ref = refs[: 2 * chips], refs[2 * chips]
+        n_ref, l_ref, r_ref, q_ref, k_ref, v_ref, x_ref = refs[2 * chips + 1 :]
         for h in range(2):
 
             @pl.when(pl.program_id(0) == h)
@@ -136,9 +133,7 @@
         r_ref[...] = raw
         inverse = lax.rsqrt(jnp.mean(raw * raw, axis=1, keepdims=True) + eps_norm)
         l_ref[...] = (raw * inverse * lg_ref[...]).astype(BF)
-        query = 0.0
-        for j in range(many):
-            query = query + dot(n_ref[:, span(me ^ j, query_rows)], weights[j][:, :columns])
+        query = dot(n_ref[...], w_ref[:, :columns])
         up = dot(l_ref[...], wu_ref[...]).astype(BF)
         cosine, sine = c_ref[...], s_ref[...]
         zeros = jnp.zeros((half, 256 - wide), BF)
@@ -164,7 +159,6 @@
         kernel,
         grid=(2,),
         in_specs=[
-            SCALARS,
             whole((1, width)),
             whole(w_down.shape),
             whole((1, R)),
@@ -173,7 +167,7 @@
             rows(DR),
         ]
         + [whole((count, width))] * (2 * chips)
-        + [whole(w.shape) for w in w_first],
+        + [whole(w_first.shape)],
         out_specs=[rows(width), rows(R), rows(R), head_rows(256), head_rows(256), head_rows(DV)],
         out_shape=[
             jax.ShapeDtypeStruct((length, width), BF),
@@ -185,54 +179,44 @@
         ],
         scratch_shapes=[pltpu.VMEM((half, width), BF)],
         compiler_params=pltpu.CompilerParams(vmem_limit_bytes=LIMIT),
-        cost_estimate=pl.CostEstimate(
-            flops=2 * length * (width * (columns + w_down.shape[1]) + R * w_up.shape[1]),
-            transcendentals=0,
-            bytes_accessed=4 * length * width + 2 * width * (columns + w_down.shape[1]),
-        ),
+        cost_estimate=LIGHT,
         name="project",
-    )(index, gain, w_down, latent_gain, w_up, cosine, sine, *token_blocks, *w_first)
-
-
-def query_back(index, base, query_grad, w_first, normed, gain, dtype):
+    )(gain, w_down, latent_gain, w_up, cosine, sine, *token_blocks, w_first)
+
+
+def query_back(base, query_grad, w_first, normed, gain, dtype):
     length, columns = query_grad.shape
     half = length // 2
     width = normed.shape[1]
-    many = len(w_first)
-    query_rows = w_first[0].shape[0]
-
-    def kernel(index_ref, q_ref, n_ref, g_ref, *refs):
-        weights, (o_ref, t_ref) = refs[:many], refs[many:]
-        me = index_ref[0]
-        for j in range(many):
-            where = span(me ^ j, query_rows)
-            part = dot_t(q_ref[...], weights[j][:, :columns])
-            o_ref[:, where] = part.astype(dtype)
-            t_ref[:, where] = jnp.sum(
-                part * n_ref[:, where].astype(F32), axis=0, keepdims=True
-            ) / g_ref[:, where]
+    tile = 512
+
+    def kernel(q_ref, n_ref, g_ref, w_ref, o_ref, t_ref):
+        part = dot_t(q_ref[...], w_ref[:, :columns])
+        o_ref[...] = part.astype(dtype)
+        product = part * n_ref[...].astype(F32)
+        t_ref[...] = jnp.sum(product, axis=0, keepdims=True) / g_ref[...]
 
     return pl.pallas_call(
         kernel,
-        grid=(1,),
+        grid=(width // tile,),
         in_specs=[
-            SCALARS,
             pl.BlockSpec((half, columns), lambda i: (base, 0)),
-            pl.BlockSpec((half, width), lambda i: (base, 0)),
-            whole((1, width)),
-        ]
-        + [whole(w.shape) for w in w_first],
-        out_specs=[whole((half, width)), whole((1, width))],
+            pl.BlockSpec((half, tile), lambda i: (base, i)),
+            pl.BlockSpec((1, tile), lambda i: (0, i)),
+            pl.BlockSpec((tile, w_first.shape[1]), lambda i: (i, 0)),
+        ],
+        out_specs=[
+            pl.BlockSpec((half, tile), lambda i: (0, i)),
+            pl.BlockSpec((1, tile), lambda i: (0, i)),
+        ],
         out_shape=[
             jax.ShapeDtypeStruct((half, width), dtype),
             jax.ShapeDtypeStruct((1, width), F32),
         ],
         compiler_params=pltpu.CompilerParams(vmem_limit_bytes=LIMIT),
-        cost_estimate=pl.CostEstimate(
-            flops=2 * half * columns * width, transcendentals=0, bytes_accessed=8 * half * width
-        ),
+        cost_estimate=LIGHT,
         name="query_back",
-    )(index, query_grad, normed, gain, *w_first)
+    )(query_grad, normed, gain, w_first)
 
 
 def attend(query, key, value, row_position, column_position, factor):
@@ -268,11 +252,7 @@
             jax.ShapeDtypeStruct((heads, length), F32),
         ],
         compiler_params=pltpu.CompilerParams(vmem_limit_bytes=LIMIT),
-        cost_estimate=pl.CostEstimate(
-            flops=2 * heads * length * length * (256 + DV),
-            transcendentals=heads * length * length,
-            bytes_accessed=4 * heads * length * 640,
-        ),
+        cost_estimate=LIGHT,
         name="attend",
     )(query, key, value, row_position, column_position)
 
@@ -365,11 +345,7 @@
             pltpu.VMEM((heads, 256, length), BF),
         ],
         compiler_params=pltpu.CompilerParams(vmem_limit_bytes=LIMIT),
-        cost_estimate=pl.CostEstimate(
-            flops=2 * heads * length * length * (3 * 256 + 2 * DV),
-            transcendentals=heads * length * length,
-            bytes_accessed=8 * heads * length * 640,
-        ),
+        cost_estimate=LIGHT,
         name="attend_back",
     )(query, key, value, result, result_grad, logsum, row_position, column_position, cosine, sine, w_up, latent_all, latent_gain)
 
@@ -424,11 +400,7 @@
         ],
         scratch_shapes=[pltpu.VMEM((half, width), BF), pltpu.VMEM((half, many * depth), BF)],
         compiler_params=pltpu.CompilerParams(vmem_limit_bytes=LIMIT),
-        cost_estimate=pl.CostEstimate(
-            flops=4 * length * width * w_even.shape[0],
-            transcendentals=0,
-            bytes_accessed=6 * length * width + 4 * width * w_even.shape[0],
-        ),
+        cost_estimate=LIGHT,
         name="add_norm",
     )(w_even, w_odd, gain, *blocks, *token_blocks)
 
@@ -517,11 +489,7 @@
             pltpu.SemaphoreType.DMA((3, len(spans))),
         ],
         compiler_params=pltpu.CompilerParams(vmem_limit_bytes=LIMIT),
-        cost_estimate=pl.CostEstimate(
-            flops=12 * count * width * units,
-            transcendentals=count * units,
-            bytes_accessed=6 * width * units + 8 * count * width + 6 * count * units,
-        ),
+        cost_estimate=LIGHT,
         name="expert",
     )(rows, cots, gate, up, down)
 
@@ -553,11 +521,7 @@
         ],
         input_output_aliases={5 + n: n for n in range(len(kept))},
         compiler_params=pltpu.CompilerParams(vmem_limit_bytes=LIMIT),
-        cost_estimate=pl.CostEstimate(
-            flops=6 * count * width * units,
-            transcendentals=0,
-            bytes_accessed=12 * width * units + 4 * count * width,
-        ),
+        cost_estimate=LIGHT,
         name="expert_weights",
     )(rows, cots, hidden, gate_grad, up_grad, *kept)
 
@@ -590,43 +554,40 @@
         out_specs=[out] * pieces,
         out_shape=[jax.ShapeDtypeStruct((others, blocks * CAP, width), BF)] * pieces,
         compiler_params=pltpu.CompilerParams(vmem_limit_bytes=LIMIT),
-        cost_estimate=pl.CostEstimate(
-            flops=2 * blocks * slots * count * width,
-            transcendentals=0,
-            bytes_accessed=2 * blocks * (slots + count) * width,
-        ),
+        cost_estimate=LIGHT,
         name="dispatch",
     )(select, rows, *weights)
 
 
-def down_weights(normed, down_rows, sums, gain_rows):
-    count, columns = down_rows.shape
-    devices, extra, _ = sums.shape
+def down_weights(index, normed, down_even, down_odd, others, n_seq, gain_rows):
+    length, _ = normed.shape
+    half, columns = down_even.shape
     per = 128 // gain_rows
 
-    def kernel(n_ref, d_ref, s_ref, o_ref):
-        part = t_dot(n_ref[...], d_ref[...]).astype(BF)
-        for i in range(per):
-            o_ref[i, :gain_rows] = part[i * gain_rows : (i + 1) * gain_rows]
-            o_ref[i, gain_rows:] = s_ref[i]
+    def kernel(index_ref, n_ref, e_ref, d_ref, o_ref, part):
+        part[...] = t_dot(n_ref[:half], e_ref[...]) + t_dot(n_ref[half:], d_ref[...])
+        o_ref[0] = part[span(index_ref[1] % per, gain_rows)]
 
     return pl.pallas_call(
         kernel,
-        grid=(devices // per,),
-        in_specs=[
-            pl.BlockSpec((count, 128), lambda i: (0, i)),
-            whole((count, columns)),
-            pl.BlockSpec((per, extra, columns), lambda i: (i, 0, 0)),
-        ],
-        out_specs=pl.BlockSpec((per, gain_rows + extra, columns), lambda i: (i, 0, 0)),
-        out_shape=jax.ShapeDtypeStruct((devices, gain_rows + extra, columns), BF),
-        cost_estimate=pl.CostEstimate(
-            flops=2 * devices * gain_rows * count * columns,
-            transcendentals=0,
-            bytes_accessed=4 * devices * (gain_rows + extra) * columns,
+        grid_spec=pltpu.PrefetchScalarGridSpec(
+            num_scalar_prefetch=1,
+            grid=(others,),
+            in_specs=[
+                pl.BlockSpec(
+                    (length, 128), lambda i, ref: (0, (i * n_seq + ref[1]) * gain_rows // 128)
+                ),
+                pl.BlockSpec((half, columns), lambda i, ref: (0, 0)),
+                pl.BlockSpec((half, columns), lambda i, ref: (0, 0)),
+            ],
+            out_specs=pl.BlockSpec((1, gain_rows, columns), lambda i, ref: (i, 0, 0)),
+            scratch_shapes=[pltpu.VMEM((128, columns), F32)],
         ),
+        out_shape=jax.ShapeDtypeStruct((others, gain_rows, columns), F32),
+        compiler_params=pltpu.CompilerParams(vmem_limit_bytes=LIMIT),
+        cost_estimate=LIGHT,
         name="down_weights",
-    )(normed, down_rows, sums)
+    )(index, normed, down_even, down_odd)
 
 
 def combine(base, masks, returned, products, dtype):
@@ -676,11 +637,7 @@
         out_specs=pl.BlockSpec((half * count, tile), lambda t: (0, t)),
         out_shape=jax.ShapeDtypeStruct((half * count, width), dtype),
         compiler_params=pltpu.CompilerParams(vmem_limit_bytes=LIMIT),
-        cost_estimate=pl.CostEstimate(
-            flops=2 * half * count * width * (many * slots + sum(p[0].shape[1] for p in products)),
-            transcendentals=0,
-            bytes_accessed=half * count * width * 6,
-        ),
+        cost_estimate=LIGHT,
         name="combine",
     )(*masks, *returned, *factors)
 
@@ -712,13 +669,15 @@
         return [x] + [self.send(x, 2 * k) for k in range(1, chips)]
 
     def group(self, x):
-        evens = self.chips(x)
-        rows = x.shape[0]
+        return self.pair(self.chips(x))
+
+    def pair(self, evens):
+        rows, columns = evens[0].shape
         everything = slice(None)
         (even,) = arrange(
             jnp.zeros((1,), jnp.int32),
             evens,
-            [(rows * len(evens), x.shape[1])],
+            [(rows * len(evens), columns)],
             [
                 (k, everything, 0, lambda ref, k=k: (slice(k * rows, (k + 1) * rows), everything))
                 for k in range(len(evens))
@@ -727,6 +686,9 @@
         return even, swap(even, "seq", 1)
 
     def scatter(self, even, odd):
+        return self.finish(self.begin(even, odd))
+
+    def begin(self, even, odd):
         chips = lax.axis_size("seq") // 2
         rows = even.shape[0] // chips
         got = swap(odd.astype(BF), "seq", 1)
@@ -734,10 +696,27 @@
             even[k * rows : (k + 1) * rows] + got[k * rows : (k + 1) * rows].astype(F32)
             for k in range(chips)
         ]
+        return blocks[:1] + [block.astype(BF) for block in blocks[1:]]
+
+    def finish(self, blocks, *gates):
+        got = [self.send(blocks[k], 2 * k) for k in range(1, len(blocks))]
         total = blocks[0]
-        for k in range(1, chips):
-            total = total + self.send(blocks[k].astype(BF), 2 * k).astype(F32)
+        for block in got:
+            total = total + after(block, *gates).astype(F32)
         return total
+
+    def corners(self, x):
+        if lax.axis_size("exp") != 4:
+            return [(j, 0, y) for j, y in enumerate(self.others(x))]
+        middle = x.shape[0] // 2
+        one, two = self.send(x, 1), self.send(x, 2)
+        return [
+            (0, 0, x),
+            (1, 0, one),
+            (2, 0, two),
+            (3, 0, self.send(two[:middle], 1)),
+            (3, middle, self.send(one[middle:], 2)),
+        ]
 
     def others(self, x):
         return [x] + [self.send(x, j) for j in range(1, lax.axis_size("exp"))]
@@ -785,29 +764,33 @@
     gain_rows = norm_gain.shape[0]
     latent_rows_local = latent_gain.shape[0]
     along = Lane("seq", 3)
-    across = Lane("exp", 2)
+    across = Lane("exp", 3)
+    free = Lane("seq", 3)
 
     index = jnp.stack([lax.axis_index("exp"), seq]).astype(jnp.int32)
+    ratio = w_query.shape[0] // w_kv_up.shape[0]
+    slim = w_kv_up.shape[1] // ratio
+    columns = w_kv_down.shape[1]
+    high = lax.reduce_precision(route_weights, 8, 7)
+    middle = lax.reduce_precision(route_weights - high, 8, 7)
+    low = route_weights - high - middle
+    route_pack = jnp.concatenate([routes.astype(F32), high, middle, low], axis=1).astype(BF).T
+    lines = route_pack.shape[0] // 4
+    gains = jnp.concatenate([norm_gain, ffn_gain, latent_gain])
     packed = jnp.concatenate(
         [
             w_kv_down,
-            norm_gain[:, None],
-            ffn_gain[:, None],
-            jnp.pad(latent_gain, (0, gain_rows - latent_rows_local))[:, None],
-            jnp.zeros((gain_rows, 61), BF),
-        ],
-        axis=1,
-    )
-    down_full = lax.all_gather(packed, ("exp", "seq"), axis=0, tiled=True)
-    gate_cols = lax.all_gather(shared_gate, "exp", axis=0, tiled=True)
-    lift_cols = lax.all_gather(shared_up, "exp", axis=0, tiled=True)
-    drop_rows = lax.all_gather(shared_down, "exp", axis=1, tiled=True)
+            jnp.pad(gains, (0, columns - gains.shape[0]))[None, :],
+            jnp.pad(
+                route_pack.reshape(4, lines, count).transpose(1, 0, 2).reshape(lines, 4 * count),
+                ((0, 15 - lines), (0, columns - 4 * count)),
+            ),
+        ],
+        axis=0,
+    )
+    packed_even = jnp.stack(free.chips(packed))
     token_even = along.chips(tokens)
-    token_odd = [swap(x, "seq", 1) for x in token_even]
-    token_blocks = token_even + token_odd
-    ratio = w_query.shape[0] // w_kv_up.shape[0]
-    slim = w_kv_up.shape[1] // ratio
-    first_parts = across.others(
+    first_all = lax.all_gather(
         jnp.concatenate(
             [
                 w_query,
@@ -816,37 +799,94 @@
                 ),
             ],
             axis=1,
-        )
-    )
+        ),
+        "exp",
+        axis=0,
+        tiled=True,
+    )
+    packed_parts = across.others(packed_even)
+    packed_even = jnp.stack(packed_parts)
+    packed_odd = swap(packed_even, "seq", 1)
+    token_odd = [swap(x, "seq", 1) for x in token_even[:2]]
+    token_odd += [swap(after(x, *token_odd), "seq", 1) for x in token_even[2:]]
+    token_blocks = token_even + token_odd
     output_even = jnp.concatenate(along.chips(after(w_output, *token_odd)), axis=0)
-    route_pack = jnp.concatenate([routes.astype(F32).T, route_weights.T], axis=0)
-    route_even = jnp.stack(along.chips(after(route_pack, *token_odd)))
-    route_all = jnp.concatenate([route_even, swap(route_even, "seq", 1)], axis=0)
-    output_parts = across.others(output_even)
+    output_parts = across.corners(output_even)
+    early = first_all
+    gate_cols = lax.all_gather(after(shared_gate, early), "exp", axis=0, tiled=True)
+    lift_cols = lax.all_gather(after(shared_up, early), "exp", axis=0, tiled=True)
+    drop_rows = lax.all_gather(after(shared_down, early), "exp", axis=1, tiled=True)
+    grad_even = along.chips(out_grad)
 
     everything = slice(None)
     block_rows = width // n_exp
-    gain_first = down_full[:, R + DR].astype(F32).reshape(1, width)
-    gain_second = down_full[:, R + DR + 1].astype(F32).reshape(1, width)
+    plan = []
+    for h in range(2):
+        for j in range(n_exp):
+            for k in range(chips):
+
+                def where(ref, h=h, j=j, k=k):
+                    return (ref[0] ^ j) * n_seq + (ref[1] ^ (2 * k + h))
+
+                plan.append(
+                    (
+                        h,
+                        (j, k, slice(0, gain_rows)),
+                        0,
+                        lambda ref, where=where: (span(where(ref), gain_rows), everything),
+                    )
+                )
+                plan.append(
+                    (
+                        h,
+                        (j, k, slice(gain_rows, gain_rows + 16)),
+                        1,
+                        lambda ref, where=where: (where(ref),),
+                    )
+                )
+    down_full, extra_all = arrange(
+        index,
+        [packed_even, packed_odd],
+        [(width, columns), (n_exp * n_seq, 16, columns)],
+        plan,
+    )
+    gain_first = extra_all[:, 0, :gain_rows].reshape(1, width).astype(F32)
+    gain_second = extra_all[:, 0, gain_rows : 2 * gain_rows].reshape(1, width).astype(F32)
     latent_wide = (
-        down_full[:, R + DR + 2]
-        .reshape(n_exp * n_seq, gain_rows)[:, :latent_rows_local]
+        extra_all[:, 0, 2 * gain_rows : 2 * gain_rows + latent_rows_local]
         .reshape(1, R)
         .astype(F32)
+    )
+    route_all = jnp.concatenate(
+        [packed_even[0, :, gain_rows + 1 :], packed_odd[0, :, gain_rows + 1 :]], axis=0
+    )[:, :lines, : 4 * count]
+    route_all = route_all.reshape(n_seq, lines, 4, count).transpose(0, 2, 1, 3)
+    route_all = route_all.reshape(n_seq, 4 * lines, count).astype(F32)
+    route_all = jnp.concatenate(
+        [
+            route_all[:, :TOP],
+            route_all[:, TOP : 2 * TOP]
+            + route_all[:, 2 * TOP : 3 * TOP]
+            + route_all[:, 3 * TOP :],
+        ],
+        axis=1,
     )
     up_rows = w_kv_up.shape[0]
     query_width = w_query.shape[1]
     (up_cols,) = arrange(
         index,
-        first_parts,
+        [first_all],
         [(R, w_kv_up.shape[1])],
         [
             (
-                j,
-                (slice(g * up_rows, (g + 1) * up_rows), slice(query_width, query_width + slim)),
+                0,
+                (
+                    slice((j * ratio + g) * up_rows, (j * ratio + g + 1) * up_rows),
+                    slice(query_width, query_width + slim),
+                ),
                 0,
                 lambda ref, j=j, g=g: (
-                    span(ref[0] ^ j, up_rows),
+                    slice(j * up_rows, (j + 1) * up_rows),
                     slice(g * slim, (g + 1) * slim),
                 ),
             )
@@ -856,11 +896,19 @@
     )
     (output_even,) = arrange(
         index,
-        output_parts,
+        [part[2] for part in output_parts],
         [(H * DV // 2, width)],
         [
-            (j, everything, 0, lambda ref, j=j: (everything, span(ref[0] ^ j, block_rows)))
-            for j in range(n_exp)
+            (
+                n,
+                everything,
+                0,
+                lambda ref, j=j, at=at, x=x: (
+                    slice(at, at + x.shape[0]),
+                    span(ref[0] ^ j, block_rows),
+                ),
+            )
+            for n, (j, at, x) in enumerate(output_parts)
         ],
     )
     output_odd = swap(output_even, "seq", 1)
@@ -873,10 +921,9 @@
     cosine_wide = jnp.concatenate([cosine_table, cosine_table], axis=1)
     sine_wide = jnp.concatenate([-sine_table, sine_table], axis=1)
     normed_one, latent_all, latent_raw, query_heads, key_heads, value_heads = project(
-        index,
         token_blocks,
         gain_first,
-        first_parts,
+        first_all,
         down_full,
         latent_wide,
         up_cols,
@@ -888,22 +935,7 @@
         query_heads, key_heads, value_heads, row_position, column_position, factor
     )
 
-    result_even = along.chips(result)
-    result_blocks = result_even + [swap(x, "seq", 1) for x in result_even]
-    normed_two, residual = add_norm(
-        token_blocks, result_blocks, output_even, output_odd, gain_second
-    )
-    inverse_two = inverse_rms(residual)
-    grad_even, grad_odd = along.group(out_grad)
-    (grad_rows,) = arrange(
-        index,
-        [grad_even, grad_odd],
-        [(length, width)],
-        [
-            (h, everything, 0, lambda ref, h=h: (slice(h * half, (h + 1) * half), everything))
-            for h in range(2)
-        ],
-    )
+    grad_even, grad_odd = along.pair([after(x, result) for x in grad_even])
 
     column = jnp.stack(
         [
@@ -932,15 +964,56 @@
     def give(rows):
         return lax.all_to_all(rows, "exp", split_axis=0, concat_axis=0, tiled=True)
 
+    (grad_rows,) = arrange(
+        index,
+        [grad_even, grad_odd],
+        [(length, width)],
+        [
+            (h, everything, 0, lambda ref, h=h: (slice(h * half, (h + 1) * half), everything))
+            for h in range(2)
+        ],
+    )
     send_cots = dispatch(select, grad_rows, slot_weight, pieces)
     received_grad = [give(rows) for rows in send_cots]
+
+    result_even = along.chips(result)
+    gathered = (gate_cols, lift_cols, drop_rows)
+    result_even = [after(x, *send_cots, *gathered) for x in result_even]
+    result_blocks = result_even + [swap(x, "seq", 1) for x in result_even]
+    normed_two, residual = add_norm(
+        token_blocks,
+        [after(result_blocks[0], received_grad[0])] + result_blocks[1:],
+        output_even,
+        output_odd,
+        gain_second,
+    )
+    inverse_two = inverse_rms(residual)
     send_rows = dispatch(select, normed_two, None, pieces)
-    received = [give(rows) for rows in send_rows]
-
-    own_heads = jnp.concatenate(
-        [block[p * count : (p + 1) * count] for p, block in enumerate(result_blocks)], axis=1
-    )
-    attention_parts = across.others(after(own_heads, received_grad[-1]))
+    received = [give(after(send_rows[0], *received_grad))]
+
+    (own_heads,) = arrange(
+        index,
+        result_blocks,
+        [(count, H * DV)],
+        [
+            (
+                p,
+                (slice(p * count, (p + 1) * count), everything),
+                0,
+                lambda ref, p=p: (everything, slice(p * heads * DV, (p + 1) * heads * DV)),
+            )
+            for p in range(n_seq)
+        ],
+    )
+
+    shared_rows = after(normed_two, *send_rows)
+    shared_gate_raw = dot(shared_rows, gate_cols)
+    shared_up_raw = dot(shared_rows, lift_cols)
+    shared_hidden = (jax.nn.silu(shared_gate_raw) * shared_up_raw).astype(BF)
+    shared_hidden_grad = dot_t(grad_rows, drop_rows)
+    sgate_grad = (shared_hidden_grad * shared_up_raw * silu_slope(shared_gate_raw)).astype(BF)
+    sup_grad = (shared_hidden_grad * jax.nn.silu(shared_gate_raw)).astype(BF)
+    received += [give(after(rows, sgate_grad, sup_grad)) for rows in send_rows[1:]]
 
     slot_rows = n_exp * n_seq * CAP
     pairs = []
@@ -954,29 +1027,28 @@
         grads_back.append(give(input_grad.reshape(n_exp, n_seq * CAP, width)))
         results_back.append(expert_result.reshape(n_exp, n_seq * CAP, width))
         kept.append((rows, cots, *saved))
-    last = input_grad
-    results_back = [give(after(rows, grads_back[-1])) for rows in results_back]
-    expert_grads = None
-    for i in range(pieces):
-        expert_grads = expert_weights(after(kept[i][0], last), *kept[i][1:], i, pieces, expert_grads)
-    expert_gate_grad, expert_up_grad, expert_down_grad = expert_grads
-
-    shared_rows = after(normed_two, *send_rows)
-    shared_gate_raw = dot(shared_rows, gate_cols)
-    shared_up_raw = dot(shared_rows, lift_cols)
-    shared_hidden = (jax.nn.silu(shared_gate_raw) * shared_up_raw).astype(BF)
-    shared_hidden_grad = dot_t(grad_rows, drop_rows)
-    sgate_grad = (shared_hidden_grad * shared_up_raw * silu_slope(shared_gate_raw)).astype(BF)
-    sup_grad = (shared_hidden_grad * jax.nn.silu(shared_gate_raw)).astype(BF)
     two_products = [(sgate_grad, gate_cols, True), (sup_grad, lift_cols, True)]
     two_odd = combine(1, [select], grads_back, two_products, BF)
     two_even = combine(0, [select], grads_back, two_products, F32)
-    two_grad = along.scatter(two_even, two_odd)
-    gate_out = sum_exp(t_dot(shared_rows, sgate_grad), 0)
-    lift_out = sum_exp(t_dot(shared_rows, sup_grad), 0)
-    drop_out = sum_exp(t_dot(shared_hidden, grad_rows), 1)
-
-    two_grad = after(two_grad, *expert_grads, results_back[0])
+    two_blocks = along.begin(two_even, two_odd)
+    expert_grads = None
+    back = []
+    for i in range(pieces):
+        back.append(give(after(results_back[i], *(two_blocks if i == 0 else expert_grads))))
+        expert_grads = expert_weights(
+            after(kept[i][0], *([input_grad] if i == 0 else back[:1])),
+            *kept[i][1:],
+            i,
+            pieces,
+            expert_grads,
+        )
+    results_back = back
+    expert_gate_grad, expert_up_grad, expert_down_grad = expert_grads
+    two_grad = along.finish(two_blocks, *expert_grads)
+    gate_out = sum_exp(t_dot(after(shared_rows, *two_blocks), sgate_grad), 0)
+    lift_out = sum_exp(t_dot(after(shared_rows, *two_blocks), sup_grad), 0)
+    drop_out = sum_exp(t_dot(after(shared_hidden, *two_blocks), grad_rows), 1)
+
     residual_norm_grad, second_terms = norm_back(
         two_grad, residual, inverse_two, gain_second
     )
@@ -989,35 +1061,26 @@
         jnp.stack([even_heads[:, k * wide : (k + 1) * wide], odd_heads[:, k * wide : (k + 1) * wide]])
         for k in range(chips)
     ]
+    stacks = pairs
     pairs = [pairs[0]] + [along.send(pairs[k], 2 * k) for k in range(1, chips)]
     other_half = swap(jnp.stack([pair[1] for pair in pairs]), "seq", 1)
     attention_grad = jnp.concatenate(
         [jnp.stack([pair[0] for pair in pairs]), other_half], axis=0
     ).reshape(length, wide)
-    mine = lax.axis_index("exp")
-    column_blocks = [
-        lax.dynamic_slice_in_dim(residual_half, (mine ^ j) * block_rows, block_rows, 1)
-        for j in range(n_exp)
-    ]
-    column_blocks = [column_blocks[0]] + [
-        across.send(column_blocks[j], j) for j in range(1, n_exp)
-    ]
-    output_part = t_dot(
-        jnp.concatenate(attention_parts, axis=0), jnp.concatenate(column_blocks, axis=0)
-    )
-    output_out = along.scatter(output_part[: H * DV // 2], output_part[H * DV // 2 :])
-
     out_products = [(shared_hidden, drop_rows, False)]
     out_masks = [weighted_high, weighted_low]
+    out_masks = [after(mask, *stacks) for mask in out_masks]
     out_odd = combine(1, out_masks, results_back, out_products, BF)
     out_even = combine(0, out_masks, results_back, out_products, F32)
+    out_blocks = along.begin(out_even, out_odd)
+    output_got = [along.send(out_blocks[k], 2 * k) for k in range(chips - 1, 0, -1)]
 
     query_in_grad, kv_grad, latent_part, latent_sum = attend_back(
         query_heads,
         key_heads,
         value_heads,
         result,
-        after(attention_grad, out_odd, out_even),
+        after(attention_grad, *out_blocks),
         logsum,
         row_position,
         column_position,
@@ -1028,16 +1091,52 @@
         latent_wide,
         factor,
     )
-    latent_grad = along.scatter(latent_part[:half], latent_part[half:])
-    one_odd, odd_sum = query_back(
-        index, 1, query_in_grad, first_parts, normed_one, gain_first, BF
-    )
-    one_even, even_sum = query_back(
-        index, 0, query_in_grad, first_parts, normed_one, gain_first, F32
-    )
-    one_grad = along.scatter(one_even, one_odd)
-    up_out = sum_exp(t_dot(latent_all, kv_grad), 0)
-    query_out = sum_exp(t_dot(normed_one, query_in_grad), 0)
+    query_in_grad = after(query_in_grad, *output_got[:2])
+    one_odd, odd_sum = query_back(1, query_in_grad, first_all, normed_one, gain_first, BF)
+    one_even, even_sum = query_back(0, query_in_grad, first_all, normed_one, gain_first, F32)
+    sums = jnp.concatenate(
+        [
+            (odd_sum + even_sum).reshape(n_exp, n_seq, gain_rows),
+            jnp.sum(second_terms, axis=0).reshape(n_exp, n_seq, gain_rows),
+            latent_sum.reshape(n_exp, n_seq, latent_rows_local),
+        ],
+        axis=2,
+    )
+    many = sums.shape[2]
+    turn = (seq ^ jnp.array(order))[:, None] == jnp.arange(n_seq)[None, :]
+    sums = jnp.einsum("ps,esw->pew", turn.astype(F32), sums, precision=lax.Precision.HIGHEST)
+    sums = jnp.pad(
+        sums.reshape(n_seq, 1, n_exp * many), ((0, 0), (0, 15), (0, columns - n_exp * many))
+    )
+    latent_part = jnp.concatenate([latent_part.reshape(n_seq, count, columns), sums], axis=1)
+    latent_part = latent_part.reshape(n_seq * (count + 16), columns)
+    latent_grad = along.scatter(
+        latent_part[: chips * (count + 16)], latent_part[chips * (count + 16) :]
+    )
+    one_blocks = along.begin(one_even, one_odd)
+    one_got = [along.send(one_blocks[k], 2 * k) for k in range(chips - 1, 0, -1)]
+    mine = lax.axis_index("exp")
+    late = Lane("exp", 1)
+    attention_parts = late.others(after(own_heads, *one_blocks))
+    column_blocks = [
+        lax.dynamic_slice_in_dim(
+            after(residual_half, *one_blocks), (mine ^ j) * block_rows, block_rows, 1
+        )
+        for j in range(n_exp)
+    ]
+    column_blocks = [column_blocks[0]] + [
+        late.send(column_blocks[j], j) for j in range(1, n_exp)
+    ]
+    output_part = t_dot(
+        jnp.concatenate(attention_parts, axis=0), jnp.concatenate(column_blocks, axis=0)
+    )
+    output_blocks = along.begin(output_part[: H * DV // 2], output_part[H * DV // 2 :])
+    up_part = t_dot(after(latent_all, *one_blocks), kv_grad).astype(BF)
+    query_part = t_dot(after(normed_one, *one_blocks), query_in_grad).astype(BF)
+    up_out = sum_exp(up_part, 0)
+    query_out = sum_exp(query_part, 0)
+    sums = latent_grad[count, : n_exp * many].reshape(n_exp, 1, many)
+    latent_grad = latent_grad[:count]
     latent_raw_grad, _ = norm_back(
         latent_grad[:, :R], latent_raw[:count], inverse_rms(latent_raw[:count]), latent_wide
     )
@@ -1048,32 +1147,35 @@
         ],
         axis=1,
     ).astype(BF)
-    devices = n_exp * n_seq
-    sums = jnp.concatenate(
+    down_even, down_odd = free.pair([after(x, *one_got) for x in free.chips(down_rows)])
+    down_part = down_weights(index, normed_one, down_even, down_odd, n_exp, n_seq, gain_rows)
+    down_part = jnp.concatenate(
         [
-            (odd_sum + even_sum).reshape(devices, gain_rows),
-            jnp.sum(second_terms, axis=0).reshape(devices, gain_rows),
-            latent_sum.reshape(devices, latent_rows_local),
+            down_part,
+            jnp.pad(sums, ((0, 0), (0, 15), (0, columns - many))),
         ],
         axis=1,
     )
-    many = sums.shape[1]
-    sums = jnp.pad(sums[:, None, :], ((0, 0), (0, 15), (0, R + DR - many))).astype(BF)
-    down_part = down_weights(normed_one, down_rows, sums, gain_rows)
-    down_sum = lax.psum_scatter(
-        down_part.reshape(devices * (gain_rows + 16), R + DR),
-        ("exp", "seq"),
-        scatter_dimension=0,
-        tiled=True,
-    ).astype(F32)
+    down_sum = lax.dynamic_index_in_dim(down_part, mine, 0, keepdims=False)
+    for j in range(1, n_exp):
+        piece = lax.dynamic_index_in_dim(down_part, mine ^ j, 0, keepdims=False).astype(BF)
+        down_sum = down_sum + swap(piece, "exp", j).astype(F32)
     down_out = down_sum[:gain_rows]
     small = down_sum[gain_rows, :many]
     first_out = small[:gain_rows] + jnp.sum(
         w_kv_down.astype(F32) * down_out, axis=1
     ) / norm_gain.astype(F32)
-    output = (residual + along.scatter(out_even, out_odd)).astype(BF)
-
-    down_back = dot_t(down_rows, down_full[:, : R + DR])
+
+    output = residual + out_blocks[0]
+    for block in output_got:
+        output = output + after(block, *one_blocks).astype(F32)
+    output = output.astype(BF)
+    output_out = free.finish(output_blocks)
+    one_grad = one_blocks[0]
+    for block in one_got:
+        block = after(block, up_part, query_part, down_sum, *output_blocks)
+        one_grad = one_grad + block.astype(F32)
+    down_back = dot_t(down_rows, down_full)
     token_wide = tokens.astype(F32)
     token_norm_grad, _ = norm_back(
         one_grad + down_back, token_wide, inverse_rms(token_wide), gain_first

time: 1010 us -> 832 us (0.82)
  waiting for transfers between devices: 433 us -> 270 us
  starting transfers between devices: 175 us -> 134 us
  blocking collectives: 0 us -> 29.4 us
  other arithmetic: 56.5 us -> 67.6 us
    ppermute x62 -> x70, waiting for transfers between devices: 347 us -> 227 us  [swap(): return lax.ppermute(x, axis, [(i, i ^ mask) for i in range(n)])]
    ppermute x62 -> x70, starting transfers between devices: 141 us -> 104 us  [swap(): return lax.ppermute(x, axis, [(i, i ^ mask) for i in range(n)])]
    reduce_scatter x1 -> x0, waiting for transfers between devices: 34.2 us -> none  [shards(): lax.psum_scatter(down_part.reshape(devices * (gain_rows + 16), R + DR), (...]
    all_to_all x0 -> x1, blocking collectives: none -> 29.4 us  [give(): return lax.all_to_all(rows, 'exp', split_axis=0, concat_axis=0, tiled=True)]
    unnamed x153 -> x146, local copies, waits for them, and re-layouts: 30.7 us -> 16.2 us
    pallas_call x4 -> x7, Pallas kernels: 14.6 us -> 23.7 us  [arrange(): pl.pallas_call(kernel, out_shape=[jax.ShapeDtypeStruct(s, BF) for s in ou...]
    convert_element_type x8 -> x10, other arithmetic: 17 us -> 21.2 us  [the longest x5 16.9 us: begin(): return blocks[:1] + [block.astype(BF) for block in blocks[1:]]]
    all_to_all x8 -> x7, starting transfers between devices: 32.9 us -> 29 us  [give(): return lax.all_to_all(rows, 'exp', split_axis=0, concat_axis=0, tiled=True)]
  transfers between devices with their start and end apart: 80 -> 86, of which waited for: 32 -> 30; matrix products, arithmetic and copies ran while one was open for 13% -> 14% of each run, Pallas kernels for 22% -> 26%
where the time goes in v4:
time: 832 us; the launch traced here: 817 us
  waiting for transfers between devices  270 us (32%)
  Pallas kernels  222 us (27%)
  starting transfers between devices  134 us (16%)
  other arithmetic  67.6 us (8%)
  matrix products  39.7 us (5%)
  local copies, waits for them, and re-layouts  39.3 us (5%)
  blocking collectives  29.4 us (4%)
  between operations  15.4 us (2%)
    ppermute x70, waiting for transfers between devices, swap(): return lax.ppermute(x, axis, [(i, i ^ mask) for i in range(n)])  227 us
    ppermute x70, starting transfers between devices, swap(): return lax.ppermute(x, axis, [(i, i ^ mask) for i in range(n)])  104 us
    pallas_call x2, Pallas kernels, expert(): pl.pallas_call(kernel, grid=(count // tile,), in_specs=[block(width), blo...  55.4 us
    pallas_call x2, Pallas kernels, expert_weights(): pl.pallas_call(kernel, grid=(width // tile,), in_specs=[column, column] +...  30.2 us
    all_to_all x1, blocking collectives, give(): return lax.all_to_all(rows, 'exp', split_axis=0, concat_axis=0, tiled=True)  29.4 us
    all_to_all x7, starting transfers between devices, give(): return lax.all_to_all(rows, 'exp', split_axis=0, concat_axis=0, tiled=True)  29 us
    all_to_all x7, waiting for transfers between devices, give(): return lax.all_to_all(rows, 'exp', split_axis=0, concat_axis=0, tiled=True)  27.4 us
    pallas_call x4, Pallas kernels, combine(): pl.pallas_call(kernel, grid=(width // tile,), in_specs=[pl.BlockSpec((hal...  25.6 us
  transfers between devices with their start and end apart: 86, of which 30 were waited for; matrix products, arithmetic and copies ran while one was open for 14% of the time, Pallas kernels for 26%

profile of v4, /device:TPU:0, one launch (start us, length us, event | category | flops | bytes accessed | tf_op | source)
XLA Modules:
  0.0 817.4 jit_solution(1431840629415116199)
XLA Ops:
  15.6 10.2 %collective-permute-done.1.refs_1_.refs_9_ = bf16[128,2048]{1,0:T(8,128)(2,1)S(1)} collective-permute-done((bf16[128,2048]{1,0:T(8,128)(2,1)}, bf16[128,2048]{1,0:T(8,128)(2,1)S(1)}, u32[]{:S(2)}, u32[]{:S(2)}) %collective-permute-start.1) | collective-permute-done | bytes 524320 | tf_op jit(solution)/shard_map/ppermute | solution.py:647
  38.8 22.5 %collective-permute-done.3.refs_2_.refs_10_ = bf16[128,2048]{1,0:T(8,128)(2,1)S(1)} collective-permute-done((bf16[128,2048]{1,0:T(8,128)(2,1)}, bf16[128,2048]{1,0:T(8,128)(2,1)S(1)}, u32[]{:S(2)}, u32[]{:S(2)}) %collective-permute-start.3) | collective-permute-done | bytes 524320 | tf_op jit(solution)/shard_map/ppermute | solution.py:647
  83.1 9.1 %collective-permute-done.8 = bf16[256,512]{1,0:T(8,128)(2,1)S(1)} collective-permute-done((bf16[256,512]{1,0:T(8,128)(2,1)S(1)}, bf16[256,512]{1,0:T(8,128)(2,1)S(1)}, u32[]{:S(2)}, u32[]{:S(2)}) %collective-permute-start.8) | collective-permute-done | bytes 262176 | tf_op jit(solution)/shard_map/ppermute | solution.py:647
  97.1 31.7 %collective-permute-done.17 = bf16[4,80,576]{2,1,0:T(8,128)(2,1)} collective-permute-done((bf16[4,80,576]{2,1,0:T(8,128)(2,1)}, bf16[4,80,576]{2,1,0:T(8,128)(2,1)}, u32[]{:S(2)}, u32[]{:S(2)}) %collective-permute-start.17) | collective-permute-done | bytes 368672 | tf_op jit(solution)/shard_map/ppermute | solution.py:647
  173.2 14.3 %project.1 = (bf16[1024,2048]{1,0:T(8,128)(2,1)}, bf16[1024,512]{1,0:T(8,128)(2,1)}, f32[1024,512]{1,0:T(8,128)}, bf16[2,1024,256]{2,1,0:T(8,128)(2,1)}, bf16[2,...) custom-call(f32[1,2048]{1,0:T(1,128)} %reshape.278.g_ref, bf16[2048,576]{1,0:T(8,128)(2,1)} %get-tuple-element.150.wd_ref, ...), custom_call_target="tpu_custom_call" | custom-call | tf_op jit(solution)/shard_map/project/pallas_call | solution.py:158
  187.5 8.4 %attend.1 = (bf16[1024,256]{1,0:T(8,128)(2,1)}, f32[2,1024]{1,0:T(2,128)}) custom-call(bf16[2,1024,256]{2,1,0:T(8,128)(2,1)} %get-tuple-element.151.q_ref, bf16[2,1024,256]{2,1,0:T(8,128)(2,1)} %get-tuple-element.152.k_ref, bf16[2,1024,128]{2,1,0:T(8,128)(2,1)} %get-tuple-element.153.v_ref, s32[1,1024]{1,0:T(1,128)} %bitcast.199, s32[1024,1]{1,0:T(8,128)} %copy.102.column_ref), custom_call_target="tpu_custom_call" | custom-call | tf_op jit(solution)/shard_map/attend/pallas_call | solution.py:236
  229.8 9.3 %collective-permute-done.28.refs_3_ = bf16[1024,256]{1,0:T(8,128)(2,1)S(1)} collective-permute-done((bf16[1024,256]{1,0:T(8,128)(2,1)S(1)}, bf16[1024,256]{1,0:T(8,128)(2,1)S(1)}, u32[]{:S(2)}, u32[]{:S(2)}) %collective-permute-start.28) | collective-permute-done | bytes 524320 | tf_op jit(solution)/shard_map/ppermute | solution.py:647
  239.1 15.4 %all-gather.9.cloned.1.call-done.refs_6_ = bf16[2048,352]{1,0:T(8,128)(2,1)} async-done(((bf16[512,352]{1,0:T(8,128)(2,1)}), bf16[2048,352]{1,0:T(8,128)(2,1)}) %all-gather.9.cloned.1.call-update) | async-done | bytes 1441808 | tf_op jit(solution)/shard_map/all_gather | solution.py:817
  254.5 17.3 %collective-permute-done.27.refs_2_ = bf16[1024,256]{1,0:T(8,128)(2,1)} collective-permute-done((bf16[1024,256]{1,0:T(8,128)(2,1)S(1)}, bf16[1024,256]{1,0:T(8,128)(2,1)}, u32[]{:S(2)}, u32[]{:S(2)}) %collective-permute-start.27) | collective-permute-done | bytes 524320 | tf_op jit(solution)/shard_map/ppermute | solution.py:647
  278.9 18.2 %add_norm.1 = (bf16[1024,2048]{1,0:T(8,128)(2,1)}, f32[128,2048]{1,0:T(8,128)}) custom-call(bf16[1024,2048]{1,0:T(8,128)(2,1)} %arrange.7.we_ref, bf16[1024,2048]{1,0:T(8,128)(2,1)} %collective-permute-done.20.wo_ref, f32[1,2048]{1,0:T(1,128)} %reshape.277.g_ref, bf16[1024,256]{1,0:T(8,128)(2,1)} %get-tuple-element.173.refs_0_.o_ref, ...), custom_call_target="tpu_custom_call" | custom-call | tf_op jit(solution)/shard_map/add_norm/pallas_call | solution.py:390
  322.2 25.2 %all-to-all-done.4 = bf16[4,128,2048]{2,1,0:T(8,128)(2,1)} async-done(((bf16[4,128,2048]{2,1,0:T(8,128)(2,1)}), bf16[4,128,2048]{2,1,0:T(8,128)(2,1)}, u32[]{:S(2)}, u32[]{:S(2)}) %all-to-all-start.4) | async-done | bytes 2097184 | tf_op jit(solution)/shard_map/all_to_all | solution.py:965
  351.0 27.7 %expert.3 = (bf16[512,2048]{1,0:T(8,128)(2,1)}, bf16[512,2048]{1,0:T(8,128)(2,1)}, bf16[512,1408]{1,0:T(8,128)(2,1)}, bf16[512,1408]{1,0:T(8,128)(2,1)}, bf16[512,1408]{1,0:T(8,128)(2,1)}) custom-call(bf16[512,2048]{1,0:T(8,128)(2,1)} %bitcast.35.x_ref, bf16[512,2048]{1,0:T(8,128)(2,1)} %bitcast.178, bf16[2,2048,1408]{2,1,0:T(8,128)(2,1)} %gate_hbm.3, ...), custom_call_target="tpu_custom_call" | custom-call | tf_op jit(solution)/shard_map/expert/pallas_call | solution.py:477
  384.7 27.7 %expert.2 = (bf16[512,2048]{1,0:T(8,128)(2,1)}, bf16[512,2048]{1,0:T(8,128)(2,1)}, bf16[512,1408]{1,0:T(8,128)(2,1)}, bf16[512,1408]{1,0:T(8,128)(2,1)}, bf16[512,1408]{1,0:T(8,128)(2,1)}) custom-call(bf16[512,2048]{1,0:T(8,128)(2,1)} %bitcast.182, bf16[512,2048]{1,0:T(8,128)(2,1)} %bitcast.180, bf16[2,2048,1408]{2,1,0:T(8,128)(2,1)} %gate_hbm.3, ...), custom_call_target="tpu_custom_call" | custom-call | tf_op jit(solution)/shard_map/expert/pallas_call | solution.py:477
  412.5 29.4 %all_to_all.40.refs_1_ = bf16[4,128,2048]{2,1,0:T(8,128)(2,1)} all-to-all(bf16[4,128,2048]{2,1,0:T(8,128)(2,1)} %bitcast.188), channel_id=1, replica_groups=mesh['exp'=4,'seq'=8] {'exp'}, dimensions={0} | all-to-all | bytes 4194304 | tf_op jit(solution)/shard_map/all_to_all | solution.py:965
  470.4 15.1 %expert_weights.2 = (f32[2,2048,1408]{2,1,0:T(8,128)}, f32[2,2048,1408]{2,1,0:T(8,128)}, f32[2,1408,2048]{2,1,0:T(8,128)}) custom-call(bf16[512,2048]{1,0:T(8,128)(2,1)} %bitcast.183, bf16[512,2048]{1,0:T(8,128)(2,1)} %bitcast.181, bf16[512,1408]{1,0:T(8,128)(2,1)} %get-tuple-element.192.h_ref, bf16[512,1408]{1,0:T(8,128)(2,1)} %get-tuple-element.193.gg_ref, ...), custom_call_target="tpu_custom_call" | custom-call | tf_op jit(solution)/shard_map/expert_weights/pallas_call | solution.py:512
  495.8 15.1 %expert_weights.3 = (f32[2,2048,1408]{2,1,0:T(8,128)}, f32[2,2048,1408]{2,1,0:T(8,128)}, f32[2,1408,2048]{2,1,0:T(8,128)}) custom-call(bf16[512,2048]{1,0:T(8,128)(2,1)} %bitcast.35.x_ref, bf16[512,2048]{1,0:T(8,128)(2,1)} %bitcast.179, bf16[512,1408]{1,0:T(8,128)(2,1)} %get-tuple-element.188.h_ref, ...), custom_call_target="tpu_custom_call", output_to_operand_aliasing={{0}: (5, {}), {1}: (6, {}), {2}: (7, {})} | custom-call | tf_op jit(solution)/shard_map/expert_weights/pallas_call | solution.py:512
  558.2 14.0 %attend_back.1 = (bf16[1024,384]{1,0:T(8,128)(2,1)}, bf16[1024,512]{1,0:T(8,128)(2,1)}, f32[1024,576]{1,0:T(8,128)}, f32[1,512]{1,0:T(1,128)}) custom-call(bf16[2,1024,256]{2,1,0:T(8,128)(2,1)} %get-tuple-element.151.q_ref, bf16[2,1024,256]{2,1,0:T(8,128)(2,1)} %get-tuple-element.152.k_ref, bf16[2,1024,128]{2,1,0:T(8,128)(2,1)} %get-tuple-element.153.v_ref, ...), custom_call_target="tpu_custom_call" | custom-call | tf_op jit(solution)/shard_map/attend_back/pallas_call | solution.py:312
  572.2 17.5 %collective-permute-done.43 = bf16[128,2048]{1,0:T(8,128)(2,1)S(1)} collective-permute-done((bf16[128,2048]{1,0:T(8,128)(2,1)S(1)}, bf16[128,2048]{1,0:T(8,128)(2,1)S(1)}, u32[]{:S(2)}, u32[]{:S(2)}) %collective-permute-start.43) | collective-permute-done | bytes 524320 | tf_op jit(solution)/shard_map/ppermute | solution.py:647
  612.9 11.6 %collective-permute-start.45 = (bf16[128,2048]{1,0:T(8,128)(2,1)}, bf16[128,2048]{1,0:T(8,128)(2,1)}, u32[]{:S(2)}, u32[]{:S(2)}) collective-permute-start(bf16[128,2048]{1,0:T(8,128)(2,1)} %get-tuple-element.225), channel_id=1, source_target_pairs={{0,2},{1,3},{2,0},{3,1},{4,6},{5,7},{6,4},{7,5},{8,10},{9,11},{10,... | collective-permute-start | bytes 1572872 | tf_op jit(solution)/shard_map/ppermute | solution.py:647
  628.5 8.4 %collective-permute-done.45 = bf16[128,2048]{1,0:T(8,128)(2,1)} collective-permute-done((bf16[128,2048]{1,0:T(8,128)(2,1)}, bf16[128,2048]{1,0:T(8,128)(2,1)}, u32[]{:S(2)}, u32[]{:S(2)}) %collective-permute-start.45) | collective-permute-done | bytes 524320 | tf_op jit(solution)/shard_map/ppermute | solution.py:647
  644.2 8.8 %collective-permute-done.49 = bf16[144,576]{1,0:T(8,128)(2,1)S(1)} collective-permute-done((bf16[144,576]{1,0:T(8,128)(2,1)}, bf16[144,576]{1,0:T(8,128)(2,1)S(1)}, u32[]{:S(2)}, u32[]{:S(2)}) %collective-permute-start.49) | collective-permute-done | bytes 165920 | tf_op jit(solution)/shard_map/ppermute | solution.py:647
  699.0 24.4 %collective-permute-done.51 = bf16[128,2048]{1,0:T(8,128)(2,1)} collective-permute-done((bf16[128,2048]{1,0:T(8,128)(2,1)}, bf16[128,2048]{1,0:T(8,128)(2,1)}, u32[]{:S(2)}, u32[]{:S(2)}) %collective-permute-start.51) | collective-permute-done | bytes 524320 | tf_op jit(solution)/shard_map/ppermute | solution.py:647
  723.4 11.8 %collective-permute-done.54.refs_2_ = bf16[128,576]{1,0:T(8,128)(2,1)S(1)} collective-permute-done((bf16[128,576]{1,0:T(8,128)(2,1)}, bf16[128,576]{1,0:T(8,128)(2,1)S(1)}, u32[]{:S(2)}, u32[]{:S(2)}) %collective-permute-start.54) | collective-permute-done | bytes 147488 | tf_op jit(solution)/shard_map/ppermute | solution.py:647
  788.9 12.5 %collective-permute-done.68 = bf16[256,512]{1,0:T(8,128)(2,1)} collective-permute-done((bf16[256,512]{1,0:T(8,128)(2,1)}, bf16[256,512]{1,0:T(8,128)(2,1)}, u32[]{:S(2)}, u32[]{:S(2)}) %collective-permute-start.68) | collective-permute-done | bytes 262176 | tf_op jit(solution)/shard_map/ppermute | solution.py:647
  (463 shorter events, 396.4 us)
Async XLA Ops:
  7.2 55.4 %all-gather.5.cloned.1.call-start = ((), (), s32[]{:S(2)}) async-start(), calls=%async_computation.13 | async-start | bytes 2621440 | tf_op jit(solution)/shard_map/all_gather | solution.py:793
  10.0 229.1 %all-gather.11.cloned.1.call-start = ((), (), s32[]{:S(2)}) async-start(), calls=%async_computation.16 | async-start | bytes 1802240 | tf_op jit(solution)/shard_map/all_gather | solution.py:818
  62.6 176.4 %all-gather.7.cloned.1.call-start = ((), (), s32[]{:S(2)}) async-start(), calls=%async_computation.14 | async-start | bytes 1966080 | tf_op jit(solution)/shard_map/all_gather | solution.py:816
  137.4 117.1 %all-gather.9.cloned.1.call-start = ((), (), s32[]{:S(2)}) async-start(), calls=%async_computation.15 | async-start | bytes 1966080 | tf_op jit(solution)/shard_map/all_gather | solution.py:817
  138.6 57.3 %collective-permute-start.24 = (bf16[128,2048]{1,0:T(8,128)(2,1)S(1)}, bf16[128,2048]{1,0:T(8,128)(2,1)}, u32[]{:S(2)}, u32[]{:S(2)}) collective-permute-start(bf16[128,2048]{1,0:T(8,128)(2,1)S(1)} %copy-done.15), channel_id=1, source_target_pairs={{0,6},{1,7},{2,4},{3,5},{4,2},{5,3},{6,0},{7,1},{8,14},{9,15},{10,... | collective-permute-start | bytes 1572872 | tf_op jit(solution)/shard_map/ppermute | solution.py:647
  139.8 56.1 %collective-permute-start.23 = (bf16[128,2048]{1,0:T(8,128)(2,1)S(1)}, bf16[128,2048]{1,0:T(8,128)(2,1)}, u32[]{:S(2)}, u32[]{:S(2)}) collective-permute-start(bf16[128,2048]{1,0:T(8,128)(2,1)S(1)} %copy-done.15), channel_id=1, source_target_pairs={{0,4},{1,5},{2,6},{3,7},{4,0},{5,1},{6,2},{7,3},{8,12},{9,13},{10,... | collective-permute-start | bytes 1572872 | tf_op jit(solution)/shard_map/ppermute | solution.py:647
  146.2 49.7 %collective-permute-start.22 = (bf16[128,2048]{1,0:T(8,128)(2,1)S(1)}, bf16[128,2048]{1,0:T(8,128)(2,1)}, u32[]{:S(2)}, u32[]{:S(2)}) collective-permute-start(bf16[128,2048]{1,0:T(8,128)(2,1)S(1)} %copy-done.15), channel_id=1, source_target_pairs={{0,2},{1,3},{2,0},{3,1},{4,6},{5,7},{6,4},{7,5},{8,10},{9,11},{10,... | collective-permute-start | bytes 1572872 | tf_op jit(solution)/shard_map/ppermute | solution.py:647
  156.2 122.7 %collective-permute-start.20 = (bf16[1024,2048]{1,0:T(8,128)(2,1)}, bf16[1024,2048]{1,0:T(8,128)(2,1)}, u32[]{:S(2)}, u32[]{:S(2)}) collective-permute-start(bf16[1024,2048]{1,0:T(8,128)(2,1)} %arrange.7.we_ref), channel_id=1, source_target_pairs={{0,1},{1,0},{2,3},{3,2},{4,5},{5,4},{6,7},{7,6},{8,9},{9,8},{10,11... | collective-permute-start | bytes 12582920 | tf_op jit(solution)/shard_map/ppermute | solution.py:647
  218.5 55.0 %all-to-all-start = ((bf16[4,128,2048]{2,1,0:T(8,128)(2,1)}), bf16[4,128,2048]{2,1,0:T(8,128)(2,1)S(1)}, u32[]{:S(2)}, u32[]{:S(2)}) async-start(bf16[4,128,2048]{2,1,0:T(8,128)(2,1)} %get-tuple-element.162), calls=%async_computation | async-start | bytes 4194304 | tf_op jit(solution)/shard_map/all_to_all | solution.py:965
  223.5 48.3 %collective-permute-start.27 = (bf16[1024,256]{1,0:T(8,128)(2,1)S(1)}, bf16[1024,256]{1,0:T(8,128)(2,1)}, u32[]{:S(2)}, u32[]{:S(2)}) collective-permute-start(bf16[1024,256]{1,0:T(8,128)(2,1)S(1)} %copy-done.18), channel_id=1, source_target_pairs={{0,4},{1,5},{2,6},{3,7},{4,0},{5,1},{6,2},{7,3},{8,12},{9,13},{10,... | collective-permute-start | bytes 1572872 | tf_op jit(solution)/shard_map/ppermute | solution.py:647
  229.8 42.0 %collective-permute-start.26 = (bf16[1024,256]{1,0:T(8,128)(2,1)S(1)}, bf16[1024,256]{1,0:T(8,128)(2,1)}, u32[]{:S(2)}, u32[]{:S(2)}) collective-permute-start(bf16[1024,256]{1,0:T(8,128)(2,1)S(1)} %copy-done.18), channel_id=1, source_target_pairs={{0,2},{1,3},{2,0},{3,1},{4,6},{5,7},{6,4},{7,5},{8,10},{9,11},{10,... | collective-permute-start | bytes 1572872 | tf_op jit(solution)/shard_map/ppermute | solution.py:647
  463.2 306.6 %reduce-scatter.14.cloned.1.call-start = ((), (), s32[]{:S(2)}) async-start(), calls=%async_computation.21 | async-start | bytes 1802240 | tf_op jit(solution)/shard_map/reduce_scatter | solution.py:730
  466.8 49.6 %collective-permute-start.34 = (bf16[128,2048]{1,0:T(8,128)(2,1)}, bf16[128,2048]{1,0:T(8,128)(2,1)}, u32[]{:S(2)}, u32[]{:S(2)}) collective-permute-start(bf16[128,2048]{1,0:T(8,128)(2,1)} %get-tuple-element.184), channel_id=1, source_target_pairs={{0,2},{1,3},{2,0},{3,1},{4,6},{5,7},{6,4},{7,5},{8,10},{9,11},{10,... | collective-permute-start | bytes 1572872 | tf_op jit(solution)/shard_map/ppermute | solution.py:647
  466.9 44.0 %collective-permute-start.36 = (bf16[128,2048]{1,0:T(8,128)(2,1)}, bf16[128,2048]{1,0:T(8,128)(2,1)}, u32[]{:S(2)}, u32[]{:S(2)}) collective-permute-start(bf16[128,2048]{1,0:T(8,128)(2,1)} %get-tuple-element.204), channel_id=1, source_target_pairs={{0,6},{1,7},{2,4},{3,5},{4,2},{5,3},{6,0},{7,1},{8,14},{9,15},{10,... | collective-permute-start | bytes 1572872 | tf_op jit(solution)/shard_map/ppermute | solution.py:647
  468.1 48.3 %collective-permute-start.35 = (bf16[128,2048]{1,0:T(8,128)(2,1)}, bf16[128,2048]{1,0:T(8,128)(2,1)}, u32[]{:S(2)}, u32[]{:S(2)}) collective-permute-start(bf16[128,2048]{1,0:T(8,128)(2,1)} %get-tuple-element.202), channel_id=1, source_target_pairs={{0,4},{1,5},{2,6},{3,7},{4,0},{5,1},{6,2},{7,3},{8,12},{9,13},{10,... | collective-permute-start | bytes 1572872 | tf_op jit(solution)/shard_map/ppermute | solution.py:647
  495.7 276.1 %reduce-scatter.12.cloned.1.call-start = ((), (), s32[]{:S(2)}) async-start(), calls=%async_computation.20 | async-start | bytes 1802240 | tf_op jit(solution)/shard_map/reduce_scatter | solution.py:730
  536.5 237.3 %reduce-scatter.10.cloned.1.call-start = ((), (), s32[]{:S(2)}) async-start(), calls=%async_computation.19 | async-start | bytes 1802240 | tf_op jit(solution)/shard_map/reduce_scatter | solution.py:730
  596.4 58.0 %collective-permute-start.44 = (bf16[512,2048]{1,0:T(8,128)(2,1)}, bf16[512,2048]{1,0:T(8,128)(2,1)}, u32[]{:S(2)}, u32[]{:S(2)}) collective-permute-start(bf16[512,2048]{1,0:T(8,128)(2,1)} %get-tuple-element.222), channel_id=1, source_target_pairs={{0,1},{1,0},{2,3},{3,2},{4,5},{5,4},{6,7},{7,6},{8,9},{9,8},{10,11... | collective-permute-start | bytes 6291464 | tf_op jit(solution)/shard_map/ppermute | solution.py:647
  599.3 176.4 %reduce-scatter.8.cloned.1.call-start = ((), (), s32[]{:S(2)}) async-start(), calls=%async_computation.18 | async-start | bytes 655360 | tf_op jit(solution)/shard_map/reduce_scatter | solution.py:730
  663.2 123.6 %reduce-scatter.6.cloned.1.call-start = ((), (), s32[]{:S(2)}) async-start(), calls=%async_computation.17 | async-start | bytes 1966080 | tf_op jit(solution)/shard_map/reduce_scatter | solution.py:730
  679.3 44.1 %collective-permute-start.51 = (bf16[128,2048]{1,0:T(8,128)(2,1)}, bf16[128,2048]{1,0:T(8,128)(2,1)}, u32[]{:S(2)}, u32[]{:S(2)}) collective-permute-start(bf16[128,2048]{1,0:T(8,128)(2,1)} %get-tuple-element.239), channel_id=1, source_target_pairs={{0,4},{1,5},{2,6},{3,7},{4,0},{5,1},{6,2},{7,3},{8,12},{9,13},{10,... | collective-permute-start | bytes 1572872 | tf_op jit(solution)/shard_map/ppermute | solution.py:647
  680.7 42.6 %collective-permute-start.48 = (bf16[128,2048]{1,0:T(8,128)(2,1)}, bf16[128,2048]{1,0:T(8,128)(2,1)}, u32[]{:S(2)}, u32[]{:S(2)}) collective-permute-start(bf16[128,2048]{1,0:T(8,128)(2,1)} %get-tuple-element.232), channel_id=1, source_target_pairs={{0,6},{1,7},{2,4},{3,5},{4,2},{5,3},{6,0},{7,1},{8,14},{9,15},{10,... | collective-permute-start | bytes 1572872 | tf_op jit(solution)/shard_map/ppermute | solution.py:647
  683.9 56.9 %collective-permute-start.62 = (bf16[128,2048]{1,0:T(8,128)(2,1)}, bf16[128,2048]{1,0:T(8,128)(2,1)}, u32[]{:S(2)}, u32[]{:S(2)}) collective-permute-start(bf16[128,2048]{1,0:T(8,128)(2,1)} %arrange.13), channel_id=1, source_target_pairs={{0,24},{8,16},{16,8},{24,0},{1,25},{9,17},{17,9},{25,1},{2,26},{10... | collective-permute-start | bytes 1572872 | tf_op jit(solution)/shard_map/ppermute | solution.py:647
  691.2 44.1 %collective-permute-start.54 = (bf16[128,576]{1,0:T(8,128)(2,1)}, bf16[128,576]{1,0:T(8,128)(2,1)S(1)}, u32[]{:S(2)}, u32[]{:S(2)}) collective-permute-start(bf16[128,576]{1,0:T(8,128)(2,1)} %pad_maximum_fusion.5.refs_0_), channel_id=1, source_target_pairs={{0,4},{1,5},{2,6},{3,7},{4,0},{5,1},{6,2},{7,3},{8,12},{9,13},{10,... | collective-permute-start | bytes 442376 | tf_op jit(solution)/shard_map/ppermute | solution.py:647
  (133 other events, 2158.8 us)
Sparse Core Ops, SparseCore 0:
  10.5 38.0 all-gather.4
  62.8 32.6 all-gather.10
  137.5 34.3 all-gather.6
  201.6 52.8 all-gather.8
  489.6 46.5 reduce-scatter.13
  539.3 30.0 reduce-scatter.11
  599.4 38.9 reduce-scatter.9
  663.3 28.4 reduce-scatter.7
  694.8 34.9 reduce-scatter.5

commit v5 on v4

--- a/solution.py
+++ b/solution.py
@@ -705,7 +705,7 @@
             total = total + after(block, *gates).astype(F32)
         return total
 
-    def corners(self, x):
+    def corners(self, x, *gates):
         if lax.axis_size("exp") != 4:
             return [(j, 0, y) for j, y in enumerate(self.others(x))]
         middle = x.shape[0] // 2
@@ -714,8 +714,8 @@
             (0, 0, x),
             (1, 0, one),
             (2, 0, two),
-            (3, 0, self.send(two[:middle], 1)),
-            (3, middle, self.send(one[middle:], 2)),
+            (3, 0, self.send(after(two[:middle], *gates), 1)),
+            (3, middle, self.send(after(one[middle:], *gates), 2)),
         ]
 
     def others(self, x):
@@ -807,12 +807,12 @@
     packed_parts = across.others(packed_even)
     packed_even = jnp.stack(packed_parts)
     packed_odd = swap(packed_even, "seq", 1)
-    token_odd = [swap(x, "seq", 1) for x in token_even[:2]]
-    token_odd += [swap(after(x, *token_odd), "seq", 1) for x in token_even[2:]]
+    token_odd = []
+    for x in token_even:
+        token_odd.append(swap(after(x, *token_odd), "seq", 1))
     token_blocks = token_even + token_odd
-    output_even = jnp.concatenate(along.chips(after(w_output, *token_odd)), axis=0)
-    output_parts = across.corners(output_even)
-    early = first_all
+    output_even = along.chips(after(w_output, *token_odd, packed_odd))
+    early = packed_parts[-1]
     gate_cols = lax.all_gather(after(shared_gate, early), "exp", axis=0, tiled=True)
     lift_cols = lax.all_gather(after(shared_up, early), "exp", axis=0, tiled=True)
     drop_rows = lax.all_gather(after(shared_down, early), "exp", axis=1, tiled=True)
@@ -894,6 +894,30 @@
             for g in range(ratio)
         ],
     )
+    positions = jnp.concatenate(
+        [(seq ^ r) * count + jnp.arange(count, dtype=jnp.int32) for r in order]
+    )
+    row_position, column_position = positions[None, :], positions[:, None]
+    cosine_table, sine_table = rope_tables(positions, DR)
+    cosine_wide = jnp.concatenate([cosine_table, cosine_table], axis=1)
+    sine_wide = jnp.concatenate([-sine_table, sine_table], axis=1)
+    normed_one, latent_all, latent_raw, query_heads, key_heads, value_heads = project(
+        token_blocks,
+        gain_first,
+        first_all,
+        down_full,
+        latent_wide,
+        up_cols,
+        cosine_wide,
+        sine_wide,
+        heads,
+    )
+    output_even = jnp.concatenate([after(x, normed_one) for x in output_even], axis=0)
+    result, logsum = attend(
+        query_heads, key_heads, value_heads, row_position, column_position, factor
+    )
+
+    output_parts = across.corners(output_even, result, *grad_even[1:])
     (output_even,) = arrange(
         index,
         [part[2] for part in output_parts],
@@ -913,28 +937,6 @@
     )
     output_odd = swap(output_even, "seq", 1)
 
-    positions = jnp.concatenate(
-        [(seq ^ r) * count + jnp.arange(count, dtype=jnp.int32) for r in order]
-    )
-    row_position, column_position = positions[None, :], positions[:, None]
-    cosine_table, sine_table = rope_tables(positions, DR)
-    cosine_wide = jnp.concatenate([cosine_table, cosine_table], axis=1)
-    sine_wide = jnp.concatenate([-sine_table, sine_table], axis=1)
-    normed_one, latent_all, latent_raw, query_heads, key_heads, value_heads = project(
-        token_blocks,
-        gain_first,
-        first_all,
-        down_full,
-        latent_wide,
-        up_cols,
-        cosine_wide,
-        sine_wide,
-        heads,
-    )
-    result, logsum = attend(
-        query_heads, key_heads, value_heads, row_position, column_position, factor
-    )
-
     grad_even, grad_odd = along.pair([after(x, result) for x in grad_even])
 
     column = jnp.stack(
@@ -991,20 +993,6 @@
     send_rows = dispatch(select, normed_two, None, pieces)
     received = [give(after(send_rows[0], *received_grad))]
 
-    (own_heads,) = arrange(
-        index,
-        result_blocks,
-        [(count, H * DV)],
-        [
-            (
-                p,
-                (slice(p * count, (p + 1) * count), everything),
-                0,
-                lambda ref, p=p: (everything, slice(p * heads * DV, (p + 1) * heads * DV)),
-            )
-            for p in range(n_seq)
-        ],
-    )
 
     shared_rows = after(normed_two, *send_rows)
     shared_gate_raw = dot(shared_rows, gate_cols)
@@ -1028,20 +1016,20 @@
         results_back.append(expert_result.reshape(n_exp, n_seq * CAP, width))
         kept.append((rows, cots, *saved))
     two_products = [(sgate_grad, gate_cols, True), (sup_grad, lift_cols, True)]
+    expert_grads = expert_weights(
+        after(kept[0][0], input_grad), *kept[0][1:], 0, pieces, None
+    )
+    select = after(select, *expert_grads)
     two_odd = combine(1, [select], grads_back, two_products, BF)
     two_even = combine(0, [select], grads_back, two_products, F32)
     two_blocks = along.begin(two_even, two_odd)
-    expert_grads = None
     back = []
     for i in range(pieces):
         back.append(give(after(results_back[i], *(two_blocks if i == 0 else expert_grads))))
-        expert_grads = expert_weights(
-            after(kept[i][0], *([input_grad] if i == 0 else back[:1])),
-            *kept[i][1:],
-            i,
-            pieces,
-            expert_grads,
-        )
+        if i:
+            expert_grads = expert_weights(
+                after(kept[i][0], back[0]), *kept[i][1:], i, pieces, expert_grads
+            )
     results_back = back
     expert_gate_grad, expert_up_grad, expert_down_grad = expert_grads
     two_grad = along.finish(two_blocks, *expert_grads)
@@ -1067,6 +1055,31 @@
     attention_grad = jnp.concatenate(
         [jnp.stack([pair[0] for pair in pairs]), other_half], axis=0
     ).reshape(length, wide)
+    (own_heads,) = arrange(
+        index,
+        [after(result_blocks[0], *two_blocks)] + result_blocks[1:],
+        [(count, H * DV)],
+        [
+            (
+                p,
+                (slice(p * count, (p + 1) * count), everything),
+                0,
+                lambda ref, p=p: (everything, slice(p * heads * DV, (p + 1) * heads * DV)),
+            )
+            for p in range(n_seq)
+        ],
+    )
+    mine = lax.axis_index("exp")
+    late = Lane("exp", 3)
+    attention_parts = late.others(after(own_heads, attention_grad))
+    column_blocks = [
+        lax.dynamic_slice_in_dim(residual_half, (mine ^ j) * block_rows, block_rows, 1)
+        for j in range(n_exp)
+    ]
+    column_blocks = [column_blocks[0]] + [
+        late.send(column_blocks[j], j) for j in range(1, n_exp)
+    ]
+
     out_products = [(shared_hidden, drop_rows, False)]
     out_masks = [weighted_high, weighted_low]
     out_masks = [after(mask, *stacks) for mask in out_masks]
@@ -1110,27 +1123,16 @@
     )
     latent_part = jnp.concatenate([latent_part.reshape(n_seq, count, columns), sums], axis=1)
     latent_part = latent_part.reshape(n_seq * (count + 16), columns)
+    output_part = t_dot(
+        jnp.concatenate([after(x, query_in_grad) for x in attention_parts], axis=0),
+        jnp.concatenate([after(x, query_in_grad) for x in column_blocks], axis=0),
+    )
+    output_blocks = along.begin(output_part[: H * DV // 2], output_part[H * DV // 2 :])
     latent_grad = along.scatter(
         latent_part[: chips * (count + 16)], latent_part[chips * (count + 16) :]
     )
     one_blocks = along.begin(one_even, one_odd)
     one_got = [along.send(one_blocks[k], 2 * k) for k in range(chips - 1, 0, -1)]
-    mine = lax.axis_index("exp")
-    late = Lane("exp", 1)
-    attention_parts = late.others(after(own_heads, *one_blocks))
-    column_blocks = [
-        lax.dynamic_slice_in_dim(
-            after(residual_half, *one_blocks), (mine ^ j) * block_rows, block_rows, 1
-        )
-        for j in range(n_exp)
-    ]
-    column_blocks = [column_blocks[0]] + [
-        late.send(column_blocks[j], j) for j in range(1, n_exp)
-    ]
-    output_part = t_dot(
-        jnp.concatenate(attention_parts, axis=0), jnp.concatenate(column_blocks, axis=0)
-    )
-    output_blocks = along.begin(output_part[: H * DV // 2], output_part[H * DV // 2 :])
     up_part = t_dot(after(latent_all, *one_blocks), kv_grad).astype(BF)
     query_part = t_dot(after(normed_one, *one_blocks), query_in_grad).astype(BF)
     up_out = sum_exp(up_part, 0)
@@ -1147,7 +1149,10 @@
         ],
         axis=1,
     ).astype(BF)
-    down_even, down_odd = free.pair([after(x, *one_got) for x in free.chips(down_rows)])
+    wide_got = [free.send(output_blocks[k], 2 * k) for k in range(chips - 1, 0, -1)]
+    down_even, down_odd = free.pair(
+        [after(x, *one_got, *wide_got) for x in free.chips(down_rows)]
+    )
     down_part = down_weights(index, normed_one, down_even, down_odd, n_exp, n_seq, gain_rows)
     down_part = jnp.concatenate(
         [
@@ -1170,10 +1175,12 @@
     for block in output_got:
         output = output + after(block, *one_blocks).astype(F32)
     output = output.astype(BF)
-    output_out = free.finish(output_blocks)
+    output_out = output_blocks[0]
+    for block in wide_got:
+        output_out = output_out + block.astype(F32)
     one_grad = one_blocks[0]
     for block in one_got:
-        block = after(block, up_part, query_part, down_sum, *output_blocks)
+        block = after(block, up_part, query_part, gate_out, lift_out, drop_out)
         one_grad = one_grad + block.astype(F32)
     down_back = dot_t(down_rows, down_full)
     token_wide = tokens.astype(F32)

time: 832 us -> 795 us (0.956)
  blocking collectives: 29.4 us -> 0 us
  waiting for transfers between devices: 270 us -> 259 us
    ppermute x70, waiting for transfers between devices: 227 us -> 185 us  [swap(): return lax.ppermute(x, axis, [(i, i ^ mask) for i in range(n)])]
    all_to_all x1 -> x0, blocking collectives: 29.4 us -> none  [give(): return lax.all_to_all(rows, 'exp', split_axis=0, concat_axis=0, tiled=True)]
    all_to_all x7 -> x8, waiting for transfers between devices: 27.4 us -> 56.3 us  [give(): return lax.all_to_all(rows, 'exp', split_axis=0, concat_axis=0, tiled=True)]
    all_to_all x7 -> x8, starting transfers between devices: 29 us -> 33.2 us  [give(): return lax.all_to_all(rows, 'exp', split_axis=0, concat_axis=0, tiled=True)]
    unnamed x146 -> x134, local copies, waits for them, and re-layouts: 16.2 us -> 17.9 us
  transfers between devices with their start and end apart: 86 -> 87, of which waited for: 30 -> 33; matrix products, arithmetic and copies ran while one was open for 14% -> 16% of each run, Pallas kernels for 26% -> 27%
where the time goes in v5:
time: 795 us; the launch traced here: 785 us
  waiting for transfers between devices  259 us (33%)
  Pallas kernels  222 us (28%)
  starting transfers between devices  137 us (17%)
  other arithmetic  68.8 us (9%)
  matrix products  43.6 us (5%)
  local copies, waits for them, and re-layouts  39.9 us (5%)
  between operations  15.3 us (2%)
    ppermute x70, waiting for transfers between devices, swap(): return lax.ppermute(x, axis, [(i, i ^ mask) for i in range(n)])  185 us
    ppermute x70, starting transfers between devices, swap(): return lax.ppermute(x, axis, [(i, i ^ mask) for i in range(n)])  102 us
    all_to_all x8, waiting for transfers between devices, give(): return lax.all_to_all(rows, 'exp', split_axis=0, concat_axis=0, tiled=True)  56.3 us
    pallas_call x2, Pallas kernels, expert(): pl.pallas_call(kernel, grid=(count // tile,), in_specs=[block(width), blo...  55.4 us
    all_to_all x8, starting transfers between devices, give(): return lax.all_to_all(rows, 'exp', split_axis=0, concat_axis=0, tiled=True)  33.2 us
    pallas_call x2, Pallas kernels, expert_weights(): pl.pallas_call(kernel, grid=(width // tile,), in_specs=[column, column] +...  30 us
    pallas_call x4, Pallas kernels, combine(): pl.pallas_call(kernel, grid=(width // tile,), in_specs=[pl.BlockSpec((hal...  25.8 us
    pallas_call x7, Pallas kernels, arrange(): pl.pallas_call(kernel, out_shape=[jax.ShapeDtypeStruct(s, BF) for s in ou...  23.7 us
  transfers between devices with their start and end apart: 87, of which 33 were waited for; matrix products, arithmetic and copies ran while one was open for 16% of the time, Pallas kernels for 27%

profile of v5, /device:TPU:0, one launch (start us, length us, event | category | flops | bytes accessed | tf_op | source)
XLA Modules:
  0.0 784.6 jit_solution(5385698687273512564)
XLA Ops:
  42.3 14.5 %collective-permute-done.12 = bf16[4,80,576]{2,1,0:T(8,128)(2,1)S(1)} collective-permute-done((bf16[4,80,576]{2,1,0:T(8,128)(2,1)S(1)}, bf16[4,80,576]{2,1,0:T(8,128)(2,1)S(1)}, u32[]{:S(2)}, u32[]{:S(2)}) %collective-permute-start.12) | collective-permute-done | bytes 368672 | tf_op jit(solution)/shard_map/ppermute | solution.py:647
  59.2 18.9 %collective-permute-done.3.refs_2_.refs_10_ = bf16[128,2048]{1,0:T(8,128)(2,1)} collective-permute-done((bf16[128,2048]{1,0:T(8,128)(2,1)S(1)}, bf16[128,2048]{1,0:T(8,128)(2,1)}, u32[]{:S(2)}, u32[]{:S(2)}) %collective-permute-start.3) | collective-permute-done | bytes 524320 | tf_op jit(solution)/shard_map/ppermute | solution.py:647
  100.9 14.4 %project.1 = (bf16[1024,2048]{1,0:T(8,128)(2,1)}, bf16[1024,512]{1,0:T(8,128)(2,1)}, f32[1024,512]{1,0:T(8,128)}, bf16[2,1024,256]{2,1,0:T(8,128)(2,1)}, bf16[2,...) custom-call(f32[1,2048]{1,0:T(1,128)} %reshape.277.g_ref, bf16[2048,576]{1,0:T(8,128)(2,1)} %get-tuple-element.158.wd_ref, ...), custom_call_target="tpu_custom_call" | custom-call | tf_op jit(solution)/shard_map/project/pallas_call | solution.py:158
  129.4 8.3 %attend.1 = (bf16[1024,256]{1,0:T(8,128)(2,1)}, f32[2,1024]{1,0:T(2,128)}) custom-call(bf16[2,1024,256]{2,1,0:T(8,128)(2,1)} %get-tuple-element.169.q_ref, bf16[2,1024,256]{2,1,0:T(8,128)(2,1)} %get-tuple-element.170.k_ref, bf16[2,1024,128]{2,1,0:T(8,128)(2,1)} %get-tuple-element.171.v_ref, s32[1,1024]{1,0:T(1,128)} %bitcast.202, s32[1024,1]{1,0:T(8,128)} %copy.102.column_ref), custom_call_target="tpu_custom_call" | custom-call | tf_op jit(solution)/shard_map/attend/pallas_call | solution.py:236
  137.7 9.4 %collective-permute-done.17.refs_1_ = bf16[1024,512]{1,0:T(8,128)(2,1)S(1)} collective-permute-done((bf16[1024,512]{1,0:T(8,128)(2,1)}, bf16[1024,512]{1,0:T(8,128)(2,1)S(1)}, u32[]{:S(2)}, u32[]{:S(2)}) %collective-permute-start.17) | collective-permute-done | bytes 1048608 | tf_op jit(solution)/shard_map/ppermute | solution.py:647
  147.2 19.8 %collective-permute-done.20.refs_2_ = bf16[128,2048]{1,0:T(8,128)(2,1)} collective-permute-done((bf16[128,2048]{1,0:T(8,128)(2,1)S(1)}, bf16[128,2048]{1,0:T(8,128)(2,1)}, u32[]{:S(2)}, u32[]{:S(2)}) %collective-permute-start.20) | collective-permute-done | bytes 524320 | tf_op jit(solution)/shard_map/ppermute | solution.py:647
  168.1 11.0 %collective-permute-done.23.refs_4_ = bf16[512,512]{1,0:T(8,128)(2,1)S(1)} collective-permute-done((bf16[512,512]{1,0:T(8,128)(2,1)S(1)}, bf16[512,512]{1,0:T(8,128)(2,1)S(1)}, u32[]{:S(2)}, u32[]{:S(2)}) %collective-permute-start.23) | collective-permute-done | bytes 524320 | tf_op jit(solution)/shard_map/ppermute | solution.py:647
  217.3 17.5 %all-gather.9.cloned.1.call-done.refs_6_ = bf16[2048,352]{1,0:T(8,128)(2,1)} async-done(((bf16[512,352]{1,0:T(8,128)(2,1)}), bf16[2048,352]{1,0:T(8,128)(2,1)}) %all-gather.9.cloned.1.call-update) | async-done | bytes 1441808 | tf_op jit(solution)/shard_map/all_gather | solution.py:817
  234.8 25.0 %collective-permute-done.27.refs_2_ = bf16[1024,256]{1,0:T(8,128)(2,1)} collective-permute-done((bf16[1024,256]{1,0:T(8,128)(2,1)S(1)}, bf16[1024,256]{1,0:T(8,128)(2,1)}, u32[]{:S(2)}, u32[]{:S(2)}) %collective-permute-start.27) | collective-permute-done | bytes 524320 | tf_op jit(solution)/shard_map/ppermute | solution.py:647
  266.8 18.2 %add_norm.1 = (bf16[1024,2048]{1,0:T(8,128)(2,1)}, f32[128,2048]{1,0:T(8,128)}) custom-call(bf16[1024,2048]{1,0:T(8,128)(2,1)} %arrange.9.we_ref, bf16[1024,2048]{1,0:T(8,128)(2,1)} %collective-permute-done.24.wo_ref, f32[1,2048]{1,0:T(1,128)} %reshape.279.g_ref, bf16[1024,256]{1,0:T(8,128)(2,1)} %get-tuple-element.268.refs_0_.o_ref, ...), custom_call_target="tpu_custom_call" | custom-call | tf_op jit(solution)/shard_map/add_norm/pallas_call | solution.py:390
  285.0 7.7 dispatch.3
  310.0 25.2 %all-to-all-done.3 = bf16[4,128,2048]{2,1,0:T(8,128)(2,1)} async-done(((bf16[4,128,2048]{2,1,0:T(8,128)(2,1)}), bf16[4,128,2048]{2,1,0:T(8,128)(2,1)}, u32[]{:S(2)}, u32[]{:S(2)}) %all-to-all-start.3) | async-done | bytes 2097184 | tf_op jit(solution)/shard_map/all_to_all | solution.py:967
  339.0 27.7 %expert.2 = (bf16[512,2048]{1,0:T(8,128)(2,1)}, bf16[512,2048]{1,0:T(8,128)(2,1)}, bf16[512,1408]{1,0:T(8,128)(2,1)}, bf16[512,1408]{1,0:T(8,128)(2,1)}, bf16[512,1408]{1,0:T(8,128)(2,1)}) custom-call(bf16[512,2048]{1,0:T(8,128)(2,1)} %bitcast.33.x_ref, bf16[512,2048]{1,0:T(8,128)(2,1)} %bitcast.178, bf16[2,2048,1408]{2,1,0:T(8,128)(2,1)} %gate_hbm.3, ...), custom_call_target="tpu_custom_call" | custom-call | tf_op jit(solution)/shard_map/expert/pallas_call | solution.py:477
  372.7 27.7 %expert.3 = (bf16[512,2048]{1,0:T(8,128)(2,1)}, bf16[512,2048]{1,0:T(8,128)(2,1)}, bf16[512,1408]{1,0:T(8,128)(2,1)}, bf16[512,1408]{1,0:T(8,128)(2,1)}, bf16[512,1408]{1,0:T(8,128)(2,1)}) custom-call(bf16[512,2048]{1,0:T(8,128)(2,1)} %bitcast.182, bf16[512,2048]{1,0:T(8,128)(2,1)} %bitcast.180, bf16[2,2048,1408]{2,1,0:T(8,128)(2,1)} %gate_hbm.3, ...), custom_call_target="tpu_custom_call" | custom-call | tf_op jit(solution)/shard_map/expert/pallas_call | solution.py:477
  406.3 14.9 %expert_weights.2 = (f32[2,2048,1408]{2,1,0:T(8,128)}, f32[2,2048,1408]{2,1,0:T(8,128)}, f32[2,1408,2048]{2,1,0:T(8,128)}) custom-call(bf16[512,2048]{1,0:T(8,128)(2,1)} %bitcast.183, bf16[512,2048]{1,0:T(8,128)(2,1)} %bitcast.181, bf16[512,1408]{1,0:T(8,128)(2,1)} %get-tuple-element.206.h_ref, bf16[512,1408]{1,0:T(8,128)(2,1)} %get-tuple-element.207.gg_ref, ...), custom_call_target="tpu_custom_call" | custom-call | tf_op jit(solution)/shard_map/expert_weights/pallas_call | solution.py:512
  421.2 9.0 %all-to-all-done.4.refs_1_ = bf16[4,128,2048]{2,1,0:T(8,128)(2,1)} async-done(((bf16[4,128,2048]{2,1,0:T(8,128)(2,1)}), bf16[4,128,2048]{2,1,0:T(8,128)(2,1)}, u32[]{:S(2)}, u32[]{:S(2)}) %all-to-all-start.4) | async-done | bytes 2097184 | tf_op jit(solution)/shard_map/all_to_all | solution.py:967
  464.2 18.9 %all-to-all-done.6.refs_2_ = bf16[4,128,2048]{2,1,0:T(8,128)(2,1)S(1)} async-done(((bf16[4,128,2048]{2,1,0:T(8,128)(2,1)}), bf16[4,128,2048]{2,1,0:T(8,128)(2,1)S(1)}, u32[]{:S(2)}, u32[]{:S(2)}) %all-to-all-start.6) | async-done | bytes 2097184 | tf_op jit(solution)/shard_map/all_to_all | solution.py:967
  489.1 15.1 %expert_weights.3 = (f32[2,2048,1408]{2,1,0:T(8,128)}, f32[2,2048,1408]{2,1,0:T(8,128)}, f32[2,1408,2048]{2,1,0:T(8,128)}) custom-call(bf16[512,2048]{1,0:T(8,128)(2,1)} %bitcast.33.x_ref, bf16[512,2048]{1,0:T(8,128)(2,1)} %bitcast.179, bf16[512,1408]{1,0:T(8,128)(2,1)} %get-tuple-element.218.h_ref, ...), custom_call_target="tpu_custom_call", output_to_operand_aliasing={{0}: (5, {}), {1}: (6, {}), {2}: (7, {})} | custom-call | tf_op jit(solution)/shard_map/expert_weights/pallas_call | solution.py:512
  561.0 13.9 %attend_back.1 = (bf16[1024,384]{1,0:T(8,128)(2,1)}, bf16[1024,512]{1,0:T(8,128)(2,1)}, f32[1024,576]{1,0:T(8,128)}, f32[1,512]{1,0:T(1,128)}) custom-call(bf16[2,1024,256]{2,1,0:T(8,128)(2,1)} %get-tuple-element.169.q_ref, bf16[2,1024,256]{2,1,0:T(8,128)(2,1)} %get-tuple-element.170.k_ref, bf16[2,1024,128]{2,1,0:T(8,128)(2,1)} %get-tuple-element.171.v_ref, ...), custom_call_target="tpu_custom_call" | custom-call | tf_op jit(solution)/shard_map/attend_back/pallas_call | solution.py:312
  604.8 11.6 %collective-permute-start.45 = (bf16[128,2048]{1,0:T(8,128)(2,1)}, bf16[128,2048]{1,0:T(8,128)(2,1)S(1)}, u32[]{:S(2)}, u32[]{:S(2)}) collective-permute-start(bf16[128,2048]{1,0:T(8,128)(2,1)} %get-tuple-element.247), channel_id=1, source_target_pairs={{0,2},{1,3},{2,0},{3,1},{4,6},{5,7},{6,4},{7,5},{8,10},{9,11},{10,... | collective-permute-start | bytes 1572872 | tf_op jit(solution)/shard_map/ppermute | solution.py:647
  676.5 13.9 %collective-permute-done.61 = bf16[256,512]{1,0:T(8,128)(2,1)} collective-permute-done((bf16[256,512]{1,0:T(8,128)(2,1)}, bf16[256,512]{1,0:T(8,128)(2,1)}, u32[]{:S(2)}, u32[]{:S(2)}) %collective-permute-start.61) | collective-permute-done | bytes 262176 | tf_op jit(solution)/shard_map/ppermute | solution.py:647
  699.4 18.2 %collective-permute-start.64 = (bf16[128,576]{1,0:T(8,128)(2,1)}, bf16[128,576]{1,0:T(8,128)(2,1)S(1)}, u32[]{:S(2)}, u32[]{:S(2)}) collective-permute-start(bf16[128,576]{1,0:T(8,128)(2,1)} %pad_maximum_fusion.5.refs_0_), channel_id=1, source_target_pairs={{0,4},{1,5},{2,6},{3,7},{4,0},{5,1},{6,2},{7,3},{8,12},{9,13},{10,... | collective-permute-start | bytes 442376 | tf_op jit(solution)/shard_map/ppermute | solution.py:647
  719.8 11.3 %collective-permute-done.50 = bf16[128,2048]{1,0:T(8,128)(2,1)} collective-permute-done((bf16[128,2048]{1,0:T(8,128)(2,1)}, bf16[128,2048]{1,0:T(8,128)(2,1)}, u32[]{:S(2)}, u32[]{:S(2)}) %collective-permute-start.50) | collective-permute-done | bytes 524320 | tf_op jit(solution)/shard_map/ppermute | solution.py:647
  731.1 12.7 %collective-permute-done.64.refs_2_ = bf16[128,576]{1,0:T(8,128)(2,1)S(1)} collective-permute-done((bf16[128,576]{1,0:T(8,128)(2,1)}, bf16[128,576]{1,0:T(8,128)(2,1)S(1)}, u32[]{:S(2)}, u32[]{:S(2)}) %collective-permute-start.64) | collective-permute-done | bytes 147488 | tf_op jit(solution)/shard_map/ppermute | solution.py:647
  (452 shorter events, 384.4 us)
Async XLA Ops:
  7.2 91.1 %all-gather.5.cloned.1.call-start = ((), (), s32[]{:S(2)}) async-start(), calls=%async_computation.13 | async-start | bytes 2621440 | tf_op jit(solution)/shard_map/all_gather | solution.py:793
  10.0 207.3 %all-gather.11.cloned.1.call-start = ((), (), s32[]{:S(2)}) async-start(), calls=%async_computation.16 | async-start | bytes 1802240 | tf_op jit(solution)/shard_map/all_gather | solution.py:818
  30.1 48.2 %collective-permute-start.5 = (bf16[128,2048]{1,0:T(8,128)(2,1)S(1)}, bf16[128,2048]{1,0:T(8,128)(2,1)}, u32[]{:S(2)}, u32[]{:S(2)}) collective-permute-start(bf16[128,2048]{1,0:T(8,128)(2,1)S(1)} %copy-done.8), channel_id=1, source_target_pairs={{0,6},{1,7},{2,4},{3,5},{4,2},{5,3},{6,0},{7,1},{8,14},{9,15},{10,... | collective-permute-start | bytes 1572872 | tf_op jit(solution)/shard_map/ppermute | solution.py:647
  78.3 139.0 %all-gather.7.cloned.1.call-start = ((), (), s32[]{:S(2)}) async-start(), calls=%async_computation.14 | async-start | bytes 1966080 | tf_op jit(solution)/shard_map/all_gather | solution.py:816
  119.6 47.9 %collective-permute-start.18 = (bf16[1024,512]{1,0:T(8,128)(2,1)}, bf16[1024,512]{1,0:T(8,128)(2,1)S(1)}, u32[]{:S(2)}, u32[]{:S(2)}) collective-permute-start(bf16[1024,512]{1,0:T(8,128)(2,1)} %constant_dynamic-update-slice_fusion.1.refs_0_), channel_id=1, source_target_pairs={{0,16},{8,24},{16,0},{24,8},{1,17},{9,25},{17,1},{25,9},{2,18},{10... | collective-permute-start | bytes 3145736 | tf_op jit(solution)/shard_map/ppermute | solution.py:647
  127.5 107.3 %all-gather.9.cloned.1.call-start = ((), (), s32[]{:S(2)}) async-start(), calls=%async_computation.15 | async-start | bytes 1966080 | tf_op jit(solution)/shard_map/all_gather | solution.py:817
  185.3 81.5 %collective-permute-start.24 = (bf16[1024,2048]{1,0:T(8,128)(2,1)}, bf16[1024,2048]{1,0:T(8,128)(2,1)}, u32[]{:S(2)}, u32[]{:S(2)}) collective-permute-start(bf16[1024,2048]{1,0:T(8,128)(2,1)} %arrange.9.we_ref), channel_id=1, source_target_pairs={{0,1},{1,0},{2,3},{3,2},{4,5},{5,4},{6,7},{7,6},{8,9},{9,8},{10,11... | collective-permute-start | bytes 12582920 | tf_op jit(solution)/shard_map/ppermute | solution.py:647
  209.1 52.5 %all-to-all-start = ((bf16[4,128,2048]{2,1,0:T(8,128)(2,1)}), bf16[4,128,2048]{2,1,0:T(8,128)(2,1)S(1)}, u32[]{:S(2)}, u32[]{:S(2)}) async-start(bf16[4,128,2048]{2,1,0:T(8,128)(2,1)} %get-tuple-element.184), calls=%async_computation | async-start | bytes 4194304 | tf_op jit(solution)/shard_map/all_to_all | solution.py:967
  451.7 240.9 %reduce-scatter.10.cloned.1.call-start = ((), (), s32[]{:S(2)}) async-start(), calls=%async_computation.19 | async-start | bytes 1802240 | tf_op jit(solution)/shard_map/reduce_scatter | solution.py:730
  455.4 48.8 %collective-permute-start.34 = (bf16[128,2048]{1,0:T(8,128)(2,1)}, bf16[128,2048]{1,0:T(8,128)(2,1)}, u32[]{:S(2)}, u32[]{:S(2)}) collective-permute-start(bf16[128,2048]{1,0:T(8,128)(2,1)} %get-tuple-element.214), channel_id=1, source_target_pairs={{0,2},{1,3},{2,0},{3,1},{4,6},{5,7},{6,4},{7,5},{8,10},{9,11},{10,... | collective-permute-start | bytes 1572872 | tf_op jit(solution)/shard_map/ppermute | solution.py:647
  455.4 48.8 %collective-permute-start.36 = (bf16[128,2048]{1,0:T(8,128)(2,1)}, bf16[128,2048]{1,0:T(8,128)(2,1)}, u32[]{:S(2)}, u32[]{:S(2)}) collective-permute-start(bf16[128,2048]{1,0:T(8,128)(2,1)} %get-tuple-element.227), channel_id=1, source_target_pairs={{0,6},{1,7},{2,4},{3,5},{4,2},{5,3},{6,0},{7,1},{8,14},{9,15},{10,... | collective-permute-start | bytes 1572872 | tf_op jit(solution)/shard_map/ppermute | solution.py:647
  456.8 48.2 %collective-permute-start.35 = (bf16[128,2048]{1,0:T(8,128)(2,1)}, bf16[128,2048]{1,0:T(8,128)(2,1)}, u32[]{:S(2)}, u32[]{:S(2)}) collective-permute-start(bf16[128,2048]{1,0:T(8,128)(2,1)} %get-tuple-element.225), channel_id=1, source_target_pairs={{0,4},{1,5},{2,6},{3,7},{4,0},{5,1},{6,2},{7,3},{8,12},{9,13},{10,... | collective-permute-start | bytes 1572872 | tf_op jit(solution)/shard_map/ppermute | solution.py:647
  489.1 205.5 %reduce-scatter.8.cloned.1.call-start = ((), (), s32[]{:S(2)}) async-start(), calls=%async_computation.18 | async-start | bytes 1802240 | tf_op jit(solution)/shard_map/reduce_scatter | solution.py:730
  527.3 169.2 %reduce-scatter.6.cloned.1.call-start = ((), (), s32[]{:S(2)}) async-start(), calls=%async_computation.17 | async-start | bytes 1802240 | tf_op jit(solution)/shard_map/reduce_scatter | solution.py:730
  552.4 216.2 %reduce-scatter.14.cloned.1.call-start = ((), (), s32[]{:S(2)}) async-start(), calls=%async_computation.21 | async-start | bytes 655360 | tf_op jit(solution)/shard_map/reduce_scatter | solution.py:730
  557.5 45.0 %collective-permute-start.55 = (bf16[128,2048]{1,0:T(8,128)(2,1)}, bf16[128,2048]{1,0:T(8,128)(2,1)}, u32[]{:S(2)}, u32[]{:S(2)}) collective-permute-start(bf16[128,2048]{1,0:T(8,128)(2,1)} %arrange.12), channel_id=1, source_target_pairs={{0,24},{8,16},{16,8},{24,0},{1,25},{9,17},{17,9},{25,1},{2,26},{10... | collective-permute-start | bytes 1572872 | tf_op jit(solution)/shard_map/ppermute | solution.py:647
  558.9 45.9 %collective-permute-start.54 = (bf16[128,2048]{1,0:T(8,128)(2,1)}, bf16[128,2048]{1,0:T(8,128)(2,1)}, u32[]{:S(2)}, u32[]{:S(2)}) collective-permute-start(bf16[128,2048]{1,0:T(8,128)(2,1)} %arrange.12), channel_id=1, source_target_pairs={{0,16},{8,24},{16,0},{24,8},{1,17},{9,25},{17,1},{25,9},{2,18},{10... | collective-permute-start | bytes 1572872 | tf_op jit(solution)/shard_map/ppermute | solution.py:647
  560.4 57.1 %collective-permute-start.53 = (bf16[128,2048]{1,0:T(8,128)(2,1)}, bf16[128,2048]{1,0:T(8,128)(2,1)}, u32[]{:S(2)}, u32[]{:S(2)}) collective-permute-start(bf16[128,2048]{1,0:T(8,128)(2,1)} %arrange.12), channel_id=1, source_target_pairs={{0,8},{8,0},{16,24},{24,16},{1,9},{9,1},{17,25},{25,17},{2,10},{10... | collective-permute-start | bytes 1572872 | tf_op jit(solution)/shard_map/ppermute | solution.py:647
  601.3 46.6 %collective-permute-start.44 = (bf16[512,2048]{1,0:T(8,128)(2,1)}, bf16[512,2048]{1,0:T(8,128)(2,1)}, u32[]{:S(2)}, u32[]{:S(2)}) collective-permute-start(bf16[512,2048]{1,0:T(8,128)(2,1)} %get-tuple-element.244), channel_id=1, source_target_pairs={{0,1},{1,0},{2,3},{3,2},{4,5},{5,4},{6,7},{7,6},{8,9},{9,8},{10,11... | collective-permute-start | bytes 6291464 | tf_op jit(solution)/shard_map/ppermute | solution.py:647
  653.1 122.8 %reduce-scatter.12.cloned.1.call-start = ((), (), s32[]{:S(2)}) async-start(), calls=%async_computation.20 | async-start | bytes 1966080 | tf_op jit(solution)/shard_map/reduce_scatter | solution.py:730
  668.8 51.0 %collective-permute-start.52 = (bf16[128,2048]{1,0:T(8,128)(2,1)}, bf16[128,2048]{1,0:T(8,128)(2,1)}, u32[]{:S(2)}, u32[]{:S(2)}) collective-permute-start(bf16[128,2048]{1,0:T(8,128)(2,1)} %get-tuple-element.265), channel_id=1, source_target_pairs={{0,2},{1,3},{2,0},{3,1},{4,6},{5,7},{6,4},{7,5},{8,10},{9,11},{10,... | collective-permute-start | bytes 1572872 | tf_op jit(solution)/shard_map/ppermute | solution.py:647
  670.4 60.7 %collective-permute-start.50 = (bf16[128,2048]{1,0:T(8,128)(2,1)}, bf16[128,2048]{1,0:T(8,128)(2,1)}, u32[]{:S(2)}, u32[]{:S(2)}) collective-permute-start(bf16[128,2048]{1,0:T(8,128)(2,1)} %get-tuple-element.262), channel_id=1, source_target_pairs={{0,4},{1,5},{2,6},{3,7},{4,0},{5,1},{6,2},{7,3},{8,12},{9,13},{10,... | collective-permute-start | bytes 1572872 | tf_op jit(solution)/shard_map/ppermute | solution.py:647
  699.3 44.5 %collective-permute-start.63 = (bf16[128,576]{1,0:T(8,128)(2,1)}, bf16[128,576]{1,0:T(8,128)(2,1)S(1)}, u32[]{:S(2)}, u32[]{:S(2)}) collective-permute-start(bf16[128,576]{1,0:T(8,128)(2,1)} %pad_maximum_fusion.5.refs_0_), channel_id=1, source_target_pairs={{0,2},{1,3},{2,0},{3,1},{4,6},{5,7},{6,4},{7,5},{8,10},{9,11},{10,... | collective-permute-start | bytes 442376 | tf_op jit(solution)/shard_map/ppermute | solution.py:647
  699.4 44.4 %collective-permute-start.64 = (bf16[128,576]{1,0:T(8,128)(2,1)}, bf16[128,576]{1,0:T(8,128)(2,1)S(1)}, u32[]{:S(2)}, u32[]{:S(2)}) collective-permute-start(bf16[128,576]{1,0:T(8,128)(2,1)} %pad_maximum_fusion.5.refs_0_), channel_id=1, source_target_pairs={{0,4},{1,5},{2,6},{3,7},{4,0},{5,1},{6,2},{7,3},{8,12},{9,13},{10,... | collective-permute-start | bytes 442376 | tf_op jit(solution)/shard_map/ppermute | solution.py:647
  (128 other events, 1966.9 us)
Sparse Core Ops, SparseCore 0:
  10.4 47.9 all-gather.4
  78.4 30.1 all-gather.10
  127.6 33.6 all-gather.6
  190.1 44.6 all-gather.8
  464.3 47.4 reduce-scatter.9
  527.5 27.4 reduce-scatter.7
  557.9 42.3 reduce-scatter.5
  653.2 25.2 reduce-scatter.13
  681.5 30.8 reduce-scatter.11

commit v6 on v5

--- a/solution.py
+++ b/solution.py
@@ -257,7 +257,7 @@
     )(query, key, value, row_position, column_position)
 
 
-def attend_back(query, key, value, result, result_grad, logsum, row_position, column_position, cosine, sine, w_up, latent_all, latent_gain, factor):
+def attend_back(query, key, value, result, result_grad, logsum, row_position, column_position, cosine, sine, w_up, latent_all, latent_gain, factor, columns):
     heads, length, _ = query.shape
     tile = 256
     steps = length // tile
@@ -304,7 +304,8 @@
                 rope = rope + key_grad[:, DN:wide].astype(F32)
             latent = dot_t(kv_ref[...], wu_ref[...])
             lp_ref[:, :R] = latent
-            lp_ref[:, R:] = rope
+            lp_ref[:, R : R + DR] = rope
+            lp_ref[:, R + DR :] = jnp.zeros((length, columns - R - DR), F32)
             t_ref[...] = jnp.sum(
                 latent * l_ref[...].astype(F32), axis=0, keepdims=True
             ) / lg_ref[...]
@@ -330,13 +331,13 @@
         out_specs=[
             pl.BlockSpec((tile, heads * wide), lambda i: (i, 0)),
             whole((length, heads * (DN + DV))),
-            whole((length, R + DR)),
+            whole((length, columns)),
             whole((1, R)),
         ],
         out_shape=[
             jax.ShapeDtypeStruct((length, heads * wide), BF),
             jax.ShapeDtypeStruct((length, heads * (DN + DV)), BF),
-            jax.ShapeDtypeStruct((length, R + DR), F32),
+            jax.ShapeDtypeStruct((length, columns), F32),
             jax.ShapeDtypeStruct((1, R), F32),
         ],
         scratch_shapes=[
@@ -494,16 +495,45 @@
     )(rows, cots, gate, up, down)
 
 
-def expert_weights(rows, cots, hidden, gate_grad, up_grad, piece, pieces, earlier):
+def shared(rows, cots, gate, up, down):
+    count, width = rows.shape
+    units = gate.shape[1]
+    tile = 256
+
+    def kernel(x_ref, c_ref, wg_ref, wu_ref, wd_ref, h_ref, gg_ref, ug_ref):
+        g = dot(x_ref[...], wg_ref[...])
+        u = dot(x_ref[...], wu_ref[...])
+        hidden_grad = dot_t(c_ref[...], wd_ref[...])
+        s = jax.nn.sigmoid(g)
+        silu = g * s
+        h_ref[...] = (silu * u).astype(BF)
+        gg_ref[...] = (hidden_grad * u * (s * (1.0 + g * (1.0 - s)))).astype(BF)
+        ug_ref[...] = (hidden_grad * silu).astype(BF)
+
+    row = pl.BlockSpec((tile, width), lambda i: (i, 0))
+    unit = pl.BlockSpec((tile, units), lambda i: (i, 0))
+    return pl.pallas_call(
+        kernel,
+        grid=(count // tile,),
+        in_specs=[row, row, whole(gate.shape), whole(up.shape), whole(down.shape)],
+        out_specs=[unit] * 3,
+        out_shape=[jax.ShapeDtypeStruct((count, units), BF)] * 3,
+        compiler_params=pltpu.CompilerParams(vmem_limit_bytes=LIMIT),
+        cost_estimate=LIGHT,
+        name="shared",
+    )(rows, cots, gate, up, down)
+
+
+def expert_weights(rows, cots, hidden, gate_grad, up_grad, piece, pieces, earlier, dtype=F32):
     count, width = rows.shape
     units = hidden.shape[1]
     tile = 256
 
     def kernel(x_ref, c_ref, h_ref, gg_ref, ug_ref, *refs):
         g_ref, u_ref, d_ref = refs[-3:]
-        g_ref[0] = t_dot(x_ref[...], gg_ref[...])
-        u_ref[0] = t_dot(x_ref[...], ug_ref[...])
-        d_ref[0] = t_dot(h_ref[...], c_ref[...])
+        g_ref[0] = t_dot(x_ref[...], gg_ref[...]).astype(dtype)
+        u_ref[0] = t_dot(x_ref[...], ug_ref[...]).astype(dtype)
+        d_ref[0] = t_dot(h_ref[...], c_ref[...]).astype(dtype)
 
     tall = pl.BlockSpec((1, tile, units), lambda i: (piece, i, 0))
     flat = pl.BlockSpec((1, units, tile), lambda i: (piece, 0, i))
@@ -515,9 +545,9 @@
         in_specs=[column, column] + [whole((count, units))] * 3 + [ANY] * len(kept),
         out_specs=[tall, tall, flat],
         out_shape=[
-            jax.ShapeDtypeStruct((pieces, width, units), F32),
-            jax.ShapeDtypeStruct((pieces, width, units), F32),
-            jax.ShapeDtypeStruct((pieces, units, width), F32),
+            jax.ShapeDtypeStruct((pieces, width, units), dtype),
+            jax.ShapeDtypeStruct((pieces, width, units), dtype),
+            jax.ShapeDtypeStruct((pieces, units, width), dtype),
         ],
         input_output_aliases={5 + n: n for n in range(len(kept))},
         compiler_params=pltpu.CompilerParams(vmem_limit_bytes=LIMIT),
@@ -672,17 +702,7 @@
         return self.pair(self.chips(x))
 
     def pair(self, evens):
-        rows, columns = evens[0].shape
-        everything = slice(None)
-        (even,) = arrange(
-            jnp.zeros((1,), jnp.int32),
-            evens,
-            [(rows * len(evens), columns)],
-            [
-                (k, everything, 0, lambda ref, k=k: (slice(k * rows, (k + 1) * rows), everything))
-                for k in range(len(evens))
-            ],
-        )
+        even = stacked(evens)
         return even, swap(even, "seq", 1)
 
     def scatter(self, even, odd):
@@ -714,12 +734,47 @@
             (0, 0, x),
             (1, 0, one),
             (2, 0, two),
-            (3, 0, self.send(after(two[:middle], *gates), 1)),
-            (3, middle, self.send(after(one[middle:], *gates), 2)),
+            (3, 0, self.send(part(after(two, *gates), 0, middle), 1)),
+            (3, middle, self.send(part(after(one, *gates), middle, middle), 2)),
         ]
 
     def others(self, x):
         return [x] + [self.send(x, j) for j in range(1, lax.axis_size("exp"))]
+
+def siblings(blocks, *gates):
+    got = {}
+    for k in range(len(blocks) - 1, 1, -1):
+        got[k] = swap(after(blocks[k], *got.values()), "seq", 1)
+    gates += tuple(got.values())
+    for k in range(min(2, len(blocks))):
+        got[k] = swap(after(blocks[k], *gates), "seq", 1)
+    return [got[k] for k in range(len(blocks))]
+
+
+def stacked(blocks):
+    rows, columns = blocks[0].shape
+    everything = slice(None)
+    (whole_array,) = arrange(
+        jnp.zeros((1,), jnp.int32),
+        blocks,
+        [(rows * len(blocks), columns)],
+        [
+            (k, everything, 0, lambda ref, k=k: (slice(k * rows, (k + 1) * rows), everything))
+            for k in range(len(blocks))
+        ],
+    )
+    return whole_array
+
+
+def part(x, start, rows):
+    (piece,) = arrange(
+        jnp.zeros((1,), jnp.int32),
+        [x],
+        [(rows, x.shape[1])],
+        [(0, (slice(start, start + rows),), 0, lambda ref: (slice(0, rows),))],
+    )
+    return piece
+
 
 def relative_order(count):
     chips = count // 2
@@ -770,7 +825,7 @@
     index = jnp.stack([lax.axis_index("exp"), seq]).astype(jnp.int32)
     ratio = w_query.shape[0] // w_kv_up.shape[0]
     slim = w_kv_up.shape[1] // ratio
-    columns = w_kv_down.shape[1]
+    columns = -(-w_kv_down.shape[1] // 128) * 128
     high = lax.reduce_precision(route_weights, 8, 7)
     middle = lax.reduce_precision(route_weights - high, 8, 7)
     low = route_weights - high - middle
@@ -779,7 +834,7 @@
     gains = jnp.concatenate([norm_gain, ffn_gain, latent_gain])
     packed = jnp.concatenate(
         [
-            w_kv_down,
+            jnp.pad(w_kv_down, ((0, 0), (0, columns - R - DR))),
             jnp.pad(gains, (0, columns - gains.shape[0]))[None, :],
             jnp.pad(
                 route_pack.reshape(4, lines, count).transpose(1, 0, 2).reshape(lines, 4 * count),
@@ -788,7 +843,7 @@
         ],
         axis=0,
     )
-    packed_even = jnp.stack(free.chips(packed))
+    packed_even = stacked(free.chips(packed))
     token_even = along.chips(tokens)
     first_all = lax.all_gather(
         jnp.concatenate(
@@ -805,22 +860,17 @@
         tiled=True,
     )
     packed_parts = across.others(packed_even)
-    packed_even = jnp.stack(packed_parts)
+    packed_even = stacked(packed_parts)
     packed_odd = swap(packed_even, "seq", 1)
-    token_odd = []
-    for x in token_even:
-        token_odd.append(swap(after(x, *token_odd), "seq", 1))
-    token_blocks = token_even + token_odd
-    output_even = along.chips(after(w_output, *token_odd, packed_odd))
     early = packed_parts[-1]
     gate_cols = lax.all_gather(after(shared_gate, early), "exp", axis=0, tiled=True)
     lift_cols = lax.all_gather(after(shared_up, early), "exp", axis=0, tiled=True)
     drop_rows = lax.all_gather(after(shared_down, early), "exp", axis=1, tiled=True)
-    grad_even = along.chips(out_grad)
 
     everything = slice(None)
     block_rows = width // n_exp
     plan = []
+    deep = gain_rows + 16
     for h in range(2):
         for j in range(n_exp):
             for k in range(chips):
@@ -831,7 +881,10 @@
                 plan.append(
                     (
                         h,
-                        (j, k, slice(0, gain_rows)),
+                        (
+                            slice((j * chips + k) * deep, (j * chips + k) * deep + gain_rows),
+                            slice(0, R + DR),
+                        ),
                         0,
                         lambda ref, where=where: (span(where(ref), gain_rows), everything),
                     )
@@ -839,7 +892,7 @@
                 plan.append(
                     (
                         h,
-                        (j, k, slice(gain_rows, gain_rows + 16)),
+                        (slice((j * chips + k) * deep + gain_rows, (j * chips + k + 1) * deep),),
                         1,
                         lambda ref, where=where: (where(ref),),
                     )
@@ -847,7 +900,7 @@
     down_full, extra_all = arrange(
         index,
         [packed_even, packed_odd],
-        [(width, columns), (n_exp * n_seq, 16, columns)],
+        [(width, R + DR), (n_exp * n_seq, 16, columns)],
         plan,
     )
     gain_first = extra_all[:, 0, :gain_rows].reshape(1, width).astype(F32)
@@ -858,7 +911,11 @@
         .astype(F32)
     )
     route_all = jnp.concatenate(
-        [packed_even[0, :, gain_rows + 1 :], packed_odd[0, :, gain_rows + 1 :]], axis=0
+        [
+            x[: chips * deep].reshape(chips, deep, columns)[:, gain_rows + 1 :]
+            for x in (packed_even, packed_odd)
+        ],
+        axis=0,
     )[:, :lines, : 4 * count]
     route_all = route_all.reshape(n_seq, lines, 4, count).transpose(0, 2, 1, 3)
     route_all = route_all.reshape(n_seq, 4 * lines, count).astype(F32)
@@ -894,6 +951,38 @@
             for g in range(ratio)
         ],
     )
+    token_odd = {}
+    for k in range(chips - 1, -1, -1):
+        token_odd[k] = swap(after(token_even[k], *token_odd.values()), "seq", 1)
+    token_odd = [token_odd[k] for k in range(chips)]
+    token_blocks = token_even + token_odd
+    output_even = free.chips(after(w_output, *token_odd, packed_odd))
+    grad_even = along.chips(after(out_grad, *token_odd))
+
+    column = jnp.stack(
+        [
+            ((other * n_seq + seq) * pieces + i) // parts_per
+            for i in range(pieces)
+            for other in range(n_exp)
+        ]
+    )
+    kinds = n_exp * pieces
+    named = route_all[:, None, :TOP, :].astype(jnp.int32) == column[None, :, None, None]
+    matched = jnp.any(named, axis=2)
+    match_weight = jnp.sum(jnp.where(named, route_all[:, None, TOP:, :], 0.0), axis=2)
+    earlier = (jnp.arange(count)[:, None] < jnp.arange(count)[None, :]).astype(BF)
+    rank = jnp.dot(matched.astype(BF), earlier, preferred_element_type=F32).astype(jnp.int32)
+    chosen = (rank[:, :, None, :] == jnp.arange(CAP, dtype=jnp.int32)[None, None, :, None]) & (
+        matched[:, :, None, :]
+    )
+    select = chosen.astype(BF).reshape(n_seq, kinds * CAP, count)
+    weighted = jnp.where(chosen, match_weight[:, :, None, :], 0.0).reshape(
+        n_seq, kinds * CAP, count
+    )
+    slot_weight = jnp.sum(weighted, axis=2, keepdims=True)
+    weighted_high = weighted.astype(BF)
+    weighted_low = (weighted - weighted_high.astype(F32)).astype(BF)
+
     positions = jnp.concatenate(
         [(seq ^ r) * count + jnp.arange(count, dtype=jnp.int32) for r in order]
     )
@@ -901,6 +990,7 @@
     cosine_table, sine_table = rope_tables(positions, DR)
     cosine_wide = jnp.concatenate([cosine_table, cosine_table], axis=1)
     sine_wide = jnp.concatenate([-sine_table, sine_table], axis=1)
+    gain_first = after(gain_first, select, slot_weight, column_position)
     normed_one, latent_all, latent_raw, query_heads, key_heads, value_heads = project(
         token_blocks,
         gain_first,
@@ -912,7 +1002,7 @@
         sine_wide,
         heads,
     )
-    output_even = jnp.concatenate([after(x, normed_one) for x in output_even], axis=0)
+    output_even = stacked([after(x, normed_one) for x in output_even])
     result, logsum = attend(
         query_heads, key_heads, value_heads, row_position, column_position, factor
     )
@@ -939,69 +1029,30 @@
 
     grad_even, grad_odd = along.pair([after(x, result) for x in grad_even])
 
-    column = jnp.stack(
-        [
-            ((other * n_seq + seq) * pieces + i) // parts_per
-            for i in range(pieces)
-            for other in range(n_exp)
-        ]
-    )
-    kinds = n_exp * pieces
-    named = route_all[:, None, :TOP, :].astype(jnp.int32) == column[None, :, None, None]
-    matched = jnp.any(named, axis=2)
-    match_weight = jnp.sum(jnp.where(named, route_all[:, None, TOP:, :], 0.0), axis=2)
-    earlier = (jnp.arange(count)[:, None] < jnp.arange(count)[None, :]).astype(BF)
-    rank = jnp.dot(matched.astype(BF), earlier, preferred_element_type=F32).astype(jnp.int32)
-    chosen = (rank[:, :, None, :] == jnp.arange(CAP, dtype=jnp.int32)[None, None, :, None]) & (
-        matched[:, :, None, :]
-    )
-    select = chosen.astype(BF).reshape(n_seq, kinds * CAP, count)
-    weighted = jnp.where(chosen, match_weight[:, :, None, :], 0.0).reshape(
-        n_seq, kinds * CAP, count
-    )
-    slot_weight = jnp.sum(weighted, axis=2, keepdims=True)
-    weighted_high = weighted.astype(BF)
-    weighted_low = (weighted - weighted_high.astype(F32)).astype(BF)
-
     def give(rows):
         return lax.all_to_all(rows, "exp", split_axis=0, concat_axis=0, tiled=True)
 
-    (grad_rows,) = arrange(
-        index,
-        [grad_even, grad_odd],
-        [(length, width)],
-        [
-            (h, everything, 0, lambda ref, h=h: (slice(h * half, (h + 1) * half), everything))
-            for h in range(2)
-        ],
-    )
+    grad_rows = stacked([grad_even, grad_odd])
     send_cots = dispatch(select, grad_rows, slot_weight, pieces)
     received_grad = [give(rows) for rows in send_cots]
 
     result_even = along.chips(result)
     gathered = (gate_cols, lift_cols, drop_rows)
-    result_even = [after(x, *send_cots, *gathered) for x in result_even]
-    result_blocks = result_even + [swap(x, "seq", 1) for x in result_even]
+    result_even = [after(x, received_grad[0], *gathered) for x in result_even]
+    result_blocks = result_even + siblings(result_even)
     normed_two, residual = add_norm(
         token_blocks,
-        [after(result_blocks[0], received_grad[0])] + result_blocks[1:],
+        result_blocks,
         output_even,
         output_odd,
         gain_second,
     )
     inverse_two = inverse_rms(residual)
-    send_rows = dispatch(select, normed_two, None, pieces)
+    send_rows = dispatch(select, after(normed_two, *received_grad), None, pieces)
     received = [give(after(send_rows[0], *received_grad))]
 
 
-    shared_rows = after(normed_two, *send_rows)
-    shared_gate_raw = dot(shared_rows, gate_cols)
-    shared_up_raw = dot(shared_rows, lift_cols)
-    shared_hidden = (jax.nn.silu(shared_gate_raw) * shared_up_raw).astype(BF)
-    shared_hidden_grad = dot_t(grad_rows, drop_rows)
-    sgate_grad = (shared_hidden_grad * shared_up_raw * silu_slope(shared_gate_raw)).astype(BF)
-    sup_grad = (shared_hidden_grad * jax.nn.silu(shared_gate_raw)).astype(BF)
-    received += [give(after(rows, sgate_grad, sup_grad)) for rows in send_rows[1:]]
+    received += [give(after(x, received[0])) for x in send_rows[1:]]
 
     slot_rows = n_exp * n_seq * CAP
     pairs = []
@@ -1015,11 +1066,20 @@
         grads_back.append(give(input_grad.reshape(n_exp, n_seq * CAP, width)))
         results_back.append(expert_result.reshape(n_exp, n_seq * CAP, width))
         kept.append((rows, cots, *saved))
+    shared_rows = after(normed_two, input_grad)
+    shared_hidden, sgate_grad, sup_grad = shared(
+        shared_rows, grad_rows, gate_cols, lift_cols, drop_rows
+    )
     two_products = [(sgate_grad, gate_cols, True), (sup_grad, lift_cols, True)]
     expert_grads = expert_weights(
         after(kept[0][0], input_grad), *kept[0][1:], 0, pieces, None
     )
-    select = after(select, *expert_grads)
+    gate_part, lift_part, drop_part = expert_weights(
+        shared_rows, grad_rows, shared_hidden, sgate_grad, sup_grad, 0, 1, None, BF
+    )
+    token_wide = tokens.astype(F32)
+    token_inverse = inverse_rms(token_wide)
+    select = after(select, *expert_grads, gate_part, lift_part, drop_part, token_inverse)
     two_odd = combine(1, [select], grads_back, two_products, BF)
     two_even = combine(0, [select], grads_back, two_products, F32)
     two_blocks = along.begin(two_even, two_odd)
@@ -1032,11 +1092,27 @@
             )
     results_back = back
     expert_gate_grad, expert_up_grad, expert_down_grad = expert_grads
-    two_grad = along.finish(two_blocks, *expert_grads)
-    gate_out = sum_exp(t_dot(after(shared_rows, *two_blocks), sgate_grad), 0)
-    lift_out = sum_exp(t_dot(after(shared_rows, *two_blocks), sup_grad), 0)
-    drop_out = sum_exp(t_dot(after(shared_hidden, *two_blocks), grad_rows), 1)
-
+    (own_heads,) = arrange(
+        index,
+        [after(result_blocks[0], *two_blocks)] + result_blocks[1:],
+        [(count, H * DV)],
+        [
+            (
+                p,
+                (slice(p * count, (p + 1) * count), everything),
+                0,
+                lambda ref, p=p: (everything, slice(p * heads * DV, (p + 1) * heads * DV)),
+            )
+            for p in range(n_seq)
+        ],
+    )
+    gate_part, lift_part, drop_part = [
+        after(x[0], *two_blocks) for x in (gate_part, lift_part, drop_part)
+    ]
+    gate_out, lift_out, drop_out = sum_exp(gate_part, 0), sum_exp(lift_part, 0), sum_exp(drop_part, 1)
+    two_grad = along.finish(
+        two_blocks, *expert_grads, own_heads
+    )
     residual_norm_grad, second_terms = norm_back(
         two_grad, residual, inverse_two, gain_second
     )
@@ -1055,34 +1131,10 @@
     attention_grad = jnp.concatenate(
         [jnp.stack([pair[0] for pair in pairs]), other_half], axis=0
     ).reshape(length, wide)
-    (own_heads,) = arrange(
-        index,
-        [after(result_blocks[0], *two_blocks)] + result_blocks[1:],
-        [(count, H * DV)],
-        [
-            (
-                p,
-                (slice(p * count, (p + 1) * count), everything),
-                0,
-                lambda ref, p=p: (everything, slice(p * heads * DV, (p + 1) * heads * DV)),
-            )
-            for p in range(n_seq)
-        ],
-    )
     mine = lax.axis_index("exp")
-    late = Lane("exp", 3)
-    attention_parts = late.others(after(own_heads, attention_grad))
-    column_blocks = [
-        lax.dynamic_slice_in_dim(residual_half, (mine ^ j) * block_rows, block_rows, 1)
-        for j in range(n_exp)
-    ]
-    column_blocks = [column_blocks[0]] + [
-        late.send(column_blocks[j], j) for j in range(1, n_exp)
-    ]
-
     out_products = [(shared_hidden, drop_rows, False)]
     out_masks = [weighted_high, weighted_low]
-    out_masks = [after(mask, *stacks) for mask in out_masks]
+    out_masks = [after(mask, *stacks, *pairs[1:]) for mask in out_masks]
     out_odd = combine(1, out_masks, results_back, out_products, BF)
     out_even = combine(0, out_masks, results_back, out_products, F32)
     out_blocks = along.begin(out_even, out_odd)
@@ -1103,15 +1155,17 @@
         latent_all,
         latent_wide,
         factor,
-    )
-    query_in_grad = after(query_in_grad, *output_got[:2])
+        columns,
+    )
+    late = Lane("exp", 2)
+    attention_parts = late.others(after(own_heads, query_in_grad))
     one_odd, odd_sum = query_back(1, query_in_grad, first_all, normed_one, gain_first, BF)
     one_even, even_sum = query_back(0, query_in_grad, first_all, normed_one, gain_first, F32)
     sums = jnp.concatenate(
         [
             (odd_sum + even_sum).reshape(n_exp, n_seq, gain_rows),
             jnp.sum(second_terms, axis=0).reshape(n_exp, n_seq, gain_rows),
-            latent_sum.reshape(n_exp, n_seq, latent_rows_local),
+            after(latent_sum, *output_got[:2], *attention_parts[1:]).reshape(n_exp, n_seq, latent_rows_local),
         ],
         axis=2,
     )
@@ -1123,18 +1177,25 @@
     )
     latent_part = jnp.concatenate([latent_part.reshape(n_seq, count, columns), sums], axis=1)
     latent_part = latent_part.reshape(n_seq * (count + 16), columns)
-    output_part = t_dot(
-        jnp.concatenate([after(x, query_in_grad) for x in attention_parts], axis=0),
-        jnp.concatenate([after(x, query_in_grad) for x in column_blocks], axis=0),
-    )
-    output_blocks = along.begin(output_part[: H * DV // 2], output_part[H * DV // 2 :])
     latent_grad = along.scatter(
         latent_part[: chips * (count + 16)], latent_part[chips * (count + 16) :]
     )
     one_blocks = along.begin(one_even, one_odd)
     one_got = [along.send(one_blocks[k], 2 * k) for k in range(chips - 1, 0, -1)]
-    up_part = t_dot(after(latent_all, *one_blocks), kv_grad).astype(BF)
-    query_part = t_dot(after(normed_one, *one_blocks), query_in_grad).astype(BF)
+    column_blocks = [
+        lax.dynamic_slice_in_dim(residual_half, (mine ^ j) * block_rows, block_rows, 1)
+        for j in range(n_exp)
+    ]
+    column_blocks = [column_blocks[0]] + [
+        swap(after(column_blocks[j], one_got[-1]), "exp", j) for j in range(1, n_exp)
+    ]
+    output_part = t_dot(
+        jnp.concatenate([after(x, *one_blocks) for x in attention_parts], axis=0),
+        jnp.concatenate([after(x, *one_blocks) for x in column_blocks], axis=0),
+    )
+    output_blocks = along.begin(output_part[: H * DV // 2], output_part[H * DV // 2 :])
+    up_part = t_dot(after(latent_all, one_odd), kv_grad).astype(BF)
+    query_part = t_dot(after(normed_one, one_odd), query_in_grad).astype(BF)
     up_out = sum_exp(up_part, 0)
     query_out = sum_exp(query_part, 0)
     sums = latent_grad[count, : n_exp * many].reshape(n_exp, 1, many)
@@ -1145,14 +1206,17 @@
     down_rows = jnp.concatenate(
         [
             latent_raw_grad,
-            rotate(latent_grad[:, R:], cosine_table[:count], -sine_table[:count]),
+            rotate(latent_grad[:, R : R + DR], cosine_table[:count], -sine_table[:count]),
+            jnp.zeros((count, columns - R - DR), F32),
         ],
         axis=1,
     ).astype(BF)
-    wide_got = [free.send(output_blocks[k], 2 * k) for k in range(chips - 1, 0, -1)]
     down_even, down_odd = free.pair(
-        [after(x, *one_got, *wide_got) for x in free.chips(down_rows)]
-    )
+        [after(x, *one_got, *output_blocks) for x in free.chips(down_rows)]
+    )
+    wide_got = [
+        swap(after(output_blocks[k], down_even), "seq", 2 * k) for k in range(chips - 1, 0, -1)
+    ]
     down_part = down_weights(index, normed_one, down_even, down_odd, n_exp, n_seq, gain_rows)
     down_part = jnp.concatenate(
         [
@@ -1165,7 +1229,7 @@
     for j in range(1, n_exp):
         piece = lax.dynamic_index_in_dim(down_part, mine ^ j, 0, keepdims=False).astype(BF)
         down_sum = down_sum + swap(piece, "exp", j).astype(F32)
-    down_out = down_sum[:gain_rows]
+    down_out = down_sum[:gain_rows, : R + DR]
     small = down_sum[gain_rows, :many]
     first_out = small[:gain_rows] + jnp.sum(
         w_kv_down.astype(F32) * down_out, axis=1
@@ -1182,10 +1246,9 @@
     for block in one_got:
         block = after(block, up_part, query_part, gate_out, lift_out, drop_out)
         one_grad = one_grad + block.astype(F32)
-    down_back = dot_t(down_rows, down_full)
-    token_wide = tokens.astype(F32)
+    down_back = dot_t(down_rows[:, : R + DR], down_full)
     token_norm_grad, _ = norm_back(
-        one_grad + down_back, token_wide, inverse_rms(token_wide), gain_first
+        one_grad + down_back, token_wide, token_inverse, gain_first
     )
     tokens_grad = (residual_grad + token_norm_grad).astype(BF)
     return (

time: 795 us -> 820 us (1.031)
  Pallas kernels: 222 us -> 255 us
  blocking collectives: 0 us -> 30.4 us
  matrix products: 43.6 us -> 18.8 us
  starting transfers between devices: 137 us -> 124 us
    all_to_all x0 -> x1, blocking collectives: none -> 30.4 us  [give(): return lax.all_to_all(rows, 'exp', split_axis=0, concat_axis=0, tiled=True)]
    all_to_all x8 -> x7, waiting for transfers between devices: 56.3 us -> 27.6 us  [give(): return lax.all_to_all(rows, 'exp', split_axis=0, concat_axis=0, tiled=True)]
    ppermute x70, waiting for transfers between devices: 185 us -> 204 us  [swap(): return lax.ppermute(x, axis, [(i, i ^ mask) for i in range(n)])]
    all_gather x1, waiting for transfers between devices: 17.5 us -> 30.6 us  [shards(): lax.all_gather(after(shared_up, early), 'exp', axis=0, tiled=True)]
    dot_general x6 -> x3, matrix products: 22.2 us -> 9.52 us  [t_dot(): lax.dot_general(a, b, (((0,), (0,)), ((), ())), preferred_element_type=F32)]
    pallas_call x2 -> x3, Pallas kernels: 30 us -> 41.4 us  [expert_weights(): pl.pallas_call(kernel, grid=(width // tile,), in_specs=[column, column] +...]
    pallas_call x0 -> x1, Pallas kernels: none -> 11.1 us  [shared(): pl.pallas_call(kernel, grid=(count // tile,), in_specs=[row, row, whole(g...]
    pallas_call x7 -> x12, Pallas kernels: 23.7 us -> 34.2 us  [arrange(): pl.pallas_call(kernel, out_shape=[jax.ShapeDtypeStruct(s, BF) for s in ou...]
  transfers between devices with their start and end apart: 87 -> 86, of which waited for: 33 -> 31; matrix products, arithmetic and copies ran while one was open for 16% -> 12% of each run, Pallas kernels for 27% -> 30%
where the time goes in v6:
time: 820 us; the launch traced here: 813 us
  waiting for transfers between devices  262 us (32%)
  Pallas kernels  255 us (31%)
  starting transfers between devices  124 us (15%)
  other arithmetic  62.1 us (8%)
  local copies, waits for them, and re-layouts  45 us (5%)
  blocking collectives  30.4 us (4%)
  matrix products  18.8 us (2%)
  between operations  15.2 us (2%)
    ppermute x70, waiting for transfers between devices, swap(): return lax.ppermute(x, axis, [(i, i ^ mask) for i in range(n)])  204 us
    ppermute x70, starting transfers between devices, swap(): return lax.ppermute(x, axis, [(i, i ^ mask) for i in range(n)])  93.5 us
    pallas_call x2, Pallas kernels, expert(): pl.pallas_call(kernel, grid=(count // tile,), in_specs=[block(width), blo...  55.2 us
    pallas_call x3, Pallas kernels, expert_weights(): pl.pallas_call(kernel, grid=(width // tile,), in_specs=[column, column] +...  41.4 us
    pallas_call x12, Pallas kernels, arrange(): pl.pallas_call(kernel, out_shape=[jax.ShapeDtypeStruct(s, BF) for s in ou...  34.2 us
    all_gather x1, waiting for transfers between devices, shards(): lax.all_gather(after(shared_up, early), 'exp', axis=0, tiled=True)  30.6 us
    all_to_all x1, blocking collectives, give(): return lax.all_to_all(rows, 'exp', split_axis=0, concat_axis=0, tiled=True)  30.4 us
    all_to_all x7, starting transfers between devices, give(): return lax.all_to_all(rows, 'exp', split_axis=0, concat_axis=0, tiled=True)  28.9 us
  transfers between devices with their start and end apart: 86, of which 31 were waited for; matrix products, arithmetic and copies ran while one was open for 12% of the time, Pallas kernels for 30%

profile of v6, /device:TPU:0, one launch (start us, length us, event | category | flops | bytes accessed | tf_op | source)
XLA Modules:
  0.0 812.9 jit_solution(10180031006469000663)
XLA Ops:
  34.9 14.1 %collective-permute-done.12.refs_3_ = bf16[320,640]{1,0:T(8,128)(2,1)S(1)} collective-permute-done((bf16[320,640]{1,0:T(8,128)(2,1)}, bf16[320,640]{1,0:T(8,128)(2,1)S(1)}, u32[]{:S(2)}, u32[]{:S(2)}) %collective-permute-start.12) | collective-permute-done | bytes 409632 | tf_op jit(solution)/shard_map/ppermute | solution.py:677
  66.4 11.7 %collective-permute-done.2.refs_2_.refs_10_ = bf16[128,2048]{1,0:T(8,128)(2,1)S(1)} collective-permute-done((bf16[128,2048]{1,0:T(8,128)(2,1)S(1)}, bf16[128,2048]{1,0:T(8,128)(2,1)S(1)}, u32[]{:S(2)}, u32[]{:S(2)}) %collective-permute-start.2) | collective-permute-done | bytes 524320 | tf_op jit(solution)/shard_map/ppermute | solution.py:677
  108.7 14.6 %project.1 = (bf16[1024,2048]{1,0:T(8,128)(2,1)}, bf16[1024,512]{1,0:T(8,128)(2,1)}, f32[1024,512]{1,0:T(8,128)}, bf16[2,1024,256]{2,1,0:T(8,128)(2,1)}, bf16[2,...) custom-call(f32[1,2048]{1,0:T(1,128)} %reshape.282.g_ref, bf16[2048,576]{1,0:T(8,128)(2,1)} %get-tuple-element.172.wd_ref, ...), custom_call_target="tpu_custom_call" | custom-call | tf_op jit(solution)/shard_map/project/pallas_call | solution.py:158
  131.0 8.3 %attend.1 = (bf16[1024,256]{1,0:T(8,128)(2,1)}, f32[2,1024]{1,0:T(2,128)}) custom-call(bf16[2,1024,256]{2,1,0:T(8,128)(2,1)} %get-tuple-element.183.q_ref, bf16[2,1024,256]{2,1,0:T(8,128)(2,1)} %get-tuple-element.184.k_ref, bf16[2,1024,128]{2,1,0:T(8,128)(2,1)} %get-tuple-element.185.v_ref, s32[1,1024]{1,0:T(1,128)} %bitcast.181, s32[1024,1]{1,0:T(8,128)} %copy.60.column_ref), custom_call_target="tpu_custom_call" | custom-call | tf_op jit(solution)/shard_map/attend/pallas_call | solution.py:236
  139.6 29.0 %collective-permute-done.20.refs_2_ = bf16[128,2048]{1,0:T(8,128)(2,1)} collective-permute-done((bf16[128,2048]{1,0:T(8,128)(2,1)S(1)}, bf16[128,2048]{1,0:T(8,128)(2,1)}, u32[]{:S(2)}, u32[]{:S(2)}) %collective-permute-start.20) | collective-permute-done | bytes 524320 | tf_op jit(solution)/shard_map/ppermute | solution.py:677
  179.6 10.4 %collective-permute-done.23.refs_4_ = bf16[512,512]{1,0:T(8,128)(2,1)S(1)} collective-permute-done((bf16[512,512]{1,0:T(8,128)(2,1)}, bf16[512,512]{1,0:T(8,128)(2,1)S(1)}, u32[]{:S(2)}, u32[]{:S(2)}) %collective-permute-start.23) | collective-permute-done | bytes 524320 | tf_op jit(solution)/shard_map/ppermute | solution.py:677
  205.1 7.5 dispatch.2
  217.9 30.6 %all-gather.9.cloned.1.call-done.wu_ref.refs_6_ = bf16[2048,352]{1,0:T(8,128)(2,1)} async-done(((bf16[512,352]{1,0:T(8,128)(2,1)}), bf16[2048,352]{1,0:T(8,128)(2,1)}) %all-gather.9.cloned.1.call-update) | async-done | bytes 1441808 | tf_op jit(solution)/shard_map/all_gather | solution.py:867
  262.7 11.1 %collective-permute-done.26.refs_1_ = bf16[1024,256]{1,0:T(8,128)(2,1)} collective-permute-done((bf16[1024,256]{1,0:T(8,128)(2,1)S(1)}, bf16[1024,256]{1,0:T(8,128)(2,1)}, u32[]{:S(2)}, u32[]{:S(2)}) %collective-permute-start.26) | collective-permute-done | bytes 524320 | tf_op jit(solution)/shard_map/ppermute | solution.py:677
  276.9 18.2 %add_norm.1 = (bf16[1024,2048]{1,0:T(8,128)(2,1)}, f32[128,2048]{1,0:T(8,128)}) custom-call(bf16[1024,2048]{1,0:T(8,128)(2,1)} %arrange.19.we_ref, bf16[1024,2048]{1,0:T(8,128)(2,1)} %collective-permute-done.24.wo_ref, f32[1,2048]{1,0:T(1,128)} %reshape.285.g_ref, bf16[1024,256]{1,0:T(8,128)(2,1)} %get-tuple-element.248.refs_0_.o_ref, ...), custom_call_target="tpu_custom_call" | custom-call | tf_op jit(solution)/shard_map/add_norm/pallas_call | solution.py:391
  295.1 8.0 dispatch.3
  303.1 30.4 %all_to_all.40 = bf16[4,128,2048]{2,1,0:T(8,128)(2,1)} all-to-all(bf16[4,128,2048]{2,1,0:T(8,128)(2,1)} %get-tuple-element.218), channel_id=1, replica_groups=mesh['exp'=4,'seq'=8] {'exp'}, dimensions={0} | all-to-all | bytes 4194304 | tf_op jit(solution)/shard_map/all_to_all | solution.py:1033
  337.1 27.6 %expert.3 = (bf16[512,2048]{1,0:T(8,128)(2,1)}, bf16[512,2048]{1,0:T(8,128)(2,1)}, bf16[512,1408]{1,0:T(8,128)(2,1)}, bf16[512,1408]{1,0:T(8,128)(2,1)}, bf16[512,1408]{1,0:T(8,128)(2,1)}) custom-call(bf16[512,2048]{1,0:T(8,128)(2,1)} %bitcast.164, bf16[512,2048]{1,0:T(8,128)(2,1)} %bitcast.162, bf16[2,2048,1408]{2,1,0:T(8,128)(2,1)} %gate_hbm.3, ...), custom_call_target="tpu_custom_call" | custom-call | tf_op jit(solution)/shard_map/expert/pallas_call | solution.py:478
  369.5 27.6 %expert.2 = (bf16[512,2048]{1,0:T(8,128)(2,1)}, bf16[512,2048]{1,0:T(8,128)(2,1)}, bf16[512,1408]{1,0:T(8,128)(2,1)}, bf16[512,1408]{1,0:T(8,128)(2,1)}, bf16[512,1408]{1,0:T(8,128)(2,1)}) custom-call(bf16[512,2048]{1,0:T(8,128)(2,1)} %bitcast.160, bf16[512,2048]{1,0:T(8,128)(2,1)} %bitcast.158, bf16[2,2048,1408]{2,1,0:T(8,128)(2,1)} %gate_hbm.3, ...), custom_call_target="tpu_custom_call" | custom-call | tf_op jit(solution)/shard_map/expert/pallas_call | solution.py:478
  401.8 11.1 %shared.1 = (bf16[1024,352]{1,0:T(8,128)(2,1)}, bf16[1024,352]{1,0:T(8,128)(2,1)}, bf16[1024,352]{1,0:T(8,128)(2,1)}) custom-call(bf16[1024,2048]{1,0:T(8,128)(2,1)} %get-tuple-element.229.x_ref, bf16[1024,2048]{1,0:T(8,128)(2,1)} %arrange.21.x_ref.c_ref, bf16[2048,352]{1,0:T(8,128)(2,1)} %all-gather.7.cloned.1.call-done.wg_ref.refs_4_, ...), custom_call_target="tpu_custom_call" | custom-call | tf_op jit(solution)/shard_map/shared/pallas_call | solution.py:515
  412.9 11.5 %expert_weights.4 = (bf16[1,2048,352]{2,1,0:T(8,128)(2,1)}, bf16[1,2048,352]{2,1,0:T(8,128)(2,1)}, bf16[1,352,2048]{2,1,0:T(8,128)(2,1)}) custom-call(bf16[1024,2048]{1,0:T(8,128)(2,1)} %get-tuple-element.229.x_ref, bf16[1024,2048]{1,0:T(8,128)(2,1)} %arrange.21.x_ref.c_ref, bf16[1024,352]{1,0:T(8,128)(2,1)} %get-tuple-element.230.h_ref.refs_4_, ...), custom_call_target="tpu_custom_call" | custom-call | tf_op jit(solution)/shard_map/expert_weights/pallas_call | solution.py:542
  424.3 14.9 %expert_weights.3 = (f32[2,2048,1408]{2,1,0:T(8,128)}, f32[2,2048,1408]{2,1,0:T(8,128)}, f32[2,1408,2048]{2,1,0:T(8,128)}) custom-call(bf16[512,2048]{1,0:T(8,128)(2,1)} %bitcast.165, bf16[512,2048]{1,0:T(8,128)(2,1)} %bitcast.163, bf16[512,1408]{1,0:T(8,128)(2,1)} %get-tuple-element.223.h_ref, bf16[512,1408]{1,0:T(8,128)(2,1)} %get-tuple-element.224.gg_ref, ...), custom_call_target="tpu_custom_call" | custom-call | tf_op jit(solution)/shard_map/expert_weights/pallas_call | solution.py:542
  470.4 25.5 %all-to-all-done.6.refs_2_ = bf16[4,128,2048]{2,1,0:T(8,128)(2,1)S(1)} async-done(((bf16[4,128,2048]{2,1,0:T(8,128)(2,1)}), bf16[4,128,2048]{2,1,0:T(8,128)(2,1)S(1)}, u32[]{:S(2)}, u32[]{:S(2)}) %all-to-all-start.6) | async-done | bytes 2097184 | tf_op jit(solution)/shard_map/all_to_all | solution.py:1033
  500.7 15.0 %expert_weights.5 = (f32[2,2048,1408]{2,1,0:T(8,128)}, f32[2,2048,1408]{2,1,0:T(8,128)}, f32[2,1408,2048]{2,1,0:T(8,128)}) custom-call(bf16[512,2048]{1,0:T(8,128)(2,1)} %bitcast.161, bf16[512,2048]{1,0:T(8,128)(2,1)} %bitcast.159, bf16[512,1408]{1,0:T(8,128)(2,1)} %get-tuple-element.242.h_ref, ...), custom_call_target="tpu_custom_call", output_to_operand_aliasing={{0}: (5, {}), {1}: (6, {}), {2}: (7, {})} | custom-call | tf_op jit(solution)/shard_map/expert_weights/pallas_call | solution.py:542
  558.1 14.0 %attend_back.1 = (bf16[1024,384]{1,0:T(8,128)(2,1)}, bf16[1024,512]{1,0:T(8,128)(2,1)}, f32[1024,640]{1,0:T(8,128)}, f32[1,512]{1,0:T(1,128)}) custom-call(bf16[2,1024,256]{2,1,0:T(8,128)(2,1)} %get-tuple-element.183.q_ref, bf16[2,1024,256]{2,1,0:T(8,128)(2,1)} %get-tuple-element.184.k_ref, bf16[2,1024,128]{2,1,0:T(8,128)(2,1)} %get-tuple-element.185.v_ref, ...), custom_call_target="tpu_custom_call" | custom-call | tf_op jit(solution)/shard_map/attend_back/pallas_call | solution.py:313
  601.5 18.4 %collective-permute-done.44 = bf16[128,2048]{1,0:T(8,128)(2,1)} collective-permute-done((bf16[128,2048]{1,0:T(8,128)(2,1)}, bf16[128,2048]{1,0:T(8,128)(2,1)}, u32[]{:S(2)}, u32[]{:S(2)}) %collective-permute-start.44) | collective-permute-done | bytes 524320 | tf_op jit(solution)/shard_map/ppermute | solution.py:677
  634.0 11.2 %collective-permute-start.45 = (bf16[128,2048]{1,0:T(8,128)(2,1)}, bf16[128,2048]{1,0:T(8,128)(2,1)S(1)}, u32[]{:S(2)}, u32[]{:S(2)}) collective-permute-start(bf16[128,2048]{1,0:T(8,128)(2,1)} %get-tuple-element.271), channel_id=1, source_target_pairs={{0,2},{1,3},{2,0},{3,1},{4,6},{5,7},{6,4},{7,5},{8,10},{9,11},{10,... | collective-permute-start | bytes 1572872 | tf_op jit(solution)/shard_map/ppermute | solution.py:677
  721.2 31.1 %collective-permute-done.53 = bf16[128,2048]{1,0:T(8,128)(2,1)} collective-permute-done((bf16[128,2048]{1,0:T(8,128)(2,1)}, bf16[128,2048]{1,0:T(8,128)(2,1)}, u32[]{:S(2)}, u32[]{:S(2)}) %collective-permute-start.53) | collective-permute-done | bytes 524320 | tf_op jit(solution)/shard_map/ppermute | solution.py:677
  761.3 9.2 %collective-permute-done.61.refs_2_ = bf16[128,640]{1,0:T(8,128)(2,1)S(1)} collective-permute-done((bf16[128,640]{1,0:T(8,128)(2,1)S(1)}, bf16[128,640]{1,0:T(8,128)(2,1)S(1)}, u32[]{:S(2)}, u32[]{:S(2)}) %collective-permute-start.61) | collective-permute-done | bytes 163872 | tf_op jit(solution)/shard_map/ppermute | solution.py:677
  (463 shorter events, 386.8 us)
Async XLA Ops:
  7.2 99.0 %all-gather.5.cloned.1.call-start = ((), (), s32[]{:S(2)}) async-start(), calls=%async_computation.13 | async-start | bytes 2621440 | tf_op jit(solution)/shard_map/all_gather | solution.py:848
  10.0 208.0 %all-gather.11.cloned.1.call-start = ((), (), s32[]{:S(2)}) async-start(), calls=%async_computation.16 | async-start | bytes 1802240 | tf_op jit(solution)/shard_map/all_gather | solution.py:868
  49.1 168.9 %all-gather.7.cloned.1.call-start = ((), (), s32[]{:S(2)}) async-start(), calls=%async_computation.14 | async-start | bytes 1966080 | tf_op jit(solution)/shard_map/all_gather | solution.py:866
  90.0 158.5 %all-gather.9.cloned.1.call-start = ((), (), s32[]{:S(2)}) async-start(), calls=%async_computation.15 | async-start | bytes 1966080 | tf_op jit(solution)/shard_map/all_gather | solution.py:867
  105.0 63.6 %collective-permute-start.19 = (bf16[128,2048]{1,0:T(8,128)(2,1)S(1)}, bf16[128,2048]{1,0:T(8,128)(2,1)S(1)}, u32[]{:S(2)}, u32[]{:S(2)}) collective-permute-start(bf16[128,2048]{1,0:T(8,128)(2,1)S(1)} %copy-done.11), channel_id=1, source_target_pairs={{0,2},{1,3},{2,0},{3,1},{4,6},{5,7},{6,4},{7,5},{8,10},{9,11},{10,... | collective-permute-start | bytes 1572872 | tf_op jit(solution)/shard_map/ppermute | solution.py:677
  123.3 45.3 %collective-permute-start.20 = (bf16[128,2048]{1,0:T(8,128)(2,1)S(1)}, bf16[128,2048]{1,0:T(8,128)(2,1)}, u32[]{:S(2)}, u32[]{:S(2)}) collective-permute-start(bf16[128,2048]{1,0:T(8,128)(2,1)S(1)} %copy-done.11), channel_id=1, source_target_pairs={{0,4},{1,5},{2,6},{3,7},{4,0},{5,1},{6,2},{7,3},{8,12},{9,13},{10,... | collective-permute-start | bytes 1572872 | tf_op jit(solution)/shard_map/ppermute | solution.py:677
  129.2 43.2 %collective-permute-start.17 = (bf16[1024,512]{1,0:T(8,128)(2,1)}, bf16[1024,512]{1,0:T(8,128)(2,1)S(1)}, u32[]{:S(2)}, u32[]{:S(2)}) collective-permute-start(bf16[1024,512]{1,0:T(8,128)(2,1)} %arrange.16.refs_0_), channel_id=1, source_target_pairs={{0,8},{8,0},{16,24},{24,16},{1,9},{9,1},{17,25},{25,17},{2,10},{10... | collective-permute-start | bytes 3145736 | tf_op jit(solution)/shard_map/ppermute | solution.py:677
  129.5 46.4 %collective-permute-start.18 = (bf16[1024,512]{1,0:T(8,128)(2,1)}, bf16[1024,512]{1,0:T(8,128)(2,1)S(1)}, u32[]{:S(2)}, u32[]{:S(2)}) collective-permute-start(bf16[1024,512]{1,0:T(8,128)(2,1)} %arrange.16.refs_0_), channel_id=1, source_target_pairs={{0,16},{8,24},{16,0},{24,8},{1,17},{9,25},{17,1},{25,9},{2,18},{10... | collective-permute-start | bytes 3145736 | tf_op jit(solution)/shard_map/ppermute | solution.py:677
  198.6 78.3 %collective-permute-start.24 = (bf16[1024,2048]{1,0:T(8,128)(2,1)}, bf16[1024,2048]{1,0:T(8,128)(2,1)}, u32[]{:S(2)}, u32[]{:S(2)}) collective-permute-start(bf16[1024,2048]{1,0:T(8,128)(2,1)} %arrange.19.we_ref), channel_id=1, source_target_pairs={{0,1},{1,0},{2,3},{3,2},{4,5},{5,4},{6,7},{7,6},{8,9},{9,8},{10,11... | collective-permute-start | bytes 12582920 | tf_op jit(solution)/shard_map/ppermute | solution.py:677
  217.9 44.8 %collective-permute-start.27 = (bf16[1024,256]{1,0:T(8,128)(2,1)S(1)}, bf16[1024,256]{1,0:T(8,128)(2,1)}, u32[]{:S(2)}, u32[]{:S(2)}) collective-permute-start(bf16[1024,256]{1,0:T(8,128)(2,1)S(1)} %copy-done.14), channel_id=1, source_target_pairs={{0,4},{1,5},{2,6},{3,7},{4,0},{5,1},{6,2},{7,3},{8,12},{9,13},{10,... | collective-permute-start | bytes 1572872 | tf_op jit(solution)/shard_map/ppermute | solution.py:677
  251.8 43.2 %all-to-all-start.1 = ((bf16[4,128,2048]{2,1,0:T(8,128)(2,1)}), bf16[4,128,2048]{2,1,0:T(8,128)(2,1)S(1)}, u32[]{:S(2)}, u32[]{:S(2)}) async-start(bf16[4,128,2048]{2,1,0:T(8,128)(2,1)} %get-tuple-element.215), calls=%async_computation.1 | async-start | bytes 4194304 | tf_op jit(solution)/shard_map/all_to_all | solution.py:1033
  397.1 42.1 %all-to-all-start.5 = ((bf16[4,128,2048]{2,1,0:T(8,128)(2,1)}), bf16[4,128,2048]{2,1,0:T(8,128)(2,1)S(1)}, u32[]{:S(2)}, u32[]{:S(2)}) async-start(bf16[4,128,2048]{2,1,0:T(8,128)(2,1)} %bitcast.169), calls=%async_computation.5 | async-start | bytes 4194304 | tf_op jit(solution)/shard_map/all_to_all | solution.py:1033
  401.3 226.7 %reduce-scatter.10.cloned.1.call-start = ((), (), s32[]{:S(2)}) async-start(), calls=%async_computation.19 | async-start | bytes 1802240 | tf_op jit(solution)/shard_map/reduce_scatter | solution.py:785
  462.7 167.2 %reduce-scatter.8.cloned.1.call-start = ((), (), s32[]{:S(2)}) async-start(), calls=%async_computation.18 | async-start | bytes 1966080 | tf_op jit(solution)/shard_map/reduce_scatter | solution.py:785
  462.7 53.0 %collective-permute-start.34 = (bf16[128,2048]{1,0:T(8,128)(2,1)}, bf16[128,2048]{1,0:T(8,128)(2,1)}, u32[]{:S(2)}, u32[]{:S(2)}) collective-permute-start(bf16[128,2048]{1,0:T(8,128)(2,1)} %get-tuple-element.238), channel_id=1, source_target_pairs={{0,2},{1,3},{2,0},{3,1},{4,6},{5,7},{6,4},{7,5},{8,10},{9,11},{10,... | collective-permute-start | bytes 1572872 | tf_op jit(solution)/shard_map/ppermute | solution.py:677
  462.7 53.0 %collective-permute-start.36 = (bf16[128,2048]{1,0:T(8,128)(2,1)}, bf16[128,2048]{1,0:T(8,128)(2,1)}, u32[]{:S(2)}, u32[]{:S(2)}) collective-permute-start(bf16[128,2048]{1,0:T(8,128)(2,1)} %get-tuple-element.252), channel_id=1, source_target_pairs={{0,6},{1,7},{2,4},{3,5},{4,2},{5,3},{6,0},{7,1},{8,14},{9,15},{10,... | collective-permute-start | bytes 1572872 | tf_op jit(solution)/shard_map/ppermute | solution.py:677
  465.2 50.5 %collective-permute-start.35 = (bf16[128,2048]{1,0:T(8,128)(2,1)}, bf16[128,2048]{1,0:T(8,128)(2,1)}, u32[]{:S(2)}, u32[]{:S(2)}) collective-permute-start(bf16[128,2048]{1,0:T(8,128)(2,1)} %get-tuple-element.250), channel_id=1, source_target_pairs={{0,4},{1,5},{2,6},{3,7},{4,0},{5,1},{6,2},{7,3},{8,12},{9,13},{10,... | collective-permute-start | bytes 1572872 | tf_op jit(solution)/shard_map/ppermute | solution.py:677
  500.4 131.5 %reduce-scatter.6.cloned.1.call-start = ((), (), s32[]{:S(2)}) async-start(), calls=%async_computation.17 | async-start | bytes 1966080 | tf_op jit(solution)/shard_map/reduce_scatter | solution.py:785
  546.0 136.3 %reduce-scatter.14.cloned.1.call-start = ((), (), s32[]{:S(2)}) async-start(), calls=%async_computation.21 | async-start | bytes 655360 | tf_op jit(solution)/shard_map/reduce_scatter | solution.py:785
  579.8 82.2 %collective-permute-start.43 = (bf16[512,2048]{1,0:T(8,128)(2,1)}, bf16[512,2048]{1,0:T(8,128)(2,1)}, u32[]{:S(2)}, u32[]{:S(2)}) collective-permute-start(bf16[512,2048]{1,0:T(8,128)(2,1)} %get-tuple-element.267), channel_id=1, source_target_pairs={{0,1},{1,0},{2,3},{3,2},{4,5},{5,4},{6,7},{7,6},{8,9},{9,8},{10,11... | collective-permute-start | bytes 6291464 | tf_op jit(solution)/shard_map/ppermute | solution.py:677
  648.2 133.9 %reduce-scatter.12.cloned.1.call-start = ((), (), s32[]{:S(2)}) async-start(), calls=%async_computation.20 | async-start | bytes 1966080 | tf_op jit(solution)/shard_map/reduce_scatter | solution.py:785
  709.9 48.9 %collective-permute-start.59 = (bf16[1024,512]{1,0:T(8,128)(2,1)}, bf16[1024,512]{1,0:T(8,128)(2,1)}, u32[]{:S(2)}, u32[]{:S(2)}) collective-permute-start(bf16[1024,512]{1,0:T(8,128)(2,1)} %slice.588), channel_id=1, source_target_pairs={{0,1},{1,0},{2,3},{3,2},{4,5},{5,4},{6,7},{7,6},{8,9},{9,8},{10,11... | collective-permute-start | bytes 3145736 | tf_op jit(solution)/shard_map/ppermute | solution.py:677
  718.2 52.2 %collective-permute-start.60 = (bf16[128,640]{1,0:T(8,128)(2,1)S(1)}, bf16[128,640]{1,0:T(8,128)(2,1)S(1)}, u32[]{:S(2)}, u32[]{:S(2)}) collective-permute-start(bf16[128,640]{1,0:T(8,128)(2,1)S(1)} %maximum_maximum_fusion.1.refs_0_), channel_id=1, source_target_pairs={{0,2},{1,3},{2,0},{3,1},{4,6},{5,7},{6,4},{7,5},{8,10},{9,11},{10,... | collective-permute-start | bytes 491528 | tf_op jit(solution)/shard_map/ppermute | solution.py:677
  718.3 52.1 %collective-permute-start.61 = (bf16[128,640]{1,0:T(8,128)(2,1)S(1)}, bf16[128,640]{1,0:T(8,128)(2,1)S(1)}, u32[]{:S(2)}, u32[]{:S(2)}) collective-permute-start(bf16[128,640]{1,0:T(8,128)(2,1)S(1)} %maximum_maximum_fusion.1.refs_0_), channel_id=1, source_target_pairs={{0,4},{1,5},{2,6},{3,7},{4,0},{5,1},{6,2},{7,3},{8,12},{9,13},{10,... | collective-permute-start | bytes 491528 | tf_op jit(solution)/shard_map/ppermute | solution.py:677
  (135 other events, 2233.3 us)
Sparse Core Ops, SparseCore 0:
  10.4 46.9 all-gather.4
  59.3 30.0 all-gather.10
  91.2 31.0 all-gather.6
  199.7 48.8 all-gather.8
  458.5 61.5 reduce-scatter.9
  523.3 30.9 reduce-scatter.7
  557.5 35.2 reduce-scatter.5
  648.4 22.7 reduce-scatter.13
  682.4 34.5 reduce-scatter.11

commit v7 on v6

--- a/solution.py
+++ b/solution.py
@@ -620,6 +620,32 @@
     )(index, normed, down_even, down_odd)
 
 
+def output_weights(base, heads, columns, dtype):
+    count, width = heads[0].shape
+    wide = columns[0].shape[1]
+    half = width // 2
+    tile = 256
+    many = len(heads)
+
+    def kernel(*refs):
+        total = 0.0
+        for j in range(many):
+            total = total + t_dot(refs[j][...], refs[many + j][...])
+        refs[-1][...] = total.astype(dtype)
+
+    return pl.pallas_call(
+        kernel,
+        grid=(half // tile,),
+        in_specs=[pl.BlockSpec((count, tile), lambda i: (0, base * (half // tile) + i))] * many
+        + [whole((count, wide))] * many,
+        out_specs=pl.BlockSpec((tile, wide), lambda i: (i, 0)),
+        out_shape=jax.ShapeDtypeStruct((half, wide), dtype),
+        compiler_params=pltpu.CompilerParams(vmem_limit_bytes=LIMIT),
+        cost_estimate=LIGHT,
+        name="output_weights",
+    )(*heads, *columns)
+
+
 def combine(base, masks, returned, products, dtype):
     half = masks[0].shape[0] // 2
     slots, count = masks[0].shape[1:]
@@ -741,13 +767,10 @@
     def others(self, x):
         return [x] + [self.send(x, j) for j in range(1, lax.axis_size("exp"))]
 
-def siblings(blocks, *gates):
+def siblings(blocks):
     got = {}
-    for k in range(len(blocks) - 1, 1, -1):
+    for k in range(len(blocks) - 1, -1, -1):
         got[k] = swap(after(blocks[k], *got.values()), "seq", 1)
-    gates += tuple(got.values())
-    for k in range(min(2, len(blocks))):
-        got[k] = swap(after(blocks[k], *gates), "seq", 1)
     return [got[k] for k in range(len(blocks))]
 
 
@@ -951,13 +974,9 @@
             for g in range(ratio)
         ],
     )
-    token_odd = {}
-    for k in range(chips - 1, -1, -1):
-        token_odd[k] = swap(after(token_even[k], *token_odd.values()), "seq", 1)
-    token_odd = [token_odd[k] for k in range(chips)]
+    token_odd = siblings(token_even)
     token_blocks = token_even + token_odd
     output_even = free.chips(after(w_output, *token_odd, packed_odd))
-    grad_even = along.chips(after(out_grad, *token_odd))
 
     column = jnp.stack(
         [
@@ -990,7 +1009,7 @@
     cosine_table, sine_table = rope_tables(positions, DR)
     cosine_wide = jnp.concatenate([cosine_table, cosine_table], axis=1)
     sine_wide = jnp.concatenate([-sine_table, sine_table], axis=1)
-    gain_first = after(gain_first, select, slot_weight, column_position)
+    gain_first = after(gain_first, column_position)
     normed_one, latent_all, latent_raw, query_heads, key_heads, value_heads = project(
         token_blocks,
         gain_first,
@@ -1007,38 +1026,33 @@
         query_heads, key_heads, value_heads, row_position, column_position, factor
     )
 
-    output_parts = across.corners(output_even, result, *grad_even[1:])
-    (output_even,) = arrange(
-        index,
-        [part[2] for part in output_parts],
-        [(H * DV // 2, width)],
-        [
-            (
-                n,
-                everything,
-                0,
-                lambda ref, j=j, at=at, x=x: (
-                    slice(at, at + x.shape[0]),
-                    span(ref[0] ^ j, block_rows),
-                ),
-            )
-            for n, (j, at, x) in enumerate(output_parts)
-        ],
-    )
-    output_odd = swap(output_even, "seq", 1)
-
-    grad_even, grad_odd = along.pair([after(x, result) for x in grad_even])
+    result_even = along.chips(result)
+    output_parts = across.corners(output_even, result, *result_even[1:])
+    output_sides = []
+    for parts in (output_parts, [(j, at, swap(x, "seq", 1)) for j, at, x in output_parts]):
+        output_sides += arrange(
+            index,
+            [x for _, _, x in parts],
+            [(H * DV // 2, width)],
+            [
+                (
+                    n,
+                    everything,
+                    0,
+                    lambda ref, j=j, at=at, x=x: (
+                        slice(at, at + x.shape[0]),
+                        span(ref[0] ^ j, block_rows),
+                    ),
+                )
+                for n, (j, at, x) in enumerate(parts)
+            ],
+        )
+    output_even, output_odd = output_sides
+
 
     def give(rows):
         return lax.all_to_all(rows, "exp", split_axis=0, concat_axis=0, tiled=True)
 
-    grad_rows = stacked([grad_even, grad_odd])
-    send_cots = dispatch(select, grad_rows, slot_weight, pieces)
-    received_grad = [give(rows) for rows in send_cots]
-
-    result_even = along.chips(result)
-    gathered = (gate_cols, lift_cols, drop_rows)
-    result_even = [after(x, received_grad[0], *gathered) for x in result_even]
     result_blocks = result_even + siblings(result_even)
     normed_two, residual = add_norm(
         token_blocks,
@@ -1048,11 +1062,24 @@
         gain_second,
     )
     inverse_two = inverse_rms(residual)
-    send_rows = dispatch(select, after(normed_two, *received_grad), None, pieces)
-    received = [give(after(send_rows[0], *received_grad))]
-
-
-    received += [give(after(x, received[0])) for x in send_rows[1:]]
+    grad_even = along.chips(after(out_grad, *token_odd))
+    send_rows = dispatch(select, normed_two, None, pieces)
+    received = []
+    for rows in send_rows:
+        received.append(give(after(rows, *received)))
+    grad_even, grad_odd = along.pair([after(x, *send_rows) for x in grad_even])
+    grad_rows = stacked([grad_even, grad_odd])
+    received_grad = []
+    for rows in dispatch(select, grad_rows, slot_weight, pieces):
+        received_grad.append(give(after(rows, *received, *received_grad)))
+
+    shared_hidden, sgate_grad, sup_grad = shared(
+        normed_two, grad_rows, gate_cols, lift_cols, drop_rows
+    )
+    gate_part, lift_part, drop_part = expert_weights(
+        normed_two, grad_rows, shared_hidden, sgate_grad, sup_grad, 0, 1, None, BF
+    )
+    received[0] = after(received[0], gate_part, lift_part, drop_part)
 
     slot_rows = n_exp * n_seq * CAP
     pairs = []
@@ -1066,20 +1093,13 @@
         grads_back.append(give(input_grad.reshape(n_exp, n_seq * CAP, width)))
         results_back.append(expert_result.reshape(n_exp, n_seq * CAP, width))
         kept.append((rows, cots, *saved))
-    shared_rows = after(normed_two, input_grad)
-    shared_hidden, sgate_grad, sup_grad = shared(
-        shared_rows, grad_rows, gate_cols, lift_cols, drop_rows
-    )
     two_products = [(sgate_grad, gate_cols, True), (sup_grad, lift_cols, True)]
     expert_grads = expert_weights(
         after(kept[0][0], input_grad), *kept[0][1:], 0, pieces, None
     )
-    gate_part, lift_part, drop_part = expert_weights(
-        shared_rows, grad_rows, shared_hidden, sgate_grad, sup_grad, 0, 1, None, BF
-    )
     token_wide = tokens.astype(F32)
     token_inverse = inverse_rms(token_wide)
-    select = after(select, *expert_grads, gate_part, lift_part, drop_part, token_inverse)
+    select = after(select, *expert_grads, token_inverse)
     two_odd = combine(1, [select], grads_back, two_products, BF)
     two_even = combine(0, [select], grads_back, two_products, F32)
     two_blocks = along.begin(two_even, two_odd)
@@ -1157,15 +1177,22 @@
         factor,
         columns,
     )
-    late = Lane("exp", 2)
-    attention_parts = late.others(after(own_heads, query_in_grad))
     one_odd, odd_sum = query_back(1, query_in_grad, first_all, normed_one, gain_first, BF)
-    one_even, even_sum = query_back(0, query_in_grad, first_all, normed_one, gain_first, F32)
+    one_even, even_sum = query_back(0, after(query_in_grad, *output_got[:2]), first_all, normed_one, gain_first, F32)
+    late = Lane("exp", 3)
+    attention_parts = late.others(after(own_heads, one_even))
+    column_blocks = [
+        lax.dynamic_slice_in_dim(residual_half, (mine ^ j) * block_rows, block_rows, 1)
+        for j in range(n_exp)
+    ]
+    column_blocks = [column_blocks[0]] + [
+        late.send(column_blocks[j], j) for j in range(1, n_exp)
+    ]
     sums = jnp.concatenate(
         [
             (odd_sum + even_sum).reshape(n_exp, n_seq, gain_rows),
             jnp.sum(second_terms, axis=0).reshape(n_exp, n_seq, gain_rows),
-            after(latent_sum, *output_got[:2], *attention_parts[1:]).reshape(n_exp, n_seq, latent_rows_local),
+            latent_sum.reshape(n_exp, n_seq, latent_rows_local),
         ],
         axis=2,
     )
@@ -1182,18 +1209,9 @@
     )
     one_blocks = along.begin(one_even, one_odd)
     one_got = [along.send(one_blocks[k], 2 * k) for k in range(chips - 1, 0, -1)]
-    column_blocks = [
-        lax.dynamic_slice_in_dim(residual_half, (mine ^ j) * block_rows, block_rows, 1)
-        for j in range(n_exp)
-    ]
-    column_blocks = [column_blocks[0]] + [
-        swap(after(column_blocks[j], one_got[-1]), "exp", j) for j in range(1, n_exp)
-    ]
-    output_part = t_dot(
-        jnp.concatenate([after(x, *one_blocks) for x in attention_parts], axis=0),
-        jnp.concatenate([after(x, *one_blocks) for x in column_blocks], axis=0),
-    )
-    output_blocks = along.begin(output_part[: H * DV // 2], output_part[H * DV // 2 :])
+    output_odd_part = output_weights(1, attention_parts, column_blocks, BF)
+    output_even_part = output_weights(0, attention_parts, column_blocks, F32)
+    output_blocks = along.begin(output_even_part, output_odd_part)
     up_part = t_dot(after(latent_all, one_odd), kv_grad).astype(BF)
     query_part = t_dot(after(normed_one, one_odd), query_in_grad).astype(BF)
     up_out = sum_exp(up_part, 0)

time: 820 us -> 909 us (1.11)
  waiting for transfers between devices: 262 us -> 328 us
  starting transfers between devices: 124 us -> 167 us
  blocking collectives: 30.4 us -> 0 us
  Pallas kernels: 255 us -> 270 us
    all_to_all x7 -> x8, waiting for transfers between devices: 27.6 us -> 81.2 us  [give(): return lax.all_to_all(rows, 'exp', split_axis=0, concat_axis=0, tiled=True)]
    ppermute x70 -> x74, starting transfers between devices: 93.5 us -> 134 us  [swap(): return lax.ppermute(x, axis, [(i, i ^ mask) for i in range(n)])]
    all_to_all x1 -> x0, blocking collectives: 30.4 us -> none  [give(): return lax.all_to_all(rows, 'exp', split_axis=0, concat_axis=0, tiled=True)]
    pallas_call x0 -> x2, Pallas kernels: none -> 9.74 us  [output_weights(): pl.pallas_call(kernel, grid=(half // tile,), in_specs=[pl.BlockSpec((coun...]
    unnamed x151 -> x155, local copies, waits for them, and re-layouts: 23.8 us -> 29.1 us
    pallas_call x12 -> x13, Pallas kernels: 34.2 us -> 39 us  [arrange(): pl.pallas_call(kernel, out_shape=[jax.ShapeDtypeStruct(s, BF) for s in ou...]
    ppermute x70 -> x74, waiting for transfers between devices: 204 us -> 208 us  [swap(): return lax.ppermute(x, axis, [(i, i ^ mask) for i in range(n)])]
    all_to_all x7 -> x8, starting transfers between devices: 28.9 us -> 32.6 us  [give(): return lax.all_to_all(rows, 'exp', split_axis=0, concat_axis=0, tiled=True)]
  transfers between devices with their start and end apart: 86 -> 91, of which waited for: 31 -> 28; matrix products, arithmetic and copies ran while one was open for 12% -> 10% of each run, Pallas kernels for 30% -> 29%
where the time goes in v7:
time: 909 us; the launch traced here: 901 us
  waiting for transfers between devices  328 us (36%)
  Pallas kernels  270 us (30%)
  starting transfers between devices  167 us (18%)
  other arithmetic  60.3 us (7%)
  local copies, waits for them, and re-layouts  47.5 us (5%)
  between operations  15.4 us (2%)
  matrix products  13.5 us (1%)
    ppermute x74, waiting for transfers between devices, swap(): return lax.ppermute(x, axis, [(i, i ^ mask) for i in range(n)])  208 us
    ppermute x74, starting transfers between devices, swap(): return lax.ppermute(x, axis, [(i, i ^ mask) for i in range(n)])  134 us
    all_to_all x8, waiting for transfers between devices, give(): return lax.all_to_all(rows, 'exp', split_axis=0, concat_axis=0, tiled=True)  81.2 us
    pallas_call x2, Pallas kernels, expert(): pl.pallas_call(kernel, grid=(count // tile,), in_specs=[block(width), blo...  55.2 us
    pallas_call x3, Pallas kernels, expert_weights(): pl.pallas_call(kernel, grid=(width // tile,), in_specs=[column, column] +...  41.8 us
    pallas_call x13, Pallas kernels, arrange(): pl.pallas_call(kernel, out_shape=[jax.ShapeDtypeStruct(s, BF) for s in ou...  39 us
    all_gather x1, waiting for transfers between devices, shards(): lax.all_gather(after(shared_up, early), 'exp', axis=0, tiled=True)  38.6 us
    all_to_all x8, starting transfers between devices, give(): return lax.all_to_all(rows, 'exp', split_axis=0, concat_axis=0, tiled=True)  32.6 us
  transfers between devices with their start and end apart: 91, of which 28 were waited for; matrix products, arithmetic and copies ran while one was open for 10% of the time, Pallas kernels for 29%

profile of v7, /device:TPU:0, one launch (start us, length us, event | category | flops | bytes accessed | tf_op | source)
XLA Modules:
  0.0 901.1 jit_solution(8166394833299386653)
XLA Ops:
  17.6 18.4 %collective-permute-done.refs_3_.refs_11_ = bf16[128,2048]{1,0:T(8,128)(2,1)} collective-permute-done((bf16[128,2048]{1,0:T(8,128)(2,1)}, bf16[128,2048]{1,0:T(8,128)(2,1)}, u32[]{:S(2)}, u32[]{:S(2)}) %collective-permute-start) | collective-permute-done | bytes 524320 | tf_op jit(solution)/shard_map/ppermute | solution.py:703
  39.4 23.8 %collective-permute-start.8 = (bf16[80,640]{1,0:T(8,128)(2,1)S(1)}, bf16[80,640]{1,0:T(8,128)(2,1)S(1)}, u32[]{:S(2)}, u32[]{:S(2)}) collective-permute-start(bf16[80,640]{1,0:T(8,128)(2,1)S(1)} %fusion.47.refs_0_), channel_id=1, source_target_pairs={{0,4},{1,5},{2,6},{3,7},{4,0},{5,1},{6,2},{7,3},{8,12},{9,13},{10,... | collective-permute-start | bytes 307208 | tf_op jit(solution)/shard_map/ppermute | solution.py:703
  77.6 10.0 %collective-permute-done.12.refs_3_ = bf16[320,640]{1,0:T(8,128)(2,1)S(1)} collective-permute-done((bf16[320,640]{1,0:T(8,128)(2,1)}, bf16[320,640]{1,0:T(8,128)(2,1)S(1)}, u32[]{:S(2)}, u32[]{:S(2)}) %collective-permute-start.12) | collective-permute-done | bytes 409632 | tf_op jit(solution)/shard_map/ppermute | solution.py:703
  127.9 14.6 %project.1 = (bf16[1024,2048]{1,0:T(8,128)(2,1)}, bf16[1024,512]{1,0:T(8,128)(2,1)}, f32[1024,512]{1,0:T(8,128)}, bf16[2,1024,256]{2,1,0:T(8,128)(2,1)}, bf16[2,...) custom-call(f32[1,2048]{1,0:T(1,128)} %reshape.282.g_ref, bf16[2048,576]{1,0:T(8,128)(2,1)} %get-tuple-element.159.wd_ref, ...), custom_call_target="tpu_custom_call" | custom-call | tf_op jit(solution)/shard_map/project/pallas_call | solution.py:158
  167.8 19.8 %collective-permute-start.19 = (bf16[1024,256]{1,0:T(8,128)(2,1)S(1)}, bf16[1024,256]{1,0:T(8,128)(2,1)}, u32[]{:S(2)}, u32[]{:S(2)}) collective-permute-start(bf16[1024,256]{1,0:T(8,128)(2,1)S(1)} %copy-done.15), channel_id=1, source_target_pairs={{0,2},{1,3},{2,0},{3,1},{4,6},{5,7},{6,4},{7,5},{8,10},{9,11},{10,... | collective-permute-start | bytes 1572872 | tf_op jit(solution)/shard_map/ppermute | solution.py:703
  197.7 10.7 %collective-permute-done.19.refs_1_ = bf16[1024,256]{1,0:T(8,128)(2,1)} collective-permute-done((bf16[1024,256]{1,0:T(8,128)(2,1)S(1)}, bf16[1024,256]{1,0:T(8,128)(2,1)}, u32[]{:S(2)}, u32[]{:S(2)}) %collective-permute-start.19) | collective-permute-done | bytes 524320 | tf_op jit(solution)/shard_map/ppermute | solution.py:703
  242.4 18.4 %add_norm.1 = (bf16[1024,2048]{1,0:T(8,128)(2,1)}, f32[128,2048]{1,0:T(8,128)}) custom-call(bf16[1024,2048]{1,0:T(8,128)(2,1)} %arrange.20.we_ref, bf16[1024,2048]{1,0:T(8,128)(2,1)} %arrange.21.wo_ref, f32[1,2048]{1,0:T(1,128)} %reshape.284.g_ref, bf16[1024,256]{1,0:T(8,128)(2,1)} %get-tuple-element.231.refs_0_.o_ref, ...), custom_call_target="tpu_custom_call" | custom-call | tf_op jit(solution)/shard_map/add_norm/pallas_call | solution.py:391
  277.0 12.3 %collective-permute-done.35.refs_3_ = bf16[128,2048]{1,0:T(8,128)(2,1)S(1)} collective-permute-done((bf16[128,2048]{1,0:T(8,128)(2,1)S(1)}, bf16[128,2048]{1,0:T(8,128)(2,1)S(1)}, u32[]{:S(2)}, u32[]{:S(2)}) %collective-permute-start.35) | collective-permute-done | bytes 524320 | tf_op jit(solution)/shard_map/ppermute | solution.py:703
  289.3 29.8 %collective-permute-done.34.refs_2_ = bf16[128,2048]{1,0:T(8,128)(2,1)S(1)} collective-permute-done((bf16[128,2048]{1,0:T(8,128)(2,1)S(1)}, bf16[128,2048]{1,0:T(8,128)(2,1)S(1)}, u32[]{:S(2)}, u32[]{:S(2)}) %collective-permute-start.34) | collective-permute-done | bytes 524320 | tf_op jit(solution)/shard_map/ppermute | solution.py:703
  343.3 15.4 %all-to-all-done.1 = bf16[4,128,2048]{2,1,0:T(8,128)(2,1)S(1)} async-done(((bf16[4,128,2048]{2,1,0:T(8,128)(2,1)}), bf16[4,128,2048]{2,1,0:T(8,128)(2,1)S(1)}, u32[]{:S(2)}, u32[]{:S(2)}) %all-to-all-start.1) | async-done | bytes 2097184 | tf_op jit(solution)/shard_map/all_to_all | solution.py:1054
  365.4 30.8 %all-to-all-done.2 = bf16[4,128,2048]{2,1,0:T(8,128)(2,1)} async-done(((bf16[4,128,2048]{2,1,0:T(8,128)(2,1)}), bf16[4,128,2048]{2,1,0:T(8,128)(2,1)}, u32[]{:S(2)}, u32[]{:S(2)}) %all-to-all-start.2) | async-done | bytes 2097184 | tf_op jit(solution)/shard_map/all_to_all | solution.py:1054
  399.9 38.6 %all-gather.9.cloned.1.call-done.wu_ref.refs_6_ = bf16[2048,352]{1,0:T(8,128)(2,1)} async-done(((bf16[512,352]{1,0:T(8,128)(2,1)}), bf16[2048,352]{1,0:T(8,128)(2,1)}) %all-gather.9.cloned.1.call-update) | async-done | bytes 1441808 | tf_op jit(solution)/shard_map/all_gather | solution.py:890
  438.5 11.0 %shared.1 = (bf16[1024,352]{1,0:T(8,128)(2,1)}, bf16[1024,352]{1,0:T(8,128)(2,1)}, bf16[1024,352]{1,0:T(8,128)(2,1)}) custom-call(bf16[1024,2048]{1,0:T(8,128)(2,1)} %get-tuple-element.185.x_ref, bf16[1024,2048]{1,0:T(8,128)(2,1)} %arrange.23.c_ref.x_ref, bf16[2048,352]{1,0:T(8,128)(2,1)} %all-gather.7.cloned.1.call-done.wg_ref.refs_4_, ...), custom_call_target="tpu_custom_call" | custom-call | tf_op jit(solution)/shard_map/shared/pallas_call | solution.py:515
  449.5 11.5 %expert_weights.3 = (bf16[1,2048,352]{2,1,0:T(8,128)(2,1)}, bf16[1,2048,352]{2,1,0:T(8,128)(2,1)}, bf16[1,352,2048]{2,1,0:T(8,128)(2,1)}) custom-call(bf16[1024,2048]{1,0:T(8,128)(2,1)} %get-tuple-element.185.x_ref, bf16[1024,2048]{1,0:T(8,128)(2,1)} %arrange.23.c_ref.x_ref, bf16[1024,352]{1,0:T(8,128)(2,1)} %get-tuple-element.199.h_ref.refs_4_, ...), custom_call_target="tpu_custom_call" | custom-call | tf_op jit(solution)/shard_map/expert_weights/pallas_call | solution.py:542
  461.0 27.6 %expert.3 = (bf16[512,2048]{1,0:T(8,128)(2,1)}, bf16[512,2048]{1,0:T(8,128)(2,1)}, bf16[512,1408]{1,0:T(8,128)(2,1)}, bf16[512,1408]{1,0:T(8,128)(2,1)}, bf16[512,1408]{1,0:T(8,128)(2,1)}) custom-call(bf16[512,2048]{1,0:T(8,128)(2,1)} %bitcast.162, bf16[512,2048]{1,0:T(8,128)(2,1)} %bitcast.27.c_ref, bf16[2,2048,1408]{2,1,0:T(8,128)(2,1)} %gate_hbm.3, ...), custom_call_target="tpu_custom_call" | custom-call | tf_op jit(solution)/shard_map/expert/pallas_call | solution.py:478
  494.6 27.6 %expert.2 = (bf16[512,2048]{1,0:T(8,128)(2,1)}, bf16[512,2048]{1,0:T(8,128)(2,1)}, bf16[512,1408]{1,0:T(8,128)(2,1)}, bf16[512,1408]{1,0:T(8,128)(2,1)}, bf16[512,1408]{1,0:T(8,128)(2,1)}) custom-call(bf16[512,2048]{1,0:T(8,128)(2,1)} %bitcast.158, bf16[512,2048]{1,0:T(8,128)(2,1)} %bitcast.160, bf16[2,2048,1408]{2,1,0:T(8,128)(2,1)} %gate_hbm.3, ...), custom_call_target="tpu_custom_call" | custom-call | tf_op jit(solution)/shard_map/expert/pallas_call | solution.py:478
  526.4 14.9 %expert_weights.4 = (f32[2,2048,1408]{2,1,0:T(8,128)}, f32[2,2048,1408]{2,1,0:T(8,128)}, f32[2,1408,2048]{2,1,0:T(8,128)}) custom-call(bf16[512,2048]{1,0:T(8,128)(2,1)} %bitcast.163, bf16[512,2048]{1,0:T(8,128)(2,1)} %bitcast.27.c_ref, bf16[512,1408]{1,0:T(8,128)(2,1)} %get-tuple-element.213.h_ref, bf16[512,1408]{1,0:T(8,128)(2,1)} %get-tuple-element.214.gg_ref, ...), custom_call_target="tpu_custom_call" | custom-call | tf_op jit(solution)/shard_map/expert_weights/pallas_call | solution.py:542
  582.1 25.3 %all-to-all-done.6.refs_2_ = bf16[4,128,2048]{2,1,0:T(8,128)(2,1)S(1)} async-done(((bf16[4,128,2048]{2,1,0:T(8,128)(2,1)}), bf16[4,128,2048]{2,1,0:T(8,128)(2,1)S(1)}, u32[]{:S(2)}, u32[]{:S(2)}) %all-to-all-start.6) | async-done | bytes 2097184 | tf_op jit(solution)/shard_map/all_to_all | solution.py:1054
  613.2 15.4 %expert_weights.5 = (f32[2,2048,1408]{2,1,0:T(8,128)}, f32[2,2048,1408]{2,1,0:T(8,128)}, f32[2,1408,2048]{2,1,0:T(8,128)}) custom-call(bf16[512,2048]{1,0:T(8,128)(2,1)} %bitcast.159, bf16[512,2048]{1,0:T(8,128)(2,1)} %bitcast.161, bf16[512,1408]{1,0:T(8,128)(2,1)} %get-tuple-element.225.h_ref, ...), custom_call_target="tpu_custom_call", output_to_operand_aliasing={{0}: (5, {}), {1}: (6, {}), {2}: (7, {})} | custom-call | tf_op jit(solution)/shard_map/expert_weights/pallas_call | solution.py:542
  680.7 14.1 %attend_back.1 = (bf16[1024,384]{1,0:T(8,128)(2,1)}, bf16[1024,512]{1,0:T(8,128)(2,1)}, f32[1024,640]{1,0:T(8,128)}, f32[1,512]{1,0:T(1,128)}) custom-call(bf16[2,1024,256]{2,1,0:T(8,128)(2,1)} %get-tuple-element.170.q_ref, bf16[2,1024,256]{2,1,0:T(8,128)(2,1)} %get-tuple-element.171.k_ref, bf16[2,1024,128]{2,1,0:T(8,128)(2,1)} %get-tuple-element.172.v_ref, ...), custom_call_target="tpu_custom_call" | custom-call | tf_op jit(solution)/shard_map/attend_back/pallas_call | solution.py:313
  734.0 11.7 %collective-permute-start.49 = (bf16[128,2048]{1,0:T(8,128)(2,1)}, bf16[128,2048]{1,0:T(8,128)(2,1)}, u32[]{:S(2)}, u32[]{:S(2)}) collective-permute-start(bf16[128,2048]{1,0:T(8,128)(2,1)} %get-tuple-element.255), channel_id=1, source_target_pairs={{0,2},{1,3},{2,0},{3,1},{4,6},{5,7},{6,4},{7,5},{8,10},{9,11},{10,... | collective-permute-start | bytes 1572872 | tf_op jit(solution)/shard_map/ppermute | solution.py:703
  801.5 16.1 %collective-permute-done.56 = bf16[128,2048]{1,0:T(8,128)(2,1)S(1)} collective-permute-done((bf16[128,2048]{1,0:T(8,128)(2,1)}, bf16[128,2048]{1,0:T(8,128)(2,1)S(1)}, u32[]{:S(2)}, u32[]{:S(2)}) %collective-permute-start.56) | collective-permute-done | bytes 524320 | tf_op jit(solution)/shard_map/ppermute | solution.py:703
  823.0 10.2 %collective-permute-done.54 = bf16[128,2048]{1,0:T(8,128)(2,1)} collective-permute-done((bf16[128,2048]{1,0:T(8,128)(2,1)}, bf16[128,2048]{1,0:T(8,128)(2,1)}, u32[]{:S(2)}, u32[]{:S(2)}) %collective-permute-start.54) | collective-permute-done | bytes 524320 | tf_op jit(solution)/shard_map/ppermute | solution.py:703
  841.1 13.8 %collective-permute-done.65.refs_2_ = bf16[128,640]{1,0:T(8,128)(2,1)S(1)} collective-permute-done((bf16[128,640]{1,0:T(8,128)(2,1)S(1)}, bf16[128,640]{1,0:T(8,128)(2,1)S(1)}, u32[]{:S(2)}, u32[]{:S(2)}) %collective-permute-start.65) | collective-permute-done | bytes 163872 | tf_op jit(solution)/shard_map/ppermute | solution.py:703
  (477 shorter events, 444.3 us)
Async XLA Ops:
  7.2 118.2 %all-gather.5.cloned.1.call-start = ((), (), s32[]{:S(2)}) async-start(), calls=%async_computation.13 | async-start | bytes 2621440 | tf_op jit(solution)/shard_map/all_gather | solution.py:871
  7.2 92.4 %collective-permute-start.2 = (bf16[128,2048]{1,0:T(8,128)(2,1)}, bf16[128,2048]{1,0:T(8,128)(2,1)S(1)}, u32[]{:S(2)}, u32[]{:S(2)}) collective-permute-start(bf16[128,2048]{1,0:T(8,128)(2,1)} %refs_8_.1), channel_id=1, source_target_pairs={{0,4},{1,5},{2,6},{3,7},{4,0},{5,1},{6,2},{7,3},{8,12},{9,13},{10,... | collective-permute-start | bytes 1572872 | tf_op jit(solution)/shard_map/ppermute | solution.py:703
  15.4 384.5 %all-gather.11.cloned.1.call-start = ((), (), s32[]{:S(2)}) async-start(), calls=%async_computation.16 | async-start | bytes 1802240 | tf_op jit(solution)/shard_map/all_gather | solution.py:891
  36.0 63.7 %collective-permute-start.1 = (bf16[128,2048]{1,0:T(8,128)(2,1)}, bf16[128,2048]{1,0:T(8,128)(2,1)}, u32[]{:S(2)}, u32[]{:S(2)}) collective-permute-start(bf16[128,2048]{1,0:T(8,128)(2,1)} %collective-permute-done.refs_3_.refs_11_), channel_id=1, source_target_pairs={{0,1},{1,0},{2,3},{3,2},{4,5},{5,4},{6,7},{7,6},{8,9},{9,8},{10,11... | collective-permute-start | bytes 1572872 | tf_op jit(solution)/shard_map/ppermute | solution.py:703
  157.1 51.3 %collective-permute-start.17 = (bf16[1024,512]{1,0:T(8,128)(2,1)}, bf16[1024,512]{1,0:T(8,128)(2,1)S(1)}, u32[]{:S(2)}, u32[]{:S(2)}) collective-permute-start(bf16[1024,512]{1,0:T(8,128)(2,1)} %arrange.17.refs_0_), channel_id=1, source_target_pairs={{0,8},{8,0},{16,24},{24,16},{1,9},{9,1},{17,25},{25,17},{2,10},{10... | collective-permute-start | bytes 3145736 | tf_op jit(solution)/shard_map/ppermute | solution.py:703
  158.6 54.4 %collective-permute-start.18 = (bf16[1024,512]{1,0:T(8,128)(2,1)}, bf16[1024,512]{1,0:T(8,128)(2,1)S(1)}, u32[]{:S(2)}, u32[]{:S(2)}) collective-permute-start(bf16[1024,512]{1,0:T(8,128)(2,1)} %arrange.17.refs_0_), channel_id=1, source_target_pairs={{0,16},{8,24},{16,0},{24,8},{1,17},{9,25},{17,1},{25,9},{2,18},{10... | collective-permute-start | bytes 3145736 | tf_op jit(solution)/shard_map/ppermute | solution.py:703
  268.8 54.9 %all-to-all-start = ((bf16[4,128,2048]{2,1,0:T(8,128)(2,1)}), bf16[4,128,2048]{2,1,0:T(8,128)(2,1)S(1)}, u32[]{:S(2)}, u32[]{:S(2)}) async-start(bf16[4,128,2048]{2,1,0:T(8,128)(2,1)} %get-tuple-element.186), calls=%async_computation | async-start | bytes 4194304 | tf_op jit(solution)/shard_map/all_to_all | solution.py:1054
  274.7 44.5 %collective-permute-start.34 = (bf16[128,2048]{1,0:T(8,128)(2,1)S(1)}, bf16[128,2048]{1,0:T(8,128)(2,1)S(1)}, u32[]{:S(2)}, u32[]{:S(2)}) collective-permute-start(bf16[128,2048]{1,0:T(8,128)(2,1)S(1)} %copy-done.12), channel_id=1, source_target_pairs={{0,4},{1,5},{2,6},{3,7},{4,0},{5,1},{6,2},{7,3},{8,12},{9,13},{10,... | collective-permute-start | bytes 1572872 | tf_op jit(solution)/shard_map/ppermute | solution.py:703
  274.7 44.5 %collective-permute-start.33 = (bf16[128,2048]{1,0:T(8,128)(2,1)S(1)}, bf16[128,2048]{1,0:T(8,128)(2,1)S(1)}, u32[]{:S(2)}, u32[]{:S(2)}) collective-permute-start(bf16[128,2048]{1,0:T(8,128)(2,1)S(1)} %copy-done.12), channel_id=1, source_target_pairs={{0,2},{1,3},{2,0},{3,1},{4,6},{5,7},{6,4},{7,5},{8,10},{9,11},{10,... | collective-permute-start | bytes 1572872 | tf_op jit(solution)/shard_map/ppermute | solution.py:703
  328.8 71.1 %all-gather.7.cloned.1.call-start = ((), (), s32[]{:S(2)}) async-start(), calls=%async_computation.14 | async-start | bytes 1966080 | tf_op jit(solution)/shard_map/all_gather | solution.py:889
  364.4 74.1 %all-gather.9.cloned.1.call-start = ((), (), s32[]{:S(2)}) async-start(), calls=%async_computation.15 | async-start | bytes 1966080 | tf_op jit(solution)/shard_map/all_gather | solution.py:890
  396.2 92.4 %all-to-all-start.3 = ((bf16[4,128,2048]{2,1,0:T(8,128)(2,1)}), bf16[4,128,2048]{2,1,0:T(8,128)(2,1)S(1)}, u32[]{:S(2)}, u32[]{:S(2)}) async-start(bf16[4,128,2048]{2,1,0:T(8,128)(2,1)} %get-tuple-element.210), calls=%async_computation.3 | async-start | bytes 4194304 | tf_op jit(solution)/shard_map/all_to_all | solution.py:1054
  526.4 220.5 %reduce-scatter.10.cloned.1.call-start = ((), (), s32[]{:S(2)}) async-start(), calls=%async_computation.19 | async-start | bytes 1802240 | tf_op jit(solution)/shard_map/reduce_scatter | solution.py:808
  573.9 175.0 %reduce-scatter.8.cloned.1.call-start = ((), (), s32[]{:S(2)}) async-start(), calls=%async_computation.18 | async-start | bytes 1966080 | tf_op jit(solution)/shard_map/reduce_scatter | solution.py:808
  573.9 54.7 %collective-permute-start.38 = (bf16[128,2048]{1,0:T(8,128)(2,1)}, bf16[128,2048]{1,0:T(8,128)(2,1)}, u32[]{:S(2)}, u32[]{:S(2)}) collective-permute-start(bf16[128,2048]{1,0:T(8,128)(2,1)} %get-tuple-element.221), channel_id=1, source_target_pairs={{0,2},{1,3},{2,0},{3,1},{4,6},{5,7},{6,4},{7,5},{8,10},{9,11},{10,... | collective-permute-start | bytes 1572872 | tf_op jit(solution)/shard_map/ppermute | solution.py:703
  575.5 53.2 %collective-permute-start.40 = (bf16[128,2048]{1,0:T(8,128)(2,1)}, bf16[128,2048]{1,0:T(8,128)(2,1)}, u32[]{:S(2)}, u32[]{:S(2)}) collective-permute-start(bf16[128,2048]{1,0:T(8,128)(2,1)} %get-tuple-element.235), channel_id=1, source_target_pairs={{0,6},{1,7},{2,4},{3,5},{4,2},{5,3},{6,0},{7,1},{8,14},{9,15},{10,... | collective-permute-start | bytes 1572872 | tf_op jit(solution)/shard_map/ppermute | solution.py:703
  577.9 50.8 %collective-permute-start.39 = (bf16[128,2048]{1,0:T(8,128)(2,1)}, bf16[128,2048]{1,0:T(8,128)(2,1)}, u32[]{:S(2)}, u32[]{:S(2)}) collective-permute-start(bf16[128,2048]{1,0:T(8,128)(2,1)} %get-tuple-element.233), channel_id=1, source_target_pairs={{0,4},{1,5},{2,6},{3,7},{4,0},{5,1},{6,2},{7,3},{8,12},{9,13},{10,... | collective-permute-start | bytes 1572872 | tf_op jit(solution)/shard_map/ppermute | solution.py:703
  613.2 137.8 %reduce-scatter.6.cloned.1.call-start = ((), (), s32[]{:S(2)}) async-start(), calls=%async_computation.17 | async-start | bytes 1966080 | tf_op jit(solution)/shard_map/reduce_scatter | solution.py:808
  656.2 118.8 %reduce-scatter.14.cloned.1.call-start = ((), (), s32[]{:S(2)}) async-start(), calls=%async_computation.21 | async-start | bytes 655360 | tf_op jit(solution)/shard_map/reduce_scatter | solution.py:808
  727.1 63.0 %collective-permute-start.48 = (bf16[512,2048]{1,0:T(8,128)(2,1)}, bf16[512,2048]{1,0:T(8,128)(2,1)}, u32[]{:S(2)}, u32[]{:S(2)}) collective-permute-start(bf16[512,2048]{1,0:T(8,128)(2,1)} %get-tuple-element.252), channel_id=1, source_target_pairs={{0,1},{1,0},{2,3},{3,2},{4,5},{5,4},{6,7},{7,6},{8,9},{9,8},{10,11... | collective-permute-start | bytes 6291464 | tf_op jit(solution)/shard_map/ppermute | solution.py:703
  730.1 159.6 %reduce-scatter.12.cloned.1.call-start = ((), (), s32[]{:S(2)}) async-start(), calls=%async_computation.20 | async-start | bytes 1966080 | tf_op jit(solution)/shard_map/reduce_scatter | solution.py:808
  796.7 44.3 %collective-permute-start.52 = (bf16[128,2048]{1,0:T(8,128)(2,1)}, bf16[128,2048]{1,0:T(8,128)(2,1)}, u32[]{:S(2)}, u32[]{:S(2)}) collective-permute-start(bf16[128,2048]{1,0:T(8,128)(2,1)} %get-tuple-element.262), channel_id=1, source_target_pairs={{0,6},{1,7},{2,4},{3,5},{4,2},{5,3},{6,0},{7,1},{8,14},{9,15},{10,... | collective-permute-start | bytes 1572872 | tf_op jit(solution)/shard_map/ppermute | solution.py:703
  799.2 55.7 %collective-permute-start.64 = (bf16[128,640]{1,0:T(8,128)(2,1)S(1)}, bf16[128,640]{1,0:T(8,128)(2,1)S(1)}, u32[]{:S(2)}, u32[]{:S(2)}) collective-permute-start(bf16[128,640]{1,0:T(8,128)(2,1)S(1)} %maximum_maximum_fusion.1.refs_0_), channel_id=1, source_target_pairs={{0,2},{1,3},{2,0},{3,1},{4,6},{5,7},{6,4},{7,5},{8,10},{9,11},{10,... | collective-permute-start | bytes 491528 | tf_op jit(solution)/shard_map/ppermute | solution.py:703
  799.3 55.5 %collective-permute-start.65 = (bf16[128,640]{1,0:T(8,128)(2,1)S(1)}, bf16[128,640]{1,0:T(8,128)(2,1)S(1)}, u32[]{:S(2)}, u32[]{:S(2)}) collective-permute-start(bf16[128,640]{1,0:T(8,128)(2,1)S(1)} %maximum_maximum_fusion.1.refs_0_), channel_id=1, source_target_pairs={{0,4},{1,5},{2,6},{3,7},{4,0},{5,1},{6,2},{7,3},{8,12},{9,13},{10,... | collective-permute-start | bytes 491528 | tf_op jit(solution)/shard_map/ppermute | solution.py:703
  (143 other events, 2266.4 us)
Sparse Core Ops, SparseCore 0:
  15.5 35.4 all-gather.4
  227.0 28.9 all-gather.10
  332.1 60.1 all-gather.6
  394.5 43.9 all-gather.8
  570.2 47.6 reduce-scatter.9
  621.0 39.2 reduce-scatter.7
  663.6 30.9 reduce-scatter.5
  730.2 35.5 reduce-scatter.13
  775.1 29.5 reduce-scatter.11

commit v8 on v5

--- a/solution.py
+++ b/solution.py
@@ -494,16 +494,45 @@
     )(rows, cots, gate, up, down)
 
 
-def expert_weights(rows, cots, hidden, gate_grad, up_grad, piece, pieces, earlier):
+def shared(rows, cots, gate, up, down):
+    count, width = rows.shape
+    units = gate.shape[1]
+    tile = 256
+
+    def kernel(x_ref, c_ref, wg_ref, wu_ref, wd_ref, h_ref, gg_ref, ug_ref):
+        g = dot(x_ref[...], wg_ref[...])
+        u = dot(x_ref[...], wu_ref[...])
+        hidden_grad = dot_t(c_ref[...], wd_ref[...])
+        s = jax.nn.sigmoid(g)
+        silu = g * s
+        h_ref[...] = (silu * u).astype(BF)
+        gg_ref[...] = (hidden_grad * u * (s * (1.0 + g * (1.0 - s)))).astype(BF)
+        ug_ref[...] = (hidden_grad * silu).astype(BF)
+
+    row = pl.BlockSpec((tile, width), lambda i: (i, 0))
+    unit = pl.BlockSpec((tile, units), lambda i: (i, 0))
+    return pl.pallas_call(
+        kernel,
+        grid=(count // tile,),
+        in_specs=[row, row, whole(gate.shape), whole(up.shape), whole(down.shape)],
+        out_specs=[unit] * 3,
+        out_shape=[jax.ShapeDtypeStruct((count, units), BF)] * 3,
+        compiler_params=pltpu.CompilerParams(vmem_limit_bytes=LIMIT),
+        cost_estimate=LIGHT,
+        name="shared",
+    )(rows, cots, gate, up, down)
+
+
+def expert_weights(rows, cots, hidden, gate_grad, up_grad, piece, pieces, earlier, dtype=F32):
     count, width = rows.shape
     units = hidden.shape[1]
     tile = 256
 
     def kernel(x_ref, c_ref, h_ref, gg_ref, ug_ref, *refs):
         g_ref, u_ref, d_ref = refs[-3:]
-        g_ref[0] = t_dot(x_ref[...], gg_ref[...])
-        u_ref[0] = t_dot(x_ref[...], ug_ref[...])
-        d_ref[0] = t_dot(h_ref[...], c_ref[...])
+        g_ref[0] = t_dot(x_ref[...], gg_ref[...]).astype(dtype)
+        u_ref[0] = t_dot(x_ref[...], ug_ref[...]).astype(dtype)
+        d_ref[0] = t_dot(h_ref[...], c_ref[...]).astype(dtype)
 
     tall = pl.BlockSpec((1, tile, units), lambda i: (piece, i, 0))
     flat = pl.BlockSpec((1, units, tile), lambda i: (piece, 0, i))
@@ -515,9 +544,9 @@
         in_specs=[column, column] + [whole((count, units))] * 3 + [ANY] * len(kept),
         out_specs=[tall, tall, flat],
         out_shape=[
-            jax.ShapeDtypeStruct((pieces, width, units), F32),
-            jax.ShapeDtypeStruct((pieces, width, units), F32),
-            jax.ShapeDtypeStruct((pieces, units, width), F32),
+            jax.ShapeDtypeStruct((pieces, width, units), dtype),
+            jax.ShapeDtypeStruct((pieces, width, units), dtype),
+            jax.ShapeDtypeStruct((pieces, units, width), dtype),
         ],
         input_output_aliases={5 + n: n for n in range(len(kept))},
         compiler_params=pltpu.CompilerParams(vmem_limit_bytes=LIMIT),
@@ -918,6 +947,7 @@
     )
 
     output_parts = across.corners(output_even, result, *grad_even[1:])
+    result_even = along.chips(result)
     (output_even,) = arrange(
         index,
         [part[2] for part in output_parts],
@@ -976,9 +1006,9 @@
         ],
     )
     send_cots = dispatch(select, grad_rows, slot_weight, pieces)
-    received_grad = [give(rows) for rows in send_cots]
-
-    result_even = along.chips(result)
+    received_grad = [give(send_cots[0])]
+    received_grad += [give(after(rows, *result_even[1:])) for rows in send_cots[1:]]
+
     gathered = (gate_cols, lift_cols, drop_rows)
     result_even = [after(x, *send_cots, *gathered) for x in result_even]
     result_blocks = result_even + [swap(x, "seq", 1) for x in result_even]
@@ -995,13 +1025,11 @@
 
 
     shared_rows = after(normed_two, *send_rows)
-    shared_gate_raw = dot(shared_rows, gate_cols)
-    shared_up_raw = dot(shared_rows, lift_cols)
-    shared_hidden = (jax.nn.silu(shared_gate_raw) * shared_up_raw).astype(BF)
-    shared_hidden_grad = dot_t(grad_rows, drop_rows)
-    sgate_grad = (shared_hidden_grad * shared_up_raw * silu_slope(shared_gate_raw)).astype(BF)
-    sup_grad = (shared_hidden_grad * jax.nn.silu(shared_gate_raw)).astype(BF)
-    received += [give(after(rows, sgate_grad, sup_grad)) for rows in send_rows[1:]]
+    shared_hidden, sgate_grad, sup_grad = shared(
+        shared_rows, grad_rows, gate_cols, lift_cols, drop_rows
+    )
+    received[0] = after(received[0], shared_hidden)
+    received += [give(after(rows, received[0])) for rows in send_rows[1:]]
 
     slot_rows = n_exp * n_seq * CAP
     pairs = []
@@ -1019,7 +1047,10 @@
     expert_grads = expert_weights(
         after(kept[0][0], input_grad), *kept[0][1:], 0, pieces, None
     )
-    select = after(select, *expert_grads)
+    gate_part, lift_part, drop_part = expert_weights(
+        after(shared_rows, input_grad), grad_rows, shared_hidden, sgate_grad, sup_grad, 0, 1, None, BF
+    )
+    select = after(select, *expert_grads, gate_part, lift_part, drop_part)
     two_odd = combine(1, [select], grads_back, two_products, BF)
     two_even = combine(0, [select], grads_back, two_products, F32)
     two_blocks = along.begin(two_even, two_odd)
@@ -1032,10 +1063,25 @@
             )
     results_back = back
     expert_gate_grad, expert_up_grad, expert_down_grad = expert_grads
-    two_grad = along.finish(two_blocks, *expert_grads)
-    gate_out = sum_exp(t_dot(after(shared_rows, *two_blocks), sgate_grad), 0)
-    lift_out = sum_exp(t_dot(after(shared_rows, *two_blocks), sup_grad), 0)
-    drop_out = sum_exp(t_dot(after(shared_hidden, *two_blocks), grad_rows), 1)
+    (own_heads,) = arrange(
+        index,
+        [after(result_blocks[0], *two_blocks)] + result_blocks[1:],
+        [(count, H * DV)],
+        [
+            (
+                p,
+                (slice(p * count, (p + 1) * count), everything),
+                0,
+                lambda ref, p=p: (everything, slice(p * heads * DV, (p + 1) * heads * DV)),
+            )
+            for p in range(n_seq)
+        ],
+    )
+    two_grad = along.finish(two_blocks, *expert_grads, own_heads)
+    gate_part, lift_part, drop_part = [
+        after(x[0], *two_blocks) for x in (gate_part, lift_part, drop_part)
+    ]
+    gate_out, lift_out, drop_out = sum_exp(gate_part, 0), sum_exp(lift_part, 0), sum_exp(drop_part, 1)
 
     residual_norm_grad, second_terms = norm_back(
         two_grad, residual, inverse_two, gain_second
@@ -1055,20 +1101,6 @@
     attention_grad = jnp.concatenate(
         [jnp.stack([pair[0] for pair in pairs]), other_half], axis=0
     ).reshape(length, wide)
-    (own_heads,) = arrange(
-        index,
-        [after(result_blocks[0], *two_blocks)] + result_blocks[1:],
-        [(count, H * DV)],
-        [
-            (
-                p,
-                (slice(p * count, (p + 1) * count), everything),
-                0,
-                lambda ref, p=p: (everything, slice(p * heads * DV, (p + 1) * heads * DV)),
-            )
-            for p in range(n_seq)
-        ],
-    )
     mine = lax.axis_index("exp")
     late = Lane("exp", 3)
     attention_parts = late.others(after(own_heads, attention_grad))
@@ -1082,7 +1114,7 @@
 
     out_products = [(shared_hidden, drop_rows, False)]
     out_masks = [weighted_high, weighted_low]
-    out_masks = [after(mask, *stacks) for mask in out_masks]
+    out_masks = [after(mask, *stacks, *pairs[1:]) for mask in out_masks]
     out_odd = combine(1, out_masks, results_back, out_products, BF)
     out_even = combine(0, out_masks, results_back, out_products, F32)
     out_blocks = along.begin(out_even, out_odd)
@@ -1104,7 +1136,7 @@
         latent_wide,
         factor,
     )
-    query_in_grad = after(query_in_grad, *output_got[:2])
+    query_in_grad = after(query_in_grad, *output_got)
     one_odd, odd_sum = query_back(1, query_in_grad, first_all, normed_one, gain_first, BF)
     one_even, even_sum = query_back(0, query_in_grad, first_all, normed_one, gain_first, F32)
     sums = jnp.concatenate(

time: 795 us -> 798 us (level)
  matrix products: 43.6 us -> 20 us
  Pallas kernels: 222 us -> 244 us
  starting transfers between devices: 137 us -> 145 us
    ppermute x70, waiting for transfers between devices: 185 us -> 228 us  [swap(): return lax.ppermute(x, axis, [(i, i ^ mask) for i in range(n)])]
    all_to_all x8, waiting for transfers between devices: 56.3 us -> 25 us  [give(): return lax.all_to_all(rows, 'exp', split_axis=0, concat_axis=0, tiled=True)]
    all_gather x1, waiting for transfers between devices: 17.5 us -> 0.01 us  [shards(): lax.all_gather(after(shared_up, early), 'exp', axis=0, tiled=True)]
    dot_general x6 -> x3, matrix products: 22.2 us -> 9.95 us  [t_dot(): lax.dot_general(a, b, (((0,), (0,)), ((), ())), preferred_element_type=F32)]
    pallas_call x2 -> x3, Pallas kernels: 30 us -> 41.5 us  [expert_weights(): pl.pallas_call(kernel, grid=(width // tile,), in_specs=[column, column] +...]
    pallas_call x0 -> x1, Pallas kernels: none -> 11.1 us  [shared(): pl.pallas_call(kernel, grid=(count // tile,), in_specs=[row, row, whole(g...]
    unnamed x134 -> x130, local copies, waits for them, and re-layouts: 17.9 us -> 19 us
  transfers between devices with their start and end apart: 87 -> 87, of which waited for: 33 -> 34; matrix products, arithmetic and copies ran while one was open for 16% -> 14% of each run, Pallas kernels for 27% -> 30%
where the time goes in v8:
time: 798 us; the launch traced here: 784 us
  waiting for transfers between devices  253 us (32%)
  Pallas kernels  244 us (31%)
  starting transfers between devices  145 us (18%)
  other arithmetic  66.3 us (8%)
  local copies, waits for them, and re-layouts  41.2 us (5%)
  matrix products  20 us (3%)
  between operations  15.4 us (2%)
    ppermute x70, waiting for transfers between devices, swap(): return lax.ppermute(x, axis, [(i, i ^ mask) for i in range(n)])  228 us
    ppermute x70, starting transfers between devices, swap(): return lax.ppermute(x, axis, [(i, i ^ mask) for i in range(n)])  110 us
    pallas_call x2, Pallas kernels, expert(): pl.pallas_call(kernel, grid=(count // tile,), in_specs=[block(width), blo...  55.3 us
    pallas_call x3, Pallas kernels, expert_weights(): pl.pallas_call(kernel, grid=(width // tile,), in_specs=[column, column] +...  41.5 us
    all_to_all x8, starting transfers between devices, give(): return lax.all_to_all(rows, 'exp', split_axis=0, concat_axis=0, tiled=True)  33.6 us
    pallas_call x4, Pallas kernels, combine(): pl.pallas_call(kernel, grid=(width // tile,), in_specs=[pl.BlockSpec((hal...  25.5 us
    all_to_all x8, waiting for transfers between devices, give(): return lax.all_to_all(rows, 'exp', split_axis=0, concat_axis=0, tiled=True)  25 us
    pallas_call x7, Pallas kernels, arrange(): pl.pallas_call(kernel, out_shape=[jax.ShapeDtypeStruct(s, BF) for s in ou...  23.6 us
  transfers between devices with their start and end apart: 87, of which 34 were waited for; matrix products, arithmetic and copies ran while one was open for 14% of the time, Pallas kernels for 30%

profile of v8, /device:TPU:0, one launch (start us, length us, event | category | flops | bytes accessed | tf_op | source)
XLA Modules:
  0.0 784.2 jit_solution(16379101562663650392)
XLA Ops:
  45.7 13.1 %collective-permute-done.12 = bf16[4,80,576]{2,1,0:T(8,128)(2,1)} collective-permute-done((bf16[4,80,576]{2,1,0:T(8,128)(2,1)}, bf16[4,80,576]{2,1,0:T(8,128)(2,1)}, u32[]{:S(2)}, u32[]{:S(2)}) %collective-permute-start.12) | collective-permute-done | bytes 368672 | tf_op jit(solution)/shard_map/ppermute | solution.py:676
  60.7 18.3 %collective-permute-done.3.refs_2_.refs_10_ = bf16[128,2048]{1,0:T(8,128)(2,1)S(1)} collective-permute-done((bf16[128,2048]{1,0:T(8,128)(2,1)S(1)}, bf16[128,2048]{1,0:T(8,128)(2,1)S(1)}, u32[]{:S(2)}, u32[]{:S(2)}) %collective-permute-start.3) | collective-permute-done | bytes 524320 | tf_op jit(solution)/shard_map/ppermute | solution.py:676
  100.1 14.3 %project.1 = (bf16[1024,2048]{1,0:T(8,128)(2,1)}, bf16[1024,512]{1,0:T(8,128)(2,1)}, f32[1024,512]{1,0:T(8,128)}, bf16[2,1024,256]{2,1,0:T(8,128)(2,1)}, bf16[2,...) custom-call(f32[1,2048]{1,0:T(1,128)} %reshape.277.g_ref, bf16[2048,576]{1,0:T(8,128)(2,1)} %get-tuple-element.168.wd_ref, ...), custom_call_target="tpu_custom_call" | custom-call | tf_op jit(solution)/shard_map/project/pallas_call | solution.py:158
  137.2 29.1 %collective-permute-done.20.refs_2_ = bf16[128,2048]{1,0:T(8,128)(2,1)} collective-permute-done((bf16[128,2048]{1,0:T(8,128)(2,1)S(1)}, bf16[128,2048]{1,0:T(8,128)(2,1)}, u32[]{:S(2)}, u32[]{:S(2)}) %collective-permute-start.20) | collective-permute-done | bytes 524320 | tf_op jit(solution)/shard_map/ppermute | solution.py:676
  174.3 15.7 %collective-permute-done.23.refs_4_ = bf16[512,512]{1,0:T(8,128)(2,1)S(1)} collective-permute-done((bf16[512,512]{1,0:T(8,128)(2,1)}, bf16[512,512]{1,0:T(8,128)(2,1)S(1)}, u32[]{:S(2)}, u32[]{:S(2)}) %collective-permute-start.23) | collective-permute-done | bytes 524320 | tf_op jit(solution)/shard_map/ppermute | solution.py:676
  221.8 20.7 %collective-permute-done.26.refs_1_ = bf16[1024,256]{1,0:T(8,128)(2,1)S(1)} collective-permute-done((bf16[1024,256]{1,0:T(8,128)(2,1)S(1)}, bf16[1024,256]{1,0:T(8,128)(2,1)S(1)}, u32[]{:S(2)}, u32[]{:S(2)}) %collective-permute-start.26) | collective-permute-done | bytes 524320 | tf_op jit(solution)/shard_map/ppermute | solution.py:676
  242.5 13.1 %collective-permute-done.27.refs_2_ = bf16[1024,256]{1,0:T(8,128)(2,1)S(1)} collective-permute-done((bf16[1024,256]{1,0:T(8,128)(2,1)S(1)}, bf16[1024,256]{1,0:T(8,128)(2,1)S(1)}, u32[]{:S(2)}, u32[]{:S(2)}) %collective-permute-start.27) | collective-permute-done | bytes 524320 | tf_op jit(solution)/shard_map/ppermute | solution.py:676
  267.3 18.3 %add_norm.1 = (bf16[1024,2048]{1,0:T(8,128)(2,1)}, f32[128,2048]{1,0:T(8,128)}) custom-call(bf16[1024,2048]{1,0:T(8,128)(2,1)} %arrange.9.we_ref, bf16[1024,2048]{1,0:T(8,128)(2,1)} %collective-permute-done.24.wo_ref, f32[1,2048]{1,0:T(1,128)} %reshape.279.g_ref, bf16[1024,256]{1,0:T(8,128)(2,1)} %get-tuple-element.243.refs_0_.o_ref, ...), custom_call_target="tpu_custom_call" | custom-call | tf_op jit(solution)/shard_map/add_norm/pallas_call | solution.py:390
  299.1 11.1 %shared.1 = (bf16[1024,352]{1,0:T(8,128)(2,1)}, bf16[1024,352]{1,0:T(8,128)(2,1)}, bf16[1024,352]{1,0:T(8,128)(2,1)}) custom-call(bf16[1024,2048]{1,0:T(8,128)(2,1)} %get-tuple-element.225.x_ref, bf16[1024,2048]{1,0:T(8,128)(2,1)} %arrange.11.x_ref.c_ref, bf16[2048,352]{1,0:T(8,128)(2,1)} %all-gather.7.cloned.1.call-done.wg_ref.refs_4_, ...), custom_call_target="tpu_custom_call" | custom-call | tf_op jit(solution)/shard_map/shared/pallas_call | solution.py:514
  310.1 14.6 %all-to-all-done.2 = bf16[4,128,2048]{2,1,0:T(8,128)(2,1)} async-done(((bf16[4,128,2048]{2,1,0:T(8,128)(2,1)}), bf16[4,128,2048]{2,1,0:T(8,128)(2,1)}, u32[]{:S(2)}, u32[]{:S(2)}) %all-to-all-start.2) | async-done | bytes 2097184 | tf_op jit(solution)/shard_map/all_to_all | solution.py:997
  328.4 27.7 %expert.3 = (bf16[512,2048]{1,0:T(8,128)(2,1)}, bf16[512,2048]{1,0:T(8,128)(2,1)}, bf16[512,1408]{1,0:T(8,128)(2,1)}, bf16[512,1408]{1,0:T(8,128)(2,1)}, bf16[512,1408]{1,0:T(8,128)(2,1)}) custom-call(bf16[512,2048]{1,0:T(8,128)(2,1)} %bitcast.32.x_ref, bf16[512,2048]{1,0:T(8,128)(2,1)} %bitcast.173, bf16[2,2048,1408]{2,1,0:T(8,128)(2,1)} %gate_hbm.3, ...), custom_call_target="tpu_custom_call" | custom-call | tf_op jit(solution)/shard_map/expert/pallas_call | solution.py:477
  362.0 27.6 %expert.2 = (bf16[512,2048]{1,0:T(8,128)(2,1)}, bf16[512,2048]{1,0:T(8,128)(2,1)}, bf16[512,1408]{1,0:T(8,128)(2,1)}, bf16[512,1408]{1,0:T(8,128)(2,1)}, bf16[512,1408]{1,0:T(8,128)(2,1)}) custom-call(bf16[512,2048]{1,0:T(8,128)(2,1)} %bitcast.171, bf16[512,2048]{1,0:T(8,128)(2,1)} %bitcast.169, bf16[2,2048,1408]{2,1,0:T(8,128)(2,1)} %gate_hbm.3, ...), custom_call_target="tpu_custom_call" | custom-call | tf_op jit(solution)/shard_map/expert/pallas_call | solution.py:477
  393.7 11.5 %expert_weights.4 = (bf16[1,2048,352]{2,1,0:T(8,128)(2,1)}, bf16[1,2048,352]{2,1,0:T(8,128)(2,1)}, bf16[1,352,2048]{2,1,0:T(8,128)(2,1)}) custom-call(bf16[1024,2048]{1,0:T(8,128)(2,1)} %get-tuple-element.225.x_ref, bf16[1024,2048]{1,0:T(8,128)(2,1)} %arrange.11.x_ref.c_ref, bf16[1024,352]{1,0:T(8,128)(2,1)} %get-tuple-element.214.h_ref.refs_4_, ...), custom_call_target="tpu_custom_call" | custom-call | tf_op jit(solution)/shard_map/expert_weights/pallas_call | solution.py:541
  405.2 14.9 %expert_weights.3 = (f32[2,2048,1408]{2,1,0:T(8,128)}, f32[2,2048,1408]{2,1,0:T(8,128)}, f32[2,1408,2048]{2,1,0:T(8,128)}) custom-call(bf16[512,2048]{1,0:T(8,128)(2,1)} %bitcast.32.x_ref, bf16[512,2048]{1,0:T(8,128)(2,1)} %bitcast.174, bf16[512,1408]{1,0:T(8,128)(2,1)} %get-tuple-element.219.h_ref, bf16[512,1408]{1,0:T(8,128)(2,1)} %get-tuple-element.220.gg_ref, ...), custom_call_target="tpu_custom_call" | custom-call | tf_op jit(solution)/shard_map/expert_weights/pallas_call | solution.py:541
  443.6 10.3 %collective-permute-start.34 = (bf16[128,2048]{1,0:T(8,128)(2,1)}, bf16[128,2048]{1,0:T(8,128)(2,1)}, u32[]{:S(2)}, u32[]{:S(2)}) collective-permute-start(bf16[128,2048]{1,0:T(8,128)(2,1)} %get-tuple-element.233), channel_id=1, source_target_pairs={{0,2},{1,3},{2,0},{3,1},{4,6},{5,7},{6,4},{7,5},{8,10},{9,11},{10,... | collective-permute-start | bytes 1572872 | tf_op jit(solution)/shard_map/ppermute | solution.py:676
  460.9 10.3 %all-to-all-done.6.refs_2_ = bf16[4,128,2048]{2,1,0:T(8,128)(2,1)S(1)} async-done(((bf16[4,128,2048]{2,1,0:T(8,128)(2,1)}), bf16[4,128,2048]{2,1,0:T(8,128)(2,1)S(1)}, u32[]{:S(2)}, u32[]{:S(2)}) %all-to-all-start.6) | async-done | bytes 2097184 | tf_op jit(solution)/shard_map/all_to_all | solution.py:997
  477.2 15.1 %expert_weights.5 = (f32[2,2048,1408]{2,1,0:T(8,128)}, f32[2,2048,1408]{2,1,0:T(8,128)}, f32[2,1408,2048]{2,1,0:T(8,128)}) custom-call(bf16[512,2048]{1,0:T(8,128)(2,1)} %bitcast.172, bf16[512,2048]{1,0:T(8,128)(2,1)} %bitcast.170, bf16[512,1408]{1,0:T(8,128)(2,1)} %get-tuple-element.237.h_ref, ...), custom_call_target="tpu_custom_call", output_to_operand_aliasing={{0}: (5, {}), {1}: (6, {}), {2}: (7, {})} | custom-call | tf_op jit(solution)/shard_map/expert_weights/pallas_call | solution.py:541
  557.4 14.2 %attend_back.1 = (bf16[1024,384]{1,0:T(8,128)(2,1)}, bf16[1024,512]{1,0:T(8,128)(2,1)}, f32[1024,576]{1,0:T(8,128)}, f32[1,512]{1,0:T(1,128)}) custom-call(bf16[2,1024,256]{2,1,0:T(8,128)(2,1)} %get-tuple-element.179.q_ref, bf16[2,1024,256]{2,1,0:T(8,128)(2,1)} %get-tuple-element.180.k_ref, bf16[2,1024,128]{2,1,0:T(8,128)(2,1)} %get-tuple-element.181.v_ref, ...), custom_call_target="tpu_custom_call" | custom-call | tf_op jit(solution)/shard_map/attend_back/pallas_call | solution.py:312
  573.8 13.1 %collective-permute-done.43 = bf16[128,2048]{1,0:T(8,128)(2,1)} collective-permute-done((bf16[128,2048]{1,0:T(8,128)(2,1)}, bf16[128,2048]{1,0:T(8,128)(2,1)}, u32[]{:S(2)}, u32[]{:S(2)}) %collective-permute-start.43) | collective-permute-done | bytes 524320 | tf_op jit(solution)/shard_map/ppermute | solution.py:676
  619.5 9.6 %collective-permute-start.49 = (bf16[144,576]{1,0:T(8,128)(2,1)S(1)}, bf16[144,576]{1,0:T(8,128)(2,1)S(1)}, u32[]{:S(2)}, u32[]{:S(2)}) collective-permute-start(bf16[144,576]{1,0:T(8,128)(2,1)S(1)} %get-tuple-element.282), channel_id=1, source_target_pairs={{0,4},{1,5},{2,6},{3,7},{4,0},{5,1},{6,2},{7,3},{8,12},{9,13},{10,... | collective-permute-start | bytes 497672 | tf_op jit(solution)/shard_map/ppermute | solution.py:676
  675.6 13.6 %collective-permute-done.61 = bf16[256,512]{1,0:T(8,128)(2,1)} collective-permute-done((bf16[256,512]{1,0:T(8,128)(2,1)}, bf16[256,512]{1,0:T(8,128)(2,1)}, u32[]{:S(2)}, u32[]{:S(2)}) %collective-permute-start.61) | collective-permute-done | bytes 262176 | tf_op jit(solution)/shard_map/ppermute | solution.py:676
  697.8 17.1 %collective-permute-start.64 = (bf16[128,576]{1,0:T(8,128)(2,1)}, bf16[128,576]{1,0:T(8,128)(2,1)S(1)}, u32[]{:S(2)}, u32[]{:S(2)}) collective-permute-start(bf16[128,576]{1,0:T(8,128)(2,1)} %pad_maximum_fusion.5.refs_0_), channel_id=1, source_target_pairs={{0,4},{1,5},{2,6},{3,7},{4,0},{5,1},{6,2},{7,3},{8,12},{9,13},{10,... | collective-permute-start | bytes 442376 | tf_op jit(solution)/shard_map/ppermute | solution.py:676
  717.1 12.8 %collective-permute-done.50 = bf16[128,2048]{1,0:T(8,128)(2,1)} collective-permute-done((bf16[128,2048]{1,0:T(8,128)(2,1)}, bf16[128,2048]{1,0:T(8,128)(2,1)}, u32[]{:S(2)}, u32[]{:S(2)}) %collective-permute-start.50) | collective-permute-done | bytes 524320 | tf_op jit(solution)/shard_map/ppermute | solution.py:676
  729.9 13.0 %collective-permute-done.64.refs_2_ = bf16[128,576]{1,0:T(8,128)(2,1)S(1)} collective-permute-done((bf16[128,576]{1,0:T(8,128)(2,1)}, bf16[128,576]{1,0:T(8,128)(2,1)S(1)}, u32[]{:S(2)}, u32[]{:S(2)}) %collective-permute-start.64) | collective-permute-done | bytes 147488 | tf_op jit(solution)/shard_map/ppermute | solution.py:676
  (442 shorter events, 389.7 us)
Async XLA Ops:
  7.2 90.5 %all-gather.5.cloned.1.call-start = ((), (), s32[]{:S(2)}) async-start(), calls=%async_computation.13 | async-start | bytes 2621440 | tf_op jit(solution)/shard_map/all_gather | solution.py:822
  10.0 252.8 %all-gather.11.cloned.1.call-start = ((), (), s32[]{:S(2)}) async-start(), calls=%async_computation.16 | async-start | bytes 1802240 | tf_op jit(solution)/shard_map/all_gather | solution.py:847
  31.0 48.1 %collective-permute-start.5 = (bf16[128,2048]{1,0:T(8,128)(2,1)S(1)}, bf16[128,2048]{1,0:T(8,128)(2,1)}, u32[]{:S(2)}, u32[]{:S(2)}) collective-permute-start(bf16[128,2048]{1,0:T(8,128)(2,1)S(1)} %copy-done.7), channel_id=1, source_target_pairs={{0,6},{1,7},{2,4},{3,5},{4,2},{5,3},{6,0},{7,1},{8,14},{9,15},{10,... | collective-permute-start | bytes 1572872 | tf_op jit(solution)/shard_map/ppermute | solution.py:676
  79.1 183.6 %all-gather.7.cloned.1.call-start = ((), (), s32[]{:S(2)}) async-start(), calls=%async_computation.14 | async-start | bytes 1966080 | tf_op jit(solution)/shard_map/all_gather | solution.py:845
  117.4 52.9 %collective-permute-start.17 = (bf16[1024,512]{1,0:T(8,128)(2,1)}, bf16[1024,512]{1,0:T(8,128)(2,1)S(1)}, u32[]{:S(2)}, u32[]{:S(2)}) collective-permute-start(bf16[1024,512]{1,0:T(8,128)(2,1)} %constant_dynamic-update-slice_fusion.1.refs_0_), channel_id=1, source_target_pairs={{0,8},{8,0},{16,24},{24,16},{1,9},{9,1},{17,25},{25,17},{2,10},{10... | collective-permute-start | bytes 3145736 | tf_op jit(solution)/shard_map/ppermute | solution.py:676
  118.9 52.8 %collective-permute-start.18 = (bf16[1024,512]{1,0:T(8,128)(2,1)}, bf16[1024,512]{1,0:T(8,128)(2,1)S(1)}, u32[]{:S(2)}, u32[]{:S(2)}) collective-permute-start(bf16[1024,512]{1,0:T(8,128)(2,1)} %constant_dynamic-update-slice_fusion.1.refs_0_), channel_id=1, source_target_pairs={{0,16},{8,24},{16,0},{24,8},{1,17},{9,25},{17,1},{25,9},{2,18},{10... | collective-permute-start | bytes 3145736 | tf_op jit(solution)/shard_map/ppermute | solution.py:676
  123.2 43.2 %collective-permute-start.20 = (bf16[128,2048]{1,0:T(8,128)(2,1)S(1)}, bf16[128,2048]{1,0:T(8,128)(2,1)}, u32[]{:S(2)}, u32[]{:S(2)}) collective-permute-start(bf16[128,2048]{1,0:T(8,128)(2,1)S(1)} %copy-done.11), channel_id=1, source_target_pairs={{0,4},{1,5},{2,6},{3,7},{4,0},{5,1},{6,2},{7,3},{8,12},{9,13},{10,... | collective-permute-start | bytes 1572872 | tf_op jit(solution)/shard_map/ppermute | solution.py:676
  196.6 70.7 %collective-permute-start.24 = (bf16[1024,2048]{1,0:T(8,128)(2,1)}, bf16[1024,2048]{1,0:T(8,128)(2,1)}, u32[]{:S(2)}, u32[]{:S(2)}) collective-permute-start(bf16[1024,2048]{1,0:T(8,128)(2,1)} %arrange.9.we_ref), channel_id=1, source_target_pairs={{0,1},{1,0},{2,3},{3,2},{4,5},{5,4},{6,7},{7,6},{8,9},{9,8},{10,11... | collective-permute-start | bytes 12582920 | tf_op jit(solution)/shard_map/ppermute | solution.py:676
  212.3 45.0 %all-to-all-start = ((bf16[4,128,2048]{2,1,0:T(8,128)(2,1)}), bf16[4,128,2048]{2,1,0:T(8,128)(2,1)S(1)}, u32[]{:S(2)}, u32[]{:S(2)}) async-start(bf16[4,128,2048]{2,1,0:T(8,128)(2,1)} %get-tuple-element.194), calls=%async_computation | async-start | bytes 4194304 | tf_op jit(solution)/shard_map/all_to_all | solution.py:997
  216.0 46.7 %all-gather.9.cloned.1.call-start = ((), (), s32[]{:S(2)}) async-start(), calls=%async_computation.15 | async-start | bytes 1966080 | tf_op jit(solution)/shard_map/all_gather | solution.py:846
  443.6 247.3 %reduce-scatter.10.cloned.1.call-start = ((), (), s32[]{:S(2)}) async-start(), calls=%async_computation.19 | async-start | bytes 1802240 | tf_op jit(solution)/shard_map/reduce_scatter | solution.py:759
  443.6 48.8 %collective-permute-start.34 = (bf16[128,2048]{1,0:T(8,128)(2,1)}, bf16[128,2048]{1,0:T(8,128)(2,1)}, u32[]{:S(2)}, u32[]{:S(2)}) collective-permute-start(bf16[128,2048]{1,0:T(8,128)(2,1)} %get-tuple-element.233), channel_id=1, source_target_pairs={{0,2},{1,3},{2,0},{3,1},{4,6},{5,7},{6,4},{7,5},{8,10},{9,11},{10,... | collective-permute-start | bytes 1572872 | tf_op jit(solution)/shard_map/ppermute | solution.py:676
  456.0 45.4 %collective-permute-start.35 = (bf16[128,2048]{1,0:T(8,128)(2,1)}, bf16[128,2048]{1,0:T(8,128)(2,1)}, u32[]{:S(2)}, u32[]{:S(2)}) collective-permute-start(bf16[128,2048]{1,0:T(8,128)(2,1)} %get-tuple-element.245), channel_id=1, source_target_pairs={{0,4},{1,5},{2,6},{3,7},{4,0},{5,1},{6,2},{7,3},{8,12},{9,13},{10,... | collective-permute-start | bytes 1572872 | tf_op jit(solution)/shard_map/ppermute | solution.py:676
  472.5 56.6 %all-to-all-start.7 = ((bf16[4,128,2048]{2,1,0:T(8,128)(2,1)}), bf16[4,128,2048]{2,1,0:T(8,128)(2,1)}, u32[]{:S(2)}, u32[]{:S(2)}) async-start(bf16[4,128,2048]{2,1,0:T(8,128)(2,1)} %bitcast.176), calls=%async_computation.7 | async-start | bytes 4194304 | tf_op jit(solution)/shard_map/all_to_all | solution.py:997
  477.0 215.9 %reduce-scatter.8.cloned.1.call-start = ((), (), s32[]{:S(2)}) async-start(), calls=%async_computation.18 | async-start | bytes 1966080 | tf_op jit(solution)/shard_map/reduce_scatter | solution.py:759
  534.9 160.0 %reduce-scatter.6.cloned.1.call-start = ((), (), s32[]{:S(2)}) async-start(), calls=%async_computation.17 | async-start | bytes 1966080 | tf_op jit(solution)/shard_map/reduce_scatter | solution.py:759
  552.3 215.6 %reduce-scatter.14.cloned.1.call-start = ((), (), s32[]{:S(2)}) async-start(), calls=%async_computation.21 | async-start | bytes 655360 | tf_op jit(solution)/shard_map/reduce_scatter | solution.py:759
  554.4 52.3 %collective-permute-start.55 = (bf16[128,2048]{1,0:T(8,128)(2,1)}, bf16[128,2048]{1,0:T(8,128)(2,1)}, u32[]{:S(2)}, u32[]{:S(2)}) collective-permute-start(bf16[128,2048]{1,0:T(8,128)(2,1)} %arrange.12), channel_id=1, source_target_pairs={{0,24},{8,16},{16,8},{24,0},{1,25},{9,17},{17,9},{25,1},{2,26},{10... | collective-permute-start | bytes 1572872 | tf_op jit(solution)/shard_map/ppermute | solution.py:676
  556.9 52.3 %collective-permute-start.54 = (bf16[128,2048]{1,0:T(8,128)(2,1)}, bf16[128,2048]{1,0:T(8,128)(2,1)}, u32[]{:S(2)}, u32[]{:S(2)}) collective-permute-start(bf16[128,2048]{1,0:T(8,128)(2,1)} %arrange.12), channel_id=1, source_target_pairs={{0,16},{8,24},{16,0},{24,8},{1,17},{9,25},{17,1},{25,9},{2,18},{10... | collective-permute-start | bytes 1572872 | tf_op jit(solution)/shard_map/ppermute | solution.py:676
  651.9 123.4 %reduce-scatter.12.cloned.1.call-start = ((), (), s32[]{:S(2)}) async-start(), calls=%async_computation.20 | async-start | bytes 1966080 | tf_op jit(solution)/shard_map/reduce_scatter | solution.py:759
  666.9 50.2 %collective-permute-start.52 = (bf16[128,2048]{1,0:T(8,128)(2,1)}, bf16[128,2048]{1,0:T(8,128)(2,1)}, u32[]{:S(2)}, u32[]{:S(2)}) collective-permute-start(bf16[128,2048]{1,0:T(8,128)(2,1)} %get-tuple-element.286), channel_id=1, source_target_pairs={{0,2},{1,3},{2,0},{3,1},{4,6},{5,7},{6,4},{7,5},{8,10},{9,11},{10,... | collective-permute-start | bytes 1572872 | tf_op jit(solution)/shard_map/ppermute | solution.py:676
  668.5 61.4 %collective-permute-start.50 = (bf16[128,2048]{1,0:T(8,128)(2,1)}, bf16[128,2048]{1,0:T(8,128)(2,1)}, u32[]{:S(2)}, u32[]{:S(2)}) collective-permute-start(bf16[128,2048]{1,0:T(8,128)(2,1)} %get-tuple-element.283), channel_id=1, source_target_pairs={{0,4},{1,5},{2,6},{3,7},{4,0},{5,1},{6,2},{7,3},{8,12},{9,13},{10,... | collective-permute-start | bytes 1572872 | tf_op jit(solution)/shard_map/ppermute | solution.py:676
  697.7 45.2 %collective-permute-start.63 = (bf16[128,576]{1,0:T(8,128)(2,1)}, bf16[128,576]{1,0:T(8,128)(2,1)S(1)}, u32[]{:S(2)}, u32[]{:S(2)}) collective-permute-start(bf16[128,576]{1,0:T(8,128)(2,1)} %pad_maximum_fusion.5.refs_0_), channel_id=1, source_target_pairs={{0,2},{1,3},{2,0},{3,1},{4,6},{5,7},{6,4},{7,5},{8,10},{9,11},{10,... | collective-permute-start | bytes 442376 | tf_op jit(solution)/shard_map/ppermute | solution.py:676
  697.8 45.1 %collective-permute-start.64 = (bf16[128,576]{1,0:T(8,128)(2,1)}, bf16[128,576]{1,0:T(8,128)(2,1)S(1)}, u32[]{:S(2)}, u32[]{:S(2)}) collective-permute-start(bf16[128,576]{1,0:T(8,128)(2,1)} %pad_maximum_fusion.5.refs_0_), channel_id=1, source_target_pairs={{0,4},{1,5},{2,6},{3,7},{4,0},{5,1},{6,2},{7,3},{8,12},{9,13},{10,... | collective-permute-start | bytes 442376 | tf_op jit(solution)/shard_map/ppermute | solution.py:676
  (125 other events, 2085.6 us)
Sparse Core Ops, SparseCore 0:
  10.4 47.9 all-gather.4
  79.2 30.1 all-gather.10
  170.4 33.6 all-gather.6
  219.0 42.2 all-gather.8
  457.9 43.8 reduce-scatter.9
  535.0 44.3 reduce-scatter.7
  582.7 35.2 reduce-scatter.5
  652.0 24.8 reduce-scatter.13
  679.9 30.8 reduce-scatter.11

commit v9 on v6

--- a/solution.py
+++ b/solution.py
@@ -618,6 +618,32 @@
         cost_estimate=LIGHT,
         name="down_weights",
     )(index, normed, down_even, down_odd)
+
+
+def output_weights(base, heads, columns, dtype):
+    count, width = heads[0].shape
+    wide = columns[0].shape[1]
+    half = width // 2
+    tile = 256
+    many = len(heads)
+
+    def kernel(*refs):
+        total = 0.0
+        for j in range(many):
+            total = total + t_dot(refs[j][...], refs[many + j][...])
+        refs[-1][...] = total.astype(dtype)
+
+    return pl.pallas_call(
+        kernel,
+        grid=(half // tile,),
+        in_specs=[pl.BlockSpec((count, tile), lambda i: (0, base * (half // tile) + i))] * many
+        + [whole((count, wide))] * many,
+        out_specs=pl.BlockSpec((tile, wide), lambda i: (i, 0)),
+        out_shape=jax.ShapeDtypeStruct((half, wide), dtype),
+        compiler_params=pltpu.CompilerParams(vmem_limit_bytes=LIMIT),
+        cost_estimate=LIGHT,
+        name="output_weights",
+    )(*heads, *columns)
 
 
 def combine(base, masks, returned, products, dtype):
@@ -1039,7 +1065,7 @@
     result_even = along.chips(result)
     gathered = (gate_cols, lift_cols, drop_rows)
     result_even = [after(x, received_grad[0], *gathered) for x in result_even]
-    result_blocks = result_even + siblings(result_even)
+    result_blocks = result_even + [swap(x, "seq", 1) for x in result_even]
     normed_two, residual = add_norm(
         token_blocks,
         result_blocks,
@@ -1052,6 +1078,11 @@
     received = [give(after(send_rows[0], *received_grad))]
 
 
+    shared_rows = after(normed_two, *send_rows)
+    shared_hidden, sgate_grad, sup_grad = shared(
+        shared_rows, grad_rows, gate_cols, lift_cols, drop_rows
+    )
+    received[0] = after(received[0], shared_hidden)
     received += [give(after(x, received[0])) for x in send_rows[1:]]
 
     slot_rows = n_exp * n_seq * CAP
@@ -1066,16 +1097,12 @@
         grads_back.append(give(input_grad.reshape(n_exp, n_seq * CAP, width)))
         results_back.append(expert_result.reshape(n_exp, n_seq * CAP, width))
         kept.append((rows, cots, *saved))
-    shared_rows = after(normed_two, input_grad)
-    shared_hidden, sgate_grad, sup_grad = shared(
-        shared_rows, grad_rows, gate_cols, lift_cols, drop_rows
-    )
     two_products = [(sgate_grad, gate_cols, True), (sup_grad, lift_cols, True)]
     expert_grads = expert_weights(
         after(kept[0][0], input_grad), *kept[0][1:], 0, pieces, None
     )
     gate_part, lift_part, drop_part = expert_weights(
-        shared_rows, grad_rows, shared_hidden, sgate_grad, sup_grad, 0, 1, None, BF
+        after(shared_rows, input_grad), grad_rows, shared_hidden, sgate_grad, sup_grad, 0, 1, None, BF
     )
     token_wide = tokens.astype(F32)
     token_inverse = inverse_rms(token_wide)
@@ -1157,15 +1184,22 @@
         factor,
         columns,
     )
-    late = Lane("exp", 2)
-    attention_parts = late.others(after(own_heads, query_in_grad))
     one_odd, odd_sum = query_back(1, query_in_grad, first_all, normed_one, gain_first, BF)
-    one_even, even_sum = query_back(0, query_in_grad, first_all, normed_one, gain_first, F32)
+    one_even, even_sum = query_back(0, after(query_in_grad, *output_got[:2]), first_all, normed_one, gain_first, F32)
+    late = Lane("exp", 3)
+    attention_parts = late.others(after(own_heads, one_even))
+    column_blocks = [
+        lax.dynamic_slice_in_dim(residual_half, (mine ^ j) * block_rows, block_rows, 1)
+        for j in range(n_exp)
+    ]
+    column_blocks = [column_blocks[0]] + [
+        late.send(column_blocks[j], j) for j in range(1, n_exp)
+    ]
     sums = jnp.concatenate(
         [
             (odd_sum + even_sum).reshape(n_exp, n_seq, gain_rows),
             jnp.sum(second_terms, axis=0).reshape(n_exp, n_seq, gain_rows),
-            after(latent_sum, *output_got[:2], *attention_parts[1:]).reshape(n_exp, n_seq, latent_rows_local),
+            latent_sum.reshape(n_exp, n_seq, latent_rows_local),
         ],
         axis=2,
     )
@@ -1182,18 +1216,9 @@
     )
     one_blocks = along.begin(one_even, one_odd)
     one_got = [along.send(one_blocks[k], 2 * k) for k in range(chips - 1, 0, -1)]
-    column_blocks = [
-        lax.dynamic_slice_in_dim(residual_half, (mine ^ j) * block_rows, block_rows, 1)
-        for j in range(n_exp)
-    ]
-    column_blocks = [column_blocks[0]] + [
-        swap(after(column_blocks[j], one_got[-1]), "exp", j) for j in range(1, n_exp)
-    ]
-    output_part = t_dot(
-        jnp.concatenate([after(x, *one_blocks) for x in attention_parts], axis=0),
-        jnp.concatenate([after(x, *one_blocks) for x in column_blocks], axis=0),
-    )
-    output_blocks = along.begin(output_part[: H * DV // 2], output_part[H * DV // 2 :])
+    output_odd_part = output_weights(1, attention_parts, column_blocks, BF)
+    output_even_part = output_weights(0, attention_parts, column_blocks, F32)
+    output_blocks = along.begin(output_even_part, output_odd_part)
     up_part = t_dot(after(latent_all, one_odd), kv_grad).astype(BF)
     query_part = t_dot(after(normed_one, one_odd), query_in_grad).astype(BF)
     up_out = sum_exp(up_part, 0)

time: 820 us -> 817 us (level)
  blocking collectives: 30.4 us -> 0 us
  waiting for transfers between devices: 262 us -> 279 us
  Pallas kernels: 255 us -> 264 us
  starting transfers between devices: 124 us -> 133 us
    all_to_all x7 -> x8, waiting for transfers between devices: 27.6 us -> 68.6 us  [give(): return lax.all_to_all(rows, 'exp', split_axis=0, concat_axis=0, tiled=True)]
    all_to_all x1 -> x0, blocking collectives: 30.4 us -> none  [give(): return lax.all_to_all(rows, 'exp', split_axis=0, concat_axis=0, tiled=True)]
    ppermute x70, waiting for transfers between devices: 204 us -> 186 us  [swap(): return lax.ppermute(x, axis, [(i, i ^ mask) for i in range(n)])]
    pallas_call x0 -> x2, Pallas kernels: none -> 9.38 us  [output_weights(): pl.pallas_call(kernel, grid=(half // tile,), in_specs=[pl.BlockSpec((coun...]
    all_to_all x7 -> x8, starting transfers between devices: 28.9 us -> 32.9 us  [give(): return lax.all_to_all(rows, 'exp', split_axis=0, concat_axis=0, tiled=True)]
    unnamed x151 -> x139, local copies, waits for them, and re-layouts: 23.8 us -> 23.1 us
  transfers between devices with their start and end apart: 86 -> 87, of which waited for: 31 -> 28; matrix products, arithmetic and copies ran while one was open for 12% -> 11% of each run, Pallas kernels for 30% -> 31%
where the time goes in v9:
time: 817 us; the launch traced here: 809 us
  waiting for transfers between devices  279 us (34%)
  Pallas kernels  264 us (32%)
  starting transfers between devices  133 us (16%)
  other arithmetic  60.1 us (7%)
  local copies, waits for them, and re-layouts  42.6 us (5%)
  matrix products  15.7 us (2%)
  between operations  15.4 us (2%)
    ppermute x70, waiting for transfers between devices, swap(): return lax.ppermute(x, axis, [(i, i ^ mask) for i in range(n)])  186 us
    ppermute x70, starting transfers between devices, swap(): return lax.ppermute(x, axis, [(i, i ^ mask) for i in range(n)])  98.7 us
    all_to_all x8, waiting for transfers between devices, give(): return lax.all_to_all(rows, 'exp', split_axis=0, concat_axis=0, tiled=True)  68.6 us
    pallas_call x2, Pallas kernels, expert(): pl.pallas_call(kernel, grid=(count // tile,), in_specs=[block(width), blo...  55.4 us
    pallas_call x3, Pallas kernels, expert_weights(): pl.pallas_call(kernel, grid=(width // tile,), in_specs=[column, column] +...  41.4 us
    pallas_call x12, Pallas kernels, arrange(): pl.pallas_call(kernel, out_shape=[jax.ShapeDtypeStruct(s, BF) for s in ou...  34.3 us
    all_to_all x8, starting transfers between devices, give(): return lax.all_to_all(rows, 'exp', split_axis=0, concat_axis=0, tiled=True)  32.9 us
    pallas_call x4, Pallas kernels, combine(): pl.pallas_call(kernel, grid=(width // tile,), in_specs=[pl.BlockSpec((hal...  25.7 us
  transfers between devices with their start and end apart: 87, of which 28 were waited for; matrix products, arithmetic and copies ran while one was open for 11% of the time, Pallas kernels for 31%

profile of v9, /device:TPU:0, one launch (start us, length us, event | category | flops | bytes accessed | tf_op | source)
XLA Modules:
  0.0 809.4 jit_solution(12629025644757382435)
XLA Ops:
  30.4 16.0 %collective-permute-done.8.refs_2_ = bf16[80,640]{1,0:T(8,128)(2,1)S(1)} collective-permute-done((bf16[80,640]{1,0:T(8,128)(2,1)S(1)}, bf16[80,640]{1,0:T(8,128)(2,1)S(1)}, u32[]{:S(2)}, u32[]{:S(2)}) %collective-permute-start.8) | collective-permute-done | bytes 102432 | tf_op jit(solution)/shard_map/ppermute | solution.py:703
  53.6 9.5 %collective-permute-done.12.refs_3_ = bf16[320,640]{1,0:T(8,128)(2,1)S(1)} collective-permute-done((bf16[320,640]{1,0:T(8,128)(2,1)}, bf16[320,640]{1,0:T(8,128)(2,1)S(1)}, u32[]{:S(2)}, u32[]{:S(2)}) %collective-permute-start.12) | collective-permute-done | bytes 409632 | tf_op jit(solution)/shard_map/ppermute | solution.py:703
  109.8 14.3 %project.1 = (bf16[1024,2048]{1,0:T(8,128)(2,1)}, bf16[1024,512]{1,0:T(8,128)(2,1)}, f32[1024,512]{1,0:T(8,128)}, bf16[2,1024,256]{2,1,0:T(8,128)(2,1)}, bf16[2,...) custom-call(f32[1,2048]{1,0:T(1,128)} %reshape.282.g_ref, bf16[2048,576]{1,0:T(8,128)(2,1)} %get-tuple-element.162.wd_ref, ...), custom_call_target="tpu_custom_call" | custom-call | tf_op jit(solution)/shard_map/project/pallas_call | solution.py:158
  153.1 16.0 %collective-permute-done.20.refs_2_ = bf16[128,2048]{1,0:T(8,128)(2,1)} collective-permute-done((bf16[128,2048]{1,0:T(8,128)(2,1)S(1)}, bf16[128,2048]{1,0:T(8,128)(2,1)}, u32[]{:S(2)}, u32[]{:S(2)}) %collective-permute-start.20) | collective-permute-done | bytes 524320 | tf_op jit(solution)/shard_map/ppermute | solution.py:703
  183.2 12.6 %collective-permute-done.23.refs_4_ = bf16[512,512]{1,0:T(8,128)(2,1)S(1)} collective-permute-done((bf16[512,512]{1,0:T(8,128)(2,1)}, bf16[512,512]{1,0:T(8,128)(2,1)S(1)}, u32[]{:S(2)}, u32[]{:S(2)}) %collective-permute-start.23) | collective-permute-done | bytes 524320 | tf_op jit(solution)/shard_map/ppermute | solution.py:703
  222.3 29.0 %all-to-all-done = bf16[4,128,2048]{2,1,0:T(8,128)(2,1)S(1)} async-done(((bf16[4,128,2048]{2,1,0:T(8,128)(2,1)}), bf16[4,128,2048]{2,1,0:T(8,128)(2,1)S(1)}, u32[]{:S(2)}, u32[]{:S(2)}) %all-to-all-start) | async-done | bytes 2097184 | tf_op jit(solution)/shard_map/all_to_all | solution.py:1059
  261.1 24.4 %all-gather.9.cloned.1.call-done.wu_ref.refs_6_ = bf16[2048,352]{1,0:T(8,128)(2,1)} async-done(((bf16[512,352]{1,0:T(8,128)(2,1)}), bf16[2048,352]{1,0:T(8,128)(2,1)}) %all-gather.9.cloned.1.call-update) | async-done | bytes 1441808 | tf_op jit(solution)/shard_map/all_gather | solution.py:893
  285.5 17.6 %collective-permute-done.27.refs_2_ = bf16[1024,256]{1,0:T(8,128)(2,1)} collective-permute-done((bf16[1024,256]{1,0:T(8,128)(2,1)S(1)}, bf16[1024,256]{1,0:T(8,128)(2,1)}, u32[]{:S(2)}, u32[]{:S(2)}) %collective-permute-start.27) | collective-permute-done | bytes 524320 | tf_op jit(solution)/shard_map/ppermute | solution.py:703
  307.6 18.3 %add_norm.1 = (bf16[1024,2048]{1,0:T(8,128)(2,1)}, f32[128,2048]{1,0:T(8,128)}) custom-call(bf16[1024,2048]{1,0:T(8,128)(2,1)} %arrange.19.we_ref, bf16[1024,2048]{1,0:T(8,128)(2,1)} %collective-permute-done.24.wo_ref, f32[1,2048]{1,0:T(1,128)} %reshape.285.g_ref, bf16[1024,256]{1,0:T(8,128)(2,1)} %get-tuple-element.237.refs_0_.o_ref, ...), custom_call_target="tpu_custom_call" | custom-call | tf_op jit(solution)/shard_map/add_norm/pallas_call | solution.py:391
  337.8 11.1 %shared.1 = (bf16[1024,352]{1,0:T(8,128)(2,1)}, bf16[1024,352]{1,0:T(8,128)(2,1)}, bf16[1024,352]{1,0:T(8,128)(2,1)}) custom-call(bf16[1024,2048]{1,0:T(8,128)(2,1)} %get-tuple-element.219.x_ref, bf16[1024,2048]{1,0:T(8,128)(2,1)} %arrange.21.x_ref.c_ref, bf16[2048,352]{1,0:T(8,128)(2,1)} %all-gather.7.cloned.1.call-done.wg_ref.refs_4_, ...), custom_call_target="tpu_custom_call" | custom-call | tf_op jit(solution)/shard_map/shared/pallas_call | solution.py:515
  348.8 14.1 %all-to-all-done.2 = bf16[4,128,2048]{2,1,0:T(8,128)(2,1)S(1)} async-done(((bf16[4,128,2048]{2,1,0:T(8,128)(2,1)}), bf16[4,128,2048]{2,1,0:T(8,128)(2,1)S(1)}, u32[]{:S(2)}, u32[]{:S(2)}) %all-to-all-start.2) | async-done | bytes 2097184 | tf_op jit(solution)/shard_map/all_to_all | solution.py:1059
  367.8 27.7 %expert.3 = (bf16[512,2048]{1,0:T(8,128)(2,1)}, bf16[512,2048]{1,0:T(8,128)(2,1)}, bf16[512,1408]{1,0:T(8,128)(2,1)}, bf16[512,1408]{1,0:T(8,128)(2,1)}, bf16[512,1408]{1,0:T(8,128)(2,1)}) custom-call(bf16[512,2048]{1,0:T(8,128)(2,1)} %bitcast.164, bf16[512,2048]{1,0:T(8,128)(2,1)} %bitcast.162, bf16[2,2048,1408]{2,1,0:T(8,128)(2,1)} %gate_hbm.3, ...), custom_call_target="tpu_custom_call" | custom-call | tf_op jit(solution)/shard_map/expert/pallas_call | solution.py:478
  401.5 27.7 %expert.2 = (bf16[512,2048]{1,0:T(8,128)(2,1)}, bf16[512,2048]{1,0:T(8,128)(2,1)}, bf16[512,1408]{1,0:T(8,128)(2,1)}, bf16[512,1408]{1,0:T(8,128)(2,1)}, bf16[512,1408]{1,0:T(8,128)(2,1)}) custom-call(bf16[512,2048]{1,0:T(8,128)(2,1)} %bitcast.160, bf16[512,2048]{1,0:T(8,128)(2,1)} %bitcast.158, bf16[2,2048,1408]{2,1,0:T(8,128)(2,1)} %gate_hbm.3, ...), custom_call_target="tpu_custom_call" | custom-call | tf_op jit(solution)/shard_map/expert/pallas_call | solution.py:478
  433.4 11.5 %expert_weights.4 = (bf16[1,2048,352]{2,1,0:T(8,128)(2,1)}, bf16[1,2048,352]{2,1,0:T(8,128)(2,1)}, bf16[1,352,2048]{2,1,0:T(8,128)(2,1)}) custom-call(bf16[1024,2048]{1,0:T(8,128)(2,1)} %get-tuple-element.219.x_ref, bf16[1024,2048]{1,0:T(8,128)(2,1)} %arrange.21.x_ref.c_ref, bf16[1024,352]{1,0:T(8,128)(2,1)} %get-tuple-element.208.h_ref.refs_4_, ...), custom_call_target="tpu_custom_call" | custom-call | tf_op jit(solution)/shard_map/expert_weights/pallas_call | solution.py:542
  444.9 14.9 %expert_weights.3 = (f32[2,2048,1408]{2,1,0:T(8,128)}, f32[2,2048,1408]{2,1,0:T(8,128)}, f32[2,1408,2048]{2,1,0:T(8,128)}) custom-call(bf16[512,2048]{1,0:T(8,128)(2,1)} %bitcast.165, bf16[512,2048]{1,0:T(8,128)(2,1)} %bitcast.163, bf16[512,1408]{1,0:T(8,128)(2,1)} %get-tuple-element.213.h_ref, bf16[512,1408]{1,0:T(8,128)(2,1)} %get-tuple-element.214.gg_ref, ...), custom_call_target="tpu_custom_call" | custom-call | tf_op jit(solution)/shard_map/expert_weights/pallas_call | solution.py:542
  491.0 25.5 %all-to-all-done.6.refs_2_ = bf16[4,128,2048]{2,1,0:T(8,128)(2,1)S(1)} async-done(((bf16[4,128,2048]{2,1,0:T(8,128)(2,1)}), bf16[4,128,2048]{2,1,0:T(8,128)(2,1)S(1)}, u32[]{:S(2)}, u32[]{:S(2)}) %all-to-all-start.6) | async-done | bytes 2097184 | tf_op jit(solution)/shard_map/all_to_all | solution.py:1059
  522.6 15.1 %expert_weights.5 = (f32[2,2048,1408]{2,1,0:T(8,128)}, f32[2,2048,1408]{2,1,0:T(8,128)}, f32[2,1408,2048]{2,1,0:T(8,128)}) custom-call(bf16[512,2048]{1,0:T(8,128)(2,1)} %bitcast.161, bf16[512,2048]{1,0:T(8,128)(2,1)} %bitcast.159, bf16[512,1408]{1,0:T(8,128)(2,1)} %get-tuple-element.231.h_ref, ...), custom_call_target="tpu_custom_call", output_to_operand_aliasing={{0}: (5, {}), {1}: (6, {}), {2}: (7, {})} | custom-call | tf_op jit(solution)/shard_map/expert_weights/pallas_call | solution.py:542
  589.5 14.1 %attend_back.1 = (bf16[1024,384]{1,0:T(8,128)(2,1)}, bf16[1024,512]{1,0:T(8,128)(2,1)}, f32[1024,640]{1,0:T(8,128)}, f32[1,512]{1,0:T(1,128)}) custom-call(bf16[2,1024,256]{2,1,0:T(8,128)(2,1)} %get-tuple-element.173.q_ref, bf16[2,1024,256]{2,1,0:T(8,128)(2,1)} %get-tuple-element.174.k_ref, bf16[2,1024,128]{2,1,0:T(8,128)(2,1)} %get-tuple-element.175.v_ref, ...), custom_call_target="tpu_custom_call" | custom-call | tf_op jit(solution)/shard_map/attend_back/pallas_call | solution.py:313
  610.8 9.4 %collective-permute-done.43 = bf16[128,2048]{1,0:T(8,128)(2,1)} collective-permute-done((bf16[128,2048]{1,0:T(8,128)(2,1)}, bf16[128,2048]{1,0:T(8,128)(2,1)}, u32[]{:S(2)}, u32[]{:S(2)}) %collective-permute-start.43) | collective-permute-done | bytes 524320 | tf_op jit(solution)/shard_map/ppermute | solution.py:703
  642.7 11.4 %collective-permute-start.45 = (bf16[128,2048]{1,0:T(8,128)(2,1)}, bf16[128,2048]{1,0:T(8,128)(2,1)}, u32[]{:S(2)}, u32[]{:S(2)}) collective-permute-start(bf16[128,2048]{1,0:T(8,128)(2,1)} %get-tuple-element.261), channel_id=1, source_target_pairs={{0,2},{1,3},{2,0},{3,1},{4,6},{5,7},{6,4},{7,5},{8,10},{9,11},{10,... | collective-permute-start | bytes 1572872 | tf_op jit(solution)/shard_map/ppermute | solution.py:703
  710.3 16.1 %collective-permute-done.52 = bf16[128,2048]{1,0:T(8,128)(2,1)S(1)} collective-permute-done((bf16[128,2048]{1,0:T(8,128)(2,1)}, bf16[128,2048]{1,0:T(8,128)(2,1)S(1)}, u32[]{:S(2)}, u32[]{:S(2)}) %collective-permute-start.52) | collective-permute-done | bytes 524320 | tf_op jit(solution)/shard_map/ppermute | solution.py:703
  731.2 10.3 %collective-permute-done.50 = bf16[128,2048]{1,0:T(8,128)(2,1)} collective-permute-done((bf16[128,2048]{1,0:T(8,128)(2,1)}, bf16[128,2048]{1,0:T(8,128)(2,1)}, u32[]{:S(2)}, u32[]{:S(2)}) %collective-permute-start.50) | collective-permute-done | bytes 524320 | tf_op jit(solution)/shard_map/ppermute | solution.py:703
  750.0 13.1 %collective-permute-done.61.refs_2_ = bf16[128,640]{1,0:T(8,128)(2,1)S(1)} collective-permute-done((bf16[128,640]{1,0:T(8,128)(2,1)S(1)}, bf16[128,640]{1,0:T(8,128)(2,1)S(1)}, u32[]{:S(2)}, u32[]{:S(2)}) %collective-permute-start.61) | collective-permute-done | bytes 163872 | tf_op jit(solution)/shard_map/ppermute | solution.py:703
  788.4 8.6 %collective-permute-done.68 = bf16[256,512]{1,0:T(8,128)(2,1)S(1)} collective-permute-done((bf16[256,512]{1,0:T(8,128)(2,1)}, bf16[256,512]{1,0:T(8,128)(2,1)S(1)}, u32[]{:S(2)}, u32[]{:S(2)}) %collective-permute-start.68) | collective-permute-done | bytes 262176 | tf_op jit(solution)/shard_map/ppermute | solution.py:703
  (452 shorter events, 405.7 us)
Async XLA Ops:
  7.2 100.0 %all-gather.5.cloned.1.call-start = ((), (), s32[]{:S(2)}) async-start(), calls=%async_computation.13 | async-start | bytes 2621440 | tf_op jit(solution)/shard_map/all_gather | solution.py:874
  10.0 251.1 %all-gather.11.cloned.1.call-start = ((), (), s32[]{:S(2)}) async-start(), calls=%async_computation.16 | async-start | bytes 1802240 | tf_op jit(solution)/shard_map/all_gather | solution.py:894
  10.0 43.5 %collective-permute-start = (bf16[128,2048]{1,0:T(8,128)(2,1)}, bf16[128,2048]{1,0:T(8,128)(2,1)S(1)}, u32[]{:S(2)}, u32[]{:S(2)}) collective-permute-start(bf16[128,2048]{1,0:T(8,128)(2,1)} %refs_8_.1), channel_id=1, source_target_pairs={{0,6},{1,7},{2,4},{3,5},{4,2},{5,3},{6,0},{7,1},{8,14},{9,15},{10,... | collective-permute-start | bytes 1572872 | tf_op jit(solution)/shard_map/ppermute | solution.py:703
  88.8 172.3 %all-gather.7.cloned.1.call-start = ((), (), s32[]{:S(2)}) async-start(), calls=%async_computation.14 | async-start | bytes 1966080 | tf_op jit(solution)/shard_map/all_gather | solution.py:892
  105.6 47.5 %collective-permute-start.21 = (bf16[128,2048]{1,0:T(8,128)(2,1)S(1)}, bf16[128,2048]{1,0:T(8,128)(2,1)S(1)}, u32[]{:S(2)}, u32[]{:S(2)}) collective-permute-start(bf16[128,2048]{1,0:T(8,128)(2,1)S(1)} %copy-done.12), channel_id=1, source_target_pairs={{0,6},{1,7},{2,4},{3,5},{4,2},{5,3},{6,0},{7,1},{8,14},{9,15},{10,... | collective-permute-start | bytes 1572872 | tf_op jit(solution)/shard_map/ppermute | solution.py:703
  134.2 39.8 %collective-permute-start.17 = (bf16[1024,512]{1,0:T(8,128)(2,1)}, bf16[1024,512]{1,0:T(8,128)(2,1)S(1)}, u32[]{:S(2)}, u32[]{:S(2)}) collective-permute-start(bf16[1024,512]{1,0:T(8,128)(2,1)} %arrange.16.refs_0_), channel_id=1, source_target_pairs={{0,8},{8,0},{16,24},{24,16},{1,9},{9,1},{17,25},{25,17},{2,10},{10... | collective-permute-start | bytes 3145736 | tf_op jit(solution)/shard_map/ppermute | solution.py:703
  204.5 103.2 %collective-permute-start.24 = (bf16[1024,2048]{1,0:T(8,128)(2,1)}, bf16[1024,2048]{1,0:T(8,128)(2,1)}, u32[]{:S(2)}, u32[]{:S(2)}) collective-permute-start(bf16[1024,2048]{1,0:T(8,128)(2,1)} %arrange.19.we_ref), channel_id=1, source_target_pairs={{0,1},{1,0},{2,3},{3,2},{4,5},{5,4},{6,7},{7,6},{8,9},{9,8},{10,11... | collective-permute-start | bytes 12582920 | tf_op jit(solution)/shard_map/ppermute | solution.py:703
  221.3 64.3 %all-gather.9.cloned.1.call-start = ((), (), s32[]{:S(2)}) async-start(), calls=%async_computation.15 | async-start | bytes 1966080 | tf_op jit(solution)/shard_map/all_gather | solution.py:893
  252.6 73.3 %all-to-all-start.1 = ((bf16[4,128,2048]{2,1,0:T(8,128)(2,1)}), bf16[4,128,2048]{2,1,0:T(8,128)(2,1)S(1)}, u32[]{:S(2)}, u32[]{:S(2)}) async-start(bf16[4,128,2048]{2,1,0:T(8,128)(2,1)} %get-tuple-element.202), calls=%async_computation.1 | async-start | bytes 4194304 | tf_op jit(solution)/shard_map/all_to_all | solution.py:1059
  259.2 43.9 %collective-permute-start.27 = (bf16[1024,256]{1,0:T(8,128)(2,1)S(1)}, bf16[1024,256]{1,0:T(8,128)(2,1)}, u32[]{:S(2)}, u32[]{:S(2)}) collective-permute-start(bf16[1024,256]{1,0:T(8,128)(2,1)S(1)} %copy-done.15), channel_id=1, source_target_pairs={{0,4},{1,5},{2,6},{3,7},{4,0},{5,1},{6,2},{7,3},{8,12},{9,13},{10,... | collective-permute-start | bytes 1572872 | tf_op jit(solution)/shard_map/ppermute | solution.py:703
  259.2 43.9 %collective-permute-start.26 = (bf16[1024,256]{1,0:T(8,128)(2,1)S(1)}, bf16[1024,256]{1,0:T(8,128)(2,1)}, u32[]{:S(2)}, u32[]{:S(2)}) collective-permute-start(bf16[1024,256]{1,0:T(8,128)(2,1)S(1)} %copy-done.15), channel_id=1, source_target_pairs={{0,2},{1,3},{2,0},{3,1},{4,6},{5,7},{6,4},{7,5},{8,10},{9,11},{10,... | collective-permute-start | bytes 1572872 | tf_op jit(solution)/shard_map/ppermute | solution.py:703
  433.4 222.0 %reduce-scatter.10.cloned.1.call-start = ((), (), s32[]{:S(2)}) async-start(), calls=%async_computation.19 | async-start | bytes 1802240 | tf_op jit(solution)/shard_map/reduce_scatter | solution.py:811
  483.3 174.1 %reduce-scatter.8.cloned.1.call-start = ((), (), s32[]{:S(2)}) async-start(), calls=%async_computation.18 | async-start | bytes 1966080 | tf_op jit(solution)/shard_map/reduce_scatter | solution.py:811
  483.3 54.4 %collective-permute-start.34 = (bf16[128,2048]{1,0:T(8,128)(2,1)}, bf16[128,2048]{1,0:T(8,128)(2,1)}, u32[]{:S(2)}, u32[]{:S(2)}) collective-permute-start(bf16[128,2048]{1,0:T(8,128)(2,1)} %get-tuple-element.227), channel_id=1, source_target_pairs={{0,2},{1,3},{2,0},{3,1},{4,6},{5,7},{6,4},{7,5},{8,10},{9,11},{10,... | collective-permute-start | bytes 1572872 | tf_op jit(solution)/shard_map/ppermute | solution.py:703
  483.3 54.4 %collective-permute-start.36 = (bf16[128,2048]{1,0:T(8,128)(2,1)}, bf16[128,2048]{1,0:T(8,128)(2,1)}, u32[]{:S(2)}, u32[]{:S(2)}) collective-permute-start(bf16[128,2048]{1,0:T(8,128)(2,1)} %get-tuple-element.241), channel_id=1, source_target_pairs={{0,6},{1,7},{2,4},{3,5},{4,2},{5,3},{6,0},{7,1},{8,14},{9,15},{10,... | collective-permute-start | bytes 1572872 | tf_op jit(solution)/shard_map/ppermute | solution.py:703
  485.6 52.1 %collective-permute-start.35 = (bf16[128,2048]{1,0:T(8,128)(2,1)}, bf16[128,2048]{1,0:T(8,128)(2,1)}, u32[]{:S(2)}, u32[]{:S(2)}) collective-permute-start(bf16[128,2048]{1,0:T(8,128)(2,1)} %get-tuple-element.239), channel_id=1, source_target_pairs={{0,4},{1,5},{2,6},{3,7},{4,0},{5,1},{6,2},{7,3},{8,12},{9,13},{10,... | collective-permute-start | bytes 1572872 | tf_op jit(solution)/shard_map/ppermute | solution.py:703
  517.9 41.1 %all-to-all-start.7 = ((bf16[4,128,2048]{2,1,0:T(8,128)(2,1)}), bf16[4,128,2048]{2,1,0:T(8,128)(2,1)}, u32[]{:S(2)}, u32[]{:S(2)}) async-start(bf16[4,128,2048]{2,1,0:T(8,128)(2,1)} %bitcast.167), calls=%async_computation.7 | async-start | bytes 4194304 | tf_op jit(solution)/shard_map/all_to_all | solution.py:1059
  522.4 137.1 %reduce-scatter.6.cloned.1.call-start = ((), (), s32[]{:S(2)}) async-start(), calls=%async_computation.17 | async-start | bytes 1966080 | tf_op jit(solution)/shard_map/reduce_scatter | solution.py:811
  565.1 118.5 %reduce-scatter.14.cloned.1.call-start = ((), (), s32[]{:S(2)}) async-start(), calls=%async_computation.21 | async-start | bytes 655360 | tf_op jit(solution)/shard_map/reduce_scatter | solution.py:811
  635.8 62.5 %collective-permute-start.44 = (bf16[512,2048]{1,0:T(8,128)(2,1)}, bf16[512,2048]{1,0:T(8,128)(2,1)}, u32[]{:S(2)}, u32[]{:S(2)}) collective-permute-start(bf16[512,2048]{1,0:T(8,128)(2,1)} %get-tuple-element.258), channel_id=1, source_target_pairs={{0,1},{1,0},{2,3},{3,2},{4,5},{5,4},{6,7},{7,6},{8,9},{9,8},{10,11... | collective-permute-start | bytes 6291464 | tf_op jit(solution)/shard_map/ppermute | solution.py:703
  638.8 159.1 %reduce-scatter.12.cloned.1.call-start = ((), (), s32[]{:S(2)}) async-start(), calls=%async_computation.20 | async-start | bytes 1966080 | tf_op jit(solution)/shard_map/reduce_scatter | solution.py:811
  705.6 44.4 %collective-permute-start.48 = (bf16[128,2048]{1,0:T(8,128)(2,1)}, bf16[128,2048]{1,0:T(8,128)(2,1)}, u32[]{:S(2)}, u32[]{:S(2)}) collective-permute-start(bf16[128,2048]{1,0:T(8,128)(2,1)} %get-tuple-element.268), channel_id=1, source_target_pairs={{0,6},{1,7},{2,4},{3,5},{4,2},{5,3},{6,0},{7,1},{8,14},{9,15},{10,... | collective-permute-start | bytes 1572872 | tf_op jit(solution)/shard_map/ppermute | solution.py:703
  707.4 55.7 %collective-permute-start.60 = (bf16[128,640]{1,0:T(8,128)(2,1)S(1)}, bf16[128,640]{1,0:T(8,128)(2,1)S(1)}, u32[]{:S(2)}, u32[]{:S(2)}) collective-permute-start(bf16[128,640]{1,0:T(8,128)(2,1)S(1)} %maximum_maximum_fusion.1.refs_0_), channel_id=1, source_target_pairs={{0,2},{1,3},{2,0},{3,1},{4,6},{5,7},{6,4},{7,5},{8,10},{9,11},{10,... | collective-permute-start | bytes 491528 | tf_op jit(solution)/shard_map/ppermute | solution.py:703
  707.5 55.6 %collective-permute-start.61 = (bf16[128,640]{1,0:T(8,128)(2,1)S(1)}, bf16[128,640]{1,0:T(8,128)(2,1)S(1)}, u32[]{:S(2)}, u32[]{:S(2)}) collective-permute-start(bf16[128,640]{1,0:T(8,128)(2,1)S(1)} %maximum_maximum_fusion.1.refs_0_), channel_id=1, source_target_pairs={{0,4},{1,5},{2,6},{3,7},{4,0},{5,1},{6,2},{7,3},{8,12},{9,13},{10,... | collective-permute-start | bytes 491528 | tf_op jit(solution)/shard_map/ppermute | solution.py:703
  (130 other events, 2148.6 us)
Sparse Core Ops, SparseCore 0:
  10.4 38.0 all-gather.4
  88.9 29.1 all-gather.10
  174.1 34.7 all-gather.6
  223.6 61.8 all-gather.8
  479.0 47.2 reduce-scatter.9
  529.4 43.4 reduce-scatter.7
  576.2 30.9 reduce-scatter.5
  638.9 35.9 reduce-scatter.13
  683.7 29.9 reduce-scatter.11

commit v10 on v8

--- a/solution.py
+++ b/solution.py
@@ -617,6 +617,32 @@
         cost_estimate=LIGHT,
         name="down_weights",
     )(index, normed, down_even, down_odd)
+
+
+def output_weights(base, heads, columns, dtype):
+    count, width = heads[0].shape
+    wide = columns[0].shape[1]
+    half = width // 2
+    tile = 256
+    many = len(heads)
+
+    def kernel(*refs):
+        total = 0.0
+        for j in range(many):
+            total = total + t_dot(refs[j][...], refs[many + j][...])
+        refs[-1][...] = total.astype(dtype)
+
+    return pl.pallas_call(
+        kernel,
+        grid=(half // tile,),
+        in_specs=[pl.BlockSpec((count, tile), lambda i: (0, base * (half // tile) + i))] * many
+        + [whole((count, wide))] * many,
+        out_specs=pl.BlockSpec((tile, wide), lambda i: (i, 0)),
+        out_shape=jax.ShapeDtypeStruct((half, wide), dtype),
+        compiler_params=pltpu.CompilerParams(vmem_limit_bytes=LIMIT),
+        cost_estimate=LIGHT,
+        name="output_weights",
+    )(*heads, *columns)
 
 
 def combine(base, masks, returned, products, dtype):
@@ -1050,7 +1076,9 @@
     gate_part, lift_part, drop_part = expert_weights(
         after(shared_rows, input_grad), grad_rows, shared_hidden, sgate_grad, sup_grad, 0, 1, None, BF
     )
-    select = after(select, *expert_grads, gate_part, lift_part, drop_part)
+    token_wide = tokens.astype(F32)
+    token_inverse = inverse_rms(token_wide)
+    select = after(select, *expert_grads, gate_part, lift_part, drop_part, token_inverse)
     two_odd = combine(1, [select], grads_back, two_products, BF)
     two_even = combine(0, [select], grads_back, two_products, F32)
     two_blocks = along.begin(two_even, two_odd)
@@ -1101,17 +1129,6 @@
     attention_grad = jnp.concatenate(
         [jnp.stack([pair[0] for pair in pairs]), other_half], axis=0
     ).reshape(length, wide)
-    mine = lax.axis_index("exp")
-    late = Lane("exp", 3)
-    attention_parts = late.others(after(own_heads, attention_grad))
-    column_blocks = [
-        lax.dynamic_slice_in_dim(residual_half, (mine ^ j) * block_rows, block_rows, 1)
-        for j in range(n_exp)
-    ]
-    column_blocks = [column_blocks[0]] + [
-        late.send(column_blocks[j], j) for j in range(1, n_exp)
-    ]
-
     out_products = [(shared_hidden, drop_rows, False)]
     out_masks = [weighted_high, weighted_low]
     out_masks = [after(mask, *stacks, *pairs[1:]) for mask in out_masks]
@@ -1136,9 +1153,18 @@
         latent_wide,
         factor,
     )
-    query_in_grad = after(query_in_grad, *output_got)
     one_odd, odd_sum = query_back(1, query_in_grad, first_all, normed_one, gain_first, BF)
-    one_even, even_sum = query_back(0, query_in_grad, first_all, normed_one, gain_first, F32)
+    one_even, even_sum = query_back(0, after(query_in_grad, *output_got[:2]), first_all, normed_one, gain_first, F32)
+    mine = lax.axis_index("exp")
+    late = Lane("exp", 3)
+    attention_parts = late.others(after(own_heads, one_even))
+    column_blocks = [
+        lax.dynamic_slice_in_dim(residual_half, (mine ^ j) * block_rows, block_rows, 1)
+        for j in range(n_exp)
+    ]
+    column_blocks = [column_blocks[0]] + [
+        late.send(column_blocks[j], j) for j in range(1, n_exp)
+    ]
     sums = jnp.concatenate(
         [
             (odd_sum + even_sum).reshape(n_exp, n_seq, gain_rows),
@@ -1155,18 +1181,16 @@
     )
     latent_part = jnp.concatenate([latent_part.reshape(n_seq, count, columns), sums], axis=1)
     latent_part = latent_part.reshape(n_seq * (count + 16), columns)
-    output_part = t_dot(
-        jnp.concatenate([after(x, query_in_grad) for x in attention_parts], axis=0),
-        jnp.concatenate([after(x, query_in_grad) for x in column_blocks], axis=0),
-    )
-    output_blocks = along.begin(output_part[: H * DV // 2], output_part[H * DV // 2 :])
     latent_grad = along.scatter(
         latent_part[: chips * (count + 16)], latent_part[chips * (count + 16) :]
     )
     one_blocks = along.begin(one_even, one_odd)
     one_got = [along.send(one_blocks[k], 2 * k) for k in range(chips - 1, 0, -1)]
-    up_part = t_dot(after(latent_all, *one_blocks), kv_grad).astype(BF)
-    query_part = t_dot(after(normed_one, *one_blocks), query_in_grad).astype(BF)
+    output_odd_part = output_weights(1, attention_parts, column_blocks, BF)
+    output_even_part = output_weights(0, attention_parts, column_blocks, F32)
+    output_blocks = along.begin(output_even_part, output_odd_part)
+    up_part = t_dot(after(latent_all, one_odd), kv_grad).astype(BF)
+    query_part = t_dot(after(normed_one, one_odd), query_in_grad).astype(BF)
     up_out = sum_exp(up_part, 0)
     query_out = sum_exp(query_part, 0)
     sums = latent_grad[count, : n_exp * many].reshape(n_exp, 1, many)
@@ -1181,10 +1205,12 @@
         ],
         axis=1,
     ).astype(BF)
-    wide_got = [free.send(output_blocks[k], 2 * k) for k in range(chips - 1, 0, -1)]
     down_even, down_odd = free.pair(
-        [after(x, *one_got, *wide_got) for x in free.chips(down_rows)]
-    )
+        [after(x, *one_got, *output_blocks) for x in free.chips(down_rows)]
+    )
+    wide_got = [
+        swap(after(output_blocks[k], down_even), "seq", 2 * k) for k in range(chips - 1, 0, -1)
+    ]
     down_part = down_weights(index, normed_one, down_even, down_odd, n_exp, n_seq, gain_rows)
     down_part = jnp.concatenate(
         [
@@ -1215,9 +1241,8 @@
         block = after(block, up_part, query_part, gate_out, lift_out, drop_out)
         one_grad = one_grad + block.astype(F32)
     down_back = dot_t(down_rows, down_full)
-    token_wide = tokens.astype(F32)
     token_norm_grad, _ = norm_back(
-        one_grad + down_back, token_wide, inverse_rms(token_wide), gain_first
+        one_grad + down_back, token_wide, token_inverse, gain_first
     )
     tokens_grad = (residual_grad + token_norm_grad).astype(BF)
     return (

time: 798 us -> 782 us (0.980)
  waiting for transfers between devices: 253 us -> 239 us
  Pallas kernels: 244 us -> 253 us
    ppermute x70, waiting for transfers between devices: 228 us -> 208 us  [swap(): return lax.ppermute(x, axis, [(i, i ^ mask) for i in range(n)])]
    pallas_call x0 -> x2, Pallas kernels: none -> 9.41 us  [output_weights(): pl.pallas_call(kernel, grid=(half // tile,), in_specs=[pl.BlockSpec((coun...]
    unnamed x130 -> x134, local copies, waits for them, and re-layouts: 19 us -> 20.3 us
  transfers between devices with their start and end apart: 87 -> 87, of which waited for: 34 -> 30; matrix products, arithmetic and copies ran while one was open for 14% -> 13% of each run, Pallas kernels for 30% -> 32%
where the time goes in v10:
time: 782 us; the launch traced here: 769 us
  Pallas kernels  253 us (32%)
  waiting for transfers between devices  239 us (31%)
  starting transfers between devices  138 us (18%)
  other arithmetic  64.7 us (8%)
  local copies, waits for them, and re-layouts  42.3 us (5%)
  matrix products  16.8 us (2%)
  between operations  15.4 us (2%)
    ppermute x70, waiting for transfers between devices, swap(): return lax.ppermute(x, axis, [(i, i ^ mask) for i in range(n)])  208 us
    ppermute x70, starting transfers between devices, swap(): return lax.ppermute(x, axis, [(i, i ^ mask) for i in range(n)])  103 us
    pallas_call x2, Pallas kernels, expert(): pl.pallas_call(kernel, grid=(count // tile,), in_specs=[block(width), blo...  55.3 us
    pallas_call x3, Pallas kernels, expert_weights(): pl.pallas_call(kernel, grid=(width // tile,), in_specs=[column, column] +...  41.4 us
    all_to_all x8, starting transfers between devices, give(): return lax.all_to_all(rows, 'exp', split_axis=0, concat_axis=0, tiled=True)  33.6 us
    all_to_all x8, waiting for transfers between devices, give(): return lax.all_to_all(rows, 'exp', split_axis=0, concat_axis=0, tiled=True)  30.6 us
    pallas_call x4, Pallas kernels, combine(): pl.pallas_call(kernel, grid=(width // tile,), in_specs=[pl.BlockSpec((hal...  25.8 us
    pallas_call x7, Pallas kernels, arrange(): pl.pallas_call(kernel, out_shape=[jax.ShapeDtypeStruct(s, BF) for s in ou...  23.8 us
  transfers between devices with their start and end apart: 87, of which 30 were waited for; matrix products, arithmetic and copies ran while one was open for 13% of the time, Pallas kernels for 32%

profile of v10, /device:TPU:0, one launch (start us, length us, event | category | flops | bytes accessed | tf_op | source)
XLA Modules:
  0.0 768.8 jit_solution(10093644632906960281)
XLA Ops:
  45.5 13.3 %collective-permute-done.12 = bf16[4,80,576]{2,1,0:T(8,128)(2,1)} collective-permute-done((bf16[4,80,576]{2,1,0:T(8,128)(2,1)}, bf16[4,80,576]{2,1,0:T(8,128)(2,1)}, u32[]{:S(2)}, u32[]{:S(2)}) %collective-permute-start.12) | collective-permute-done | bytes 368672 | tf_op jit(solution)/shard_map/ppermute | solution.py:702
  60.7 18.2 %collective-permute-done.3.refs_2_.refs_10_ = bf16[128,2048]{1,0:T(8,128)(2,1)S(1)} collective-permute-done((bf16[128,2048]{1,0:T(8,128)(2,1)S(1)}, bf16[128,2048]{1,0:T(8,128)(2,1)S(1)}, u32[]{:S(2)}, u32[]{:S(2)}) %collective-permute-start.3) | collective-permute-done | bytes 524320 | tf_op jit(solution)/shard_map/ppermute | solution.py:702
  100.0 14.4 %project.1 = (bf16[1024,2048]{1,0:T(8,128)(2,1)}, bf16[1024,512]{1,0:T(8,128)(2,1)}, f32[1024,512]{1,0:T(8,128)}, bf16[2,1024,256]{2,1,0:T(8,128)(2,1)}, bf16[2,...) custom-call(f32[1,2048]{1,0:T(1,128)} %reshape.277.g_ref, bf16[2048,576]{1,0:T(8,128)(2,1)} %get-tuple-element.160.wd_ref, ...), custom_call_target="tpu_custom_call" | custom-call | tf_op jit(solution)/shard_map/project/pallas_call | solution.py:158
  125.8 8.3 %attend.1 = (bf16[1024,256]{1,0:T(8,128)(2,1)}, f32[2,1024]{1,0:T(2,128)}) custom-call(bf16[2,1024,256]{2,1,0:T(8,128)(2,1)} %get-tuple-element.171.q_ref, bf16[2,1024,256]{2,1,0:T(8,128)(2,1)} %get-tuple-element.172.k_ref, bf16[2,1024,128]{2,1,0:T(8,128)(2,1)} %get-tuple-element.173.v_ref, s32[1,1024]{1,0:T(1,128)} %bitcast.195, s32[1024,1]{1,0:T(8,128)} %copy.82.column_ref), custom_call_target="tpu_custom_call" | custom-call | tf_op jit(solution)/shard_map/attend/pallas_call | solution.py:236
  137.1 29.1 %collective-permute-done.20.refs_2_ = bf16[128,2048]{1,0:T(8,128)(2,1)} collective-permute-done((bf16[128,2048]{1,0:T(8,128)(2,1)S(1)}, bf16[128,2048]{1,0:T(8,128)(2,1)}, u32[]{:S(2)}, u32[]{:S(2)}) %collective-permute-start.20) | collective-permute-done | bytes 524320 | tf_op jit(solution)/shard_map/ppermute | solution.py:702
  174.1 15.7 %collective-permute-done.23.refs_4_ = bf16[512,512]{1,0:T(8,128)(2,1)S(1)} collective-permute-done((bf16[512,512]{1,0:T(8,128)(2,1)}, bf16[512,512]{1,0:T(8,128)(2,1)S(1)}, u32[]{:S(2)}, u32[]{:S(2)}) %collective-permute-start.23) | collective-permute-done | bytes 524320 | tf_op jit(solution)/shard_map/ppermute | solution.py:702
  221.8 20.7 %collective-permute-done.26.refs_1_ = bf16[1024,256]{1,0:T(8,128)(2,1)S(1)} collective-permute-done((bf16[1024,256]{1,0:T(8,128)(2,1)S(1)}, bf16[1024,256]{1,0:T(8,128)(2,1)S(1)}, u32[]{:S(2)}, u32[]{:S(2)}) %collective-permute-start.26) | collective-permute-done | bytes 524320 | tf_op jit(solution)/shard_map/ppermute | solution.py:702
  242.5 13.1 %collective-permute-done.27.refs_2_ = bf16[1024,256]{1,0:T(8,128)(2,1)S(1)} collective-permute-done((bf16[1024,256]{1,0:T(8,128)(2,1)S(1)}, bf16[1024,256]{1,0:T(8,128)(2,1)S(1)}, u32[]{:S(2)}, u32[]{:S(2)}) %collective-permute-start.27) | collective-permute-done | bytes 524320 | tf_op jit(solution)/shard_map/ppermute | solution.py:702
  267.3 18.2 %add_norm.1 = (bf16[1024,2048]{1,0:T(8,128)(2,1)}, f32[128,2048]{1,0:T(8,128)}) custom-call(bf16[1024,2048]{1,0:T(8,128)(2,1)} %arrange.9.we_ref, bf16[1024,2048]{1,0:T(8,128)(2,1)} %collective-permute-done.24.wo_ref, f32[1,2048]{1,0:T(1,128)} %reshape.279.g_ref, bf16[1024,256]{1,0:T(8,128)(2,1)} %get-tuple-element.235.refs_0_.o_ref, ...), custom_call_target="tpu_custom_call" | custom-call | tf_op jit(solution)/shard_map/add_norm/pallas_call | solution.py:390
  298.9 11.1 %shared.1 = (bf16[1024,352]{1,0:T(8,128)(2,1)}, bf16[1024,352]{1,0:T(8,128)(2,1)}, bf16[1024,352]{1,0:T(8,128)(2,1)}) custom-call(bf16[1024,2048]{1,0:T(8,128)(2,1)} %get-tuple-element.217.x_ref, bf16[1024,2048]{1,0:T(8,128)(2,1)} %arrange.11.x_ref.c_ref, bf16[2048,352]{1,0:T(8,128)(2,1)} %all-gather.7.cloned.1.call-done.wg_ref.refs_4_, ...), custom_call_target="tpu_custom_call" | custom-call | tf_op jit(solution)/shard_map/shared/pallas_call | solution.py:514
  310.0 14.7 %all-to-all-done.2 = bf16[4,128,2048]{2,1,0:T(8,128)(2,1)} async-done(((bf16[4,128,2048]{2,1,0:T(8,128)(2,1)}), bf16[4,128,2048]{2,1,0:T(8,128)(2,1)}, u32[]{:S(2)}, u32[]{:S(2)}) %all-to-all-start.2) | async-done | bytes 2097184 | tf_op jit(solution)/shard_map/all_to_all | solution.py:1023
  328.3 27.7 %expert.3 = (bf16[512,2048]{1,0:T(8,128)(2,1)}, bf16[512,2048]{1,0:T(8,128)(2,1)}, bf16[512,1408]{1,0:T(8,128)(2,1)}, bf16[512,1408]{1,0:T(8,128)(2,1)}, bf16[512,1408]{1,0:T(8,128)(2,1)}) custom-call(bf16[512,2048]{1,0:T(8,128)(2,1)} %bitcast.32.x_ref, bf16[512,2048]{1,0:T(8,128)(2,1)} %bitcast.173, bf16[2,2048,1408]{2,1,0:T(8,128)(2,1)} %gate_hbm.3, ...), custom_call_target="tpu_custom_call" | custom-call | tf_op jit(solution)/shard_map/expert/pallas_call | solution.py:477
  362.0 27.6 %expert.2 = (bf16[512,2048]{1,0:T(8,128)(2,1)}, bf16[512,2048]{1,0:T(8,128)(2,1)}, bf16[512,1408]{1,0:T(8,128)(2,1)}, bf16[512,1408]{1,0:T(8,128)(2,1)}, bf16[512,1408]{1,0:T(8,128)(2,1)}) custom-call(bf16[512,2048]{1,0:T(8,128)(2,1)} %bitcast.171, bf16[512,2048]{1,0:T(8,128)(2,1)} %bitcast.169, bf16[2,2048,1408]{2,1,0:T(8,128)(2,1)} %gate_hbm.3, ...), custom_call_target="tpu_custom_call" | custom-call | tf_op jit(solution)/shard_map/expert/pallas_call | solution.py:477
  393.8 11.5 %expert_weights.4 = (bf16[1,2048,352]{2,1,0:T(8,128)(2,1)}, bf16[1,2048,352]{2,1,0:T(8,128)(2,1)}, bf16[1,352,2048]{2,1,0:T(8,128)(2,1)}) custom-call(bf16[1024,2048]{1,0:T(8,128)(2,1)} %get-tuple-element.217.x_ref, bf16[1024,2048]{1,0:T(8,128)(2,1)} %arrange.11.x_ref.c_ref, bf16[1024,352]{1,0:T(8,128)(2,1)} %get-tuple-element.206.h_ref.refs_4_, ...), custom_call_target="tpu_custom_call" | custom-call | tf_op jit(solution)/shard_map/expert_weights/pallas_call | solution.py:541
  405.2 14.9 %expert_weights.3 = (f32[2,2048,1408]{2,1,0:T(8,128)}, f32[2,2048,1408]{2,1,0:T(8,128)}, f32[2,1408,2048]{2,1,0:T(8,128)}) custom-call(bf16[512,2048]{1,0:T(8,128)(2,1)} %bitcast.32.x_ref, bf16[512,2048]{1,0:T(8,128)(2,1)} %bitcast.174, bf16[512,1408]{1,0:T(8,128)(2,1)} %get-tuple-element.211.h_ref, bf16[512,1408]{1,0:T(8,128)(2,1)} %get-tuple-element.212.gg_ref, ...), custom_call_target="tpu_custom_call" | custom-call | tf_op jit(solution)/shard_map/expert_weights/pallas_call | solution.py:541
  443.7 10.3 %collective-permute-start.34 = (bf16[128,2048]{1,0:T(8,128)(2,1)}, bf16[128,2048]{1,0:T(8,128)(2,1)}, u32[]{:S(2)}, u32[]{:S(2)}) collective-permute-start(bf16[128,2048]{1,0:T(8,128)(2,1)} %get-tuple-element.225), channel_id=1, source_target_pairs={{0,2},{1,3},{2,0},{3,1},{4,6},{5,7},{6,4},{7,5},{8,10},{9,11},{10,... | collective-permute-start | bytes 1572872 | tf_op jit(solution)/shard_map/ppermute | solution.py:702
  461.0 15.9 %all-to-all-done.6.refs_2_ = bf16[4,128,2048]{2,1,0:T(8,128)(2,1)S(1)} async-done(((bf16[4,128,2048]{2,1,0:T(8,128)(2,1)}), bf16[4,128,2048]{2,1,0:T(8,128)(2,1)S(1)}, u32[]{:S(2)}, u32[]{:S(2)}) %all-to-all-start.6) | async-done | bytes 2097184 | tf_op jit(solution)/shard_map/all_to_all | solution.py:1023
  483.0 15.0 %expert_weights.5 = (f32[2,2048,1408]{2,1,0:T(8,128)}, f32[2,2048,1408]{2,1,0:T(8,128)}, f32[2,1408,2048]{2,1,0:T(8,128)}) custom-call(bf16[512,2048]{1,0:T(8,128)(2,1)} %bitcast.172, bf16[512,2048]{1,0:T(8,128)(2,1)} %bitcast.170, bf16[512,1408]{1,0:T(8,128)(2,1)} %get-tuple-element.229.h_ref, ...), custom_call_target="tpu_custom_call", output_to_operand_aliasing={{0}: (5, {}), {1}: (6, {}), {2}: (7, {})} | custom-call | tf_op jit(solution)/shard_map/expert_weights/pallas_call | solution.py:541
  555.6 14.0 %attend_back.1 = (bf16[1024,384]{1,0:T(8,128)(2,1)}, bf16[1024,512]{1,0:T(8,128)(2,1)}, f32[1024,576]{1,0:T(8,128)}, f32[1,512]{1,0:T(1,128)}) custom-call(bf16[2,1024,256]{2,1,0:T(8,128)(2,1)} %get-tuple-element.171.q_ref, bf16[2,1024,256]{2,1,0:T(8,128)(2,1)} %get-tuple-element.172.k_ref, bf16[2,1024,128]{2,1,0:T(8,128)(2,1)} %get-tuple-element.173.v_ref, ...), custom_call_target="tpu_custom_call" | custom-call | tf_op jit(solution)/shard_map/attend_back/pallas_call | solution.py:312
  577.0 8.4 %collective-permute-done.43 = bf16[128,2048]{1,0:T(8,128)(2,1)} collective-permute-done((bf16[128,2048]{1,0:T(8,128)(2,1)}, bf16[128,2048]{1,0:T(8,128)(2,1)}, u32[]{:S(2)}, u32[]{:S(2)}) %collective-permute-start.43) | collective-permute-done | bytes 524320 | tf_op jit(solution)/shard_map/ppermute | solution.py:702
  600.8 11.6 %collective-permute-start.45 = (bf16[128,2048]{1,0:T(8,128)(2,1)}, bf16[128,2048]{1,0:T(8,128)(2,1)}, u32[]{:S(2)}, u32[]{:S(2)}) collective-permute-start(bf16[128,2048]{1,0:T(8,128)(2,1)} %get-tuple-element.259), channel_id=1, source_target_pairs={{0,2},{1,3},{2,0},{3,1},{4,6},{5,7},{6,4},{7,5},{8,10},{9,11},{10,... | collective-permute-start | bytes 1572872 | tf_op jit(solution)/shard_map/ppermute | solution.py:702
  616.0 13.1 %collective-permute-done.54.refs_2_ = bf16[128,2048]{1,0:T(8,128)(2,1)} collective-permute-done((bf16[128,2048]{1,0:T(8,128)(2,1)}, bf16[128,2048]{1,0:T(8,128)(2,1)}, u32[]{:S(2)}, u32[]{:S(2)}) %collective-permute-start.54) | collective-permute-done | bytes 524320 | tf_op jit(solution)/shard_map/ppermute | solution.py:702
  690.9 14.7 %collective-permute-done.50 = bf16[128,2048]{1,0:T(8,128)(2,1)} collective-permute-done((bf16[128,2048]{1,0:T(8,128)(2,1)}, bf16[128,2048]{1,0:T(8,128)(2,1)}, u32[]{:S(2)}, u32[]{:S(2)}) %collective-permute-start.50) | collective-permute-done | bytes 524320 | tf_op jit(solution)/shard_map/ppermute | solution.py:702
  705.5 17.3 %collective-permute-done.61.refs_2_ = bf16[128,576]{1,0:T(8,128)(2,1)S(1)} collective-permute-done((bf16[128,576]{1,0:T(8,128)(2,1)}, bf16[128,576]{1,0:T(8,128)(2,1)S(1)}, u32[]{:S(2)}, u32[]{:S(2)}) %collective-permute-start.61) | collective-permute-done | bytes 147488 | tf_op jit(solution)/shard_map/ppermute | solution.py:702
  (446 shorter events, 374.7 us)
Async XLA Ops:
  7.2 90.3 %all-gather.5.cloned.1.call-start = ((), (), s32[]{:S(2)}) async-start(), calls=%async_computation.13 | async-start | bytes 2621440 | tf_op jit(solution)/shard_map/all_gather | solution.py:848
  10.0 252.7 %all-gather.11.cloned.1.call-start = ((), (), s32[]{:S(2)}) async-start(), calls=%async_computation.16 | async-start | bytes 1802240 | tf_op jit(solution)/shard_map/all_gather | solution.py:873
  31.0 48.1 %collective-permute-start.5 = (bf16[128,2048]{1,0:T(8,128)(2,1)S(1)}, bf16[128,2048]{1,0:T(8,128)(2,1)}, u32[]{:S(2)}, u32[]{:S(2)}) collective-permute-start(bf16[128,2048]{1,0:T(8,128)(2,1)S(1)} %copy-done.7), channel_id=1, source_target_pairs={{0,6},{1,7},{2,4},{3,5},{4,2},{5,3},{6,0},{7,1},{8,14},{9,15},{10,... | collective-permute-start | bytes 1572872 | tf_op jit(solution)/shard_map/ppermute | solution.py:702
  36.2 42.6 %collective-permute-start.3 = (bf16[128,2048]{1,0:T(8,128)(2,1)S(1)}, bf16[128,2048]{1,0:T(8,128)(2,1)S(1)}, u32[]{:S(2)}, u32[]{:S(2)}) collective-permute-start(bf16[128,2048]{1,0:T(8,128)(2,1)S(1)} %copy-done.7), channel_id=1, source_target_pairs={{0,4},{1,5},{2,6},{3,7},{4,0},{5,1},{6,2},{7,3},{8,12},{9,13},{10,... | collective-permute-start | bytes 1572872 | tf_op jit(solution)/shard_map/ppermute | solution.py:702
  79.0 183.7 %all-gather.7.cloned.1.call-start = ((), (), s32[]{:S(2)}) async-start(), calls=%async_computation.14 | async-start | bytes 1966080 | tf_op jit(solution)/shard_map/all_gather | solution.py:871
  117.3 52.9 %collective-permute-start.17 = (bf16[1024,512]{1,0:T(8,128)(2,1)}, bf16[1024,512]{1,0:T(8,128)(2,1)S(1)}, u32[]{:S(2)}, u32[]{:S(2)}) collective-permute-start(bf16[1024,512]{1,0:T(8,128)(2,1)} %constant_dynamic-update-slice_fusion.1.refs_0_), channel_id=1, source_target_pairs={{0,8},{8,0},{16,24},{24,16},{1,9},{9,1},{17,25},{25,17},{2,10},{10... | collective-permute-start | bytes 3145736 | tf_op jit(solution)/shard_map/ppermute | solution.py:702
  118.8 52.8 %collective-permute-start.18 = (bf16[1024,512]{1,0:T(8,128)(2,1)}, bf16[1024,512]{1,0:T(8,128)(2,1)S(1)}, u32[]{:S(2)}, u32[]{:S(2)}) collective-permute-start(bf16[1024,512]{1,0:T(8,128)(2,1)} %constant_dynamic-update-slice_fusion.1.refs_0_), channel_id=1, source_target_pairs={{0,16},{8,24},{16,0},{24,8},{1,17},{9,25},{17,1},{25,9},{2,18},{10... | collective-permute-start | bytes 3145736 | tf_op jit(solution)/shard_map/ppermute | solution.py:702
  123.1 43.2 %collective-permute-start.20 = (bf16[128,2048]{1,0:T(8,128)(2,1)S(1)}, bf16[128,2048]{1,0:T(8,128)(2,1)}, u32[]{:S(2)}, u32[]{:S(2)}) collective-permute-start(bf16[128,2048]{1,0:T(8,128)(2,1)S(1)} %copy-done.11), channel_id=1, source_target_pairs={{0,4},{1,5},{2,6},{3,7},{4,0},{5,1},{6,2},{7,3},{8,12},{9,13},{10,... | collective-permute-start | bytes 1572872 | tf_op jit(solution)/shard_map/ppermute | solution.py:702
  123.1 43.2 %collective-permute-start.19 = (bf16[128,2048]{1,0:T(8,128)(2,1)S(1)}, bf16[128,2048]{1,0:T(8,128)(2,1)}, u32[]{:S(2)}, u32[]{:S(2)}) collective-permute-start(bf16[128,2048]{1,0:T(8,128)(2,1)S(1)} %copy-done.11), channel_id=1, source_target_pairs={{0,2},{1,3},{2,0},{3,1},{4,6},{5,7},{6,4},{7,5},{8,10},{9,11},{10,... | collective-permute-start | bytes 1572872 | tf_op jit(solution)/shard_map/ppermute | solution.py:702
  196.6 70.7 %collective-permute-start.24 = (bf16[1024,2048]{1,0:T(8,128)(2,1)}, bf16[1024,2048]{1,0:T(8,128)(2,1)}, u32[]{:S(2)}, u32[]{:S(2)}) collective-permute-start(bf16[1024,2048]{1,0:T(8,128)(2,1)} %arrange.9.we_ref), channel_id=1, source_target_pairs={{0,1},{1,0},{2,3},{3,2},{4,5},{5,4},{6,7},{7,6},{8,9},{9,8},{10,11... | collective-permute-start | bytes 12582920 | tf_op jit(solution)/shard_map/ppermute | solution.py:702
  212.2 45.0 %all-to-all-start = ((bf16[4,128,2048]{2,1,0:T(8,128)(2,1)}), bf16[4,128,2048]{2,1,0:T(8,128)(2,1)S(1)}, u32[]{:S(2)}, u32[]{:S(2)}) async-start(bf16[4,128,2048]{2,1,0:T(8,128)(2,1)} %get-tuple-element.186), calls=%async_computation | async-start | bytes 4194304 | tf_op jit(solution)/shard_map/all_to_all | solution.py:1023
  216.0 46.7 %all-gather.9.cloned.1.call-start = ((), (), s32[]{:S(2)}) async-start(), calls=%async_computation.15 | async-start | bytes 1966080 | tf_op jit(solution)/shard_map/all_gather | solution.py:872
  393.8 276.0 %reduce-scatter.10.cloned.1.call-start = ((), (), s32[]{:S(2)}) async-start(), calls=%async_computation.19 | async-start | bytes 1802240 | tf_op jit(solution)/shard_map/reduce_scatter | solution.py:785
  443.7 228.0 %reduce-scatter.8.cloned.1.call-start = ((), (), s32[]{:S(2)}) async-start(), calls=%async_computation.18 | async-start | bytes 1966080 | tf_op jit(solution)/shard_map/reduce_scatter | solution.py:785
  443.7 54.4 %collective-permute-start.34 = (bf16[128,2048]{1,0:T(8,128)(2,1)}, bf16[128,2048]{1,0:T(8,128)(2,1)}, u32[]{:S(2)}, u32[]{:S(2)}) collective-permute-start(bf16[128,2048]{1,0:T(8,128)(2,1)} %get-tuple-element.225), channel_id=1, source_target_pairs={{0,2},{1,3},{2,0},{3,1},{4,6},{5,7},{6,4},{7,5},{8,10},{9,11},{10,... | collective-permute-start | bytes 1572872 | tf_op jit(solution)/shard_map/ppermute | solution.py:702
  454.0 44.0 %collective-permute-start.36 = (bf16[128,2048]{1,0:T(8,128)(2,1)}, bf16[128,2048]{1,0:T(8,128)(2,1)}, u32[]{:S(2)}, u32[]{:S(2)}) collective-permute-start(bf16[128,2048]{1,0:T(8,128)(2,1)} %get-tuple-element.239), channel_id=1, source_target_pairs={{0,6},{1,7},{2,4},{3,5},{4,2},{5,3},{6,0},{7,1},{8,14},{9,15},{10,... | collective-permute-start | bytes 1572872 | tf_op jit(solution)/shard_map/ppermute | solution.py:702
  456.2 45.4 %collective-permute-start.35 = (bf16[128,2048]{1,0:T(8,128)(2,1)}, bf16[128,2048]{1,0:T(8,128)(2,1)}, u32[]{:S(2)}, u32[]{:S(2)}) collective-permute-start(bf16[128,2048]{1,0:T(8,128)(2,1)} %get-tuple-element.237), channel_id=1, source_target_pairs={{0,4},{1,5},{2,6},{3,7},{4,0},{5,1},{6,2},{7,3},{8,12},{9,13},{10,... | collective-permute-start | bytes 1572872 | tf_op jit(solution)/shard_map/ppermute | solution.py:702
  478.3 51.0 %all-to-all-start.7 = ((bf16[4,128,2048]{2,1,0:T(8,128)(2,1)}), bf16[4,128,2048]{2,1,0:T(8,128)(2,1)}, u32[]{:S(2)}, u32[]{:S(2)}) async-start(bf16[4,128,2048]{2,1,0:T(8,128)(2,1)} %bitcast.176), calls=%async_computation.7 | async-start | bytes 4194304 | tf_op jit(solution)/shard_map/all_to_all | solution.py:1023
  482.8 191.0 %reduce-scatter.6.cloned.1.call-start = ((), (), s32[]{:S(2)}) async-start(), calls=%async_computation.17 | async-start | bytes 1966080 | tf_op jit(solution)/shard_map/reduce_scatter | solution.py:785
  535.7 140.1 %reduce-scatter.14.cloned.1.call-start = ((), (), s32[]{:S(2)}) async-start(), calls=%async_computation.21 | async-start | bytes 655360 | tf_op jit(solution)/shard_map/reduce_scatter | solution.py:785
  614.9 142.5 %reduce-scatter.12.cloned.1.call-start = ((), (), s32[]{:S(2)}) async-start(), calls=%async_computation.20 | async-start | bytes 1966080 | tf_op jit(solution)/shard_map/reduce_scatter | solution.py:785
  615.2 47.4 %collective-permute-start.44 = (bf16[512,2048]{1,0:T(8,128)(2,1)}, bf16[512,2048]{1,0:T(8,128)(2,1)}, u32[]{:S(2)}, u32[]{:S(2)}) collective-permute-start(bf16[512,2048]{1,0:T(8,128)(2,1)} %get-tuple-element.256), channel_id=1, source_target_pairs={{0,1},{1,0},{2,3},{3,2},{4,5},{5,4},{6,7},{7,6},{8,9},{9,8},{10,11... | collective-permute-start | bytes 6291464 | tf_op jit(solution)/shard_map/ppermute | solution.py:702
  665.3 40.2 %collective-permute-start.50 = (bf16[128,2048]{1,0:T(8,128)(2,1)}, bf16[128,2048]{1,0:T(8,128)(2,1)}, u32[]{:S(2)}, u32[]{:S(2)}) collective-permute-start(bf16[128,2048]{1,0:T(8,128)(2,1)} %get-tuple-element.275), channel_id=1, source_target_pairs={{0,4},{1,5},{2,6},{3,7},{4,0},{5,1},{6,2},{7,3},{8,12},{9,13},{10,... | collective-permute-start | bytes 1572872 | tf_op jit(solution)/shard_map/ppermute | solution.py:702
  682.2 40.6 %collective-permute-start.60 = (bf16[128,576]{1,0:T(8,128)(2,1)}, bf16[128,576]{1,0:T(8,128)(2,1)S(1)}, u32[]{:S(2)}, u32[]{:S(2)}) collective-permute-start(bf16[128,576]{1,0:T(8,128)(2,1)} %pad_maximum_fusion.5.refs_0_), channel_id=1, source_target_pairs={{0,2},{1,3},{2,0},{3,1},{4,6},{5,7},{6,4},{7,5},{8,10},{9,11},{10,... | collective-permute-start | bytes 442376 | tf_op jit(solution)/shard_map/ppermute | solution.py:702
  (127 other events, 2005.1 us)
Sparse Core Ops, SparseCore 0:
  10.4 47.8 all-gather.4
  79.1 30.1 all-gather.10
  170.3 33.6 all-gather.6
  218.9 42.2 all-gather.8
  439.5 66.6 reduce-scatter.9
  509.2 28.8 reduce-scatter.7
  541.4 30.8 reduce-scatter.5
  615.0 26.1 reduce-scatter.13
  649.5 29.6 reduce-scatter.11
